TPU v7x, 128 devices: a whole 4x4x4 slice. The times are simulated.
128 devices in a mesh: fsdp: 32 (over y, z, core), dp: 4 (over x).
Axes of the slice: x: 4, y: 4, z: 4, core: 2. Of those that a mesh axis runs over, the one named last changes fastest.
Arguments:
- tokens: bfloat16 [16384, 4096], P(('fsdp', 'dp')), may hold values from -6 to 6
- gain: float32 [4096], replicated, may hold values from 0.5 to 1.5
- tiles: bfloat16 [512, 128, 128], P('fsdp'), may hold values from -0.25 to 0.25
- tile_rows: int32 [512], replicated, may hold values from 0 to 31, as said below
- tile_cols: int32 [512], replicated, may hold values from 0 to 111, as said below
- cotangent: bfloat16 [16384, 14336], P(('fsdp', 'dp')), may hold values from -6 to 6
Outputs:
- projected: bfloat16 [16384, 14336], P(('fsdp', 'dp'))
- token_grad: bfloat16 [16384, 4096], P(('fsdp', 'dp'))
- tile_grad: float32 [512, 128, 128], P('fsdp')
- gain_grad: float32 [4096], replicated
Inputs may be any that keep to these rules, and one draw needn't show every extreme that they name: The pairs (tile_rows[i], tile_cols[i]) are all different. `tile_cols`: pairs with tile_rows as above.
All inputs are finite; a program needn't handle non-finite values.
Results may differ from a plain program's by a relative error of at most 0.0049.
Values may be sent and summed in bfloat16 or wider, within the bound.
No kernel may reach another device: no remote copies, remote signals or barrier semaphores. Data moves between devices by JAX's collectives and lax.ppermute only.
A program may use at most 256 MiB of HBM per device.

v0:
```python
import jax
import jax.numpy as jnp
from jax import lax
from jax.sharding import PartitionSpec as P


def shards(tokens, gain, tiles, tile_rows, tile_cols, cotangent):
    count = tokens.shape[0]
    width = tokens.shape[1]
    tile = tiles.shape[1]
    row_blocks = width // tile
    col_blocks = cotangent.shape[1] // tile
    x32 = tokens.astype(jnp.float32)
    scale = lax.rsqrt(jnp.mean(x32 * x32, axis=-1, keepdims=True) + 1e-05)
    normed = (x32 * scale * gain).astype(jnp.bfloat16)
    xblocks = normed.reshape(count, row_blocks, tile)
    gblocks = cotangent.reshape(count, col_blocks, tile)
    piece = lax.all_gather(tiles, "fsdp", axis=0, tiled=True)
    rows = tile_rows
    cols = tile_cols
    xsel = jnp.take(xblocks, rows, axis=1)
    gsel = jnp.take(gblocks, cols, axis=1)
    forward = jnp.einsum("tkj,kjm->tkm", xsel, piece, preferred_element_type=jnp.float32)
    backward = jnp.einsum("tkm,kjm->tkj", gsel, piece, preferred_element_type=jnp.float32)
    stacked = jnp.stack([forward, backward], axis=0)
    outsum = jnp.zeros((count, col_blocks, tile), jnp.float32).at[:, tile_cols].add(stacked[0])
    back = jnp.zeros((count, row_blocks, tile), jnp.float32).at[:, tile_rows].add(stacked[1])
    projected = outsum.reshape(count, col_blocks * tile).astype(jnp.bfloat16)
    dnormed = back.reshape(count, width)
    gain_grad = lax.psum(jnp.sum(dnormed * x32 * scale, axis=0), ("fsdp", "dp"))
    inner = jnp.mean(x32 * gain * dnormed, axis=-1, keepdims=True)
    token_grad = (scale * gain * dnormed - x32 * scale**3 * inner).astype(jnp.bfloat16)
    group = tiles.shape[0]
    number = tiles.shape[0] * lax.axis_size("fsdp")

    def group_terms(first):
        rows = lax.dynamic_slice_in_dim(tile_rows, first, group, 0)
        cols = lax.dynamic_slice_in_dim(tile_cols, first, group, 0)
        xsel = jnp.take(xblocks, rows, axis=1)
        gsel = jnp.take(gblocks, cols, axis=1)
        return jnp.einsum("tkj,tkm->kjm", xsel, gsel, preferred_element_type=jnp.float32)

    firsts = group * jnp.arange(number // group, dtype=jnp.int32)
    result = lax.map(group_terms, firsts)
    owned = lax.psum_scatter(
        result.reshape(number, tile, tile), "fsdp", scatter_dimension=0, tiled=True
    )
    tile_grad = lax.psum(owned, "dp")
    return (projected, token_grad, tile_grad, gain_grad)


def solution(mesh):
    placed = (
        P(("fsdp", "dp"), None),
        P(),
        P("fsdp", None, None),
        P(),
        P(),
        P(("fsdp", "dp"), None),
    )
    return jax.shard_map(
        shards,
        mesh=mesh,
        in_specs=placed,
        out_specs=(P(("fsdp", "dp"), None), P(("fsdp", "dp"), None), P("fsdp", None, None), P()),
        check_vma=False,
    )
```

profile of v0, /device:TPU:0, one launch (start us, length us, event | category | flops | bytes accessed | tf_op | source)
XLA Modules:
  0.0 813.5 jit_solution(1176212291491571832)
XLA Ops:
  8.0 6.1 copy.35
  14.0 6.0 copy.36
  21.7 16.3 %gather_fusion.3 = bf16[512,128,128]{2,1,0:T(8,128)(2,1)} fusion(bf16[128,112,128]{2,0,1:T(8,128)(2,1)} %copy.36, s32[1024]{0:T(1024)S(1)} %pad_clamp_fusion.2), kind=kCustom, calls=%fused_computation.3 | custom fusion | bytes 33556480 | tf_op jit(solution)/shard_map/jit(_take)/gather | solution.py:22
  38.6 46.8 %all-gather.2.cloned.1.call-done = bf16[512,128,128]{2,1,0:T(8,128)(2,1)} async-done(((bf16[16,128,128]{2,1,0:T(8,128)(2,1)}), bf16[512,128,128]{2,1,0:T(8,128)(2,1)}) %all-gather.2.cloned.1.call-update) | async-done | bytes 16777232 | tf_op jit(solution)/shard_map/all_gather | solution.py:18
  85.4 28.2 %fusion.9 = f32[512,128,128]{2,1,0:T(8,128)} fusion(bf16[512,128,128]{2,1,0:T(8,128)(2,1)} %all-gather.2.cloned.1.call-done, bf16[512,128,128]{2,1,0:T(8,128)(2,1)} %gather_fusion.3, pred[512]{0:T(512)(128)(4,1)S(1)} %compare_and_fusion.2), kind=kOutput, calls=%fused_computation.22 | convolution fusion | flops 2155872256 | bytes 67109376 | tf_op jit(solution)/shard_map/tkm,kjm->tkj/dot_general | solution.py:24
  113.8 66.1 %scatter_fusion.1 = f32[128,32,128]{2,0,1:T(8,128)S(1)} fusion(f32[128,32,128]{2,0,1:T(8,128)S(1)} %broadcast_in_dim.69, s32[512]{0:T(512)S(1)} %compare_select_fusion.2, f32[512,128,128]{2,1,0:T(8,128)} %fusion.9), kind=kCustom, calls=%fused_computation.5 | custom fusion | flops 8388608 | bytes 100665344 | tf_op jit(solution)/shard_map/scatter-add | solution.py:27
  184.3 2.8 fusion.24
  187.8 237.1 %while.10 = (s32[]{:T(128)}, f32[32,16,128,128]{3,2,1,0:T(8,128)}, s32[32]{0:T(128)S(1)}, s32[512]{0:T(512)S(1)}, bf16[128,32,128]{2,0,1:T(8,128)(2,1)S(1)}, /*i...) while((s32[]{:T(128)}, f32[32,16,128,128]{3,2,1,0:T(8,128)}, ...), condition=%wide.region_5.6_spmd, body=%wide.region_4.5_spmd.sunk | while | flops 67635392 | bytes 4203735 | solution.py:44
  190.4 2.7 gather_fusion
  197.8 2.7 gather_fusion
  205.3 2.7 gather_fusion
  212.7 2.7 gather_fusion
  220.1 2.7 gather_fusion
  227.5 2.7 gather_fusion
  234.9 2.7 gather_fusion
  242.3 2.7 gather_fusion
  249.7 2.7 gather_fusion
  257.2 2.7 gather_fusion
  264.6 2.7 gather_fusion
  272.0 2.7 gather_fusion
  279.3 2.7 gather_fusion
  286.8 2.7 gather_fusion
  294.2 2.7 gather_fusion
  301.6 2.7 gather_fusion
  309.0 2.7 gather_fusion
  316.4 2.7 gather_fusion
  323.8 2.7 gather_fusion
  331.2 2.7 gather_fusion
  338.6 2.7 gather_fusion
  346.0 2.7 gather_fusion
  353.4 2.7 gather_fusion
  360.9 2.7 gather_fusion
  368.2 2.7 gather_fusion
  375.7 2.7 gather_fusion
  383.1 2.7 gather_fusion
  390.5 2.7 gather_fusion
  397.9 2.7 gather_fusion
  412.7 2.7 gather_fusion
  420.1 2.7 gather_fusion
  425.2 14.9 %gather_fusion.2 = bf16[512,128,128]{2,1,0:T(8,128)(2,1)} fusion(bf16[128,32,128]{2,0,1:T(8,128)(2,1)S(1)} %get-tuple-element.182, s32[1024]{0:T(1024)S(1)} %pad_clamp_fusion.3), kind=kCustom, calls=%fused_computation.2 | custom fusion | bytes 33556480 | tf_op jit(solution)/shard_map/jit(_take)/gather | solution.py:21
  440.1 149.4 %reduce-scatter.2.cloned.1.call-done = f32[16,128,128]{2,1,0:T(8,128)} async-done(((f32[512,128,128]{2,1,0:T(8,128)}), f32[16,128,128]{2,1,0:T(8,128)}) %reduce-scatter.2.cloned.1.call-update) | async-done | bytes 1048592 | tf_op jit(solution)/shard_map/reduce_scatter | solution.py:45
  589.5 24.5 %fusion.11 = f32[512,128,128]{2,1,0:T(8,128)} fusion(bf16[512,128,128]{2,1,0:T(8,128)(2,1)} %all-gather.2.cloned.1.call-done, bf16[512,128,128]{2,1,0:T(8,128)(2,1)} %gather_fusion.2, pred[512]{0:T(512)(128)(4,1)S(1)} %compare_and_fusion.3), kind=kOutput, calls=%fused_computation.24 | convolution fusion | flops 2155872256 | bytes 67109376 | tf_op jit(solution)/shard_map/tkj,kjm->tkm/dot_general | solution.py:23
  614.0 3.8 broadcast_in_dim.64
  617.8 103.1 %scatter_fusion = f32[128,112,128]{2,0,1:T(8,128)} fusion(f32[128,112,128]{2,0,1:T(8,128)} %broadcast_in_dim.64, s32[512]{0:T(512)S(1)} %compare_select_fusion.3, f32[512,128,128]{2,1,0:T(8,128)} %fusion.11), kind=kCustom, calls=%fused_computation.4 | custom fusion | flops 8388608 | bytes 100665344 | tf_op jit(solution)/shard_map/scatter-add | solution.py:26
  721.0 5.8 convert_element_type.17
  726.8 6.1 copy.34
  732.9 6.1 copy.40
  740.3 64.4 %psum.15 = f32[4096]{0:T(1024)} all-reduce(f32[4096]{0:T(1024)S(1)} %get-tuple-element.68), channel_id=1, replica_groups=mesh['fsdp'=32,'dp'=4] {'fsdp','dp'}, use_global_device_ids=true, to_apply=%region_9.10 | all-reduce | flops 4096 | bytes 32768 | tf_op jit(solution)/shard_map/psum | solution.py:30
  (226 shorter events, 102.7 us)
Async XLA Ops:
  7.2 14.5 %copy-start.2 = (s32[512]{0:T(512)S(1)}, s32[512]{0:T(512)}, u32[]{:S(2)}) copy-start(s32[512]{0:T(512)} %param.12) | copy-start | bytes 6148
  7.2 78.2 %all-gather.2.cloned.1.call-start = ((), (), s32[]{:S(2)}) async-start(), calls=%async_computation.1 | async-start | bytes 17301504 | tf_op jit(solution)/shard_map/all_gather | solution.py:18
  7.9 581.6 %reduce-scatter.2.cloned.1.call-start = ((), (), s32[]{:S(2)}) async-start(), calls=%async_computation.2 | async-start | bytes 34603008 | tf_op jit(solution)/shard_map/reduce_scatter | solution.py:45
  21.7 16.9 %copy-start.3 = (s32[512]{0:T(512)S(1)}, s32[512]{0:T(512)}, u32[]{:S(2)}) copy-start(s32[512]{0:T(512)} %param.11) | copy-start | bytes 6148
  113.8 68.0 %copy-start.1 = (f32[4096]{0:T(1024)S(1)}, f32[4096]{0:T(1024)}, u32[]{:S(2)}) copy-start(f32[4096]{0:T(1024)} %param.9) | copy-start | bytes 49156
  424.9 379.7 %all-reduce.2.cloned.1.call-start = ((), (), s32[]{:S(2)}) async-start(), calls=%async_computation.3 | async-start | bytes 2097152 | tf_op jit(solution)/shard_map/psum | solution.py:48
  721.0 18.0 %copy-start = (bf16[128,4096]{0,1:T(8,128)(2,1)S(1)}, bf16[128,4096]{0,1:T(8,128)(2,1)}, u32[]{:S(2)}) copy-start(bf16[128,4096]{0,1:T(8,128)(2,1)} %get-tuple-element.90) | copy-start | bytes 3145732
Sparse Core Ops, SparseCore 0:
  10.3 75.0 all-gather.1
  425.0 164.4 reduce-scatter.1
  592.0 45.1 all-reduce.1
where the time goes:
time: 819 us; the launch traced here: 813 us
  waiting for transfers between devices  197 us (24%)
  local copies, waits for them, and re-layouts  192 us (23%)
  other arithmetic  184 us (22%)
  matrix products  98.3 us (12%)
  blocking collectives  64.4 us (8%)
  loops' own time  63.1 us (8%)
  between operations  13.9 us (2%)
    reduce_scatter x1, waiting for transfers between devices, shards(): lax.psum_scatter(result.reshape(number, tile, tile), 'fsdp', scatter_dime...  149 us
    scatter-add x1, other arithmetic, shards(): jnp.zeros((count, col_blocks, tile), jnp.float32).at[:, tile_cols]  103 us
    gather x32, local copies, waits for them, and re-layouts, group_terms(): gsel = jnp.take(gblocks, cols, axis=1)  85.9 us
    scatter-add x1, other arithmetic, shards(): jnp.zeros((count, row_blocks, tile), jnp.float32).at[:, tile_rows]  66.1 us
    psum x1, blocking collectives, shards(): gain_grad = lax.psum(jnp.sum(dnormed * x32 * scale, axis=0), ('fsdp', 'dp'))  64.4 us
    another operation x1, loops' own time, shards(): result = lax.map(group_terms, firsts)  63.1 us
    all_gather x1, waiting for transfers between devices, shards(): piece = lax.all_gather(tiles, 'fsdp', axis=0, tiled=True)  46.8 us
    dot_general x32, matrix products, group_terms(): jnp.einsum('tkj,tkm->kjm', xsel, gsel, preferred_element_type=jnp.float32)  45.6 us
  transfers between devices with their start and end apart: 3, of which 2 were waited for; matrix products, arithmetic and copies ran while one was open for 24% of the time, Pallas kernels for 0%

commit v1 on v0

v1 whole, which is shorter than its diff:
```python
import jax
import jax.numpy as jnp
from jax import lax
from jax.experimental import pallas as pl
from jax.experimental.pallas import tpu as pltpu
from jax.sharding import Mesh, PartitionSpec as P

BF = jnp.bfloat16
F4 = jnp.float32
T = 128
ALL = ("y", "z", "c", "x")


def params(limit=56):
    return pltpu.CompilerParams(vmem_limit_bytes=limit * 1024 * 1024)


def whole(shape):
    zeros = (0,) * len(shape)
    return pl.BlockSpec(shape, lambda *_: zeros, pipeline_mode=pl.Buffered(1))


def dot(a, b):
    return jnp.dot(a, b, preferred_element_type=F4)


def dot_t(a, b):
    return lax.dot_general(a, b, (((1,), (1,)), ((), ())), preferred_element_type=F4)


def cols_at(index):
    return pl.ds(pl.multiple_of(index * T, T), T)


def norm_kernel(own_ref, other_ref, gain_ref, normed_ref, turned_ref, scale_ref):
    count, width = own_ref.shape
    blocks = width // T
    for half, ref in enumerate((own_ref, other_ref)):
        def squares(b, total):
            x = ref[:, cols_at(b)].astype(F4)
            return total + x * x

        total = lax.fori_loop(0, blocks, squares, jnp.zeros((count, T), F4), unroll=4)
        mean = jnp.sum(total, axis=1, keepdims=True) / width
        scale = lax.rsqrt(mean + 1e-05)
        if half == 0:
            scale_ref[...] = jnp.broadcast_to(scale, (count, T))

        def fill(b, carry):
            x = ref[:, cols_at(b)].astype(F4)
            normed = (x * scale * gain_ref[:, cols_at(b)]).astype(BF)
            if half == 0:
                normed_ref[:, cols_at(b)] = normed
            turned_ref[b, :, half * count : (half + 1) * count] = normed.T
            return carry

        lax.fori_loop(0, blocks, fill, 0, unroll=4)


def norm(own, other, gain):
    count, width = own.shape
    blocks = width // T
    return pl.pallas_call(
        norm_kernel,
        out_shape=(
            jax.ShapeDtypeStruct((count, width), BF),
            jax.ShapeDtypeStruct((blocks, T, 2 * count), BF),
            jax.ShapeDtypeStruct((count, T), F4),
        ),
        compiler_params=params(),
        cost_estimate=pl.CostEstimate(flops=8 * count * width, bytes_accessed=10 * count * width, transcendentals=0),
        name="norm",
    )(own, other, gain)


def grad_kernel(first, per, step, rows, cols, pos, turned_ref, own_ref, other_ref, out_ref):
    base = pl.program_id(0) * step
    y, z, c = pos[0], pos[1], pos[2]

    def one(k, carry):
        i = base + k
        major, minor, t = i // (4 * per), (i // per) % 4, i % per
        if first == "y":
            place = lax.rem(y + major, 4) * 4 + lax.rem(z + minor, 4)
        else:
            place = lax.rem(y + minor, 4) * 4 + lax.rem(z + major, 4)
        index = place * 32 + c * 16 + (0 if first == "y" else 16 - per) + t
        r, q = rows[index], cols[index]
        left = turned_ref[r]
        right = jnp.concatenate([own_ref[:, cols_at(q)], other_ref[:, cols_at(q)]], axis=0)
        out_ref[k] = dot(left, right).astype(BF)
        return carry

    lax.fori_loop(0, step, one, 0, unroll=8)


def grads(first, per, rows, cols, pos, turned, own, other):
    total, step = 16 * per, 16
    return pl.pallas_call(
        lambda *refs: grad_kernel(first, per, step, *refs),
        out_shape=jax.ShapeDtypeStruct((total, T, T), BF),
        grid_spec=pltpu.PrefetchScalarGridSpec(
            num_scalar_prefetch=3,
            grid=(total // step,),
            in_specs=[whole(turned.shape), whole(own.shape), whole(other.shape)],
            out_specs=pl.BlockSpec((step, T, T), lambda i, *_: (i, 0, 0)),
        ),
        compiler_params=params(),
        cost_estimate=pl.CostEstimate(
            flops=total * T * T * 512, bytes_accessed=2 * total * T * T + 10 * 2**20, transcendentals=0
        ),
        name="grads_" + first,
    )(rows, cols, pos, turned, own, other)


def project_kernel(
    step, rows, cols, tiles_ref, x_ref, normed_ref, scale_ref, gain_ref, g_ref,
    projected_ref, token_grad_ref, gain_ref_out, out_acc, back_acc,
):
    s = pl.program_id(0)
    count, width = x_ref.shape
    blocks = width // T

    @pl.when(s == 0)
    def _():
        out_acc[...] = jnp.zeros_like(out_acc)
        back_acc[...] = jnp.zeros_like(back_acc)

    def one(k, carry):
        r, q = rows[s * step + k], cols[s * step + k]
        weight = tiles_ref[k]
        out_acc[:, cols_at(q)] += dot(normed_ref[:, cols_at(r)], weight)
        back_acc[:, cols_at(r)] += dot_t(g_ref[:, cols_at(q)], weight)
        return carry

    lax.fori_loop(0, step, one, 0, unroll=8)

    @pl.when(s == pl.num_programs(0) - 1)
    def _():
        scale = scale_ref[...]

        def products(b, total):
            at = cols_at(b)
            x = x_ref[:, at].astype(F4)
            back = back_acc[:, at]
            gain_ref_out[:, at] = jnp.sum(back * x * scale, axis=0, keepdims=True)
            return total + x * gain_ref[:, at] * back

        total = lax.fori_loop(0, blocks, products, jnp.zeros((count, T), F4), unroll=2)
        inner = jnp.sum(total, axis=1, keepdims=True) / width
        cubed = scale * scale * scale * inner

        def finish(b, carry):
            at = cols_at(b)
            x = x_ref[:, at].astype(F4)
            token_grad_ref[:, at] = (scale * gain_ref[:, at] * back_acc[:, at] - x * cubed).astype(BF)
            return carry

        lax.fori_loop(0, blocks, finish, 0, unroll=2)

        def write(b, carry):
            projected_ref[:, cols_at(b)] = out_acc[:, cols_at(b)].astype(BF)
            return carry

        lax.fori_loop(0, g_ref.shape[1] // T, write, 0, unroll=4)


def project(rows, cols, tiles, x, normed, scale, gain, g):
    number, step = tiles.shape[0], 32
    count, width = x.shape
    return pl.pallas_call(
        lambda *refs: project_kernel(step, *refs),
        out_shape=(
            jax.ShapeDtypeStruct(g.shape, BF),
            jax.ShapeDtypeStruct(x.shape, BF),
            jax.ShapeDtypeStruct((1, width), F4),
        ),
        grid_spec=pltpu.PrefetchScalarGridSpec(
            num_scalar_prefetch=2,
            grid=(number // step,),
            in_specs=[pl.BlockSpec((step, T, T), lambda i, *_: (i, 0, 0))]
            + [whole(a.shape) for a in (x, normed, scale, gain, g)],
            out_specs=[whole(g.shape), whole(x.shape), whole((1, width))],
            scratch_shapes=[pltpu.VMEM(g.shape, F4), pltpu.VMEM(x.shape, F4)],
        ),
        compiler_params=params(),
        cost_estimate=pl.CostEstimate(
            flops=number * T * T * count * 4, bytes_accessed=2 * number * T * T + 10 * 2**20, transcendentals=0
        ),
        name="project",
    )(rows, cols, tiles, x, normed, scale, gain, g)


def ring(piece, axis, shift):
    return lax.ppermute(piece, axis, [(i, (i + shift) % 4) for i in range(4)])


def stage(pieces, axis):
    got = [ring(pieces[j], axis, j) for j in (1, 3, 2)]
    return sum((p.astype(F4) for p in got), pieces[0].astype(F4))


def shards(tokens, gain, tiles, tile_rows, tile_cols, cotangent):
    gain2 = gain.reshape(1, -1)
    pos = jnp.stack([lax.axis_index(a).astype(jnp.int32) for a in ("y", "z", "c", "x")])
    piece = lax.all_gather(tiles, ("y", "z", "c"), axis=0, tiled=True)
    swap = [(0, 1), (1, 0)]
    tokens_other = lax.ppermute(tokens, "c", swap)
    g_other = lax.ppermute(cotangent, "c", swap)
    normed, turned, scale = norm(tokens, tokens_other, gain2)
    sums = []
    for first, second in (("y", "z"), ("z", "y")):
        part = grads(first, 8, tile_rows, tile_cols, pos, turned, cotangent, g_other)
        part = part.reshape(4, 32, T, T)
        mid = stage([part[j] for j in range(4)], first).astype(BF)
        mid = mid.reshape(4, 8, T, T)
        sums.append(stage([mid[j] for j in range(4)], second))
    projected, token_grad, gain_part = project(
        tile_rows, tile_cols, piece, tokens, normed, scale, gain2, cotangent
    )
    owned = jnp.concatenate(sums, axis=0)
    sent = owned.astype(BF)
    one, three, two = (ring(sent, "x", j).astype(F4) for j in (1, 3, 2))
    tile_grad = (sent.astype(F4) + two) + (one + three)
    gains = lax.all_gather(gain_part.reshape(1, -1, T), ALL, axis=0, tiled=True)
    gain_grad = jnp.sum(gains, axis=0).reshape(-1)
    return (projected, token_grad, tile_grad, gain_grad)


def solution(mesh):
    grid = Mesh(mesh.devices.reshape(4, 4, 2, 4), ALL)
    owners = ("y", "z", "c")
    placed = (P(ALL, None), P(), P(owners, None, None), P(), P(), P(ALL, None))
    return jax.shard_map(
        shards,
        mesh=grid,
        in_specs=placed,
        out_specs=(P(ALL, None), P(ALL, None), P(owners, None, None), P()),
        check_vma=False,
    )
```

time: 819 us -> 262 us (0.32)
  local copies, waits for them, and re-layouts: 192 us -> 6.48 us
  other arithmetic: 184 us -> 8.49 us
  matrix products: 98.3 us -> 0 us
  Pallas kernels: 0 us -> 67.6 us
  blocking collectives: 64.4 us -> 0 us
  waiting for transfers between devices: 197 us -> 133 us
  loops' own time: 63.1 us -> 0 us
  starting transfers between devices: 0.3 us -> 30 us
    scatter-add x2 -> x0, other arithmetic: 169 us -> none  [the longest x1 103 us: shards(): jnp.zeros((count, col_blocks, tile), jnp.float32).at[:, tile_cols]]
    reduce_scatter x1 -> x0, waiting for transfers between devices: 149 us -> none  [shards(): lax.psum_scatter(result.reshape(number, tile, tile), 'fsdp', scatter_dime...]
    gather x66 -> x0, local copies, waits for them, and re-layouts: 138 us -> none  [the longest x32 85.9 us: group_terms(): gsel = jnp.take(gblocks, cols, axis=1)]
    dot_general x34 -> x0, matrix products: 98.3 us -> none  [the longest x32 45.6 us: group_terms(): jnp.einsum('tkj,tkm->kjm', xsel, gsel, preferred_element_type=jnp.float32)]
    ppermute x0 -> x17, waiting for transfers between devices: none -> 71.4 us  [the longest x15 64.8 us: ring(): return lax.ppermute(piece, axis, [(i, (i + shift) % 4) for i in range(4)])]
    pallas_call x0 -> x4, Pallas kernels: none -> 67.6 us  [the longest x1 39 us: project(): pl.pallas_call(lambda *refs: project_kernel(step, *refs), out_shape=(jax....]
    psum x1 -> x0, blocking collectives: 64.4 us -> none  [shards(): gain_grad = lax.psum(jnp.sum(dnormed * x32 * scale, axis=0), ('fsdp', 'dp'))]
    another operation x1 -> x0, loops' own time: 63.1 us -> none  [shards(): result = lax.map(group_terms, firsts)]
  transfers between devices with their start and end apart: 3 -> 19, of which waited for: 2 -> 12; matrix products, arithmetic and copies ran while one was open for 24% -> 4% of each run, Pallas kernels for 0% -> 26%
where the time goes in v1:
time: 262 us; the launch traced here: 260 us
  waiting for transfers between devices  133 us (51%)
  Pallas kernels  67.6 us (26%)
  starting transfers between devices  30 us (11%)
  between operations  14.1 us (5%)
  other arithmetic  8.49 us (3%)
  local copies, waits for them, and re-layouts  6.48 us (2%)
    ppermute x15, waiting for transfers between devices, ring(): return lax.ppermute(piece, axis, [(i, (i + shift) % 4) for i in range(4)])  64.8 us
    all_gather x1, waiting for transfers between devices, shards(): piece = lax.all_gather(tiles, ('y', 'z', 'c'), axis=0, tiled=True)  60.8 us
    pallas_call x1, Pallas kernels, project(): pl.pallas_call(lambda *refs: project_kernel(step, *refs), out_shape=(jax....  39 us
    ppermute x15, starting transfers between devices, ring(): return lax.ppermute(piece, axis, [(i, (i + shift) % 4) for i in range(4)])  29.4 us
    pallas_call x2, Pallas kernels, grads(): pl.pallas_call(lambda *refs: grad_kernel(first, per, step, *refs), out_sh...  22.9 us
    ppermute x1, waiting for transfers between devices, shards(): tokens_other = lax.ppermute(tokens, 'c', swap)  6.59 us
    pallas_call x1, Pallas kernels, norm(): pl.pallas_call(norm_kernel, out_shape=(jax.ShapeDtypeStruct((count, width...  5.72 us
    slice x2, local copies, waits for them, and re-layouts, shards(): mid = stage([part[j] for j in range(4)], first).astype(BF)  5.37 us
  transfers between devices with their start and end apart: 19, of which 12 were waited for; matrix products, arithmetic and copies ran while one was open for 4% of the time, Pallas kernels for 26%

profile of v1, /device:TPU:0, one launch (start us, length us, event | category | flops | bytes accessed | tf_op | source)
XLA Modules:
  0.0 259.6 jit_solution(11005051261663731561)
XLA Ops:
  7.2 0.0 all-gather.3.cloned.1.call-start
  7.2 0.7 all-gather.3.cloned.1.call-update
  7.9 0.0 all-gather.5.cloned.1.call-start
  7.9 0.1 collective-permute-start.1
  8.0 0.5 collective-permute-start
  8.5 0.7 pad_add_fusion.refs_2_
  9.2 6.6 %collective-permute-done.other_ref = bf16[128,4096]{1,0:T(8,128)(2,1)S(1)} collective-permute-done((bf16[128,4096]{1,0:T(8,128)(2,1)}, bf16[128,4096]{1,0:T(8,128)(2,1)S(1)}, u32[]{:S(2)}, u32[]{:S(2)}) %collective-permute-start) | collective-permute-done | bytes 1048608 | tf_op jit(solution)/shard_map/ppermute | solution.py:208
  15.8 1.0 copy-done
  16.8 5.7 %norm.1 = (bf16[128,4096]{1,0:T(8,128)(2,1)}, bf16[32,128,256]{2,1,0:T(8,128)(2,1)}, f32[128,128]{1,0:T(8,128)}) custom-call(bf16[128,4096]{1,0:T(8,128)(2,1)} %refs_3_.1, bf16[128,4096]{1,0:T(8,128)(2,1)} %copy-done, f32[1,4096]{1,0:T(1,128)} %bitcast.7), custom_call_target="tpu_custom_call" | custom-call | flops 4194304 | bytes 5242880 | tf_op jit(solution)/shard_map/norm/pallas_call | solution.py:63
  22.5 11.5 %grads_y.1 = bf16[128,128,128]{2,1,0:T(8,128)(2,1)} custom-call(s32[512]{0:T(512)} %refs_0_.5, s32[512]{0:T(512)} %refs_1_.5, s32[4]{0:T(128)} %pad_add_fusion.refs_2_, bf16[32,128,256]{2,1,0:T(8,128)(2,1)} %get-tuple-element.14.refs_3_, bf16[128,14336]{1,0:T(8,128)(2,1)} %refs_4_.3, bf16[128,14336]{1,0:T(8,128)(2,1)} %collective-permute-done.1.refs_5_), custom_call_target="tpu_custom_call" | custom-call | flops 1073741824 | bytes 14680064 | tf_op jit(solution)/shard_map/grads_y/pallas_call | solution.py:99
  34.0 3.2 %fusion = (bf16[32,128,128]{2,1,0:T(8,128)(2,1)}, bf16[32,128,128]{2,1,0:T(8,128)(2,1)S(1)}, bf16[32,128,128]{2,1,0:T(8,128)(2,1)S(1)}) fusion(bf16[128,128,128]{2,1,0:T(8,128)(2,1)} %grads_y.1), kind=kLoop, calls=%fused_computation.7 | loop fusion | bytes 6291456 | tf_op jit(solution)/shard_map/slice | solution.py:215
  37.1 1.6 collective-permute-start.2
  38.8 60.8 %all-gather.3.cloned.1.call-done.refs_2_ = bf16[512,128,128]{2,1,0:T(8,128)(2,1)} async-done(((bf16[16,128,128]{2,1,0:T(8,128)(2,1)}), bf16[512,128,128]{2,1,0:T(8,128)(2,1)}) %all-gather.3.cloned.1.call-update) | async-done | bytes 16777232 | tf_op jit(solution)/shard_map/all_gather | solution.py:206
  99.6 39.0 %project.1 = (bf16[128,14336]{1,0:T(8,128)(2,1)}, bf16[128,4096]{1,0:T(8,128)(2,1)}, f32[1,4096]{1,0:T(1,128)}) custom-call(s32[512]{0:T(512)} %refs_0_.5, s32[512]{0:T(512)} %refs_1_.5, bf16[512,128,128]{2,1,0:T(8,128)(2,1)} %all-gather.3.cloned.1.call-done.refs_2_, bf16[128,4096]{1,0:T(8,128)(2,1)} %refs_3_.1, ...), custom_call_target="tpu_custom_call" | custom-call | flops 4294967296 | bytes 27262976 | tf_op jit(solution)/shard_map/project/pallas_call | solution.py:171
  138.6 1.8 collective-permute-start.3
  140.4 0.7 collective-permute-start.4
  141.1 11.4 %grads_z.1 = bf16[128,128,128]{2,1,0:T(8,128)(2,1)} custom-call(s32[512]{0:T(512)} %refs_0_.5, s32[512]{0:T(512)} %refs_1_.5, s32[4]{0:T(128)} %pad_add_fusion.refs_2_, bf16[32,128,256]{2,1,0:T(8,128)(2,1)} %get-tuple-element.14.refs_3_, bf16[128,14336]{1,0:T(8,128)(2,1)} %refs_4_.3, bf16[128,14336]{1,0:T(8,128)(2,1)} %collective-permute-done.1.refs_5_), custom_call_target="tpu_custom_call" | custom-call | flops 1073741824 | bytes 14680064 | tf_op jit(solution)/shard_map/grads_z/pallas_call | solution.py:99
  152.5 2.2 fusion.1
  154.7 3.9 %collective-permute-start.10 = (bf16[32,128,128]{2,1,0:T(8,128)(2,1)S(1)}, bf16[32,128,128]{2,1,0:T(8,128)(2,1)S(1)}, u32[]{:S(2)}, u32[]{:S(2)}) collective-permute-start(bf16[32,128,128]{2,1,0:T(8,128)(2,1)S(1)} %get-tuple-element.20), channel_id=1, source_target_pairs={{0,16},{8,24},{16,0},{24,8},{1,17},{9,25},{17,1},{25,9},{2,18},{10... | collective-permute-start | bytes 3145736 | tf_op jit(solution)/shard_map/ppermute | solution.py:195
  158.6 1.1 collective-permute-start.8
  159.6 2.2 collective-permute-start.9
  161.8 24.0 %collective-permute-done.3 = bf16[32,128,128]{2,1,0:T(8,128)(2,1)S(1)} collective-permute-done((bf16[32,128,128]{2,1,0:T(8,128)(2,1)S(1)}, bf16[32,128,128]{2,1,0:T(8,128)(2,1)S(1)}, u32[]{:S(2)}, u32[]{:S(2)}) %collective-permute-start.3) | collective-permute-done | bytes 1048608 | tf_op jit(solution)/shard_map/ppermute | solution.py:195
  185.9 1.9 add_convert_fusion.1
  187.8 0.1 fusion.2
  187.8 2.0 collective-permute-start.5
  189.9 2.3 collective-permute-start.6
  192.1 1.7 collective-permute-start.7
  193.9 11.4 %collective-permute-done.8 = bf16[32,128,128]{2,1,0:T(8,128)(2,1)S(1)} collective-permute-done((bf16[32,128,128]{2,1,0:T(8,128)(2,1)S(1)}, bf16[32,128,128]{2,1,0:T(8,128)(2,1)S(1)}, u32[]{:S(2)}, u32[]{:S(2)}) %collective-permute-start.8) | collective-permute-done | bytes 1048608 | tf_op jit(solution)/shard_map/ppermute | solution.py:195
  205.3 1.5 collective-permute-done.9
  206.8 1.9 add_convert_fusion
  208.8 0.1 fusion.3
  208.9 1.1 collective-permute-start.11
  209.9 2.2 collective-permute-start.12
  212.2 2.4 collective-permute-start.13
  214.6 3.0 %collective-permute-done.7 = bf16[8,128,128]{2,1,0:T(8,128)(2,1)S(1)} collective-permute-done((bf16[8,128,128]{2,1,0:T(8,128)(2,1)S(1)}, bf16[8,128,128]{2,1,0:T(8,128)(2,1)S(1)}, u32[]{:S(2)}, u32[]{:S(2)}) %collective-permute-start.7) | collective-permute-done | bytes 262176 | tf_op jit(solution)/shard_map/ppermute | solution.py:195
  217.5 0.1 add_convert_fusion.3
  217.7 1.8 collective-permute-done.11
  219.5 2.8 %collective-permute-done.12 = bf16[8,128,128]{2,1,0:T(8,128)(2,1)S(1)} collective-permute-done((bf16[8,128,128]{2,1,0:T(8,128)(2,1)S(1)}, bf16[8,128,128]{2,1,0:T(8,128)(2,1)S(1)}, u32[]{:S(2)}, u32[]{:S(2)}) %collective-permute-start.12) | collective-permute-done | bytes 262176 | tf_op jit(solution)/shard_map/ppermute | solution.py:195
  222.3 2.4 collective-permute-done.13
  224.7 0.1 add_convert_fusion.2
  224.9 3.1 %collective-permute-start.14 = (bf16[16,128,128]{2,1,0:T(8,128)(2,1)S(1)}, bf16[16,128,128]{2,1,0:T(8,128)(2,1)S(1)}, u32[]{:S(2)}, u32[]{:S(2)}) collective-permute-start(bf16[16,128,128]{2,1,0:T(8,128)(2,1)S(1)} %pad_maximum_fusion), channel_id=1, source_target_pairs={{0,2},{1,3},{2,0},{3,1},{4,6},{5,7},{6,4},{7,5},{8,10},{9,11},{10,... | collective-permute-start | bytes 1572872 | tf_op jit(solution)/shard_map/ppermute | solution.py:195
  228.0 0.6 collective-permute-start.15
  228.6 2.6 %collective-permute-start.16 = (bf16[16,128,128]{2,1,0:T(8,128)(2,1)S(1)}, bf16[16,128,128]{2,1,0:T(8,128)(2,1)S(1)}, u32[]{:S(2)}, u32[]{:S(2)}) collective-permute-start(bf16[16,128,128]{2,1,0:T(8,128)(2,1)S(1)} %pad_maximum_fusion), channel_id=1, source_target_pairs={{0,3},{1,0},{2,1},{3,2},{4,7},{5,4},{6,5},{7,6},{8,11},{9,8},{10,9... | collective-permute-start | bytes 1572872 | tf_op jit(solution)/shard_map/ppermute | solution.py:195
  231.3 10.1 %collective-permute-done.14 = bf16[16,128,128]{2,1,0:T(8,128)(2,1)S(1)} collective-permute-done((bf16[16,128,128]{2,1,0:T(8,128)(2,1)S(1)}, bf16[16,128,128]{2,1,0:T(8,128)(2,1)S(1)}, u32[]{:S(2)}, u32[]{:S(2)}) %collective-permute-start.14) | collective-permute-done | bytes 524320 | tf_op jit(solution)/shard_map/ppermute | solution.py:195
  241.4 7.6 %collective-permute-done.15 = bf16[16,128,128]{2,1,0:T(8,128)(2,1)S(1)} collective-permute-done((bf16[16,128,128]{2,1,0:T(8,128)(2,1)S(1)}, bf16[16,128,128]{2,1,0:T(8,128)(2,1)S(1)}, u32[]{:S(2)}, u32[]{:S(2)}) %collective-permute-start.15) | collective-permute-done | bytes 524320 | tf_op jit(solution)/shard_map/ppermute | solution.py:195
  249.0 0.2 collective-permute-done.16
  249.1 1.3 add_add_fusion
  250.4 2.4 reduce_sum.9
  (10 shorter events, 0.1 us)
Async XLA Ops:
  7.2 92.4 %all-gather.3.cloned.1.call-start = ((), (), s32[]{:S(2)}) async-start(), calls=%async_computation | async-start | bytes 17301504 | tf_op jit(solution)/shard_map/all_gather | solution.py:206
  7.9 242.5 %all-gather.5.cloned.1.call-start = ((), (), s32[]{:S(2)}) async-start(), calls=%async_computation.1 | async-start | bytes 2113536 | tf_op jit(solution)/shard_map/all_gather | solution.py:225
  7.9 14.5 %collective-permute-start.1 = (bf16[128,14336]{1,0:T(8,128)(2,1)}, bf16[128,14336]{1,0:T(8,128)(2,1)}, u32[]{:S(2)}, u32[]{:S(2)}) collective-permute-start(bf16[128,14336]{1,0:T(8,128)(2,1)} %refs_4_.3), channel_id=1, source_target_pairs={{0,4},{4,0},{1,5},{5,1},{2,6},{6,2},{3,7},{7,3},{8,12},{12,8},{9,1... | collective-permute-start | bytes 11010056 | tf_op jit(solution)/shard_map/ppermute | solution.py:209
  8.0 7.7 %collective-permute-start = (bf16[128,4096]{1,0:T(8,128)(2,1)}, bf16[128,4096]{1,0:T(8,128)(2,1)S(1)}, u32[]{:S(2)}, u32[]{:S(2)}) collective-permute-start(bf16[128,4096]{1,0:T(8,128)(2,1)} %refs_3_.1), channel_id=1, source_target_pairs={{0,4},{4,0},{1,5},{5,1},{2,6},{6,2},{3,7},{7,3},{8,12},{12,8},{9,1... | collective-permute-start | bytes 3145736 | tf_op jit(solution)/shard_map/ppermute | solution.py:208
  15.8 1.0 copy-start
  37.1 122.5 %collective-permute-start.2 = (bf16[32,128,128]{2,1,0:T(8,128)(2,1)}, bf16[32,128,128]{2,1,0:T(8,128)(2,1)S(1)}, u32[]{:S(2)}, u32[]{:S(2)}) collective-permute-start(bf16[32,128,128]{2,1,0:T(8,128)(2,1)} %get-tuple-element.16), channel_id=1, source_target_pairs={{0,32},{32,64},{64,96},{96,0},{1,33},{33,65},{65,97},{97,1},{2,34}... | collective-permute-start | bytes 3145736 | tf_op jit(solution)/shard_map/ppermute | solution.py:195
  138.6 47.3 %collective-permute-start.3 = (bf16[32,128,128]{2,1,0:T(8,128)(2,1)S(1)}, bf16[32,128,128]{2,1,0:T(8,128)(2,1)S(1)}, u32[]{:S(2)}, u32[]{:S(2)}) collective-permute-start(bf16[32,128,128]{2,1,0:T(8,128)(2,1)S(1)} %get-tuple-element.18), channel_id=1, source_target_pairs={{0,96},{32,0},{64,32},{96,64},{1,97},{33,1},{65,33},{97,65},{2,98}... | collective-permute-start | bytes 3145736 | tf_op jit(solution)/shard_map/ppermute | solution.py:195
  140.4 45.5 %collective-permute-start.4 = (bf16[32,128,128]{2,1,0:T(8,128)(2,1)S(1)}, bf16[32,128,128]{2,1,0:T(8,128)(2,1)S(1)}, u32[]{:S(2)}, u32[]{:S(2)}) collective-permute-start(bf16[32,128,128]{2,1,0:T(8,128)(2,1)S(1)} %get-tuple-element.17), channel_id=1, source_target_pairs={{0,64},{32,96},{64,0},{96,32},{1,65},{33,97},{65,1},{97,33},{2,66}... | collective-permute-start | bytes 3145736 | tf_op jit(solution)/shard_map/ppermute | solution.py:195
  154.7 37.5 %collective-permute-start.10 = (bf16[32,128,128]{2,1,0:T(8,128)(2,1)S(1)}, bf16[32,128,128]{2,1,0:T(8,128)(2,1)S(1)}, u32[]{:S(2)}, u32[]{:S(2)}) collective-permute-start(bf16[32,128,128]{2,1,0:T(8,128)(2,1)S(1)} %get-tuple-element.20), channel_id=1, source_target_pairs={{0,16},{8,24},{16,0},{24,8},{1,17},{9,25},{17,1},{25,9},{2,18},{10... | collective-permute-start | bytes 3145736 | tf_op jit(solution)/shard_map/ppermute | solution.py:195
  158.6 46.7 %collective-permute-start.8 = (bf16[32,128,128]{2,1,0:T(8,128)(2,1)S(1)}, bf16[32,128,128]{2,1,0:T(8,128)(2,1)S(1)}, u32[]{:S(2)}, u32[]{:S(2)}) collective-permute-start(bf16[32,128,128]{2,1,0:T(8,128)(2,1)S(1)} %get-tuple-element.19), channel_id=1, source_target_pairs={{0,8},{8,16},{16,24},{24,0},{1,9},{9,17},{17,25},{25,1},{2,10},{10... | collective-permute-start | bytes 3145736 | tf_op jit(solution)/shard_map/ppermute | solution.py:195
  159.6 47.2 %collective-permute-start.9 = (bf16[32,128,128]{2,1,0:T(8,128)(2,1)S(1)}, bf16[32,128,128]{2,1,0:T(8,128)(2,1)S(1)}, u32[]{:S(2)}, u32[]{:S(2)}) collective-permute-start(bf16[32,128,128]{2,1,0:T(8,128)(2,1)S(1)} %get-tuple-element.21), channel_id=1, source_target_pairs={{0,24},{8,0},{16,8},{24,16},{1,25},{9,1},{17,9},{25,17},{2,26},{10... | collective-permute-start | bytes 3145736 | tf_op jit(solution)/shard_map/ppermute | solution.py:195
  187.8 24.3 %collective-permute-start.5 = (bf16[8,128,128]{2,1,0:T(8,128)(2,1)S(1)}, bf16[8,128,128]{2,1,0:T(8,128)(2,1)S(1)}, u32[]{:S(2)}, u32[]{:S(2)}) collective-permute-start(bf16[8,128,128]{2,1,0:T(8,128)(2,1)S(1)} %get-tuple-element.22), channel_id=1, source_target_pairs={{0,8},{8,16},{16,24},{24,0},{1,9},{9,17},{17,25},{25,1},{2,10},{10... | collective-permute-start | bytes 786440 | tf_op jit(solution)/shard_map/ppermute | solution.py:195
  189.9 24.7 %collective-permute-start.6 = (bf16[8,128,128]{2,1,0:T(8,128)(2,1)S(1)}, bf16[8,128,128]{2,1,0:T(8,128)(2,1)S(1)}, u32[]{:S(2)}, u32[]{:S(2)}) collective-permute-start(bf16[8,128,128]{2,1,0:T(8,128)(2,1)S(1)} %get-tuple-element.24), channel_id=1, source_target_pairs={{0,24},{8,0},{16,8},{24,16},{1,25},{9,1},{17,9},{25,17},{2,26},{10... | collective-permute-start | bytes 786440 | tf_op jit(solution)/shard_map/ppermute | solution.py:195
  192.1 25.4 %collective-permute-start.7 = (bf16[8,128,128]{2,1,0:T(8,128)(2,1)S(1)}, bf16[8,128,128]{2,1,0:T(8,128)(2,1)S(1)}, u32[]{:S(2)}, u32[]{:S(2)}) collective-permute-start(bf16[8,128,128]{2,1,0:T(8,128)(2,1)S(1)} %get-tuple-element.23), channel_id=1, source_target_pairs={{0,16},{8,24},{16,0},{24,8},{1,17},{9,25},{17,1},{25,9},{2,18},{10... | collective-permute-start | bytes 786440 | tf_op jit(solution)/shard_map/ppermute | solution.py:195
  208.9 10.6 %collective-permute-start.11 = (bf16[8,128,128]{2,1,0:T(8,128)(2,1)S(1)}, bf16[8,128,128]{2,1,0:T(8,128)(2,1)S(1)}, u32[]{:S(2)}, u32[]{:S(2)}) collective-permute-start(bf16[8,128,128]{2,1,0:T(8,128)(2,1)S(1)} %get-tuple-element.25), channel_id=1, source_target_pairs={{0,32},{32,64},{64,96},{96,0},{1,33},{33,65},{65,97},{97,1},{2,34}... | collective-permute-start | bytes 786440 | tf_op jit(solution)/shard_map/ppermute | solution.py:195
  209.9 12.4 %collective-permute-start.12 = (bf16[8,128,128]{2,1,0:T(8,128)(2,1)S(1)}, bf16[8,128,128]{2,1,0:T(8,128)(2,1)S(1)}, u32[]{:S(2)}, u32[]{:S(2)}) collective-permute-start(bf16[8,128,128]{2,1,0:T(8,128)(2,1)S(1)} %get-tuple-element.27), channel_id=1, source_target_pairs={{0,96},{32,0},{64,32},{96,64},{1,97},{33,1},{65,33},{97,65},{2,98}... | collective-permute-start | bytes 786440 | tf_op jit(solution)/shard_map/ppermute | solution.py:195
  212.2 12.5 %collective-permute-start.13 = (bf16[8,128,128]{2,1,0:T(8,128)(2,1)S(1)}, bf16[8,128,128]{2,1,0:T(8,128)(2,1)S(1)}, u32[]{:S(2)}, u32[]{:S(2)}) collective-permute-start(bf16[8,128,128]{2,1,0:T(8,128)(2,1)S(1)} %get-tuple-element.26), channel_id=1, source_target_pairs={{0,64},{32,96},{64,0},{96,32},{1,65},{33,97},{65,1},{97,33},{2,66}... | collective-permute-start | bytes 786440 | tf_op jit(solution)/shard_map/ppermute | solution.py:195
  224.9 16.5 %collective-permute-start.14 = (bf16[16,128,128]{2,1,0:T(8,128)(2,1)S(1)}, bf16[16,128,128]{2,1,0:T(8,128)(2,1)S(1)}, u32[]{:S(2)}, u32[]{:S(2)}) collective-permute-start(bf16[16,128,128]{2,1,0:T(8,128)(2,1)S(1)} %pad_maximum_fusion), channel_id=1, source_target_pairs={{0,2},{1,3},{2,0},{3,1},{4,6},{5,7},{6,4},{7,5},{8,10},{9,11},{10,... | collective-permute-start | bytes 1572872 | tf_op jit(solution)/shard_map/ppermute | solution.py:195
  228.0 20.9 %collective-permute-start.15 = (bf16[16,128,128]{2,1,0:T(8,128)(2,1)S(1)}, bf16[16,128,128]{2,1,0:T(8,128)(2,1)S(1)}, u32[]{:S(2)}, u32[]{:S(2)}) collective-permute-start(bf16[16,128,128]{2,1,0:T(8,128)(2,1)S(1)} %pad_maximum_fusion), channel_id=1, source_target_pairs={{0,1},{1,2},{2,3},{3,0},{4,5},{5,6},{6,7},{7,4},{8,9},{9,10},{10,1... | collective-permute-start | bytes 1572872 | tf_op jit(solution)/shard_map/ppermute | solution.py:195
  228.6 20.5 %collective-permute-start.16 = (bf16[16,128,128]{2,1,0:T(8,128)(2,1)S(1)}, bf16[16,128,128]{2,1,0:T(8,128)(2,1)S(1)}, u32[]{:S(2)}, u32[]{:S(2)}) collective-permute-start(bf16[16,128,128]{2,1,0:T(8,128)(2,1)S(1)} %pad_maximum_fusion), channel_id=1, source_target_pairs={{0,3},{1,0},{2,1},{3,2},{4,7},{5,4},{6,5},{7,6},{8,11},{9,8},{10,9... | collective-permute-start | bytes 1572872 | tf_op jit(solution)/shard_map/ppermute | solution.py:195
Sparse Core Ops, SparseCore 0:
  10.3 89.2 all-gather.2
  138.7 88.3 all-gather.4

commit v2 on v1

v2 whole, which is shorter than its diff:
```python
import jax
import jax.numpy as jnp
from jax import lax
from jax.experimental import pallas as pl
from jax.experimental.pallas import tpu as pltpu
from jax.sharding import Mesh, PartitionSpec as P

BF = jnp.bfloat16
F4 = jnp.float32
T = 128
ALL = ("y", "z", "c", "x")


def params(limit):
    return pltpu.CompilerParams(vmem_limit_bytes=limit * 1024 * 1024)


def cost(micros, nbytes):
    return pl.CostEstimate(flops=int(micros * 1.1e9), bytes_accessed=nbytes, transcendentals=0)


def whole(shape):
    zeros = (0,) * len(shape)
    return pl.BlockSpec(shape, lambda *_: zeros, pipeline_mode=pl.Buffered(1))


def dot(a, b):
    return jnp.dot(a, b, preferred_element_type=F4)


def dot_t(a, b):
    return lax.dot_general(a, b, (((1,), (1,)), ((), ())), preferred_element_type=F4)


ANY = pl.BlockSpec(memory_space=pl.ANY)


def cols_at(index):
    return pl.ds(pl.multiple_of(index * T, T), T)


def norm_kernel(x_ref, gain_ref, normed_ref, turned_ref, scale_ref):
    count, width = x_ref.shape
    blocks = width // T

    def squares(b, total):
        x = x_ref[:, cols_at(b)].astype(F4)
        return total + x * x

    total = lax.fori_loop(0, blocks, squares, jnp.zeros((count, T), F4), unroll=4)
    scale = lax.rsqrt(jnp.sum(total, axis=1, keepdims=True) / width + 1e-05)
    scale_ref[...] = jnp.broadcast_to(scale, (count, T))

    def fill(b, carry):
        x = x_ref[:, cols_at(b)].astype(F4)
        normed = (x * scale * gain_ref[:, cols_at(b)]).astype(BF)
        normed_ref[:, cols_at(b)] = normed
        turned_ref[b] = normed.T
        return carry

    lax.fori_loop(0, blocks, fill, 0, unroll=4)


def norm(x, gain):
    count, width = x.shape
    return pl.pallas_call(
        norm_kernel,
        out_shape=(
            jax.ShapeDtypeStruct((count, width), BF),
            jax.ShapeDtypeStruct((width // T, T, count), BF),
            jax.ShapeDtypeStruct((count, T), F4),
        ),
        compiler_params=params(56),
        cost_estimate=cost(1, 0),
        name="norm",
    )(x, gain)


def grad_kernel(first, per, step, rows, cols, pos, turned_ref, turned_other_ref, own_ref, other_ref, *refs):
    out_refs = refs[-4:]
    base = pl.program_id(0) * step
    y, z, c = pos[0], pos[1], pos[2]
    each = 4 * per // step

    for major, out_ref in enumerate(out_refs):

        @pl.when(pl.program_id(0) // each == major)
        def _(major=major, out_ref=out_ref):
            def one(k, carry):
                i = base + k - major * 4 * per
                minor, t = i // per, i % per
                if first == "y":
                    place = lax.rem(y + major, 4) * 4 + lax.rem(z + minor, 4)
                else:
                    place = lax.rem(y + minor, 4) * 4 + lax.rem(z + major, 4)
                index = place * 32 + c * 16 + (0 if first == "y" else 16 - per) + t
                r, q = rows[index], cols[index]
                left = jnp.concatenate([turned_ref[r], turned_other_ref[r]], axis=1)
                right = jnp.concatenate([own_ref[:, cols_at(q)], other_ref[:, cols_at(q)]], axis=0)
                out_ref[k] = dot(left, right).astype(BF)
                return carry

            lax.fori_loop(0, step, one, 0, unroll=8)


def grads(first, per, rows, cols, pos, turned, turned_other, own, other, ties=()):
    piece, step = 4 * per, 16
    each = piece // step

    def out_spec(major):
        return pl.BlockSpec((step, T, T), lambda i, *_: (jnp.clip(i - major * each, 0, each - 1), 0, 0))

    return pl.pallas_call(
        lambda *refs: grad_kernel(first, per, step, *refs),
        out_shape=[jax.ShapeDtypeStruct((piece, T, T), BF)] * 4,
        grid_spec=pltpu.PrefetchScalarGridSpec(
            num_scalar_prefetch=3,
            grid=(4 * each,),
            in_specs=[whole(a.shape) for a in (turned, turned_other, own, other)] + [ANY] * len(ties),
            out_specs=[out_spec(major) for major in range(4)],
        ),
        compiler_params=params(56),
        cost_estimate=cost(2, 0),
        name="grads_" + first,
    )(rows, cols, pos, turned, turned_other, own, other, *ties)


def place_of(k, half, step):
    i = pl.program_id(0) * step + k
    return i // 8 * 16 + half * 8 + i % 8


def both_kernel(half, step, rows, cols, tiles_ref, normed_ref, g_ref, *refs):
    out_ref, back_ref = refs[-2:]

    @pl.when(pl.program_id(0) == 0)
    def _():
        out_ref[...] = jnp.zeros_like(out_ref)
        back_ref[...] = jnp.zeros_like(back_ref)

    def one(k, carry):
        index = place_of(k, half, step)
        r, q = rows[index], cols[index]
        weight = tiles_ref[k]
        out_ref[:, cols_at(q)] += dot(normed_ref[:, cols_at(r)], weight)
        back_ref[:, cols_at(r)] += dot_t(g_ref[:, cols_at(q)], weight)
        return carry

    lax.fori_loop(0, step, one, 0, unroll=8)


def both(half, rows, cols, tiles, normed, g, ties=()):
    number, step = tiles.shape[0], 32
    return pl.pallas_call(
        lambda *refs: both_kernel(half, step, *refs),
        out_shape=(jax.ShapeDtypeStruct(g.shape, F4), jax.ShapeDtypeStruct(normed.shape, F4)),
        grid_spec=pltpu.PrefetchScalarGridSpec(
            num_scalar_prefetch=2,
            grid=(number // step,),
            in_specs=[pl.BlockSpec((step, T, T), lambda i, *_: (i, 0, 0)), whole(normed.shape), whole(g.shape)]
            + [ANY] * len(ties),
            out_specs=[whole(g.shape), whole(normed.shape)],
        ),
        compiler_params=params(56),
        cost_estimate=cost(2, 0),
        name="both",
    )(rows, cols, tiles, normed, g, *ties)


def back_kernel(
    half, step, rows, cols, tiles_ref, back_in_ref, x_ref, scale_ref, gain_ref, g_ref, *refs
):
    token_grad_ref, sums_ref, back_acc = refs[-3:]
    count, width = x_ref.shape
    blocks = width // T

    @pl.when(pl.program_id(0) == 0)
    def _():
        back_acc[...] = back_in_ref[...]

    def one(k, carry):
        index = place_of(k, half, step)
        r, q = rows[index], cols[index]
        back_acc[:, cols_at(r)] += dot_t(g_ref[:, cols_at(q)], tiles_ref[k])
        return carry

    lax.fori_loop(0, step, one, 0, unroll=8)

    @pl.when(pl.program_id(0) == pl.num_programs(0) - 1)
    def _():
        scale = scale_ref[...]

        def products(b, total):
            at = cols_at(b)
            x = x_ref[:, at].astype(F4)
            back = back_acc[:, at]
            sums_ref[:, at] = jnp.sum(back * x * scale, axis=0, keepdims=True)
            return total + x * gain_ref[:, at] * back

        total = lax.fori_loop(0, blocks, products, jnp.zeros((count, T), F4), unroll=2)
        inner = jnp.sum(total, axis=1, keepdims=True) / width
        cubed = scale * scale * scale * inner

        def finish(b, carry):
            at = cols_at(b)
            x = x_ref[:, at].astype(F4)
            token_grad_ref[:, at] = (scale * gain_ref[:, at] * back_acc[:, at] - x * cubed).astype(BF)
            return carry

        lax.fori_loop(0, blocks, finish, 0, unroll=2)


def back(half, rows, cols, tiles, back_in, x, scale, gain, g, ties=()):
    number, step = tiles.shape[0], 32
    width = x.shape[1]
    return pl.pallas_call(
        lambda *refs: back_kernel(half, step, *refs),
        out_shape=(jax.ShapeDtypeStruct(x.shape, BF), jax.ShapeDtypeStruct((1, width), F4)),
        grid_spec=pltpu.PrefetchScalarGridSpec(
            num_scalar_prefetch=2,
            grid=(number // step,),
            in_specs=[pl.BlockSpec((step, T, T), lambda i, *_: (i, 0, 0))]
            + [whole(a.shape) for a in (back_in, x, scale, gain, g)]
            + [ANY] * len(ties),
            out_specs=[whole(x.shape), whole((1, width))],
            scratch_shapes=[pltpu.VMEM(x.shape, F4)],
        ),
        compiler_params=params(56),
        cost_estimate=cost(2, 0),
        name="back",
    )(rows, cols, tiles, back_in, x, scale, gain, g, *ties)


def fore_kernel(half, step, rows, cols, tiles_ref, out_in_ref, normed_ref, *refs):
    projected_ref, out_acc = refs[-2:]

    @pl.when(pl.program_id(0) == 0)
    def _():
        out_acc[...] = out_in_ref[...]

    def one(k, carry):
        index = place_of(k, half, step)
        r, q = rows[index], cols[index]
        out_acc[:, cols_at(q)] += dot(normed_ref[:, cols_at(r)], tiles_ref[k])
        return carry

    lax.fori_loop(0, step, one, 0, unroll=8)

    @pl.when(pl.program_id(0) == pl.num_programs(0) - 1)
    def _():
        projected_ref[...] = out_acc[...].astype(BF)


def fore(half, rows, cols, tiles, out_in, normed, ties=()):
    number, step = tiles.shape[0], 32
    return pl.pallas_call(
        lambda *refs: fore_kernel(half, step, *refs),
        out_shape=jax.ShapeDtypeStruct(out_in.shape, BF),
        grid_spec=pltpu.PrefetchScalarGridSpec(
            num_scalar_prefetch=2,
            grid=(number // step,),
            in_specs=[pl.BlockSpec((step, T, T), lambda i, *_: (i, 0, 0)), whole(out_in.shape), whole(normed.shape)]
            + [ANY] * len(ties),
            out_specs=whole(out_in.shape),
            scratch_shapes=[pltpu.VMEM(out_in.shape, F4)],
        ),
        compiler_params=params(56),
        cost_estimate=cost(2, 0),
        name="fore",
    )(rows, cols, tiles, out_in, normed, *ties)


def ring(piece, axis, shift):
    return lax.ppermute(piece, axis, [(i, (i + shift) % 4) for i in range(4)])


def first_sum(pieces, ties):
    each = pieces[0].shape[0] // 4

    def kernel(*refs):
        ins, outs = refs[:4], refs[-4:]
        a, b, c, d = (r[...].astype(F4) for r in ins)
        total = ((a + c) + (b + d)).astype(BF)
        for major, out in enumerate(outs):

            @pl.when(pl.program_id(0) == major)
            def _(out=out):
                out[...] = total

    return pl.pallas_call(
        kernel,
        out_shape=[jax.ShapeDtypeStruct((each, T, T), BF)] * 4,
        grid=(4,),
        in_specs=[pl.BlockSpec((each, T, T), lambda i: (i, 0, 0))] * 4 + [ANY] * len(ties),
        out_specs=[whole((each, T, T))] * 4,
        compiler_params=params(32),
        cost_estimate=cost(1, 0),
        name="first_sum",
    )(*pieces, *ties)


def sum_of_four(groups, dtype, ties, name):
    count = groups[0][0].shape[0]

    def kernel(*refs):
        out = refs[-1]
        for g in range(len(groups)):
            for i in range(count):
                a, b, c, d = (r[i].astype(F4) for r in refs[4 * g : 4 * g + 4])
                out[g * count + i] = ((a + c) + (b + d)).astype(dtype)

    arrays = [a for group in groups for a in group]
    return pl.pallas_call(
        kernel,
        out_shape=jax.ShapeDtypeStruct((count * len(groups), T, T), dtype),
        in_specs=[pl.BlockSpec(memory_space=pltpu.VMEM)] * len(arrays) + [ANY] * len(ties),
        compiler_params=params(32),
        cost_estimate=cost(1, 0),
        name=name,
    )(*arrays, *ties)


def exchange(pieces, axis):
    return [pieces[0]] + [ring(pieces[j], axis, j) for j in (1, 2, 3)]


def shards(tokens, gain, tiles, rows, cols, cotangent):
    gain2 = gain.reshape(1, -1)
    pos = jnp.stack([lax.axis_index(a).astype(jnp.int32) for a in ("y", "z", "c", "x")])
    owners = ("y", "z", "c")
    piece0 = lax.all_gather(tiles[:8], owners, axis=0, tiled=True)
    swap = [(0, 1), (1, 0)]
    tokens_other = lax.ppermute(tokens, "c", swap)
    g_other = lax.ppermute(cotangent, "c", swap)
    normed, turned, scale = norm(tokens, gain2)
    _, turned_other, _ = norm(tokens_other, gain2)
    part_y = grads("y", 8, rows, cols, pos, turned, turned_other, cotangent, g_other)
    part_z = grads("z", 8, rows, cols, pos, turned, turned_other, cotangent, g_other, (part_y[3],))
    piece1 = lax.all_gather(tiles[8:], owners, axis=0, tiled=True)
    out0, back0 = both(0, rows, cols, piece0, normed, cotangent, (part_z[3],))
    mid_y = first_sum(exchange(part_y, "y"), (back0,))
    mid_z = first_sum(exchange(part_z, "z"), (back0,))
    token_grad, gain_part = back(
        1, rows, cols, piece1, back0, tokens, scale, gain2, cotangent, (mid_y[0], mid_z[0])
    )
    gains = lax.all_gather(gain_part.reshape(1, -1, T), ALL, axis=0, tiled=True)
    sent = sum_of_four([exchange(mid_y, "z"), exchange(mid_z, "y")], BF, (token_grad,), "second_sum")
    projected = fore(1, rows, cols, piece1, out0, normed, (sent,))
    tile_grad = sum_of_four([exchange([sent] * 4, "x")], F4, (projected,), "last_sum")
    gain_grad = jnp.sum(gains, axis=0).reshape(-1)
    return (projected, token_grad, tile_grad, gain_grad)


def solution(mesh):
    grid = Mesh(mesh.devices.reshape(4, 4, 2, 4), ALL)
    owners = ("y", "z", "c")
    placed = (P(ALL, None), P(), P(owners, None, None), P(), P(), P(ALL, None))
    return jax.shard_map(
        shards,
        mesh=grid,
        in_specs=placed,
        out_specs=(P(ALL, None), P(ALL, None), P(owners, None, None), P()),
        check_vma=False,
    )
```

time: 262 us -> 251 us (0.958)
  waiting for transfers between devices: 133 us -> 88.8 us
  Pallas kernels: 67.6 us -> 93.6 us
  local copies, waits for them, and re-layouts: 6.48 us -> 14.7 us
  other arithmetic: 8.49 us -> 2.94 us
  starting transfers between devices: 30 us -> 34.9 us
    all_gather x1 -> x2, waiting for transfers between devices: 60.8 us -> 24.3 us  [the longest x1 24.3 us: shards(): piece1 = lax.all_gather(tiles[8:], owners, axis=0, tiled=True)]
    pallas_call x1 -> x7, Pallas kernels: 39 us -> 61.4 us  [the longest x1 22.1 us: both(): pl.pallas_call(lambda *refs: both_kernel(half, step, *refs), out_shape=(j...]
    ppermute x15, waiting for transfers between devices: 64.8 us -> 42.4 us  [ring(): return lax.ppermute(piece, axis, [(i, (i + shift) % 4) for i in range(4)])]
    all_gather x1, waiting for transfers between devices: 0.01 us -> 18.5 us  [shards(): gains = lax.all_gather(gain_part.reshape(1, -1, T), ALL, axis=0, tiled=True)]
    unnamed x2 -> x48, local copies, waits for them, and re-layouts: 0.97 us -> 12.8 us
    ppermute x15, starting transfers between devices: 29.4 us -> 34.2 us  [ring(): return lax.ppermute(piece, axis, [(i, (i + shift) % 4) for i in range(4)])]
    convert_element_type x2 -> x0, other arithmetic: 3.83 us -> none  [shards(): mid = stage([part[j] for j in range(4)], first).astype(BF)]
    ppermute x1, waiting for transfers between devices: 6.59 us -> 2.91 us  [shards(): tokens_other = lax.ppermute(tokens, 'c', swap)]
  transfers between devices with their start and end apart: 19 -> 20, of which waited for: 12 -> 9; matrix products, arithmetic and copies ran while one was open for 4% -> 0% of each run, Pallas kernels for 26% -> 31%
where the time goes in v2:
time: 251 us; the launch traced here: 249 us
  Pallas kernels  93.6 us (37%)
  waiting for transfers between devices  88.8 us (35%)
  starting transfers between devices  34.9 us (14%)
  local copies, waits for them, and re-layouts  14.7 us (6%)
  between operations  13.9 us (6%)
  other arithmetic  2.94 us (1%)
    ppermute x15, waiting for transfers between devices, ring(): return lax.ppermute(piece, axis, [(i, (i + shift) % 4) for i in range(4)])  42.4 us
    ppermute x15, starting transfers between devices, ring(): return lax.ppermute(piece, axis, [(i, (i + shift) % 4) for i in range(4)])  34.2 us
    pallas_call x2, Pallas kernels, grads(): pl.pallas_call(lambda *refs: grad_kernel(first, per, step, *refs), out_sh...  24.6 us
    all_gather x1, waiting for transfers between devices, shards(): piece1 = lax.all_gather(tiles[8:], owners, axis=0, tiled=True)  24.3 us
    pallas_call x1, Pallas kernels, both(): pl.pallas_call(lambda *refs: both_kernel(half, step, *refs), out_shape=(j...  22.1 us
    all_gather x1, waiting for transfers between devices, shards(): gains = lax.all_gather(gain_part.reshape(1, -1, T), ALL, axis=0, tiled=True)  18.5 us
    pallas_call x1, Pallas kernels, back(): pl.pallas_call(lambda *refs: back_kernel(half, step, *refs), out_shape=(j...  17.7 us
    pallas_call x1, Pallas kernels, fore(): pl.pallas_call(lambda *refs: fore_kernel(half, step, *refs), out_shape=ja...  16 us
  transfers between devices with their start and end apart: 20, of which 9 were waited for; matrix products, arithmetic and copies ran while one was open for 0% of the time, Pallas kernels for 31%

profile of v2, /device:TPU:0, one launch (start us, length us, event | category | flops | bytes accessed | tf_op | source)
XLA Modules:
  0.0 248.8 jit_solution(13413688104438011936)
XLA Ops:
  7.2 1.9 fusion
  9.2 0.7 all-gather.4.cloned.1.call-update
  10.5 3.8 %norm.2 = (bf16[128,4096]{1,0:T(8,128)(2,1)}, bf16[32,128,128]{2,1,0:T(8,128)(2,1)}, f32[128,128]{1,0:T(8,128)}) custom-call(bf16[128,4096]{1,0:T(8,128)(2,1)} %refs_4_.3, f32[1,4096]{1,0:T(1,128)} %bitcast.7), custom_call_target="tpu_custom_call" | custom-call | flops 1100000000 | tf_op jit(solution)/shard_map/norm/pallas_call | solution.py:66
  14.3 0.6 pad_add_fusion.refs_2_
  14.8 2.9 %collective-permute-done.x_ref = bf16[128,4096]{1,0:T(8,128)(2,1)S(1)} collective-permute-done((bf16[128,4096]{1,0:T(8,128)(2,1)}, bf16[128,4096]{1,0:T(8,128)(2,1)S(1)}, u32[]{:S(2)}, u32[]{:S(2)}) %collective-permute-start) | collective-permute-done | bytes 1048608 | tf_op jit(solution)/shard_map/ppermute | solution.py:333
  17.8 1.0 copy-done.23
  18.7 3.8 %norm.3 = (bf16[128,4096]{1,0:T(8,128)(2,1)}, bf16[32,128,128]{2,1,0:T(8,128)(2,1)}, f32[128,128]{1,0:T(8,128)}) custom-call(bf16[128,4096]{1,0:T(8,128)(2,1)} %copy-done.23, f32[1,4096]{1,0:T(1,128)} %bitcast.8), custom_call_target="tpu_custom_call" | custom-call | flops 1100000000 | tf_op jit(solution)/shard_map/norm/pallas_call | solution.py:66
  22.5 12.4 %grads_y.1 = (bf16[32,128,128]{2,1,0:T(8,128)(2,1)}, bf16[32,128,128]{2,1,0:T(8,128)(2,1)}, bf16[32,128,128]{2,1,0:T(8,128)(2,1)}, bf16[32,128,128]{2,1,0:T(8,128)(2,1)}) custom-call(s32[512]{0:T(512)} %refs_0_.9, s32[512]{0:T(512)} %refs_1_.9, s32[4]{0:T(128)} %pad_add_fusion.refs_2_, bf16[32,128,128]{2,1,0:T(8,128)(2,1)} %get-tuple-element.29.refs_3_, ...), custom_call_target="tpu_custom_call" | custom-call | flops 2200000000 | tf_op jit(solution)/shard_map/grads_y/pallas_call | solution.py:113
  35.0 12.2 %grads_z.1 = (bf16[32,128,128]{2,1,0:T(8,128)(2,1)}, bf16[32,128,128]{2,1,0:T(8,128)(2,1)}, bf16[32,128,128]{2,1,0:T(8,128)(2,1)}, bf16[32,128,128]{2,1,0:T(8,128)(2,1)}) custom-call(s32[512]{0:T(512)} %refs_0_.9, s32[512]{0:T(512)} %refs_1_.9, s32[4]{0:T(128)} %pad_add_fusion.refs_2_, bf16[32,128,128]{2,1,0:T(8,128)(2,1)} %get-tuple-element.29.refs_3_, ...), custom_call_target="tpu_custom_call" | custom-call | flops 2200000000 | tf_op jit(solution)/shard_map/grads_z/pallas_call | solution.py:113
  47.1 4.1 %collective-permute-start.10 = (bf16[32,128,128]{2,1,0:T(8,128)(2,1)}, bf16[32,128,128]{2,1,0:T(8,128)(2,1)S(1)}, u32[]{:S(2)}, u32[]{:S(2)}) collective-permute-start(bf16[32,128,128]{2,1,0:T(8,128)(2,1)} %get-tuple-element.32.refs_5_), channel_id=1, source_target_pairs={{0,24},{8,0},{16,8},{24,16},{1,25},{9,1},{17,9},{25,17},{2,26},{10... | collective-permute-start | bytes 3145736 | tf_op jit(solution)/shard_map/ppermute | solution.py:274
  51.3 1.9 collective-permute-start.9
  53.2 3.1 %collective-permute-start.4 = (bf16[32,128,128]{2,1,0:T(8,128)(2,1)}, bf16[32,128,128]{2,1,0:T(8,128)(2,1)S(1)}, u32[]{:S(2)}, u32[]{:S(2)}) collective-permute-start(bf16[32,128,128]{2,1,0:T(8,128)(2,1)} %get-tuple-element.31.refs_7_), channel_id=1, source_target_pairs={{0,96},{32,0},{64,32},{96,64},{1,97},{33,1},{65,33},{97,65},{2,98}... | collective-permute-start | bytes 3145736 | tf_op jit(solution)/shard_map/ppermute | solution.py:274
  56.2 28.9 %collective-permute-done.10.refs_3_ = bf16[32,128,128]{2,1,0:T(8,128)(2,1)S(1)} collective-permute-done((bf16[32,128,128]{2,1,0:T(8,128)(2,1)}, bf16[32,128,128]{2,1,0:T(8,128)(2,1)S(1)}, u32[]{:S(2)}, u32[]{:S(2)}) %collective-permute-start.10) | collective-permute-done | bytes 1048608 | tf_op jit(solution)/shard_map/ppermute | solution.py:274
  85.1 1.0 copy-done.6
  86.1 3.0 %collective-permute-start.3 = (bf16[32,128,128]{2,1,0:T(8,128)(2,1)}, bf16[32,128,128]{2,1,0:T(8,128)(2,1)S(1)}, u32[]{:S(2)}, u32[]{:S(2)}) collective-permute-start(bf16[32,128,128]{2,1,0:T(8,128)(2,1)} %get-tuple-element.36), channel_id=1, source_target_pairs={{0,64},{32,96},{64,0},{96,32},{1,65},{33,97},{65,1},{97,33},{2,66}... | collective-permute-start | bytes 3145736 | tf_op jit(solution)/shard_map/ppermute | solution.py:274
  89.1 22.1 %both.1 = (f32[128,14336]{1,0:T(8,128)}, f32[128,4096]{1,0:T(8,128)}) custom-call(s32[512]{0:T(512)} %refs_0_.9, s32[512]{0:T(512)} %refs_1_.9, bf16[256,128,128]{2,1,0:T(8,128)(2,1)} %all-gather.6.cloned.1.call-done.refs_2_, bf16[128,4096]{1,0:T(8,128)(2,1)} %get-tuple-element.28.refs_3_.refs_4_, bf16[128,14336]{1,0:T(8,128)(2,1)} %refs_7_.1, ...), custom_call_target="tpu_custom_call" | custom-call | flops 2200000000 | tf_op jit(solution)/shard_map/both/pallas_call | solution.py:154
  111.2 2.2 collective-permute-done.9.refs_2_
  113.4 1.6 copy-done
  115.0 3.0 %first_sum.3 = (bf16[8,128,128]{2,1,0:T(8,128)(2,1)S(1)}, bf16[8,128,128]{2,1,0:T(8,128)(2,1)S(1)}, bf16[8,128,128]{2,1,0:T(8,128)(2,1)S(1)}, bf16[8,128,128]{2,1,0:T(8,128)(2,1)S(1)}) custom-call(bf16[32,128,128]{2,1,0:T(8,128)(2,1)S(1)} %copy-done.5, bf16[32,128,128]{2,1,0:T(8,128)(2,1)} %collective-permute-done.8.refs_1_, ...), custom_call_target="tpu_custom_call" | custom-call | flops 1100000000 | tf_op jit(solution)/shard_map/first_sum/pallas_call | solution.py:290
  118.0 0.7 copy-done.8
  118.7 0.7 copy-done.13
  119.4 0.7 copy-done.17
  120.1 1.2 first_sum.2
  121.3 0.7 copy-done.10
  122.0 0.7 copy-done.15
  122.7 0.7 copy-done.19
  123.4 0.7 copy-done.21
  124.1 24.3 %all-gather.4.cloned.1.call-done.refs_2_ = bf16[256,128,128]{2,1,0:T(8,128)(2,1)} async-done(((bf16[8,128,128]{2,1,0:T(8,128)(2,1)}), bf16[256,128,128]{2,1,0:T(8,128)(2,1)}) %all-gather.4.cloned.1.call-update) | async-done | bytes 8388624 | tf_op jit(solution)/shard_map/all_gather | solution.py:339
  148.4 17.7 %back.1 = (bf16[128,4096]{1,0:T(8,128)(2,1)}, f32[1,4096]{1,0:T(1,128)}) custom-call(s32[512]{0:T(512)} %refs_0_.9, s32[512]{0:T(512)} %refs_1_.9, bf16[256,128,128]{2,1,0:T(8,128)(2,1)} %all-gather.4.cloned.1.call-done.refs_2_, f32[128,4096]{1,0:T(8,128)} %get-tuple-element.37.refs_4_.refs_3_, bf16[128,4096]{1,0:T(8,128)(2,1)} %refs_4_.3, ...), custom_call_target="tpu_custom_call" | custom-call | flops 2200000000 | tf_op jit(solution)/shard_map/back/pallas_call | solution.py:216
  166.2 1.6 collective-permute-start.11
  167.8 2.7 %collective-permute-start.12 = (bf16[8,128,128]{2,1,0:T(8,128)(2,1)S(1)}, bf16[8,128,128]{2,1,0:T(8,128)(2,1)S(1)}, u32[]{:S(2)}, u32[]{:S(2)}) collective-permute-start(bf16[8,128,128]{2,1,0:T(8,128)(2,1)S(1)} %copy-done.14), channel_id=1, source_target_pairs={{0,64},{32,96},{64,0},{96,32},{1,65},{33,97},{65,1},{97,33},{2,66}... | collective-permute-start | bytes 786440 | tf_op jit(solution)/shard_map/ppermute | solution.py:274
  170.5 1.4 collective-permute-start.13
  172.0 2.3 collective-permute-start.6
  174.3 1.6 collective-permute-done.11.refs_5_
  176.0 8.2 %collective-permute-start.7 = (bf16[8,128,128]{2,1,0:T(8,128)(2,1)S(1)}, bf16[8,128,128]{2,1,0:T(8,128)(2,1)S(1)}, u32[]{:S(2)}, u32[]{:S(2)}) collective-permute-start(bf16[8,128,128]{2,1,0:T(8,128)(2,1)S(1)} %copy-done.16), channel_id=1, source_target_pairs={{0,24},{8,0},{16,8},{24,16},{1,25},{9,1},{17,9},{25,17},{2,26},{10... | collective-permute-start | bytes 786440 | tf_op jit(solution)/shard_map/ppermute | solution.py:274
  184.2 2.3 collective-permute-done.5.refs_1_
  186.5 2.9 %collective-permute-done.7.refs_3_ = bf16[8,128,128]{2,1,0:T(8,128)(2,1)S(1)} collective-permute-done((bf16[8,128,128]{2,1,0:T(8,128)(2,1)S(1)}, bf16[8,128,128]{2,1,0:T(8,128)(2,1)S(1)}, u32[]{:S(2)}, u32[]{:S(2)}) %collective-permute-start.7) | collective-permute-done | bytes 262176 | tf_op jit(solution)/shard_map/ppermute | solution.py:274
  189.4 1.2 copy-done.12
  190.9 1.5 collective-permute-start.14
  192.4 2.7 %collective-permute-start.15 = (bf16[16,128,128]{2,1,0:T(8,128)(2,1)S(1)}, bf16[16,128,128]{2,1,0:T(8,128)(2,1)S(1)}, u32[]{:S(2)}, u32[]{:S(2)}) collective-permute-start(bf16[16,128,128]{2,1,0:T(8,128)(2,1)S(1)} %second_sum.1.refs_5_.refs_0_), channel_id=1, source_target_pairs={{0,2},{1,3},{2,0},{3,1},{4,6},{5,7},{6,4},{7,5},{8,10},{9,11},{10,... | collective-permute-start | bytes 1572872 | tf_op jit(solution)/shard_map/ppermute | solution.py:274
  195.1 1.4 collective-permute-start.16
  196.5 16.0 %fore.1.refs_4_ = bf16[128,14336]{1,0:T(8,128)(2,1)} custom-call(s32[512]{0:T(512)} %refs_0_.9, s32[512]{0:T(512)} %refs_1_.9, bf16[256,128,128]{2,1,0:T(8,128)(2,1)} %all-gather.4.cloned.1.call-done.refs_2_, f32[128,14336]{1,0:T(8,128)} %get-tuple-element.33.refs_3_, bf16[128,4096]{1,0:T(8,128)(2,1)} %get-tuple-element.28.refs_3_.refs_4_, ...), custom_call_target="tpu_custom_call" | custom-call | flops 2200000000 | tf_op jit(solution)/shard_map/fore/pallas_call | solution.py:256
  212.5 4.6 %collective-permute-done.15.refs_2_ = bf16[16,128,128]{2,1,0:T(8,128)(2,1)S(1)} collective-permute-done((bf16[16,128,128]{2,1,0:T(8,128)(2,1)S(1)}, bf16[16,128,128]{2,1,0:T(8,128)(2,1)S(1)}, u32[]{:S(2)}, u32[]{:S(2)}) %collective-permute-start.15) | collective-permute-done | bytes 524320 | tf_op jit(solution)/shard_map/ppermute | solution.py:274
  217.1 2.0 copy-done.1
  219.2 1.0 copy-done.3
  220.2 1.2 last_sum.1
  221.4 18.5 %all-gather.8.cloned.1.call-done = f32[128,32,128]{2,1,0:T(8,128)} async-done(((f32[1,32,128]{2,1,0:T(8,128)}), f32[128,32,128]{2,1,0:T(8,128)}) %all-gather.8.cloned.1.call-update) | async-done | bytes 2097168 | tf_op jit(solution)/shard_map/all_gather | solution.py:346
  239.9 2.4 reduce_sum.9
  (57 shorter events, 1.2 us)
Async XLA Ops:
  7.2 82.0 %all-gather.6.cloned.1.call-start = ((), (), s32[]{:S(2)}) async-start(), calls=%async_computation.1 | async-start | bytes 8650752 | tf_op jit(solution)/shard_map/all_gather | solution.py:331
  9.1 139.3 %all-gather.4.cloned.1.call-start = ((), (), s32[]{:S(2)}) async-start(), calls=%async_computation | async-start | bytes 8650752 | tf_op jit(solution)/shard_map/all_gather | solution.py:339
  9.9 230.0 %all-gather.8.cloned.1.call-start = ((), (), s32[]{:S(2)}) async-start(), calls=%async_computation.2 | async-start | bytes 2113536 | tf_op jit(solution)/shard_map/all_gather | solution.py:346
  9.9 12.6 %collective-permute-start.1 = (bf16[128,14336]{1,0:T(8,128)(2,1)}, bf16[128,14336]{1,0:T(8,128)(2,1)}, u32[]{:S(2)}, u32[]{:S(2)}) collective-permute-start(bf16[128,14336]{1,0:T(8,128)(2,1)} %refs_7_.1), channel_id=1, source_target_pairs={{0,4},{4,0},{1,5},{5,1},{2,6},{6,2},{3,7},{7,3},{8,12},{12,8},{9,1... | collective-permute-start | bytes 11010056 | tf_op jit(solution)/shard_map/ppermute | solution.py:334
  10.0 7.7 %collective-permute-start = (bf16[128,4096]{1,0:T(8,128)(2,1)}, bf16[128,4096]{1,0:T(8,128)(2,1)S(1)}, u32[]{:S(2)}, u32[]{:S(2)}) collective-permute-start(bf16[128,4096]{1,0:T(8,128)(2,1)} %refs_4_.3), channel_id=1, source_target_pairs={{0,4},{4,0},{1,5},{5,1},{2,6},{6,2},{3,7},{7,3},{8,12},{12,8},{9,1... | collective-permute-start | bytes 3145736 | tf_op jit(solution)/shard_map/ppermute | solution.py:333
  17.8 1.0 copy-start.23
  47.1 38.0 %collective-permute-start.10 = (bf16[32,128,128]{2,1,0:T(8,128)(2,1)}, bf16[32,128,128]{2,1,0:T(8,128)(2,1)S(1)}, u32[]{:S(2)}, u32[]{:S(2)}) collective-permute-start(bf16[32,128,128]{2,1,0:T(8,128)(2,1)} %get-tuple-element.32.refs_5_), channel_id=1, source_target_pairs={{0,24},{8,0},{16,8},{24,16},{1,25},{9,1},{17,9},{25,17},{2,26},{10... | collective-permute-start | bytes 3145736 | tf_op jit(solution)/shard_map/ppermute | solution.py:274
  51.3 59.9 %collective-permute-start.8 = (bf16[32,128,128]{2,1,0:T(8,128)(2,1)}, bf16[32,128,128]{2,1,0:T(8,128)(2,1)}, u32[]{:S(2)}, u32[]{:S(2)}) collective-permute-start(bf16[32,128,128]{2,1,0:T(8,128)(2,1)} %get-tuple-element.43), channel_id=1, source_target_pairs={{0,8},{8,16},{16,24},{24,0},{1,9},{9,17},{17,25},{25,1},{2,10},{10... | collective-permute-start | bytes 3145736 | tf_op jit(solution)/shard_map/ppermute | solution.py:274
  51.3 62.1 %collective-permute-start.9 = (bf16[32,128,128]{2,1,0:T(8,128)(2,1)}, bf16[32,128,128]{2,1,0:T(8,128)(2,1)}, u32[]{:S(2)}, u32[]{:S(2)}) collective-permute-start(bf16[32,128,128]{2,1,0:T(8,128)(2,1)} %get-tuple-element.44), channel_id=1, source_target_pairs={{0,16},{8,24},{16,0},{24,8},{1,17},{9,25},{17,1},{25,9},{2,18},{10... | collective-permute-start | bytes 3145736 | tf_op jit(solution)/shard_map/ppermute | solution.py:274
  53.2 66.9 %collective-permute-start.4 = (bf16[32,128,128]{2,1,0:T(8,128)(2,1)}, bf16[32,128,128]{2,1,0:T(8,128)(2,1)S(1)}, u32[]{:S(2)}, u32[]{:S(2)}) collective-permute-start(bf16[32,128,128]{2,1,0:T(8,128)(2,1)} %get-tuple-element.31.refs_7_), channel_id=1, source_target_pairs={{0,96},{32,0},{64,32},{96,64},{1,97},{33,1},{65,33},{97,65},{2,98}... | collective-permute-start | bytes 3145736 | tf_op jit(solution)/shard_map/ppermute | solution.py:274
  56.2 63.8 %collective-permute-start.2 = (bf16[32,128,128]{2,1,0:T(8,128)(2,1)}, bf16[32,128,128]{2,1,0:T(8,128)(2,1)S(1)}, u32[]{:S(2)}, u32[]{:S(2)}) collective-permute-start(bf16[32,128,128]{2,1,0:T(8,128)(2,1)} %get-tuple-element.35), channel_id=1, source_target_pairs={{0,32},{32,64},{64,96},{96,0},{1,33},{33,65},{65,97},{97,1},{2,34}... | collective-permute-start | bytes 3145736 | tf_op jit(solution)/shard_map/ppermute | solution.py:274
  85.1 1.0 copy-start.6
  86.1 34.0 %collective-permute-start.3 = (bf16[32,128,128]{2,1,0:T(8,128)(2,1)}, bf16[32,128,128]{2,1,0:T(8,128)(2,1)S(1)}, u32[]{:S(2)}, u32[]{:S(2)}) collective-permute-start(bf16[32,128,128]{2,1,0:T(8,128)(2,1)} %get-tuple-element.36), channel_id=1, source_target_pairs={{0,64},{32,96},{64,0},{96,32},{1,65},{33,97},{65,1},{97,33},{2,66}... | collective-permute-start | bytes 3145736 | tf_op jit(solution)/shard_map/ppermute | solution.py:274
  89.1 24.3 %copy-start.5 = (bf16[32,128,128]{2,1,0:T(8,128)(2,1)S(1)}, bf16[32,128,128]{2,1,0:T(8,128)(2,1)}, u32[]{:S(2)}) copy-start(bf16[32,128,128]{2,1,0:T(8,128)(2,1)} %get-tuple-element.42.refs_0_) | copy-start | bytes 3145732
  89.1 24.3 %copy-start.7 = (bf16[32,128,128]{2,1,0:T(8,128)(2,1)S(1)}, bf16[32,128,128]{2,1,0:T(8,128)(2,1)}, u32[]{:S(2)}) copy-start(bf16[32,128,128]{2,1,0:T(8,128)(2,1)} %copy-done.6) | copy-start | bytes 3145732
  89.1 31.0 %copy-start.4 = (bf16[32,128,128]{2,1,0:T(8,128)(2,1)S(1)}, bf16[32,128,128]{2,1,0:T(8,128)(2,1)}, u32[]{:S(2)}) copy-start(bf16[32,128,128]{2,1,0:T(8,128)(2,1)} %get-tuple-element.34.refs_0_) | copy-start | bytes 3145732
  113.4 1.6 copy-start
  118.0 0.7 copy-start.8
  118.7 0.7 copy-start.13
  119.4 0.7 copy-start.17
  121.3 0.7 copy-start.10
  122.0 0.7 copy-start.15
  122.7 0.7 copy-start.19
  123.4 0.7 copy-start.21
  148.4 17.8 %copy-start.18 = (bf16[8,128,128]{2,1,0:T(8,128)(2,1)S(1)}, bf16[8,128,128]{2,1,0:T(8,128)(2,1)}, u32[]{:S(2)}) copy-start(bf16[8,128,128]{2,1,0:T(8,128)(2,1)} %copy-done.17) | copy-start | bytes 786436
  148.4 19.3 %copy-start.14 = (bf16[8,128,128]{2,1,0:T(8,128)(2,1)S(1)}, bf16[8,128,128]{2,1,0:T(8,128)(2,1)}, u32[]{:S(2)}) copy-start(bf16[8,128,128]{2,1,0:T(8,128)(2,1)} %copy-done.13) | copy-start | bytes 786436
  148.4 23.5 %copy-start.22 = (bf16[8,128,128]{2,1,0:T(8,128)(2,1)S(1)}, bf16[8,128,128]{2,1,0:T(8,128)(2,1)}, u32[]{:S(2)}) copy-start(bf16[8,128,128]{2,1,0:T(8,128)(2,1)} %copy-done.21) | copy-start | bytes 786436
  148.4 23.6 %copy-start.20 = (bf16[8,128,128]{2,1,0:T(8,128)(2,1)S(1)}, bf16[8,128,128]{2,1,0:T(8,128)(2,1)}, u32[]{:S(2)}) copy-start(bf16[8,128,128]{2,1,0:T(8,128)(2,1)} %copy-done.19) | copy-start | bytes 786436
  148.4 27.5 %copy-start.16 = (bf16[8,128,128]{2,1,0:T(8,128)(2,1)S(1)}, bf16[8,128,128]{2,1,0:T(8,128)(2,1)}, u32[]{:S(2)}) copy-start(bf16[8,128,128]{2,1,0:T(8,128)(2,1)} %copy-done.15) | copy-start | bytes 786436
  148.4 40.9 %copy-start.9 = (bf16[8,128,128]{2,1,0:T(8,128)(2,1)S(1)}, bf16[8,128,128]{2,1,0:T(8,128)(2,1)}, u32[]{:S(2)}) copy-start(bf16[8,128,128]{2,1,0:T(8,128)(2,1)} %copy-done.8) | copy-start | bytes 786436
  148.4 40.9 %copy-start.11 = (bf16[8,128,128]{2,1,0:T(8,128)(2,1)S(1)}, bf16[8,128,128]{2,1,0:T(8,128)(2,1)}, u32[]{:S(2)}) copy-start(bf16[8,128,128]{2,1,0:T(8,128)(2,1)} %copy-done.10) | copy-start | bytes 786436
  166.2 9.8 %collective-permute-start.11 = (bf16[8,128,128]{2,1,0:T(8,128)(2,1)S(1)}, bf16[8,128,128]{2,1,0:T(8,128)(2,1)S(1)}, u32[]{:S(2)}, u32[]{:S(2)}) collective-permute-start(bf16[8,128,128]{2,1,0:T(8,128)(2,1)S(1)} %copy-done.18), channel_id=1, source_target_pairs={{0,32},{32,64},{64,96},{96,0},{1,33},{33,65},{65,97},{97,1},{2,34}... | collective-permute-start | bytes 786440 | tf_op jit(solution)/shard_map/ppermute | solution.py:274
  167.8 16.4 %collective-permute-start.12 = (bf16[8,128,128]{2,1,0:T(8,128)(2,1)S(1)}, bf16[8,128,128]{2,1,0:T(8,128)(2,1)S(1)}, u32[]{:S(2)}, u32[]{:S(2)}) collective-permute-start(bf16[8,128,128]{2,1,0:T(8,128)(2,1)S(1)} %copy-done.14), channel_id=1, source_target_pairs={{0,64},{32,96},{64,0},{96,32},{1,65},{33,97},{65,1},{97,33},{2,66}... | collective-permute-start | bytes 786440 | tf_op jit(solution)/shard_map/ppermute | solution.py:274
  170.5 13.7 %collective-permute-start.13 = (bf16[8,128,128]{2,1,0:T(8,128)(2,1)S(1)}, bf16[8,128,128]{2,1,0:T(8,128)(2,1)S(1)}, u32[]{:S(2)}, u32[]{:S(2)}) collective-permute-start(bf16[8,128,128]{2,1,0:T(8,128)(2,1)S(1)} %get-tuple-element.48), channel_id=1, source_target_pairs={{0,96},{32,0},{64,32},{96,64},{1,97},{33,1},{65,33},{97,65},{2,98}... | collective-permute-start | bytes 786440 | tf_op jit(solution)/shard_map/ppermute | solution.py:274
  171.9 14.6 %collective-permute-start.5 = (bf16[8,128,128]{2,1,0:T(8,128)(2,1)S(1)}, bf16[8,128,128]{2,1,0:T(8,128)(2,1)S(1)}, u32[]{:S(2)}, u32[]{:S(2)}) collective-permute-start(bf16[8,128,128]{2,1,0:T(8,128)(2,1)S(1)} %copy-done.22), channel_id=1, source_target_pairs={{0,8},{8,16},{16,24},{24,0},{1,9},{9,17},{17,25},{25,1},{2,10},{10... | collective-permute-start | bytes 786440 | tf_op jit(solution)/shard_map/ppermute | solution.py:274
  172.0 14.5 %collective-permute-start.6 = (bf16[8,128,128]{2,1,0:T(8,128)(2,1)S(1)}, bf16[8,128,128]{2,1,0:T(8,128)(2,1)S(1)}, u32[]{:S(2)}, u32[]{:S(2)}) collective-permute-start(bf16[8,128,128]{2,1,0:T(8,128)(2,1)S(1)} %copy-done.20), channel_id=1, source_target_pairs={{0,16},{8,24},{16,0},{24,8},{1,17},{9,25},{17,1},{25,9},{2,18},{10... | collective-permute-start | bytes 786440 | tf_op jit(solution)/shard_map/ppermute | solution.py:274
  176.0 13.4 %collective-permute-start.7 = (bf16[8,128,128]{2,1,0:T(8,128)(2,1)S(1)}, bf16[8,128,128]{2,1,0:T(8,128)(2,1)S(1)}, u32[]{:S(2)}, u32[]{:S(2)}) collective-permute-start(bf16[8,128,128]{2,1,0:T(8,128)(2,1)S(1)} %copy-done.16), channel_id=1, source_target_pairs={{0,24},{8,0},{16,8},{24,16},{1,25},{9,1},{17,9},{25,17},{2,26},{10... | collective-permute-start | bytes 786440 | tf_op jit(solution)/shard_map/ppermute | solution.py:274
  189.4 1.2 copy-start.12
  190.8 5.7 %copy-start.2 = (bf16[16,128,128]{2,1,0:T(8,128)(2,1)}, bf16[16,128,128]{2,1,0:T(8,128)(2,1)S(1)}, u32[]{:S(2)}) copy-start(bf16[16,128,128]{2,1,0:T(8,128)(2,1)S(1)} %second_sum.1.refs_5_.refs_0_) | copy-start | bytes 1572868
  190.9 21.7 %collective-permute-start.14 = (bf16[16,128,128]{2,1,0:T(8,128)(2,1)S(1)}, bf16[16,128,128]{2,1,0:T(8,128)(2,1)S(1)}, u32[]{:S(2)}, u32[]{:S(2)}) collective-permute-start(bf16[16,128,128]{2,1,0:T(8,128)(2,1)S(1)} %second_sum.1.refs_5_.refs_0_), channel_id=1, source_target_pairs={{0,1},{1,2},{2,3},{3,0},{4,5},{5,6},{6,7},{7,4},{8,9},{9,10},{10,1... | collective-permute-start | bytes 1572872 | tf_op jit(solution)/shard_map/ppermute | solution.py:274
  192.4 24.7 %collective-permute-start.15 = (bf16[16,128,128]{2,1,0:T(8,128)(2,1)S(1)}, bf16[16,128,128]{2,1,0:T(8,128)(2,1)S(1)}, u32[]{:S(2)}, u32[]{:S(2)}) collective-permute-start(bf16[16,128,128]{2,1,0:T(8,128)(2,1)S(1)} %second_sum.1.refs_5_.refs_0_), channel_id=1, source_target_pairs={{0,2},{1,3},{2,0},{3,1},{4,6},{5,7},{6,4},{7,5},{8,10},{9,11},{10,... | collective-permute-start | bytes 1572872 | tf_op jit(solution)/shard_map/ppermute | solution.py:274
  195.1 22.0 %collective-permute-start.16 = (bf16[16,128,128]{2,1,0:T(8,128)(2,1)S(1)}, bf16[16,128,128]{2,1,0:T(8,128)(2,1)S(1)}, u32[]{:S(2)}, u32[]{:S(2)}) collective-permute-start(bf16[16,128,128]{2,1,0:T(8,128)(2,1)S(1)} %second_sum.1.refs_5_.refs_0_), channel_id=1, source_target_pairs={{0,3},{1,0},{2,1},{3,2},{4,7},{5,4},{6,5},{7,6},{8,11},{9,8},{10,9... | collective-permute-start | bytes 1572872 | tf_op jit(solution)/shard_map/ppermute | solution.py:274
  217.1 2.0 copy-start.1
  219.2 1.0 copy-start.3
Sparse Core Ops, SparseCore 0:
  10.3 66.1 all-gather.5
  78.7 69.6 all-gather.3
  166.3 73.5 all-gather.7

commit v3 on v2

--- a/solution.py
+++ b/solution.py
@@ -125,68 +125,29 @@
     )(rows, cols, pos, turned, turned_other, own, other, *ties)
 
 
-def place_of(k, half, step):
-    i = pl.program_id(0) * step + k
-    return i // 8 * 16 + half * 8 + i % 8
-
-
-def both_kernel(half, step, rows, cols, tiles_ref, normed_ref, g_ref, *refs):
-    out_ref, back_ref = refs[-2:]
-
-    @pl.when(pl.program_id(0) == 0)
-    def _():
-        out_ref[...] = jnp.zeros_like(out_ref)
-        back_ref[...] = jnp.zeros_like(back_ref)
-
-    def one(k, carry):
-        index = place_of(k, half, step)
-        r, q = rows[index], cols[index]
-        weight = tiles_ref[k]
-        out_ref[:, cols_at(q)] += dot(normed_ref[:, cols_at(r)], weight)
-        back_ref[:, cols_at(r)] += dot_t(g_ref[:, cols_at(q)], weight)
-        return carry
-
-    lax.fori_loop(0, step, one, 0, unroll=8)
-
-
-def both(half, rows, cols, tiles, normed, g, ties=()):
-    number, step = tiles.shape[0], 32
-    return pl.pallas_call(
-        lambda *refs: both_kernel(half, step, *refs),
-        out_shape=(jax.ShapeDtypeStruct(g.shape, F4), jax.ShapeDtypeStruct(normed.shape, F4)),
-        grid_spec=pltpu.PrefetchScalarGridSpec(
-            num_scalar_prefetch=2,
-            grid=(number // step,),
-            in_specs=[pl.BlockSpec((step, T, T), lambda i, *_: (i, 0, 0)), whole(normed.shape), whole(g.shape)]
-            + [ANY] * len(ties),
-            out_specs=[whole(g.shape), whole(normed.shape)],
-        ),
-        compiler_params=params(56),
-        cost_estimate=cost(2, 0),
-        name="both",
-    )(rows, cols, tiles, normed, g, *ties)
-
-
-def back_kernel(
-    half, step, rows, cols, tiles_ref, back_in_ref, x_ref, scale_ref, gain_ref, g_ref, *refs
+def project_kernel(
+    step, rows, cols, tiles_ref, x_ref, normed_ref, scale_ref, gain_ref, g_ref, *refs
 ):
-    token_grad_ref, sums_ref, back_acc = refs[-3:]
+    projected_ref, token_grad_ref, sums_ref, out_acc, back_acc = refs[-5:]
+    s = pl.program_id(0)
     count, width = x_ref.shape
     blocks = width // T
 
-    @pl.when(pl.program_id(0) == 0)
+    @pl.when(s == 0)
     def _():
-        back_acc[...] = back_in_ref[...]
+        out_acc[...] = jnp.zeros_like(out_acc)
+        back_acc[...] = jnp.zeros_like(back_acc)
 
     def one(k, carry):
-        index = place_of(k, half, step)
-        r, q = rows[index], cols[index]
-        back_acc[:, cols_at(r)] += dot_t(g_ref[:, cols_at(q)], tiles_ref[k])
+        r, q = rows[s * step + k], cols[s * step + k]
+        weight = tiles_ref[k]
+        out_acc[:, cols_at(q)] += dot(normed_ref[:, cols_at(r)], weight)
+        back_acc[:, cols_at(r)] += dot_t(g_ref[:, cols_at(q)], weight)
         return carry
 
     lax.fori_loop(0, step, one, 0, unroll=8)
 
-    @pl.when(pl.program_id(0) == pl.num_programs(0) - 1)
+    @pl.when(s == pl.num_programs(0) - 1)
     def _():
         scale = scale_ref[...]
 
@@ -209,65 +170,36 @@
 
         lax.fori_loop(0, blocks, finish, 0, unroll=2)
 
-
-def back(half, rows, cols, tiles, back_in, x, scale, gain, g, ties=()):
+        def write(b, carry):
+            projected_ref[:, cols_at(b)] = out_acc[:, cols_at(b)].astype(BF)
+            return carry
+
+        lax.fori_loop(0, g_ref.shape[1] // T, write, 0, unroll=4)
+
+
+def project(rows, cols, tiles, x, normed, scale, gain, g, ties=()):
     number, step = tiles.shape[0], 32
-    width = x.shape[1]
-    return pl.pallas_call(
-        lambda *refs: back_kernel(half, step, *refs),
-        out_shape=(jax.ShapeDtypeStruct(x.shape, BF), jax.ShapeDtypeStruct((1, width), F4)),
+    count, width = x.shape
+    return pl.pallas_call(
+        lambda *refs: project_kernel(step, *refs),
+        out_shape=(
+            jax.ShapeDtypeStruct(g.shape, BF),
+            jax.ShapeDtypeStruct(x.shape, BF),
+            jax.ShapeDtypeStruct((1, width), F4),
+        ),
         grid_spec=pltpu.PrefetchScalarGridSpec(
             num_scalar_prefetch=2,
             grid=(number // step,),
             in_specs=[pl.BlockSpec((step, T, T), lambda i, *_: (i, 0, 0))]
-            + [whole(a.shape) for a in (back_in, x, scale, gain, g)]
+            + [whole(a.shape) for a in (x, normed, scale, gain, g)]
             + [ANY] * len(ties),
-            out_specs=[whole(x.shape), whole((1, width))],
-            scratch_shapes=[pltpu.VMEM(x.shape, F4)],
-        ),
-        compiler_params=params(56),
+            out_specs=[whole(g.shape), whole(x.shape), whole((1, width))],
+            scratch_shapes=[pltpu.VMEM(g.shape, F4), pltpu.VMEM(x.shape, F4)],
+        ),
+        compiler_params=params(32),
         cost_estimate=cost(2, 0),
-        name="back",
-    )(rows, cols, tiles, back_in, x, scale, gain, g, *ties)
-
-
-def fore_kernel(half, step, rows, cols, tiles_ref, out_in_ref, normed_ref, *refs):
-    projected_ref, out_acc = refs[-2:]
-
-    @pl.when(pl.program_id(0) == 0)
-    def _():
-        out_acc[...] = out_in_ref[...]
-
-    def one(k, carry):
-        index = place_of(k, half, step)
-        r, q = rows[index], cols[index]
-        out_acc[:, cols_at(q)] += dot(normed_ref[:, cols_at(r)], tiles_ref[k])
-        return carry
-
-    lax.fori_loop(0, step, one, 0, unroll=8)
-
-    @pl.when(pl.program_id(0) == pl.num_programs(0) - 1)
-    def _():
-        projected_ref[...] = out_acc[...].astype(BF)
-
-
-def fore(half, rows, cols, tiles, out_in, normed, ties=()):
-    number, step = tiles.shape[0], 32
-    return pl.pallas_call(
-        lambda *refs: fore_kernel(half, step, *refs),
-        out_shape=jax.ShapeDtypeStruct(out_in.shape, BF),
-        grid_spec=pltpu.PrefetchScalarGridSpec(
-            num_scalar_prefetch=2,
-            grid=(number // step,),
-            in_specs=[pl.BlockSpec((step, T, T), lambda i, *_: (i, 0, 0)), whole(out_in.shape), whole(normed.shape)]
-            + [ANY] * len(ties),
-            out_specs=whole(out_in.shape),
-            scratch_shapes=[pltpu.VMEM(out_in.shape, F4)],
-        ),
-        compiler_params=params(56),
-        cost_estimate=cost(2, 0),
-        name="fore",
-    )(rows, cols, tiles, out_in, normed, *ties)
+        name="project",
+    )(rows, cols, tiles, x, normed, scale, gain, g, *ties)
 
 
 def ring(piece, axis, shift):
@@ -299,25 +231,28 @@
     )(*pieces, *ties)
 
 
-def sum_of_four(groups, dtype, ties, name):
+def sum_of_four(groups, dtype, passed, name):
     count = groups[0][0].shape[0]
+    arrays = [a for group in groups for a in group]
 
     def kernel(*refs):
-        out = refs[-1]
+        out = refs[len(arrays) + len(passed)]
         for g in range(len(groups)):
             for i in range(count):
                 a, b, c, d = (r[i].astype(F4) for r in refs[4 * g : 4 * g + 4])
                 out[g * count + i] = ((a + c) + (b + d)).astype(dtype)
-
-    arrays = [a for group in groups for a in group]
+        for k in range(len(passed)):
+            refs[len(arrays) + len(passed) + 1 + k][...] = refs[len(arrays) + k][...]
+
     return pl.pallas_call(
         kernel,
-        out_shape=jax.ShapeDtypeStruct((count * len(groups), T, T), dtype),
-        in_specs=[pl.BlockSpec(memory_space=pltpu.VMEM)] * len(arrays) + [ANY] * len(ties),
+        out_shape=[jax.ShapeDtypeStruct((count * len(groups), T, T), dtype)]
+        + [jax.ShapeDtypeStruct(a.shape, a.dtype) for a in passed],
+        in_specs=[pl.BlockSpec(memory_space=pltpu.VMEM)] * (len(arrays) + len(passed)),
         compiler_params=params(32),
         cost_estimate=cost(1, 0),
         name=name,
-    )(*arrays, *ties)
+    )(*arrays, *passed)
 
 
 def exchange(pieces, axis):
@@ -328,7 +263,7 @@
     gain2 = gain.reshape(1, -1)
     pos = jnp.stack([lax.axis_index(a).astype(jnp.int32) for a in ("y", "z", "c", "x")])
     owners = ("y", "z", "c")
-    piece0 = lax.all_gather(tiles[:8], owners, axis=0, tiled=True)
+    piece = lax.all_gather(tiles, owners, axis=0, tiled=True)
     swap = [(0, 1), (1, 0)]
     tokens_other = lax.ppermute(tokens, "c", swap)
     g_other = lax.ppermute(cotangent, "c", swap)
@@ -336,19 +271,19 @@
     _, turned_other, _ = norm(tokens_other, gain2)
     part_y = grads("y", 8, rows, cols, pos, turned, turned_other, cotangent, g_other)
     part_z = grads("z", 8, rows, cols, pos, turned, turned_other, cotangent, g_other, (part_y[3],))
-    piece1 = lax.all_gather(tiles[8:], owners, axis=0, tiled=True)
-    out0, back0 = both(0, rows, cols, piece0, normed, cotangent, (part_z[3],))
-    mid_y = first_sum(exchange(part_y, "y"), (back0,))
-    mid_z = first_sum(exchange(part_z, "z"), (back0,))
-    token_grad, gain_part = back(
-        1, rows, cols, piece1, back0, tokens, scale, gain2, cotangent, (mid_y[0], mid_z[0])
+    mid_y = first_sum(exchange(part_y, "y"), (part_z[3],))
+    mid_z = first_sum(exchange(part_z, "z"), ())
+    projected, token_grad, sums = project(
+        rows, cols, piece, tokens, normed, scale, gain2, cotangent, (mid_y[0], mid_z[0])
     )
-    gains = lax.all_gather(gain_part.reshape(1, -1, T), ALL, axis=0, tiled=True)
-    sent = sum_of_four([exchange(mid_y, "z"), exchange(mid_z, "y")], BF, (token_grad,), "second_sum")
-    projected = fore(1, rows, cols, piece1, out0, normed, (sent,))
-    tile_grad = sum_of_four([exchange([sent] * 4, "x")], F4, (projected,), "last_sum")
-    gain_grad = jnp.sum(gains, axis=0).reshape(-1)
-    return (projected, token_grad, tile_grad, gain_grad)
+    sums = sums.reshape(-1, T)
+    sent, sums = sum_of_four([exchange(mid_y, "z"), exchange(mid_z, "y")], BF, (sums,), "second_sum")
+    (tile_grad,) = sum_of_four([exchange([sent] * 4, "x")], F4, (), "last_sum")
+    sums = sums + lax.ppermute(sums, "c", swap)
+    for axis in ("z", "y", "x"):
+        own, right, opposite, left = exchange([sums] * 4, axis)
+        sums = (own + opposite) + (right + left)
+    return (projected, token_grad, tile_grad, sums.reshape(-1))
 
 
 def solution(mesh):

time: 251 us -> 230 us (0.916)
  Pallas kernels: 93.6 us -> 76.3 us
  local copies, waits for them, and re-layouts: 14.7 us -> 4.27 us
  starting transfers between devices: 34.9 us -> 41.1 us
  waiting for transfers between devices: 88.8 us -> 92.1 us
    ppermute x15 -> x24, waiting for transfers between devices: 42.4 us -> 87.4 us  [ring(): return lax.ppermute(piece, axis, [(i, (i + shift) % 4) for i in range(4)])]
    all_gather x3 -> x1, waiting for transfers between devices: 42.8 us -> 0.01 us  [shards(): piece = lax.all_gather(tiles, owners, axis=0, tiled=True)]
    pallas_call x5 -> x3, Pallas kernels: 57.3 us -> 39.3 us  [the longest x1 36.7 us: project(): pl.pallas_call(lambda *refs: project_kernel(step, *refs), out_shape=(jax....]
    unnamed x48 -> x28, local copies, waits for them, and re-layouts: 12.8 us -> 4.27 us
    ppermute x15 -> x24, starting transfers between devices: 34.2 us -> 40.4 us  [ring(): return lax.ppermute(piece, axis, [(i, (i + shift) % 4) for i in range(4)])]
  transfers between devices with their start and end apart: 20 -> 28, of which waited for: 9 -> 9; matrix products, arithmetic and copies ran while one was open for 0% -> 1% of each run, Pallas kernels for 31% -> 32%
where the time goes in v3:
time: 230 us; the launch traced here: 229 us
  waiting for transfers between devices  92.1 us (40%)
  Pallas kernels  76.3 us (33%)
  starting transfers between devices  41.1 us (18%)
  between operations  14.2 us (6%)
  local copies, waits for them, and re-layouts  4.27 us (2%)
    ppermute x24, waiting for transfers between devices, ring(): return lax.ppermute(piece, axis, [(i, (i + shift) % 4) for i in range(4)])  87.4 us
    ppermute x24, starting transfers between devices, ring(): return lax.ppermute(piece, axis, [(i, (i + shift) % 4) for i in range(4)])  40.4 us
    pallas_call x1, Pallas kernels, project(): pl.pallas_call(lambda *refs: project_kernel(step, *refs), out_shape=(jax....  36.7 us
    pallas_call x2, Pallas kernels, grads(): pl.pallas_call(lambda *refs: grad_kernel(first, per, step, *refs), out_sh...  25.4 us
    pallas_call x2, Pallas kernels, norm(): pl.pallas_call(norm_kernel, out_shape=(jax.ShapeDtypeStruct((count, width...  7.56 us
  transfers between devices with their start and end apart: 28, of which 9 were waited for; matrix products, arithmetic and copies ran while one was open for 1% of the time, Pallas kernels for 32%

profile of v3, /device:TPU:0, one launch (start us, length us, event | category | flops | bytes accessed | tf_op | source)
XLA Modules:
  0.0 229.1 jit_solution(3137212102386784950)
XLA Ops:
  7.2 0.7 all-gather.2.cloned.1.call-update
  7.9 0.1 collective-permute-start.1
  8.0 0.5 collective-permute-start
  8.5 3.8 %norm.2 = (bf16[128,4096]{1,0:T(8,128)(2,1)}, bf16[32,128,128]{2,1,0:T(8,128)(2,1)}, f32[128,128]{1,0:T(8,128)}) custom-call(bf16[128,4096]{1,0:T(8,128)(2,1)} %refs_3_.1, f32[1,4096]{1,0:T(1,128)} %bitcast.8), custom_call_target="tpu_custom_call" | custom-call | flops 1100000000 | tf_op jit(solution)/shard_map/norm/pallas_call | solution.py:66
  12.3 0.6 pad_add_fusion.refs_2_
  12.9 2.9 %collective-permute-done.x_ref = bf16[128,4096]{1,0:T(8,128)(2,1)S(1)} collective-permute-done((bf16[128,4096]{1,0:T(8,128)(2,1)}, bf16[128,4096]{1,0:T(8,128)(2,1)S(1)}, u32[]{:S(2)}, u32[]{:S(2)}) %collective-permute-start) | collective-permute-done | bytes 1048608 | tf_op jit(solution)/shard_map/ppermute | solution.py:268
  15.7 1.0 copy-done.13
  16.7 3.8 %norm.3 = (bf16[128,4096]{1,0:T(8,128)(2,1)}, bf16[32,128,128]{2,1,0:T(8,128)(2,1)}, f32[128,128]{1,0:T(8,128)}) custom-call(bf16[128,4096]{1,0:T(8,128)(2,1)} %copy-done.13, f32[1,4096]{1,0:T(1,128)} %bitcast.9), custom_call_target="tpu_custom_call" | custom-call | flops 1100000000 | tf_op jit(solution)/shard_map/norm/pallas_call | solution.py:66
  20.5 12.9 %grads_y.1 = (bf16[32,128,128]{2,1,0:T(8,128)(2,1)}, bf16[32,128,128]{2,1,0:T(8,128)(2,1)}, bf16[32,128,128]{2,1,0:T(8,128)(2,1)}, bf16[32,128,128]{2,1,0:T(8,128)(2,1)}) custom-call(s32[512]{0:T(512)} %refs_0_.5, s32[512]{0:T(512)} %refs_1_.5, s32[4]{0:T(128)} %pad_add_fusion.refs_2_, bf16[32,128,128]{2,1,0:T(8,128)(2,1)} %get-tuple-element.31.refs_3_, ...), custom_call_target="tpu_custom_call" | custom-call | flops 2200000000 | tf_op jit(solution)/shard_map/grads_y/pallas_call | solution.py:113
  33.4 12.5 %grads_z.1 = (bf16[32,128,128]{2,1,0:T(8,128)(2,1)}, bf16[32,128,128]{2,1,0:T(8,128)(2,1)}, bf16[32,128,128]{2,1,0:T(8,128)(2,1)}, bf16[32,128,128]{2,1,0:T(8,128)(2,1)}) custom-call(s32[512]{0:T(512)} %refs_0_.5, s32[512]{0:T(512)} %refs_1_.5, s32[4]{0:T(128)} %pad_add_fusion.refs_2_, bf16[32,128,128]{2,1,0:T(8,128)(2,1)} %get-tuple-element.31.refs_3_, ...), custom_call_target="tpu_custom_call" | custom-call | flops 2200000000 | tf_op jit(solution)/shard_map/grads_z/pallas_call | solution.py:113
  45.9 3.9 %collective-permute-start.7 = (bf16[32,128,128]{2,1,0:T(8,128)(2,1)}, bf16[32,128,128]{2,1,0:T(8,128)(2,1)S(1)}, u32[]{:S(2)}, u32[]{:S(2)}) collective-permute-start(bf16[32,128,128]{2,1,0:T(8,128)(2,1)} %get-tuple-element.37.refs_4_), channel_id=1, source_target_pairs={{0,24},{8,0},{16,8},{24,16},{1,25},{9,1},{17,9},{25,17},{2,26},{10... | collective-permute-start | bytes 3145736 | tf_op jit(solution)/shard_map/ppermute | solution.py:206
  49.8 2.0 collective-permute-start.6
  51.7 2.9 %collective-permute-start.4 = (bf16[32,128,128]{2,1,0:T(8,128)(2,1)S(1)}, bf16[32,128,128]{2,1,0:T(8,128)(2,1)S(1)}, u32[]{:S(2)}, u32[]{:S(2)}) collective-permute-start(bf16[32,128,128]{2,1,0:T(8,128)(2,1)S(1)} %copy-done.10), channel_id=1, source_target_pairs={{0,96},{32,0},{64,32},{96,64},{1,97},{33,1},{65,33},{97,65},{2,98}... | collective-permute-start | bytes 3145736 | tf_op jit(solution)/shard_map/ppermute | solution.py:206
  54.7 43.0 %collective-permute-done.7.refs_3_ = bf16[32,128,128]{2,1,0:T(8,128)(2,1)S(1)} collective-permute-done((bf16[32,128,128]{2,1,0:T(8,128)(2,1)}, bf16[32,128,128]{2,1,0:T(8,128)(2,1)S(1)}, u32[]{:S(2)}, u32[]{:S(2)}) %collective-permute-start.7) | collective-permute-done | bytes 1048608 | tf_op jit(solution)/shard_map/ppermute | solution.py:206
  97.7 3.2 %collective-permute-start.3 = (bf16[32,128,128]{2,1,0:T(8,128)(2,1)S(1)}, bf16[32,128,128]{2,1,0:T(8,128)(2,1)S(1)}, u32[]{:S(2)}, u32[]{:S(2)}) collective-permute-start(bf16[32,128,128]{2,1,0:T(8,128)(2,1)S(1)} %copy-done.11), channel_id=1, source_target_pairs={{0,64},{32,96},{64,0},{96,32},{1,65},{33,97},{65,1},{97,33},{2,66}... | collective-permute-start | bytes 3145736 | tf_op jit(solution)/shard_map/ppermute | solution.py:206
  100.9 27.3 %collective-permute-done.6.refs_2_ = bf16[32,128,128]{2,1,0:T(8,128)(2,1)S(1)} collective-permute-done((bf16[32,128,128]{2,1,0:T(8,128)(2,1)}, bf16[32,128,128]{2,1,0:T(8,128)(2,1)S(1)}, u32[]{:S(2)}, u32[]{:S(2)}) %collective-permute-start.6) | collective-permute-done | bytes 1048608 | tf_op jit(solution)/shard_map/ppermute | solution.py:206
  128.3 1.2 copy-done.5
  129.5 2.0 first_sum.3
  131.5 1.6 collective-permute-start.11
  133.0 2.7 %collective-permute-start.12 = (bf16[8,128,128]{2,1,0:T(8,128)(2,1)}, bf16[8,128,128]{2,1,0:T(8,128)(2,1)S(1)}, u32[]{:S(2)}, u32[]{:S(2)}) collective-permute-start(bf16[8,128,128]{2,1,0:T(8,128)(2,1)} %get-tuple-element.49), channel_id=1, source_target_pairs={{0,64},{32,96},{64,0},{96,32},{1,65},{33,97},{65,1},{97,33},{2,66}... | collective-permute-start | bytes 786440 | tf_op jit(solution)/shard_map/ppermute | solution.py:206
  135.8 1.4 collective-permute-start.13
  137.2 2.1 first_sum.2
  139.3 1.1 collective-permute-start.10
  140.4 0.9 collective-permute-start.8
  141.4 0.7 collective-permute-start.9
  142.1 2.0 copy-done
  144.2 36.7 %project.1 = (bf16[128,14336]{1,0:T(8,128)(2,1)}, bf16[128,4096]{1,0:T(8,128)(2,1)}, f32[1,4096]{1,0:T(1,128)S(1)}) custom-call(s32[512]{0:T(512)S(1)} %copy-done.7, s32[512]{0:T(512)S(1)} %copy-done.8, bf16[512,128,128]{2,1,0:T(8,128)(2,1)} %all-gather.2.cloned.1.call-done.refs_2_, bf16[128,4096]{1,0:T(8,128)(2,1)S(1)} %copy-done.1, ...), custom_call_target="tpu_custom_call" | custom-call | flops 2200000000 | tf_op jit(solution)/shard_map/project/pallas_call | solution.py:183
  180.9 1.4 second_sum.1
  182.3 0.1 collective-permute-start.17
  182.4 1.2 collective-permute-done.17
  183.6 2.8 %collective-permute-start.18 = (f32[32,128]{1,0:T(8,128)S(1)}, f32[32,128]{1,0:T(8,128)S(1)}, u32[]{:S(2)}, u32[]{:S(2)}) collective-permute-start(f32[32,128]{1,0:T(8,128)S(1)} %add.30), channel_id=1, source_target_pairs={{0,16},{8,24},{16,0},{24,8},{1,17},{9,25},{17,1},{25,9},{2,18},{10... | collective-permute-start | bytes 49160 | tf_op jit(solution)/shard_map/ppermute | solution.py:206
  186.4 0.7 collective-permute-start.19
  187.1 2.6 %collective-permute-start.20 = (f32[32,128]{1,0:T(8,128)S(1)}, f32[32,128]{1,0:T(8,128)S(1)}, u32[]{:S(2)}, u32[]{:S(2)}) collective-permute-start(f32[32,128]{1,0:T(8,128)S(1)} %add.30), channel_id=1, source_target_pairs={{0,24},{8,0},{16,8},{24,16},{1,25},{9,1},{17,9},{25,17},{2,26},{10... | collective-permute-start | bytes 49160 | tf_op jit(solution)/shard_map/ppermute | solution.py:206
  189.6 1.5 collective-permute-start.14
  191.1 2.7 %collective-permute-start.15 = (bf16[16,128,128]{2,1,0:T(8,128)(2,1)S(1)}, bf16[16,128,128]{2,1,0:T(8,128)(2,1)S(1)}, u32[]{:S(2)}, u32[]{:S(2)}) collective-permute-start(bf16[16,128,128]{2,1,0:T(8,128)(2,1)S(1)} %get-tuple-element.52.refs_0_), channel_id=1, source_target_pairs={{0,2},{1,3},{2,0},{3,1},{4,6},{5,7},{6,4},{7,5},{8,10},{9,11},{10,... | collective-permute-start | bytes 1572872 | tf_op jit(solution)/shard_map/ppermute | solution.py:206
  193.8 1.5 collective-permute-start.16
  195.3 2.5 %collective-permute-start.21 = (f32[32,128]{1,0:T(8,128)S(1)}, f32[32,128]{1,0:T(8,128)S(1)}, u32[]{:S(2)}, u32[]{:S(2)}) collective-permute-start(f32[32,128]{1,0:T(8,128)S(1)} %add_add_fusion.1), channel_id=1, source_target_pairs={{0,64},{32,96},{64,0},{96,32},{1,65},{33,97},{65,1},{97,33},{2,66}... | collective-permute-start | bytes 49160 | tf_op jit(solution)/shard_map/ppermute | solution.py:206
  197.8 0.6 collective-permute-start.22
  198.3 2.3 collective-permute-done.21
  200.6 2.1 collective-permute-start.23
  202.7 1.6 collective-permute-done.23
  204.3 0.6 collective-permute-start.24
  205.0 0.3 collective-permute-start.25
  205.3 11.4 %collective-permute-done.24 = f32[32,128]{1,0:T(8,128)S(1)} collective-permute-done((f32[32,128]{1,0:T(8,128)S(1)}, f32[32,128]{1,0:T(8,128)S(1)}, u32[]{:S(2)}, u32[]{:S(2)}) %collective-permute-start.24) | collective-permute-done | bytes 16416 | tf_op jit(solution)/shard_map/ppermute | solution.py:206
  216.7 2.2 collective-permute-start.26
  218.9 1.6 collective-permute-done.26
  220.5 0.6 add_bitcast_fusion
  221.1 1.2 last_sum.1
  (51 shorter events, 0.2 us)
Async XLA Ops:
  7.2 134.9 %all-gather.2.cloned.1.call-start = ((), (), s32[]{:S(2)}) async-start(), calls=%async_computation | async-start | bytes 17301504 | tf_op jit(solution)/shard_map/all_gather | solution.py:266
  7.9 12.6 %collective-permute-start.1 = (bf16[128,14336]{1,0:T(8,128)(2,1)}, bf16[128,14336]{1,0:T(8,128)(2,1)}, u32[]{:S(2)}, u32[]{:S(2)}) collective-permute-start(bf16[128,14336]{1,0:T(8,128)(2,1)} %refs_7_.1), channel_id=1, source_target_pairs={{0,4},{4,0},{1,5},{5,1},{2,6},{6,2},{3,7},{7,3},{8,12},{12,8},{9,1... | collective-permute-start | bytes 11010056 | tf_op jit(solution)/shard_map/ppermute | solution.py:269
  8.0 7.7 %collective-permute-start = (bf16[128,4096]{1,0:T(8,128)(2,1)}, bf16[128,4096]{1,0:T(8,128)(2,1)S(1)}, u32[]{:S(2)}, u32[]{:S(2)}) collective-permute-start(bf16[128,4096]{1,0:T(8,128)(2,1)} %refs_3_.1), channel_id=1, source_target_pairs={{0,4},{4,0},{1,5},{5,1},{2,6},{6,2},{3,7},{7,3},{8,12},{12,8},{9,1... | collective-permute-start | bytes 3145736 | tf_op jit(solution)/shard_map/ppermute | solution.py:268
  15.7 1.0 copy-start.13
  33.4 18.3 %copy-start.10 = (bf16[32,128,128]{2,1,0:T(8,128)(2,1)S(1)}, bf16[32,128,128]{2,1,0:T(8,128)(2,1)}, u32[]{:S(2)}) copy-start(bf16[32,128,128]{2,1,0:T(8,128)(2,1)} %get-tuple-element.36.refs_7_) | copy-start | bytes 3145732
  33.4 21.3 %copy-start.12 = (bf16[32,128,128]{2,1,0:T(8,128)(2,1)S(1)}, bf16[32,128,128]{2,1,0:T(8,128)(2,1)}, u32[]{:S(2)}) copy-start(bf16[32,128,128]{2,1,0:T(8,128)(2,1)} %get-tuple-element.34) | copy-start | bytes 3145732
  33.4 64.3 %copy-start.11 = (bf16[32,128,128]{2,1,0:T(8,128)(2,1)S(1)}, bf16[32,128,128]{2,1,0:T(8,128)(2,1)}, u32[]{:S(2)}) copy-start(bf16[32,128,128]{2,1,0:T(8,128)(2,1)} %get-tuple-element.35) | copy-start | bytes 3145732
  45.9 91.4 %copy-start.3 = (bf16[32,128,128]{2,1,0:T(8,128)(2,1)S(1)}, bf16[32,128,128]{2,1,0:T(8,128)(2,1)}, u32[]{:S(2)}) copy-start(bf16[32,128,128]{2,1,0:T(8,128)(2,1)} %get-tuple-element.33.refs_0_) | copy-start | bytes 3145732
  45.9 91.4 %copy-start.4 = (bf16[32,128,128]{2,1,0:T(8,128)(2,1)S(1)}, bf16[32,128,128]{2,1,0:T(8,128)(2,1)}, u32[]{:S(2)}) copy-start(bf16[32,128,128]{2,1,0:T(8,128)(2,1)} %get-tuple-element.37.refs_4_) | copy-start | bytes 3145732
  45.9 51.8 %collective-permute-start.7 = (bf16[32,128,128]{2,1,0:T(8,128)(2,1)}, bf16[32,128,128]{2,1,0:T(8,128)(2,1)S(1)}, u32[]{:S(2)}, u32[]{:S(2)}) collective-permute-start(bf16[32,128,128]{2,1,0:T(8,128)(2,1)} %get-tuple-element.37.refs_4_), channel_id=1, source_target_pairs={{0,24},{8,0},{16,8},{24,16},{1,25},{9,1},{17,9},{25,17},{2,26},{10... | collective-permute-start | bytes 3145736 | tf_op jit(solution)/shard_map/ppermute | solution.py:206
  49.7 51.2 %collective-permute-start.5 = (bf16[32,128,128]{2,1,0:T(8,128)(2,1)}, bf16[32,128,128]{2,1,0:T(8,128)(2,1)S(1)}, u32[]{:S(2)}, u32[]{:S(2)}) collective-permute-start(bf16[32,128,128]{2,1,0:T(8,128)(2,1)} %get-tuple-element.40), channel_id=1, source_target_pairs={{0,8},{8,16},{16,24},{24,0},{1,9},{9,17},{17,25},{25,1},{2,10},{10... | collective-permute-start | bytes 3145736 | tf_op jit(solution)/shard_map/ppermute | solution.py:206
  49.8 78.5 %collective-permute-start.6 = (bf16[32,128,128]{2,1,0:T(8,128)(2,1)}, bf16[32,128,128]{2,1,0:T(8,128)(2,1)S(1)}, u32[]{:S(2)}, u32[]{:S(2)}) collective-permute-start(bf16[32,128,128]{2,1,0:T(8,128)(2,1)} %get-tuple-element.41), channel_id=1, source_target_pairs={{0,16},{8,24},{16,0},{24,8},{1,17},{9,25},{17,1},{25,9},{2,18},{10... | collective-permute-start | bytes 3145736 | tf_op jit(solution)/shard_map/ppermute | solution.py:206
  51.7 84.1 %collective-permute-start.4 = (bf16[32,128,128]{2,1,0:T(8,128)(2,1)S(1)}, bf16[32,128,128]{2,1,0:T(8,128)(2,1)S(1)}, u32[]{:S(2)}, u32[]{:S(2)}) collective-permute-start(bf16[32,128,128]{2,1,0:T(8,128)(2,1)S(1)} %copy-done.10), channel_id=1, source_target_pairs={{0,96},{32,0},{64,32},{96,64},{1,97},{33,1},{65,33},{97,65},{2,98}... | collective-permute-start | bytes 3145736 | tf_op jit(solution)/shard_map/ppermute | solution.py:206
  54.6 82.6 %collective-permute-start.2 = (bf16[32,128,128]{2,1,0:T(8,128)(2,1)S(1)}, bf16[32,128,128]{2,1,0:T(8,128)(2,1)S(1)}, u32[]{:S(2)}, u32[]{:S(2)}) collective-permute-start(bf16[32,128,128]{2,1,0:T(8,128)(2,1)S(1)} %copy-done.12), channel_id=1, source_target_pairs={{0,32},{32,64},{64,96},{96,0},{1,33},{33,65},{65,97},{97,1},{2,34}... | collective-permute-start | bytes 3145736 | tf_op jit(solution)/shard_map/ppermute | solution.py:206
  97.7 39.5 %collective-permute-start.3 = (bf16[32,128,128]{2,1,0:T(8,128)(2,1)S(1)}, bf16[32,128,128]{2,1,0:T(8,128)(2,1)S(1)}, u32[]{:S(2)}, u32[]{:S(2)}) collective-permute-start(bf16[32,128,128]{2,1,0:T(8,128)(2,1)S(1)} %copy-done.11), channel_id=1, source_target_pairs={{0,64},{32,96},{64,0},{96,32},{1,65},{33,97},{65,1},{97,33},{2,66}... | collective-permute-start | bytes 3145736 | tf_op jit(solution)/shard_map/ppermute | solution.py:206
  128.3 1.2 copy-start.5
  131.5 10.6 %copy-start.1 = (bf16[128,4096]{1,0:T(8,128)(2,1)S(1)}, bf16[128,4096]{1,0:T(8,128)(2,1)}, u32[]{:S(2)}) copy-start(bf16[128,4096]{1,0:T(8,128)(2,1)} %refs_3_.1) | copy-start | bytes 3145732
  131.5 10.6 %copy-start.2 = (bf16[128,4096]{1,0:T(8,128)(2,1)S(1)}, bf16[128,4096]{1,0:T(8,128)(2,1)}, u32[]{:S(2)}) copy-start(bf16[128,4096]{1,0:T(8,128)(2,1)} %get-tuple-element.29.refs_4_) | copy-start | bytes 3145732
  131.5 10.6 %copy-start.6 = (f32[128,128]{1,0:T(8,128)S(1)}, f32[128,128]{1,0:T(8,128)}, u32[]{:S(2)}) copy-start(f32[128,128]{1,0:T(8,128)} %get-tuple-element.30.refs_5_) | copy-start | bytes 196612
  131.5 10.6 %copy-start.7 = (s32[512]{0:T(512)S(1)}, s32[512]{0:T(512)}, u32[]{:S(2)}) copy-start(s32[512]{0:T(512)} %refs_0_.5) | copy-start | bytes 6148
  131.5 10.6 %copy-start.8 = (s32[512]{0:T(512)S(1)}, s32[512]{0:T(512)}, u32[]{:S(2)}) copy-start(s32[512]{0:T(512)} %refs_1_.5) | copy-start | bytes 6148
  131.5 10.6 %copy-start.9 = (f32[4096]{0:T(1024)S(1)}, f32[4096]{0:T(1024)}, u32[]{:S(2)}) copy-start(f32[4096]{0:T(1024)} %param.7) | copy-start | bytes 49156
  131.5 9.9 %collective-permute-start.11 = (bf16[8,128,128]{2,1,0:T(8,128)(2,1)S(1)}, bf16[8,128,128]{2,1,0:T(8,128)(2,1)S(1)}, u32[]{:S(2)}, u32[]{:S(2)}) collective-permute-start(bf16[8,128,128]{2,1,0:T(8,128)(2,1)S(1)} %get-tuple-element.48), channel_id=1, source_target_pairs={{0,32},{32,64},{64,96},{96,0},{1,33},{33,65},{65,97},{97,1},{2,34}... | collective-permute-start | bytes 786440 | tf_op jit(solution)/shard_map/ppermute | solution.py:206
  133.0 47.9 %collective-permute-start.12 = (bf16[8,128,128]{2,1,0:T(8,128)(2,1)}, bf16[8,128,128]{2,1,0:T(8,128)(2,1)S(1)}, u32[]{:S(2)}, u32[]{:S(2)}) collective-permute-start(bf16[8,128,128]{2,1,0:T(8,128)(2,1)} %get-tuple-element.49), channel_id=1, source_target_pairs={{0,64},{32,96},{64,0},{96,32},{1,65},{33,97},{65,1},{97,33},{2,66}... | collective-permute-start | bytes 786440 | tf_op jit(solution)/shard_map/ppermute | solution.py:206
  135.8 45.1 %collective-permute-start.13 = (bf16[8,128,128]{2,1,0:T(8,128)(2,1)}, bf16[8,128,128]{2,1,0:T(8,128)(2,1)S(1)}, u32[]{:S(2)}, u32[]{:S(2)}) collective-permute-start(bf16[8,128,128]{2,1,0:T(8,128)(2,1)} %get-tuple-element.50), channel_id=1, source_target_pairs={{0,96},{32,0},{64,32},{96,64},{1,97},{33,1},{65,33},{97,65},{2,98}... | collective-permute-start | bytes 786440 | tf_op jit(solution)/shard_map/ppermute | solution.py:206
  139.3 41.6 %collective-permute-start.10 = (bf16[8,128,128]{2,1,0:T(8,128)(2,1)}, bf16[8,128,128]{2,1,0:T(8,128)(2,1)}, u32[]{:S(2)}, u32[]{:S(2)}) collective-permute-start(bf16[8,128,128]{2,1,0:T(8,128)(2,1)} %get-tuple-element.47), channel_id=1, source_target_pairs={{0,24},{8,0},{16,8},{24,16},{1,25},{9,1},{17,9},{25,17},{2,26},{10... | collective-permute-start | bytes 786440 | tf_op jit(solution)/shard_map/ppermute | solution.py:206
  140.4 40.5 %collective-permute-start.8 = (bf16[8,128,128]{2,1,0:T(8,128)(2,1)}, bf16[8,128,128]{2,1,0:T(8,128)(2,1)}, u32[]{:S(2)}, u32[]{:S(2)}) collective-permute-start(bf16[8,128,128]{2,1,0:T(8,128)(2,1)} %get-tuple-element.45), channel_id=1, source_target_pairs={{0,8},{8,16},{16,24},{24,0},{1,9},{9,17},{17,25},{25,1},{2,10},{10... | collective-permute-start | bytes 786440 | tf_op jit(solution)/shard_map/ppermute | solution.py:206
  141.4 39.6 %collective-permute-start.9 = (bf16[8,128,128]{2,1,0:T(8,128)(2,1)}, bf16[8,128,128]{2,1,0:T(8,128)(2,1)}, u32[]{:S(2)}, u32[]{:S(2)}) collective-permute-start(bf16[8,128,128]{2,1,0:T(8,128)(2,1)} %get-tuple-element.46), channel_id=1, source_target_pairs={{0,16},{8,24},{16,0},{24,8},{1,17},{9,25},{17,1},{25,9},{2,18},{10... | collective-permute-start | bytes 786440 | tf_op jit(solution)/shard_map/ppermute | solution.py:206
  142.1 2.0 copy-start
  182.3 1.3 collective-permute-start.17
  183.6 10.2 %collective-permute-start.18 = (f32[32,128]{1,0:T(8,128)S(1)}, f32[32,128]{1,0:T(8,128)S(1)}, u32[]{:S(2)}, u32[]{:S(2)}) collective-permute-start(f32[32,128]{1,0:T(8,128)S(1)} %add.30), channel_id=1, source_target_pairs={{0,16},{8,24},{16,0},{24,8},{1,17},{9,25},{17,1},{25,9},{2,18},{10... | collective-permute-start | bytes 49160 | tf_op jit(solution)/shard_map/ppermute | solution.py:206
  186.4 8.9 %collective-permute-start.19 = (f32[32,128]{1,0:T(8,128)S(1)}, f32[32,128]{1,0:T(8,128)S(1)}, u32[]{:S(2)}, u32[]{:S(2)}) collective-permute-start(f32[32,128]{1,0:T(8,128)S(1)} %add.30), channel_id=1, source_target_pairs={{0,8},{8,16},{16,24},{24,0},{1,9},{9,17},{17,25},{25,1},{2,10},{10... | collective-permute-start | bytes 49160 | tf_op jit(solution)/shard_map/ppermute | solution.py:206
  187.1 8.2 %collective-permute-start.20 = (f32[32,128]{1,0:T(8,128)S(1)}, f32[32,128]{1,0:T(8,128)S(1)}, u32[]{:S(2)}, u32[]{:S(2)}) collective-permute-start(f32[32,128]{1,0:T(8,128)S(1)} %add.30), channel_id=1, source_target_pairs={{0,24},{8,0},{16,8},{24,16},{1,25},{9,1},{17,9},{25,17},{2,26},{10... | collective-permute-start | bytes 49160 | tf_op jit(solution)/shard_map/ppermute | solution.py:206
  189.6 31.4 %collective-permute-start.14 = (bf16[16,128,128]{2,1,0:T(8,128)(2,1)S(1)}, bf16[16,128,128]{2,1,0:T(8,128)(2,1)S(1)}, u32[]{:S(2)}, u32[]{:S(2)}) collective-permute-start(bf16[16,128,128]{2,1,0:T(8,128)(2,1)S(1)} %get-tuple-element.52.refs_0_), channel_id=1, source_target_pairs={{0,1},{1,2},{2,3},{3,0},{4,5},{5,6},{6,7},{7,4},{8,9},{9,10},{10,1... | collective-permute-start | bytes 1572872 | tf_op jit(solution)/shard_map/ppermute | solution.py:206
  191.1 30.0 %collective-permute-start.15 = (bf16[16,128,128]{2,1,0:T(8,128)(2,1)S(1)}, bf16[16,128,128]{2,1,0:T(8,128)(2,1)S(1)}, u32[]{:S(2)}, u32[]{:S(2)}) collective-permute-start(bf16[16,128,128]{2,1,0:T(8,128)(2,1)S(1)} %get-tuple-element.52.refs_0_), channel_id=1, source_target_pairs={{0,2},{1,3},{2,0},{3,1},{4,6},{5,7},{6,4},{7,5},{8,10},{9,11},{10,... | collective-permute-start | bytes 1572872 | tf_op jit(solution)/shard_map/ppermute | solution.py:206
  193.8 27.3 %collective-permute-start.16 = (bf16[16,128,128]{2,1,0:T(8,128)(2,1)S(1)}, bf16[16,128,128]{2,1,0:T(8,128)(2,1)S(1)}, u32[]{:S(2)}, u32[]{:S(2)}) collective-permute-start(bf16[16,128,128]{2,1,0:T(8,128)(2,1)S(1)} %get-tuple-element.52.refs_0_), channel_id=1, source_target_pairs={{0,3},{1,0},{2,1},{3,2},{4,7},{5,4},{6,5},{7,6},{8,11},{9,8},{10,9... | collective-permute-start | bytes 1572872 | tf_op jit(solution)/shard_map/ppermute | solution.py:206
  195.3 5.3 %collective-permute-start.21 = (f32[32,128]{1,0:T(8,128)S(1)}, f32[32,128]{1,0:T(8,128)S(1)}, u32[]{:S(2)}, u32[]{:S(2)}) collective-permute-start(f32[32,128]{1,0:T(8,128)S(1)} %add_add_fusion.1), channel_id=1, source_target_pairs={{0,64},{32,96},{64,0},{96,32},{1,65},{33,97},{65,1},{97,33},{2,66}... | collective-permute-start | bytes 49160 | tf_op jit(solution)/shard_map/ppermute | solution.py:206
  197.8 5.0 %collective-permute-start.22 = (f32[32,128]{1,0:T(8,128)S(1)}, f32[32,128]{1,0:T(8,128)S(1)}, u32[]{:S(2)}, u32[]{:S(2)}) collective-permute-start(f32[32,128]{1,0:T(8,128)S(1)} %add_add_fusion.1), channel_id=1, source_target_pairs={{0,32},{32,64},{64,96},{96,0},{1,33},{33,65},{65,97},{97,1},{2,34}... | collective-permute-start | bytes 49160 | tf_op jit(solution)/shard_map/ppermute | solution.py:206
  200.6 3.7 %collective-permute-start.23 = (f32[32,128]{1,0:T(8,128)S(1)}, f32[32,128]{1,0:T(8,128)S(1)}, u32[]{:S(2)}, u32[]{:S(2)}) collective-permute-start(f32[32,128]{1,0:T(8,128)S(1)} %add_add_fusion.1), channel_id=1, source_target_pairs={{0,96},{32,0},{64,32},{96,64},{1,97},{33,1},{65,33},{97,65},{2,98}... | collective-permute-start | bytes 49160 | tf_op jit(solution)/shard_map/ppermute | solution.py:206
  204.3 12.4 %collective-permute-start.24 = (f32[32,128]{1,0:T(8,128)S(1)}, f32[32,128]{1,0:T(8,128)S(1)}, u32[]{:S(2)}, u32[]{:S(2)}) collective-permute-start(f32[32,128]{1,0:T(8,128)S(1)} %add_add_fusion), channel_id=1, source_target_pairs={{0,2},{1,3},{2,0},{3,1},{4,6},{5,7},{6,4},{7,5},{8,10},{9,11},{10,... | collective-permute-start | bytes 49160 | tf_op jit(solution)/shard_map/ppermute | solution.py:206
  205.0 13.9 %collective-permute-start.25 = (f32[32,128]{1,0:T(8,128)S(1)}, f32[32,128]{1,0:T(8,128)S(1)}, u32[]{:S(2)}, u32[]{:S(2)}) collective-permute-start(f32[32,128]{1,0:T(8,128)S(1)} %add_add_fusion), channel_id=1, source_target_pairs={{0,1},{1,2},{2,3},{3,0},{4,5},{5,6},{6,7},{7,4},{8,9},{9,10},{10,1... | collective-permute-start | bytes 49160 | tf_op jit(solution)/shard_map/ppermute | solution.py:206
  216.7 3.7 %collective-permute-start.26 = (f32[32,128]{1,0:T(8,128)S(1)}, f32[32,128]{1,0:T(8,128)S(1)}, u32[]{:S(2)}, u32[]{:S(2)}) collective-permute-start(f32[32,128]{1,0:T(8,128)S(1)} %add_add_fusion), channel_id=1, source_target_pairs={{0,3},{1,0},{2,1},{3,2},{4,7},{5,4},{6,5},{7,6},{8,11},{9,8},{10,9... | collective-permute-start | bytes 49160 | tf_op jit(solution)/shard_map/ppermute | solution.py:206
Sparse Core Ops, SparseCore 0:
  10.3 106.3 all-gather.1

commit v4 on v3

--- a/solution.py
+++ b/solution.py
@@ -76,52 +76,61 @@
     )(x, gain)
 
 
-def grad_kernel(first, per, step, rows, cols, pos, turned_ref, turned_other_ref, own_ref, other_ref, *refs):
-    out_refs = refs[-4:]
-    base = pl.program_id(0) * step
-    y, z, c = pos[0], pos[1], pos[2]
-    each = 4 * per // step
-
-    for major, out_ref in enumerate(out_refs):
-
-        @pl.when(pl.program_id(0) // each == major)
-        def _(major=major, out_ref=out_ref):
+def listed(kind, ahead, i, y, z, c, x):
+    if kind == "x":
+        to_y, to_z, t = i // 8, i // 2 % 4, 2 * lax.rem(x + ahead, 4) + i % 2
+    elif kind == "y":
+        to_y, to_z, t = ahead, i // 4, 8 + i % 4
+    else:
+        to_y, to_z, t = i // 4, ahead, 12 + i % 4
+    return (lax.rem(y + to_y, 4) * 4 + lax.rem(z + to_z, 4)) * 32 + c * 16 + t
+
+
+STEP = 16
+
+
+def grad_kernel(plan, rows, cols, pos, turned_ref, turned_other_ref, own_ref, other_ref, *refs):
+    out_refs = refs[-len(plan) :]
+    y, z, c, x = pos[0], pos[1], pos[2], pos[3]
+
+    for (kind, ahead, start, each), out_ref in zip(plan, out_refs):
+        at = pl.program_id(0)
+
+        @pl.when((at >= start) & (at < start + each))
+        def _(kind=kind, ahead=ahead, start=start, out_ref=out_ref, at=at):
             def one(k, carry):
-                i = base + k - major * 4 * per
-                minor, t = i // per, i % per
-                if first == "y":
-                    place = lax.rem(y + major, 4) * 4 + lax.rem(z + minor, 4)
-                else:
-                    place = lax.rem(y + minor, 4) * 4 + lax.rem(z + major, 4)
-                index = place * 32 + c * 16 + (0 if first == "y" else 16 - per) + t
+                index = listed(kind, ahead, (at - start) * STEP + k, y, z, c, x)
                 r, q = rows[index], cols[index]
                 left = jnp.concatenate([turned_ref[r], turned_other_ref[r]], axis=1)
                 right = jnp.concatenate([own_ref[:, cols_at(q)], other_ref[:, cols_at(q)]], axis=0)
                 out_ref[k] = dot(left, right).astype(BF)
                 return carry
 
-            lax.fori_loop(0, step, one, 0, unroll=8)
-
-
-def grads(first, per, rows, cols, pos, turned, turned_other, own, other, ties=()):
-    piece, step = 4 * per, 16
-    each = piece // step
-
-    def out_spec(major):
-        return pl.BlockSpec((step, T, T), lambda i, *_: (jnp.clip(i - major * each, 0, each - 1), 0, 0))
-
-    return pl.pallas_call(
-        lambda *refs: grad_kernel(first, per, step, *refs),
-        out_shape=[jax.ShapeDtypeStruct((piece, T, T), BF)] * 4,
+            lax.fori_loop(0, STEP, one, 0, unroll=8)
+
+
+def grads(kinds, rows, cols, pos, turned, turned_other, own, other, ties=()):
+    plan, steps = [], 0
+    for kind, size in kinds:
+        for ahead in range(4):
+            plan.append((kind, ahead, steps, size // STEP))
+            steps += size // STEP
+
+    def out_spec(start, each):
+        return pl.BlockSpec((STEP, T, T), lambda i, *_: (jnp.clip(i - start, 0, each - 1), 0, 0))
+
+    return pl.pallas_call(
+        lambda *refs: grad_kernel(plan, *refs),
+        out_shape=[jax.ShapeDtypeStruct((each * STEP, T, T), BF) for _, _, _, each in plan],
         grid_spec=pltpu.PrefetchScalarGridSpec(
             num_scalar_prefetch=3,
-            grid=(4 * each,),
+            grid=(steps,),
             in_specs=[whole(a.shape) for a in (turned, turned_other, own, other)] + [ANY] * len(ties),
-            out_specs=[out_spec(major) for major in range(4)],
-        ),
-        compiler_params=params(56),
+            out_specs=[out_spec(start, each) for _, _, start, each in plan],
+        ),
+        compiler_params=params(40),
         cost_estimate=cost(2, 0),
-        name="grads_" + first,
+        name="grads_" + kinds[0][0],
     )(rows, cols, pos, turned, turned_other, own, other, *ties)
 
 
@@ -211,8 +220,7 @@
 
     def kernel(*refs):
         ins, outs = refs[:4], refs[-4:]
-        a, b, c, d = (r[...].astype(F4) for r in ins)
-        total = ((a + c) + (b + d)).astype(BF)
+        total = add_four(ins, ...).astype(BF)
         for major, out in enumerate(outs):
 
             @pl.when(pl.program_id(0) == major)
@@ -231,28 +239,71 @@
     )(*pieces, *ties)
 
 
-def sum_of_four(groups, dtype, passed, name):
+def add_four(refs, i):
+    a, b, c, d = (r[i].astype(F4) for r in refs)
+    return (a + c) + (b + d)
+
+
+def second_sum(groups):
     count = groups[0][0].shape[0]
     arrays = [a for group in groups for a in group]
 
     def kernel(*refs):
-        out = refs[len(arrays) + len(passed)]
         for g in range(len(groups)):
             for i in range(count):
-                a, b, c, d = (r[i].astype(F4) for r in refs[4 * g : 4 * g + 4])
-                out[g * count + i] = ((a + c) + (b + d)).astype(dtype)
-        for k in range(len(passed)):
-            refs[len(arrays) + len(passed) + 1 + k][...] = refs[len(arrays) + k][...]
+                refs[-1][g * count + i] = add_four(refs[4 * g : 4 * g + 4], i).astype(BF)
 
     return pl.pallas_call(
         kernel,
-        out_shape=[jax.ShapeDtypeStruct((count * len(groups), T, T), dtype)]
-        + [jax.ShapeDtypeStruct(a.shape, a.dtype) for a in passed],
-        in_specs=[pl.BlockSpec(memory_space=pltpu.VMEM)] * (len(arrays) + len(passed)),
-        compiler_params=params(32),
-        cost_estimate=cost(1, 0),
-        name=name,
-    )(*arrays, *passed)
+        out_shape=jax.ShapeDtypeStruct((count * len(groups), T, T), BF),
+        in_specs=[pl.BlockSpec(memory_space=pltpu.VMEM)] * len(arrays),
+        compiler_params=params(32),
+        cost_estimate=cost(1, 0),
+        name="second_sum",
+    )(*arrays)
+
+
+def third_sum(pieces, others, passed):
+    count, more = pieces[0].shape[0], others.shape[0]
+
+    def kernel(*refs):
+        others_ref, passed_ref, out_ref, passed_out = refs[4:]
+        for i in range(count):
+            out_ref[i] = add_four(refs[:4], i).astype(BF)
+        out_ref[count:] = others_ref[...]
+        passed_out[...] = passed_ref[...]
+
+    return pl.pallas_call(
+        kernel,
+        out_shape=(
+            jax.ShapeDtypeStruct((count + more, T, T), BF),
+            jax.ShapeDtypeStruct(passed.shape, passed.dtype),
+        ),
+        in_specs=[pl.BlockSpec(memory_space=pltpu.VMEM)] * 6,
+        compiler_params=params(32),
+        cost_estimate=cost(1, 0),
+        name="third_sum",
+    )(*pieces, others, passed)
+
+
+def last_sum(pieces, pos):
+    def kernel(pos_ref, *refs):
+        out_ref = refs[-1]
+        for back in range(4):
+            source = lax.rem(pos_ref[3] + 4 - back, 4)
+            for u in range(2):
+                out_ref[2 * source + u] = refs[back][u].astype(F4)
+        for i in range(2, 10):
+            out_ref[6 + i] = add_four(refs[:4], i)
+
+    return pl.pallas_call(
+        kernel,
+        out_shape=jax.ShapeDtypeStruct((16, T, T), F4),
+        in_specs=[pl.BlockSpec(memory_space=pltpu.SMEM)] + [pl.BlockSpec(memory_space=pltpu.VMEM)] * 4,
+        compiler_params=params(32),
+        cost_estimate=cost(1, 0),
+        name="last_sum",
+    )(pos, *pieces)
 
 
 def exchange(pieces, axis):
@@ -269,16 +320,18 @@
     g_other = lax.ppermute(cotangent, "c", swap)
     normed, turned, scale = norm(tokens, gain2)
     _, turned_other, _ = norm(tokens_other, gain2)
-    part_y = grads("y", 8, rows, cols, pos, turned, turned_other, cotangent, g_other)
-    part_z = grads("z", 8, rows, cols, pos, turned, turned_other, cotangent, g_other, (part_y[3],))
-    mid_y = first_sum(exchange(part_y, "y"), (part_z[3],))
-    mid_z = first_sum(exchange(part_z, "z"), ())
+    part_x = grads([("x", 32)], rows, cols, pos, turned, turned_other, cotangent, g_other)
+    parts = grads([("y", 16), ("z", 16)], rows, cols, pos, turned, turned_other, cotangent, g_other, (part_x[3],))
+    mid_y = first_sum(exchange(parts[:4], "y"), ())
+    mid_z = first_sum(exchange(parts[4:], "z"), (mid_y[0],))
+    mid_x = first_sum(exchange(part_x, "x"), (mid_z[0],))
+    over_x = second_sum([exchange(mid_y, "z"), exchange(mid_z, "y")])
+    last_x = first_sum(exchange(mid_x, "y"), (over_x,))
     projected, token_grad, sums = project(
-        rows, cols, piece, tokens, normed, scale, gain2, cotangent, (mid_y[0], mid_z[0])
+        rows, cols, piece, tokens, normed, scale, gain2, cotangent, (last_x[0], over_x)
     )
-    sums = sums.reshape(-1, T)
-    sent, sums = sum_of_four([exchange(mid_y, "z"), exchange(mid_z, "y")], BF, (sums,), "second_sum")
-    (tile_grad,) = sum_of_four([exchange([sent] * 4, "x")], F4, (), "last_sum")
+    sent, sums = third_sum(exchange(last_x, "z"), over_x, sums.reshape(-1, T))
+    tile_grad = last_sum(exchange([sent] * 4, "x"), pos)
     sums = sums + lax.ppermute(sums, "c", swap)
     for axis in ("z", "y", "x"):
         own, right, opposite, left = exchange([sums] * 4, axis)

time: 230 us -> 231 us (level)
  starting transfers between devices: 41.1 us -> 56.2 us
  Pallas kernels: 76.3 us -> 65.8 us
  waiting for transfers between devices: 92.1 us -> 83.3 us
  local copies, waits for them, and re-layouts: 4.27 us -> 10 us
    ppermute x24 -> x33, starting transfers between devices: 40.4 us -> 55.5 us  [ring(): return lax.ppermute(piece, axis, [(i, (i + shift) % 4) for i in range(4)])]
    ppermute x24 -> x33, waiting for transfers between devices: 87.4 us -> 78.2 us  [ring(): return lax.ppermute(piece, axis, [(i, (i + shift) % 4) for i in range(4)])]
    pallas_call x4 -> x5, Pallas kernels: 27.9 us -> 20.2 us  [the longest x2 18.4 us: grads(): pl.pallas_call(lambda *refs: grad_kernel(plan, *refs), out_shape=[jax.Sha...]
    unnamed x28 -> x24, local copies, waits for them, and re-layouts: 4.27 us -> 10 us
  transfers between devices with their start and end apart: 28 -> 37, of which waited for: 9 -> 16; matrix products, arithmetic and copies ran while one was open for 1% -> 0% of each run, Pallas kernels for 32% -> 28%
where the time goes in v4:
time: 231 us; the launch traced here: 230 us
  waiting for transfers between devices  83.3 us (36%)
  Pallas kernels  65.8 us (28%)
  starting transfers between devices  56.2 us (24%)
  between operations  14.2 us (6%)
  local copies, waits for them, and re-layouts  10 us (4%)
    ppermute x33, waiting for transfers between devices, ring(): return lax.ppermute(piece, axis, [(i, (i + shift) % 4) for i in range(4)])  78.2 us
    ppermute x33, starting transfers between devices, ring(): return lax.ppermute(piece, axis, [(i, (i + shift) % 4) for i in range(4)])  55.5 us
    pallas_call x1, Pallas kernels, project(): pl.pallas_call(lambda *refs: project_kernel(step, *refs), out_shape=(jax....  35.2 us
    pallas_call x2, Pallas kernels, grads(): pl.pallas_call(lambda *refs: grad_kernel(plan, *refs), out_shape=[jax.Sha...  18.4 us
    unnamed x24, local copies, waits for them, and re-layouts  10 us
    pallas_call x2, Pallas kernels, norm(): pl.pallas_call(norm_kernel, out_shape=(jax.ShapeDtypeStruct((count, width...  7.77 us
  transfers between devices with their start and end apart: 37, of which 16 were waited for; matrix products, arithmetic and copies ran while one was open for 0% of the time, Pallas kernels for 28%

profile of v4, /device:TPU:0, one launch (start us, length us, event | category | flops | bytes accessed | tf_op | source)
XLA Modules:
  0.0 230.3 jit_solution(4501725458014897389)
XLA Ops:
  8.5 3.9 %norm.2 = (bf16[128,4096]{1,0:T(8,128)(2,1)}, bf16[32,128,128]{2,1,0:T(8,128)(2,1)}, f32[128,128]{1,0:T(8,128)}) custom-call(bf16[128,4096]{1,0:T(8,128)(2,1)} %refs_3_.1, f32[1,4096]{1,0:T(1,128)} %bitcast.8), custom_call_target="tpu_custom_call" | custom-call | flops 1100000000 | tf_op jit(solution)/shard_map/norm/pallas_call | solution.py:66
  12.5 3.2 %collective-permute-done.x_ref = bf16[128,4096]{1,0:T(8,128)(2,1)S(1)} collective-permute-done((bf16[128,4096]{1,0:T(8,128)(2,1)}, bf16[128,4096]{1,0:T(8,128)(2,1)S(1)}, u32[]{:S(2)}, u32[]{:S(2)}) %collective-permute-start) | collective-permute-done | bytes 1048608 | tf_op jit(solution)/shard_map/ppermute | solution.py:319
  15.7 1.0 copy-done.11
  16.7 3.8 %norm.3 = (bf16[128,4096]{1,0:T(8,128)(2,1)}, bf16[32,128,128]{2,1,0:T(8,128)(2,1)}, f32[128,128]{1,0:T(8,128)}) custom-call(bf16[128,4096]{1,0:T(8,128)(2,1)} %copy-done.11, f32[1,4096]{1,0:T(1,128)} %bitcast.9), custom_call_target="tpu_custom_call" | custom-call | flops 1100000000 | tf_op jit(solution)/shard_map/norm/pallas_call | solution.py:66
  20.6 1.2 copy-done.4
  21.8 9.3 %grads_x.1 = (bf16[32,128,128]{2,1,0:T(8,128)(2,1)S(1)}, bf16[32,128,128]{2,1,0:T(8,128)(2,1)S(1)}, bf16[32,128,128]{2,1,0:T(8,128)(2,1)S(1)}, bf16[32,128,128]{2,1,0:T(8,128)(2,1)S(1)}) custom-call(s32[512]{0:T(512)S(1)} %copy-done.8, s32[512]{0:T(512)S(1)} %copy-done.9, s32[4]{0:T(128)S(1)} %pad_add_fusion.refs_2_.pos_ref, ...), custom_call_target="tpu_custom_call" | custom-call | flops 2200000000 | tf_op jit(solution)/shard_map/grads_x/pallas_call | solution.py:122
  31.2 9.1 %grads_y.1 = (bf16[16,128,128]{2,1,0:T(8,128)(2,1)S(1)}, bf16[16,128,128]{2,1,0:T(8,128)(2,1)S(1)}, bf16[16,128,128]{2,1,0:T(8,128)(2,1)S(1)}, bf16[16,128,128]{...) custom-call(s32[512]{0:T(512)S(1)} %copy-done.8, ...), custom_call_target="tpu_custom_call" | custom-call | flops 2200000000 | tf_op jit(solution)/shard_map/grads_y/pallas_call | solution.py:122
  40.2 3.2 %collective-permute-start.10 = (bf16[16,128,128]{2,1,0:T(8,128)(2,1)S(1)}, bf16[16,128,128]{2,1,0:T(8,128)(2,1)S(1)}, u32[]{:S(2)}, u32[]{:S(2)}) collective-permute-start(bf16[16,128,128]{2,1,0:T(8,128)(2,1)S(1)} %get-tuple-element.56), channel_id=1, source_target_pairs={{0,96},{32,0},{64,32},{96,64},{1,97},{33,1},{65,33},{97,65},{2,98}... | collective-permute-start | bytes 1572872 | tf_op jit(solution)/shard_map/ppermute | solution.py:215
  43.5 2.2 collective-permute-start.9
  45.7 1.9 collective-permute-start.5
  47.6 2.8 %collective-permute-start.4 = (bf16[32,128,128]{2,1,0:T(8,128)(2,1)S(1)}, bf16[32,128,128]{2,1,0:T(8,128)(2,1)S(1)}, u32[]{:S(2)}, u32[]{:S(2)}) collective-permute-start(bf16[32,128,128]{2,1,0:T(8,128)(2,1)S(1)} %get-tuple-element.48.refs_7_), channel_id=1, source_target_pairs={{0,3},{1,0},{2,1},{3,2},{4,7},{5,4},{6,5},{7,6},{8,11},{9,8},{10,9... | collective-permute-start | bytes 3145736 | tf_op jit(solution)/shard_map/ppermute | solution.py:215
  50.3 18.9 %collective-permute-done.10.refs_3_ = bf16[16,128,128]{2,1,0:T(8,128)(2,1)S(1)} collective-permute-done((bf16[16,128,128]{2,1,0:T(8,128)(2,1)S(1)}, bf16[16,128,128]{2,1,0:T(8,128)(2,1)S(1)}, u32[]{:S(2)}, u32[]{:S(2)}) %collective-permute-start.10) | collective-permute-done | bytes 524320 | tf_op jit(solution)/shard_map/ppermute | solution.py:215
  69.9 2.2 collective-permute-done.8.refs_1_
  72.1 3.1 %collective-permute-start.3 = (bf16[32,128,128]{2,1,0:T(8,128)(2,1)S(1)}, bf16[32,128,128]{2,1,0:T(8,128)(2,1)S(1)}, u32[]{:S(2)}, u32[]{:S(2)}) collective-permute-start(bf16[32,128,128]{2,1,0:T(8,128)(2,1)S(1)} %get-tuple-element.47), channel_id=1, source_target_pairs={{0,2},{1,3},{2,0},{3,1},{4,6},{5,7},{6,4},{7,5},{8,10},{9,11},{10,... | collective-permute-start | bytes 3145736 | tf_op jit(solution)/shard_map/ppermute | solution.py:215
  75.2 13.6 %collective-permute-done.9.refs_2_ = bf16[16,128,128]{2,1,0:T(8,128)(2,1)S(1)} collective-permute-done((bf16[16,128,128]{2,1,0:T(8,128)(2,1)S(1)}, bf16[16,128,128]{2,1,0:T(8,128)(2,1)S(1)}, u32[]{:S(2)}, u32[]{:S(2)}) %collective-permute-start.9) | collective-permute-done | bytes 524320 | tf_op jit(solution)/shard_map/ppermute | solution.py:215
  88.8 4.4 %collective-permute-start.6 = (bf16[16,128,128]{2,1,0:T(8,128)(2,1)S(1)}, bf16[16,128,128]{2,1,0:T(8,128)(2,1)S(1)}, u32[]{:S(2)}, u32[]{:S(2)}) collective-permute-start(bf16[16,128,128]{2,1,0:T(8,128)(2,1)S(1)} %get-tuple-element.51), channel_id=1, source_target_pairs={{0,16},{8,24},{16,0},{24,8},{1,17},{9,25},{17,1},{25,9},{2,18},{10... | collective-permute-start | bytes 1572872 | tf_op jit(solution)/shard_map/ppermute | solution.py:215
  94.2 12.5 %collective-permute-done.6.refs_2_ = bf16[16,128,128]{2,1,0:T(8,128)(2,1)S(1)} collective-permute-done((bf16[16,128,128]{2,1,0:T(8,128)(2,1)S(1)}, bf16[16,128,128]{2,1,0:T(8,128)(2,1)S(1)}, u32[]{:S(2)}, u32[]{:S(2)}) %collective-permute-start.6) | collective-permute-done | bytes 524320 | tf_op jit(solution)/shard_map/ppermute | solution.py:215
  106.7 11.0 %collective-permute-done.7.refs_3_ = bf16[16,128,128]{2,1,0:T(8,128)(2,1)S(1)} collective-permute-done((bf16[16,128,128]{2,1,0:T(8,128)(2,1)S(1)}, bf16[16,128,128]{2,1,0:T(8,128)(2,1)S(1)}, u32[]{:S(2)}, u32[]{:S(2)}) %collective-permute-start.7) | collective-permute-done | bytes 524320 | tf_op jit(solution)/shard_map/ppermute | solution.py:215
  118.4 1.8 collective-permute-start.18
  120.2 1.6 collective-permute-start.19
  121.8 1.1 collective-permute-start.14
  122.9 1.2 first_sum.6
  124.1 1.0 collective-permute-start.11
  125.1 1.4 collective-permute-done.17.refs_5_
  126.8 2.5 %collective-permute-start.13 = (bf16[8,128,128]{2,1,0:T(8,128)(2,1)S(1)}, bf16[8,128,128]{2,1,0:T(8,128)(2,1)S(1)}, u32[]{:S(2)}, u32[]{:S(2)}) collective-permute-start(bf16[8,128,128]{2,1,0:T(8,128)(2,1)S(1)} %get-tuple-element.62), channel_id=1, source_target_pairs={{0,96},{32,0},{64,32},{96,64},{1,97},{33,1},{65,33},{97,65},{2,98}... | collective-permute-start | bytes 786440 | tf_op jit(solution)/shard_map/ppermute | solution.py:215
  129.3 2.2 collective-permute-start.15
  131.6 1.8 collective-permute-start.16
  133.4 2.5 %collective-permute-done.15.refs_2_ = bf16[4,128,128]{2,1,0:T(8,128)(2,1)S(1)} collective-permute-done((bf16[4,128,128]{2,1,0:T(8,128)(2,1)S(1)}, bf16[4,128,128]{2,1,0:T(8,128)(2,1)S(1)}, u32[]{:S(2)}, u32[]{:S(2)}) %collective-permute-start.15) | collective-permute-done | bytes 131104 | tf_op jit(solution)/shard_map/ppermute | solution.py:215
  135.8 1.0 collective-permute-done.16.refs_3_
  138.7 1.9 collective-permute-start.20
  140.6 1.7 collective-permute-start.21
  142.3 1.7 collective-permute-start.22
  144.0 2.0 copy-done.1
  146.1 5.8 %copy-done.2 = bf16[512,128,128]{2,1,0:T(8,128)(2,1)S(1)} copy-done((bf16[512,128,128]{2,1,0:T(8,128)(2,1)S(1)}, bf16[512,128,128]{2,1,0:T(8,128)(2,1)}, u32[]{:S(2)}) %copy-start.2) | copy-done | bytes 16777240
  151.8 35.2 %project.1 = (bf16[128,14336]{1,0:T(8,128)(2,1)}, bf16[128,4096]{1,0:T(8,128)(2,1)}, f32[1,4096]{1,0:T(1,128)S(1)}) custom-call(s32[512]{0:T(512)S(1)} %copy-done.8, s32[512]{0:T(512)S(1)} %copy-done.9, bf16[512,128,128]{2,1,0:T(8,128)(2,1)S(1)} %copy-done.2, bf16[128,4096]{1,0:T(8,128)(2,1)S(1)} %copy-done.5, bf16[128,4096]{1,0:T(8,128)(2,1)S(1)} %copy-done.6, ...), custom_call_target="tpu_custom_call" | custom-call | flops 2200000000 | tf_op jit(solution)/shard_map/project/pallas_call | solution.py:192
  187.2 1.2 collective-permute-done.26
  190.0 2.6 %collective-permute-start.29 = (f32[32,128]{1,0:T(8,128)S(1)}, f32[32,128]{1,0:T(8,128)S(1)}, u32[]{:S(2)}, u32[]{:S(2)}) collective-permute-start(f32[32,128]{1,0:T(8,128)S(1)} %add.30), channel_id=1, source_target_pairs={{0,24},{8,0},{16,8},{24,16},{1,25},{9,1},{17,9},{25,17},{2,26},{10... | collective-permute-start | bytes 49160 | tf_op jit(solution)/shard_map/ppermute | solution.py:215
  192.6 1.1 collective-permute-done.27
  194.3 2.6 %collective-permute-start.30 = (f32[32,128]{1,0:T(8,128)S(1)}, f32[32,128]{1,0:T(8,128)S(1)}, u32[]{:S(2)}, u32[]{:S(2)}) collective-permute-start(f32[32,128]{1,0:T(8,128)S(1)} %add_add_fusion.1), channel_id=1, source_target_pairs={{0,64},{32,96},{64,0},{96,32},{1,65},{33,97},{65,1},{97,33},{2,66}... | collective-permute-start | bytes 49160 | tf_op jit(solution)/shard_map/ppermute | solution.py:215
  196.9 1.6 collective-permute-start.31
  198.6 1.6 collective-permute-start.32
  200.2 1.4 collective-permute-start.23
  201.6 2.7 %collective-permute-start.24 = (bf16[10,128,128]{2,1,0:T(8,128)(2,1)S(1)}, bf16[10,128,128]{2,1,0:T(8,128)(2,1)S(1)}, u32[]{:S(2)}, u32[]{:S(2)}) collective-permute-start(bf16[10,128,128]{2,1,0:T(8,128)(2,1)S(1)} %get-tuple-element.76.refs_0_), channel_id=1, source_target_pairs={{0,2},{1,3},{2,0},{3,1},{4,6},{5,7},{6,4},{7,5},{8,10},{9,11},{10,... | collective-permute-start | bytes 983048 | tf_op jit(solution)/shard_map/ppermute | solution.py:215
  204.2 1.5 collective-permute-start.25
  206.7 10.6 %collective-permute-done.33 = f32[32,128]{1,0:T(8,128)S(1)} collective-permute-done((f32[32,128]{1,0:T(8,128)S(1)}, f32[32,128]{1,0:T(8,128)S(1)}, u32[]{:S(2)}, u32[]{:S(2)}) %collective-permute-start.33) | collective-permute-done | bytes 16416 | tf_op jit(solution)/shard_map/ppermute | solution.py:215
  217.3 2.4 %collective-permute-start.35 = (f32[32,128]{1,0:T(8,128)S(1)}, f32[32,128]{1,0:T(8,128)S(1)}, u32[]{:S(2)}, u32[]{:S(2)}) collective-permute-start(f32[32,128]{1,0:T(8,128)S(1)} %add_add_fusion), channel_id=1, source_target_pairs={{0,3},{1,0},{2,1},{3,2},{4,7},{5,4},{6,5},{7,6},{8,11},{9,8},{10,9... | collective-permute-start | bytes 49160 | tf_op jit(solution)/shard_map/ppermute | solution.py:215
  219.7 1.4 collective-permute-done.35
  221.8 1.7 last_sum.1
  (68 shorter events, 9.9 us)
Async XLA Ops:
  7.2 136.8 %all-gather.2.cloned.1.call-start = ((), (), s32[]{:S(2)}) async-start(), calls=%async_computation | async-start | bytes 17301504 | tf_op jit(solution)/shard_map/all_gather | solution.py:317
  7.9 12.7 %collective-permute-start.1 = (bf16[128,14336]{1,0:T(8,128)(2,1)}, bf16[128,14336]{1,0:T(8,128)(2,1)}, u32[]{:S(2)}, u32[]{:S(2)}) collective-permute-start(bf16[128,14336]{1,0:T(8,128)(2,1)} %refs_7_.1), channel_id=1, source_target_pairs={{0,4},{4,0},{1,5},{5,1},{2,6},{6,2},{3,7},{7,3},{8,12},{12,8},{9,1... | collective-permute-start | bytes 11010056 | tf_op jit(solution)/shard_map/ppermute | solution.py:320
  8.0 7.7 %collective-permute-start = (bf16[128,4096]{1,0:T(8,128)(2,1)}, bf16[128,4096]{1,0:T(8,128)(2,1)S(1)}, u32[]{:S(2)}, u32[]{:S(2)}) collective-permute-start(bf16[128,4096]{1,0:T(8,128)(2,1)} %refs_3_.1), channel_id=1, source_target_pairs={{0,4},{4,0},{1,5},{5,1},{2,6},{6,2},{3,7},{7,3},{8,12},{12,8},{9,1... | collective-permute-start | bytes 3145736 | tf_op jit(solution)/shard_map/ppermute | solution.py:319
  8.5 12.1 %copy-start = (bf16[128,14336]{1,0:T(8,128)(2,1)S(1)}, bf16[128,14336]{1,0:T(8,128)(2,1)}, u32[]{:S(2)}) copy-start(bf16[128,14336]{1,0:T(8,128)(2,1)} %refs_7_.1) | copy-start | bytes 11010052
  8.5 12.1 %copy-start.8 = (s32[512]{0:T(512)S(1)}, s32[512]{0:T(512)}, u32[]{:S(2)}) copy-start(s32[512]{0:T(512)} %refs_0_.5) | copy-start | bytes 6148
  8.5 12.1 %copy-start.9 = (s32[512]{0:T(512)S(1)}, s32[512]{0:T(512)}, u32[]{:S(2)}) copy-start(s32[512]{0:T(512)} %refs_1_.5) | copy-start | bytes 6148
  12.4 8.1 %copy-start.3 = (bf16[32,128,128]{2,1,0:T(8,128)(2,1)S(1)}, bf16[32,128,128]{2,1,0:T(8,128)(2,1)}, u32[]{:S(2)}) copy-start(bf16[32,128,128]{2,1,0:T(8,128)(2,1)} %get-tuple-element.43.refs_3_) | copy-start | bytes 3145732
  20.6 1.2 copy-start.4
  40.2 29.0 %collective-permute-start.10 = (bf16[16,128,128]{2,1,0:T(8,128)(2,1)S(1)}, bf16[16,128,128]{2,1,0:T(8,128)(2,1)S(1)}, u32[]{:S(2)}, u32[]{:S(2)}) collective-permute-start(bf16[16,128,128]{2,1,0:T(8,128)(2,1)S(1)} %get-tuple-element.56), channel_id=1, source_target_pairs={{0,96},{32,0},{64,32},{96,64},{1,97},{33,1},{65,33},{97,65},{2,98}... | collective-permute-start | bytes 1572872 | tf_op jit(solution)/shard_map/ppermute | solution.py:215
  43.5 28.7 %collective-permute-start.8 = (bf16[16,128,128]{2,1,0:T(8,128)(2,1)S(1)}, bf16[16,128,128]{2,1,0:T(8,128)(2,1)S(1)}, u32[]{:S(2)}, u32[]{:S(2)}) collective-permute-start(bf16[16,128,128]{2,1,0:T(8,128)(2,1)S(1)} %get-tuple-element.54), channel_id=1, source_target_pairs={{0,32},{32,64},{64,96},{96,0},{1,33},{33,65},{65,97},{97,1},{2,34}... | collective-permute-start | bytes 1572872 | tf_op jit(solution)/shard_map/ppermute | solution.py:215
  43.5 45.4 %collective-permute-start.9 = (bf16[16,128,128]{2,1,0:T(8,128)(2,1)S(1)}, bf16[16,128,128]{2,1,0:T(8,128)(2,1)S(1)}, u32[]{:S(2)}, u32[]{:S(2)}) collective-permute-start(bf16[16,128,128]{2,1,0:T(8,128)(2,1)S(1)} %get-tuple-element.55), channel_id=1, source_target_pairs={{0,64},{32,96},{64,0},{96,32},{1,65},{33,97},{65,1},{97,33},{2,66}... | collective-permute-start | bytes 1572872 | tf_op jit(solution)/shard_map/ppermute | solution.py:215
  45.7 47.5 %collective-permute-start.5 = (bf16[16,128,128]{2,1,0:T(8,128)(2,1)S(1)}, bf16[16,128,128]{2,1,0:T(8,128)(2,1)S(1)}, u32[]{:S(2)}, u32[]{:S(2)}) collective-permute-start(bf16[16,128,128]{2,1,0:T(8,128)(2,1)S(1)} %get-tuple-element.50), channel_id=1, source_target_pairs={{0,8},{8,16},{16,24},{24,0},{1,9},{9,17},{17,25},{25,1},{2,10},{10... | collective-permute-start | bytes 1572872 | tf_op jit(solution)/shard_map/ppermute | solution.py:215
  47.6 72.6 %collective-permute-start.4 = (bf16[32,128,128]{2,1,0:T(8,128)(2,1)S(1)}, bf16[32,128,128]{2,1,0:T(8,128)(2,1)S(1)}, u32[]{:S(2)}, u32[]{:S(2)}) collective-permute-start(bf16[32,128,128]{2,1,0:T(8,128)(2,1)S(1)} %get-tuple-element.48.refs_7_), channel_id=1, source_target_pairs={{0,3},{1,0},{2,1},{3,2},{4,7},{5,4},{6,5},{7,6},{8,11},{9,8},{10,9... | collective-permute-start | bytes 3145736 | tf_op jit(solution)/shard_map/ppermute | solution.py:215
  69.2 52.6 %collective-permute-start.2 = (bf16[32,128,128]{2,1,0:T(8,128)(2,1)S(1)}, bf16[32,128,128]{2,1,0:T(8,128)(2,1)S(1)}, u32[]{:S(2)}, u32[]{:S(2)}) collective-permute-start(bf16[32,128,128]{2,1,0:T(8,128)(2,1)S(1)} %get-tuple-element.46), channel_id=1, source_target_pairs={{0,1},{1,2},{2,3},{3,0},{4,5},{5,6},{6,7},{7,4},{8,9},{9,10},{10,1... | collective-permute-start | bytes 3145736 | tf_op jit(solution)/shard_map/ppermute | solution.py:215
  72.1 50.8 %collective-permute-start.3 = (bf16[32,128,128]{2,1,0:T(8,128)(2,1)S(1)}, bf16[32,128,128]{2,1,0:T(8,128)(2,1)S(1)}, u32[]{:S(2)}, u32[]{:S(2)}) collective-permute-start(bf16[32,128,128]{2,1,0:T(8,128)(2,1)S(1)} %get-tuple-element.47), channel_id=1, source_target_pairs={{0,2},{1,3},{2,0},{3,1},{4,6},{5,7},{6,4},{7,5},{8,10},{9,11},{10,... | collective-permute-start | bytes 3145736 | tf_op jit(solution)/shard_map/ppermute | solution.py:215
  88.8 17.9 %collective-permute-start.6 = (bf16[16,128,128]{2,1,0:T(8,128)(2,1)S(1)}, bf16[16,128,128]{2,1,0:T(8,128)(2,1)S(1)}, u32[]{:S(2)}, u32[]{:S(2)}) collective-permute-start(bf16[16,128,128]{2,1,0:T(8,128)(2,1)S(1)} %get-tuple-element.51), channel_id=1, source_target_pairs={{0,16},{8,24},{16,0},{24,8},{1,17},{9,25},{17,1},{25,9},{2,18},{10... | collective-permute-start | bytes 1572872 | tf_op jit(solution)/shard_map/ppermute | solution.py:215
  93.2 24.5 %collective-permute-start.7 = (bf16[16,128,128]{2,1,0:T(8,128)(2,1)S(1)}, bf16[16,128,128]{2,1,0:T(8,128)(2,1)S(1)}, u32[]{:S(2)}, u32[]{:S(2)}) collective-permute-start(bf16[16,128,128]{2,1,0:T(8,128)(2,1)S(1)} %get-tuple-element.52), channel_id=1, source_target_pairs={{0,24},{8,0},{16,8},{24,16},{1,25},{9,1},{17,9},{25,17},{2,26},{10... | collective-permute-start | bytes 1572872 | tf_op jit(solution)/shard_map/ppermute | solution.py:215
  118.3 8.2 %collective-permute-start.17 = (bf16[4,128,128]{2,1,0:T(8,128)(2,1)S(1)}, bf16[4,128,128]{2,1,0:T(8,128)(2,1)S(1)}, u32[]{:S(2)}, u32[]{:S(2)}) collective-permute-start(bf16[4,128,128]{2,1,0:T(8,128)(2,1)S(1)} %get-tuple-element.66), channel_id=1, source_target_pairs={{0,32},{32,64},{64,96},{96,0},{1,33},{33,65},{65,97},{97,1},{2,34}... | collective-permute-start | bytes 393224 | tf_op jit(solution)/shard_map/ppermute | solution.py:215
  118.4 8.5 %collective-permute-start.18 = (bf16[4,128,128]{2,1,0:T(8,128)(2,1)S(1)}, bf16[4,128,128]{2,1,0:T(8,128)(2,1)S(1)}, u32[]{:S(2)}, u32[]{:S(2)}) collective-permute-start(bf16[4,128,128]{2,1,0:T(8,128)(2,1)S(1)} %get-tuple-element.67), channel_id=1, source_target_pairs={{0,64},{32,96},{64,0},{96,32},{1,65},{33,97},{65,1},{97,33},{2,66}... | collective-permute-start | bytes 393224 | tf_op jit(solution)/shard_map/ppermute | solution.py:215
  120.2 9.2 %collective-permute-start.19 = (bf16[4,128,128]{2,1,0:T(8,128)(2,1)S(1)}, bf16[4,128,128]{2,1,0:T(8,128)(2,1)S(1)}, u32[]{:S(2)}, u32[]{:S(2)}) collective-permute-start(bf16[4,128,128]{2,1,0:T(8,128)(2,1)S(1)} %get-tuple-element.68), channel_id=1, source_target_pairs={{0,96},{32,0},{64,32},{96,64},{1,97},{33,1},{65,33},{97,65},{2,98}... | collective-permute-start | bytes 393224 | tf_op jit(solution)/shard_map/ppermute | solution.py:215
  121.8 9.8 %collective-permute-start.14 = (bf16[4,128,128]{2,1,0:T(8,128)(2,1)S(1)}, bf16[4,128,128]{2,1,0:T(8,128)(2,1)S(1)}, u32[]{:S(2)}, u32[]{:S(2)}) collective-permute-start(bf16[4,128,128]{2,1,0:T(8,128)(2,1)S(1)} %get-tuple-element.63), channel_id=1, source_target_pairs={{0,8},{8,16},{16,24},{24,0},{1,9},{9,17},{17,25},{25,1},{2,10},{10... | collective-permute-start | bytes 393224 | tf_op jit(solution)/shard_map/ppermute | solution.py:215
  124.1 13.6 %collective-permute-start.11 = (bf16[8,128,128]{2,1,0:T(8,128)(2,1)S(1)}, bf16[8,128,128]{2,1,0:T(8,128)(2,1)S(1)}, u32[]{:S(2)}, u32[]{:S(2)}) collective-permute-start(bf16[8,128,128]{2,1,0:T(8,128)(2,1)S(1)} %get-tuple-element.60), channel_id=1, source_target_pairs={{0,32},{32,64},{64,96},{96,0},{1,33},{33,65},{65,97},{97,1},{2,34}... | collective-permute-start | bytes 786440 | tf_op jit(solution)/shard_map/ppermute | solution.py:215
  126.5 11.2 %collective-permute-start.12 = (bf16[8,128,128]{2,1,0:T(8,128)(2,1)S(1)}, bf16[8,128,128]{2,1,0:T(8,128)(2,1)S(1)}, u32[]{:S(2)}, u32[]{:S(2)}) collective-permute-start(bf16[8,128,128]{2,1,0:T(8,128)(2,1)S(1)} %get-tuple-element.61), channel_id=1, source_target_pairs={{0,64},{32,96},{64,0},{96,32},{1,65},{33,97},{65,1},{97,33},{2,66}... | collective-permute-start | bytes 786440 | tf_op jit(solution)/shard_map/ppermute | solution.py:215
  126.8 11.6 %collective-permute-start.13 = (bf16[8,128,128]{2,1,0:T(8,128)(2,1)S(1)}, bf16[8,128,128]{2,1,0:T(8,128)(2,1)S(1)}, u32[]{:S(2)}, u32[]{:S(2)}) collective-permute-start(bf16[8,128,128]{2,1,0:T(8,128)(2,1)S(1)} %get-tuple-element.62), channel_id=1, source_target_pairs={{0,96},{32,0},{64,32},{96,64},{1,97},{33,1},{65,33},{97,65},{2,98}... | collective-permute-start | bytes 786440 | tf_op jit(solution)/shard_map/ppermute | solution.py:215
  129.3 6.5 %collective-permute-start.15 = (bf16[4,128,128]{2,1,0:T(8,128)(2,1)S(1)}, bf16[4,128,128]{2,1,0:T(8,128)(2,1)S(1)}, u32[]{:S(2)}, u32[]{:S(2)}) collective-permute-start(bf16[4,128,128]{2,1,0:T(8,128)(2,1)S(1)} %get-tuple-element.64), channel_id=1, source_target_pairs={{0,16},{8,24},{16,0},{24,8},{1,17},{9,25},{17,1},{25,9},{2,18},{10... | collective-permute-start | bytes 393224 | tf_op jit(solution)/shard_map/ppermute | solution.py:215
  131.5 12.5 %copy-start.5 = (bf16[128,4096]{1,0:T(8,128)(2,1)S(1)}, bf16[128,4096]{1,0:T(8,128)(2,1)}, u32[]{:S(2)}) copy-start(bf16[128,4096]{1,0:T(8,128)(2,1)} %refs_3_.1) | copy-start | bytes 3145732
  131.5 12.5 %copy-start.6 = (bf16[128,4096]{1,0:T(8,128)(2,1)S(1)}, bf16[128,4096]{1,0:T(8,128)(2,1)}, u32[]{:S(2)}) copy-start(bf16[128,4096]{1,0:T(8,128)(2,1)} %get-tuple-element.41.refs_4_) | copy-start | bytes 3145732
  131.5 12.5 %copy-start.7 = (f32[128,128]{1,0:T(8,128)S(1)}, f32[128,128]{1,0:T(8,128)}, u32[]{:S(2)}) copy-start(f32[128,128]{1,0:T(8,128)} %get-tuple-element.42.refs_5_) | copy-start | bytes 196612
  131.5 12.5 %copy-start.10 = (f32[4096]{0:T(1024)S(1)}, f32[4096]{0:T(1024)}, u32[]{:S(2)}) copy-start(f32[4096]{0:T(1024)} %param.7) | copy-start | bytes 49156
  131.6 5.3 %collective-permute-start.16 = (bf16[4,128,128]{2,1,0:T(8,128)(2,1)S(1)}, bf16[4,128,128]{2,1,0:T(8,128)(2,1)S(1)}, u32[]{:S(2)}, u32[]{:S(2)}) collective-permute-start(bf16[4,128,128]{2,1,0:T(8,128)(2,1)S(1)} %get-tuple-element.65), channel_id=1, source_target_pairs={{0,24},{8,0},{16,8},{24,16},{1,25},{9,1},{17,9},{25,17},{2,26},{10... | collective-permute-start | bytes 393224 | tf_op jit(solution)/shard_map/ppermute | solution.py:215
  138.7 48.4 %collective-permute-start.20 = (bf16[2,128,128]{2,1,0:T(8,128)(2,1)S(1)}, bf16[2,128,128]{2,1,0:T(8,128)(2,1)S(1)}, u32[]{:S(2)}, u32[]{:S(2)}) collective-permute-start(bf16[2,128,128]{2,1,0:T(8,128)(2,1)S(1)} %get-tuple-element.72), channel_id=1, source_target_pairs={{0,8},{8,16},{16,24},{24,0},{1,9},{9,17},{17,25},{25,1},{2,10},{10... | collective-permute-start | bytes 196616 | tf_op jit(solution)/shard_map/ppermute | solution.py:215
  140.6 46.5 %collective-permute-start.21 = (bf16[2,128,128]{2,1,0:T(8,128)(2,1)S(1)}, bf16[2,128,128]{2,1,0:T(8,128)(2,1)S(1)}, u32[]{:S(2)}, u32[]{:S(2)}) collective-permute-start(bf16[2,128,128]{2,1,0:T(8,128)(2,1)S(1)} %get-tuple-element.73), channel_id=1, source_target_pairs={{0,16},{8,24},{16,0},{24,8},{1,17},{9,25},{17,1},{25,9},{2,18},{10... | collective-permute-start | bytes 196616 | tf_op jit(solution)/shard_map/ppermute | solution.py:215
  142.3 44.8 %collective-permute-start.22 = (bf16[2,128,128]{2,1,0:T(8,128)(2,1)S(1)}, bf16[2,128,128]{2,1,0:T(8,128)(2,1)S(1)}, u32[]{:S(2)}, u32[]{:S(2)}) collective-permute-start(bf16[2,128,128]{2,1,0:T(8,128)(2,1)S(1)} %get-tuple-element.74), channel_id=1, source_target_pairs={{0,24},{8,0},{16,8},{24,16},{1,25},{9,1},{17,9},{25,17},{2,26},{10... | collective-permute-start | bytes 196616 | tf_op jit(solution)/shard_map/ppermute | solution.py:215
  144.0 2.0 copy-start.1
  146.1 5.8 %copy-start.2 = (bf16[512,128,128]{2,1,0:T(8,128)(2,1)S(1)}, bf16[512,128,128]{2,1,0:T(8,128)(2,1)}, u32[]{:S(2)}) copy-start(bf16[512,128,128]{2,1,0:T(8,128)(2,1)} %all-gather.2.cloned.1.call-done.refs_2_) | copy-start | bytes 50331652
  187.1 1.3 collective-permute-start.26
  188.4 5.3 %collective-permute-start.27 = (f32[32,128]{1,0:T(8,128)S(1)}, f32[32,128]{1,0:T(8,128)S(1)}, u32[]{:S(2)}, u32[]{:S(2)}) collective-permute-start(f32[32,128]{1,0:T(8,128)S(1)} %add.30), channel_id=1, source_target_pairs={{0,16},{8,24},{16,0},{24,8},{1,17},{9,25},{17,1},{25,9},{2,18},{10... | collective-permute-start | bytes 49160 | tf_op jit(solution)/shard_map/ppermute | solution.py:215
  189.3 4.9 %collective-permute-start.28 = (f32[32,128]{1,0:T(8,128)S(1)}, f32[32,128]{1,0:T(8,128)S(1)}, u32[]{:S(2)}, u32[]{:S(2)}) collective-permute-start(f32[32,128]{1,0:T(8,128)S(1)} %add.30), channel_id=1, source_target_pairs={{0,8},{8,16},{16,24},{24,0},{1,9},{9,17},{17,25},{25,1},{2,10},{10... | collective-permute-start | bytes 49160 | tf_op jit(solution)/shard_map/ppermute | solution.py:215
  190.0 4.3 %collective-permute-start.29 = (f32[32,128]{1,0:T(8,128)S(1)}, f32[32,128]{1,0:T(8,128)S(1)}, u32[]{:S(2)}, u32[]{:S(2)}) collective-permute-start(f32[32,128]{1,0:T(8,128)S(1)} %add.30), channel_id=1, source_target_pairs={{0,24},{8,0},{16,8},{24,16},{1,25},{9,1},{17,9},{25,17},{2,26},{10... | collective-permute-start | bytes 49160 | tf_op jit(solution)/shard_map/ppermute | solution.py:215
  194.3 9.9 %collective-permute-start.30 = (f32[32,128]{1,0:T(8,128)S(1)}, f32[32,128]{1,0:T(8,128)S(1)}, u32[]{:S(2)}, u32[]{:S(2)}) collective-permute-start(f32[32,128]{1,0:T(8,128)S(1)} %add_add_fusion.1), channel_id=1, source_target_pairs={{0,64},{32,96},{64,0},{96,32},{1,65},{33,97},{65,1},{97,33},{2,66}... | collective-permute-start | bytes 49160 | tf_op jit(solution)/shard_map/ppermute | solution.py:215
  196.9 8.8 %collective-permute-start.31 = (f32[32,128]{1,0:T(8,128)S(1)}, f32[32,128]{1,0:T(8,128)S(1)}, u32[]{:S(2)}, u32[]{:S(2)}) collective-permute-start(f32[32,128]{1,0:T(8,128)S(1)} %add_add_fusion.1), channel_id=1, source_target_pairs={{0,32},{32,64},{64,96},{96,0},{1,33},{33,65},{65,97},{97,1},{2,34}... | collective-permute-start | bytes 49160 | tf_op jit(solution)/shard_map/ppermute | solution.py:215
  198.6 7.2 %collective-permute-start.32 = (f32[32,128]{1,0:T(8,128)S(1)}, f32[32,128]{1,0:T(8,128)S(1)}, u32[]{:S(2)}, u32[]{:S(2)}) collective-permute-start(f32[32,128]{1,0:T(8,128)S(1)} %add_add_fusion.1), channel_id=1, source_target_pairs={{0,96},{32,0},{64,32},{96,64},{1,97},{33,1},{65,33},{97,65},{2,98}... | collective-permute-start | bytes 49160 | tf_op jit(solution)/shard_map/ppermute | solution.py:215
  200.2 21.6 %collective-permute-start.23 = (bf16[10,128,128]{2,1,0:T(8,128)(2,1)S(1)}, bf16[10,128,128]{2,1,0:T(8,128)(2,1)S(1)}, u32[]{:S(2)}, u32[]{:S(2)}) collective-permute-start(bf16[10,128,128]{2,1,0:T(8,128)(2,1)S(1)} %get-tuple-element.76.refs_0_), channel_id=1, source_target_pairs={{0,1},{1,2},{2,3},{3,0},{4,5},{5,6},{6,7},{7,4},{8,9},{9,10},{10,1... | collective-permute-start | bytes 983048 | tf_op jit(solution)/shard_map/ppermute | solution.py:215
  201.6 20.2 %collective-permute-start.24 = (bf16[10,128,128]{2,1,0:T(8,128)(2,1)S(1)}, bf16[10,128,128]{2,1,0:T(8,128)(2,1)S(1)}, u32[]{:S(2)}, u32[]{:S(2)}) collective-permute-start(bf16[10,128,128]{2,1,0:T(8,128)(2,1)S(1)} %get-tuple-element.76.refs_0_), channel_id=1, source_target_pairs={{0,2},{1,3},{2,0},{3,1},{4,6},{5,7},{6,4},{7,5},{8,10},{9,11},{10,... | collective-permute-start | bytes 983048 | tf_op jit(solution)/shard_map/ppermute | solution.py:215
  204.2 17.5 %collective-permute-start.25 = (bf16[10,128,128]{2,1,0:T(8,128)(2,1)S(1)}, bf16[10,128,128]{2,1,0:T(8,128)(2,1)S(1)}, u32[]{:S(2)}, u32[]{:S(2)}) collective-permute-start(bf16[10,128,128]{2,1,0:T(8,128)(2,1)S(1)} %get-tuple-element.76.refs_0_), channel_id=1, source_target_pairs={{0,3},{1,0},{2,1},{3,2},{4,7},{5,4},{6,5},{7,6},{8,11},{9,8},{10,9... | collective-permute-start | bytes 983048 | tf_op jit(solution)/shard_map/ppermute | solution.py:215
  205.7 11.5 %collective-permute-start.33 = (f32[32,128]{1,0:T(8,128)S(1)}, f32[32,128]{1,0:T(8,128)S(1)}, u32[]{:S(2)}, u32[]{:S(2)}) collective-permute-start(f32[32,128]{1,0:T(8,128)S(1)} %add_add_fusion), channel_id=1, source_target_pairs={{0,2},{1,3},{2,0},{3,1},{4,6},{5,7},{6,4},{7,5},{8,10},{9,11},{10,... | collective-permute-start | bytes 49160 | tf_op jit(solution)/shard_map/ppermute | solution.py:215
  206.4 13.3 %collective-permute-start.34 = (f32[32,128]{1,0:T(8,128)S(1)}, f32[32,128]{1,0:T(8,128)S(1)}, u32[]{:S(2)}, u32[]{:S(2)}) collective-permute-start(f32[32,128]{1,0:T(8,128)S(1)} %add_add_fusion), channel_id=1, source_target_pairs={{0,1},{1,2},{2,3},{3,0},{4,5},{5,6},{6,7},{7,4},{8,9},{9,10},{10,1... | collective-permute-start | bytes 49160 | tf_op jit(solution)/shard_map/ppermute | solution.py:215
  217.3 3.9 %collective-permute-start.35 = (f32[32,128]{1,0:T(8,128)S(1)}, f32[32,128]{1,0:T(8,128)S(1)}, u32[]{:S(2)}, u32[]{:S(2)}) collective-permute-start(f32[32,128]{1,0:T(8,128)S(1)} %add_add_fusion), channel_id=1, source_target_pairs={{0,3},{1,0},{2,1},{3,2},{4,7},{5,4},{6,5},{7,6},{8,11},{9,8},{10,9... | collective-permute-start | bytes 49160 | tf_op jit(solution)/shard_map/ppermute | solution.py:215
  (1 other events, 1.0 us)
Sparse Core Ops, SparseCore 0:
  10.3 95.0 all-gather.1

commit v5 on v3

--- a/solution.py
+++ b/solution.py
@@ -76,52 +76,52 @@
     )(x, gain)
 
 
-def grad_kernel(first, per, step, rows, cols, pos, turned_ref, turned_other_ref, own_ref, other_ref, *refs):
-    out_refs = refs[-4:]
-    base = pl.program_id(0) * step
-    y, z, c = pos[0], pos[1], pos[2]
-    each = 4 * per // step
-
-    for major, out_ref in enumerate(out_refs):
-
-        @pl.when(pl.program_id(0) // each == major)
-        def _(major=major, out_ref=out_ref):
+def listed(half, ahead, i, y, z, c, x):
+    owner = lax.rem(y + i // 8, 4) * 4 + lax.rem(z + i // 2 % 4, 4)
+    return owner * 32 + c * 16 + 8 * half + 2 * lax.rem(x + ahead, 4) + i % 2
+
+
+STEP = 16
+
+
+def grad_kernel(half, each, rows, cols, pos, turned_ref, turned_other_ref, own_ref, other_ref, *refs):
+    at = pl.program_id(0)
+    y, z, c, x = pos[0], pos[1], pos[2], pos[3]
+
+    for ahead, out_ref in enumerate(refs[-4:]):
+
+        @pl.when(at // each == ahead)
+        def _(ahead=ahead, out_ref=out_ref):
             def one(k, carry):
-                i = base + k - major * 4 * per
-                minor, t = i // per, i % per
-                if first == "y":
-                    place = lax.rem(y + major, 4) * 4 + lax.rem(z + minor, 4)
-                else:
-                    place = lax.rem(y + minor, 4) * 4 + lax.rem(z + major, 4)
-                index = place * 32 + c * 16 + (0 if first == "y" else 16 - per) + t
+                index = listed(half, ahead, (at - ahead * each) * STEP + k, y, z, c, x)
                 r, q = rows[index], cols[index]
                 left = jnp.concatenate([turned_ref[r], turned_other_ref[r]], axis=1)
                 right = jnp.concatenate([own_ref[:, cols_at(q)], other_ref[:, cols_at(q)]], axis=0)
                 out_ref[k] = dot(left, right).astype(BF)
                 return carry
 
-            lax.fori_loop(0, step, one, 0, unroll=8)
-
-
-def grads(first, per, rows, cols, pos, turned, turned_other, own, other, ties=()):
-    piece, step = 4 * per, 16
-    each = piece // step
-
-    def out_spec(major):
-        return pl.BlockSpec((step, T, T), lambda i, *_: (jnp.clip(i - major * each, 0, each - 1), 0, 0))
-
-    return pl.pallas_call(
-        lambda *refs: grad_kernel(first, per, step, *refs),
+            lax.fori_loop(0, STEP, one, 0, unroll=8)
+
+
+def grads(half, rows, cols, pos, turned, turned_other, own, other, ties=()):
+    piece = 32
+    each = piece // STEP
+
+    def out_spec(ahead):
+        return pl.BlockSpec((STEP, T, T), lambda i, *_: (jnp.clip(i - ahead * each, 0, each - 1), 0, 0))
+
+    return pl.pallas_call(
+        lambda *refs: grad_kernel(half, each, *refs),
         out_shape=[jax.ShapeDtypeStruct((piece, T, T), BF)] * 4,
         grid_spec=pltpu.PrefetchScalarGridSpec(
             num_scalar_prefetch=3,
             grid=(4 * each,),
             in_specs=[whole(a.shape) for a in (turned, turned_other, own, other)] + [ANY] * len(ties),
-            out_specs=[out_spec(major) for major in range(4)],
+            out_specs=[out_spec(ahead) for ahead in range(4)],
         ),
-        compiler_params=params(56),
+        compiler_params=params(40),
         cost_estimate=cost(2, 0),
-        name="grads_" + first,
+        name="grads",
     )(rows, cols, pos, turned, turned_other, own, other, *ties)
 
 
@@ -155,7 +155,7 @@
             at = cols_at(b)
             x = x_ref[:, at].astype(F4)
             back = back_acc[:, at]
-            sums_ref[:, at] = jnp.sum(back * x * scale, axis=0, keepdims=True)
+            sums_ref[pl.ds(b, 1), :] = jnp.sum(back * x * scale, axis=0, keepdims=True)
             return total + x * gain_ref[:, at] * back
 
         total = lax.fori_loop(0, blocks, products, jnp.zeros((count, T), F4), unroll=2)
@@ -185,7 +185,7 @@
         out_shape=(
             jax.ShapeDtypeStruct(g.shape, BF),
             jax.ShapeDtypeStruct(x.shape, BF),
-            jax.ShapeDtypeStruct((1, width), F4),
+            jax.ShapeDtypeStruct((width // T, T), F4),
         ),
         grid_spec=pltpu.PrefetchScalarGridSpec(
             num_scalar_prefetch=2,
@@ -193,10 +193,10 @@
             in_specs=[pl.BlockSpec((step, T, T), lambda i, *_: (i, 0, 0))]
             + [whole(a.shape) for a in (x, normed, scale, gain, g)]
             + [ANY] * len(ties),
-            out_specs=[whole(g.shape), whole(x.shape), whole((1, width))],
+            out_specs=[whole(g.shape), whole(x.shape), whole((width // T, T))],
             scratch_shapes=[pltpu.VMEM(g.shape, F4), pltpu.VMEM(x.shape, F4)],
         ),
-        compiler_params=params(32),
+        compiler_params=params(50),
         cost_estimate=cost(2, 0),
         name="project",
     )(rows, cols, tiles, x, normed, scale, gain, g, *ties)
@@ -206,53 +206,115 @@
     return lax.ppermute(piece, axis, [(i, (i + shift) % 4) for i in range(4)])
 
 
-def first_sum(pieces, ties):
+def add_four(refs, i):
+    a, b, c, d = (r[i].astype(F4) for r in refs)
+    return (a + c) + (b + d)
+
+
+def put_sums(ref, i, value):
+    rows = value.shape[0]
+    for part in range(3):
+        rounded = value.astype(BF)
+        ref[i, part * rows : (part + 1) * rows] = rounded
+        value = value - rounded.astype(F4)
+    ref[i, 3 * rows :] = jnp.zeros((T - 3 * rows, T), BF)
+
+
+def get_sums(ref, i, rows):
+    low, mid, high = (ref[i, part * rows : (part + 1) * rows].astype(F4) for part in (2, 1, 0))
+    return (low + mid) + high
+
+
+def add_sums(refs, i, rows):
+    a, b, c, d = (get_sums(r, i, rows) for r in refs)
+    return (a + c) + (b + d)
+
+
+def first_sum(pieces, sums=()):
     each = pieces[0].shape[0] // 4
+    more = 1 if sums else 0
 
     def kernel(*refs):
-        ins, outs = refs[:4], refs[-4:]
-        a, b, c, d = (r[...].astype(F4) for r in ins)
-        total = ((a + c) + (b + d)).astype(BF)
-        for major, out in enumerate(outs):
-
-            @pl.when(pl.program_id(0) == major)
+        outs = refs[-4:]
+        total = add_four(refs[:4], ...).astype(BF)
+        for ahead, out in enumerate(outs):
+
+            @pl.when(pl.program_id(0) == ahead)
             def _(out=out):
-                out[...] = total
+                out[:each] = total
+                if sums:
+                    put_sums(out, each, refs[4][...] + refs[5][...])
 
     return pl.pallas_call(
         kernel,
-        out_shape=[jax.ShapeDtypeStruct((each, T, T), BF)] * 4,
+        out_shape=[jax.ShapeDtypeStruct((each + more, T, T), BF)] * 4,
         grid=(4,),
-        in_specs=[pl.BlockSpec((each, T, T), lambda i: (i, 0, 0))] * 4 + [ANY] * len(ties),
-        out_specs=[whole((each, T, T))] * 4,
+        in_specs=[pl.BlockSpec((each, T, T), lambda i: (i, 0, 0))] * 4 + [whole(a.shape) for a in sums],
+        out_specs=[whole((each + more, T, T))] * 4,
         compiler_params=params(32),
         cost_estimate=cost(1, 0),
         name="first_sum",
-    )(*pieces, *ties)
-
-
-def sum_of_four(groups, dtype, passed, name):
-    count = groups[0][0].shape[0]
-    arrays = [a for group in groups for a in group]
+    )(*pieces, *sums)
+
+
+def second_sum(plain, with_sums, rows):
+    each = plain[0].shape[0] // 4
 
     def kernel(*refs):
-        out = refs[len(arrays) + len(passed)]
-        for g in range(len(groups)):
-            for i in range(count):
-                a, b, c, d = (r[i].astype(F4) for r in refs[4 * g : 4 * g + 4])
-                out[g * count + i] = ((a + c) + (b + d)).astype(dtype)
-        for k in range(len(passed)):
-            refs[len(arrays) + len(passed) + 1 + k][...] = refs[len(arrays) + k][...]
+        ins, outs = refs[:8], refs[8:]
+        sums = add_sums(ins[4:], 4 * each, rows)
+        for ahead, out in enumerate(outs):
+            for i in range(each):
+                out[i] = add_four(ins[:4], ahead * each + i).astype(BF)
+                out[each + i] = add_four(ins[4:], ahead * each + i).astype(BF)
+            put_sums(out, 2 * each, sums)
 
     return pl.pallas_call(
         kernel,
-        out_shape=[jax.ShapeDtypeStruct((count * len(groups), T, T), dtype)]
-        + [jax.ShapeDtypeStruct(a.shape, a.dtype) for a in passed],
-        in_specs=[pl.BlockSpec(memory_space=pltpu.VMEM)] * (len(arrays) + len(passed)),
+        out_shape=[jax.ShapeDtypeStruct((2 * each + 1, T, T), BF)] * 4,
+        in_specs=[pl.BlockSpec(memory_space=pltpu.VMEM)] * 8,
         compiler_params=params(32),
         cost_estimate=cost(1, 0),
-        name=name,
-    )(*arrays, *passed)
+        name="second_sum",
+    )(*plain, *with_sums)
+
+
+def third_sum(pieces, rows):
+    count = pieces[0].shape[0] - 1
+
+    def kernel(*refs):
+        for i in range(count):
+            refs[4][i] = add_four(refs[:4], i).astype(BF)
+        put_sums(refs[4], count, add_sums(refs[:4], count, rows))
+
+    return pl.pallas_call(
+        kernel,
+        out_shape=jax.ShapeDtypeStruct((count + 1, T, T), BF),
+        in_specs=[pl.BlockSpec(memory_space=pltpu.VMEM)] * 4,
+        compiler_params=params(32),
+        cost_estimate=cost(1, 0),
+        name="third_sum",
+    )(*pieces)
+
+
+def last_sum(pieces, pos, rows):
+    def kernel(pos_ref, *refs):
+        out_ref, sums_ref = refs[4:]
+        for back in range(4):
+            source = lax.rem(pos_ref[3] + 4 - back, 4)
+            for half in range(2):
+                for u in range(2):
+                    out_ref[8 * half + 2 * source + u] = refs[back][2 * half + u].astype(F4)
+        sums_ref[...] = add_sums(refs[:4], 4, rows)
+
+    return pl.pallas_call(
+        kernel,
+        out_shape=(jax.ShapeDtypeStruct((16, T, T), F4), jax.ShapeDtypeStruct((rows, T), F4)),
+        in_specs=[pl.BlockSpec(memory_space=pltpu.SMEM)] + [pl.BlockSpec(memory_space=pltpu.VMEM)] * 4,
+        compiler_params=params(32),
+        cost_estimate=cost(1, 0),
+        name="last_sum",
+    )(pos, *pieces)
 
 
 def exchange(pieces, axis):
@@ -269,20 +331,17 @@
     g_other = lax.ppermute(cotangent, "c", swap)
     normed, turned, scale = norm(tokens, gain2)
     _, turned_other, _ = norm(tokens_other, gain2)
-    part_y = grads("y", 8, rows, cols, pos, turned, turned_other, cotangent, g_other)
-    part_z = grads("z", 8, rows, cols, pos, turned, turned_other, cotangent, g_other, (part_y[3],))
-    mid_y = first_sum(exchange(part_y, "y"), (part_z[3],))
-    mid_z = first_sum(exchange(part_z, "z"), ())
+    part0 = grads(0, rows, cols, pos, turned, turned_other, cotangent, g_other)
+    part1 = grads(1, rows, cols, pos, turned, turned_other, cotangent, g_other, (part0[3],))
+    mid0 = first_sum(exchange(part0, "x"))
     projected, token_grad, sums = project(
-        rows, cols, piece, tokens, normed, scale, gain2, cotangent, (mid_y[0], mid_z[0])
+        rows, cols, piece, tokens, normed, scale, gain2, cotangent, (mid0[0],)
     )
-    sums = sums.reshape(-1, T)
-    sent, sums = sum_of_four([exchange(mid_y, "z"), exchange(mid_z, "y")], BF, (sums,), "second_sum")
-    (tile_grad,) = sum_of_four([exchange([sent] * 4, "x")], F4, (), "last_sum")
-    sums = sums + lax.ppermute(sums, "c", swap)
-    for axis in ("z", "y", "x"):
-        own, right, opposite, left = exchange([sums] * 4, axis)
-        sums = (own + opposite) + (right + left)
+    mid1 = first_sum(exchange(part1, "x"), (sums, lax.ppermute(sums, "c", swap)))
+    count = sums.shape[0]
+    ends = second_sum(exchange(mid0, "y"), exchange(mid1, "y"), count)
+    sent = third_sum(exchange(ends, "z"), count)
+    tile_grad, sums = last_sum(exchange([sent] * 4, "x"), pos, count)
     return (projected, token_grad, tile_grad, sums.reshape(-1))
 
 

time: 230 us -> 195 us (0.85)
  waiting for transfers between devices: 92.1 us -> 71.7 us
  starting transfers between devices: 41.1 us -> 27.5 us
  Pallas kernels: 76.3 us -> 73.8 us
    ppermute x24 -> x18, waiting for transfers between devices: 87.4 us -> 66.6 us  [ring(): return lax.ppermute(piece, axis, [(i, (i + shift) % 4) for i in range(4)])]
    ppermute x24 -> x18, starting transfers between devices: 40.4 us -> 26.9 us  [ring(): return lax.ppermute(piece, axis, [(i, (i + shift) % 4) for i in range(4)])]
    pallas_call x6 -> x7, Pallas kernels: 32 us -> 28.1 us  [the longest x2 20.5 us: grads(): pl.pallas_call(lambda *refs: grad_kernel(half, each, *refs), out_shape=[j...]
  transfers between devices with their start and end apart: 28 -> 22, of which waited for: 9 -> 10; matrix products, arithmetic and copies ran while one was open for 1% -> 0% of each run, Pallas kernels for 32% -> 37%
where the time goes in v5:
time: 195 us; the launch traced here: 193 us
  Pallas kernels  73.8 us (38%)
  waiting for transfers between devices  71.7 us (37%)
  starting transfers between devices  27.5 us (14%)
  between operations  14.2 us (7%)
  local copies, waits for them, and re-layouts  6.09 us (3%)
    ppermute x18, waiting for transfers between devices, ring(): return lax.ppermute(piece, axis, [(i, (i + shift) % 4) for i in range(4)])  66.6 us
    pallas_call x1, Pallas kernels, project(): pl.pallas_call(lambda *refs: project_kernel(step, *refs), out_shape=(jax....  37.9 us
    ppermute x18, starting transfers between devices, ring(): return lax.ppermute(piece, axis, [(i, (i + shift) % 4) for i in range(4)])  26.9 us
    pallas_call x2, Pallas kernels, grads(): pl.pallas_call(lambda *refs: grad_kernel(half, each, *refs), out_shape=[j...  20.5 us
    pallas_call x2, Pallas kernels, norm(): pl.pallas_call(norm_kernel, out_shape=(jax.ShapeDtypeStruct((count, width...  7.78 us
    unnamed x28, local copies, waits for them, and re-layouts  6.09 us
    pallas_call x2, Pallas kernels, first_sum(): pl.pallas_call(kernel, out_shape=[jax.ShapeDtypeStruct((each + more, T, T...  4.7 us
  transfers between devices with their start and end apart: 22, of which 10 were waited for; matrix products, arithmetic and copies ran while one was open for 0% of the time, Pallas kernels for 37%

profile of v5, /device:TPU:0, one launch (start us, length us, event | category | flops | bytes accessed | tf_op | source)
XLA Modules:
  0.0 193.3 jit_solution(11016961465036947861)
XLA Ops:
  7.2 0.0 all-gather.2.cloned.1.call-start
  7.2 0.7 all-gather.2.cloned.1.call-update
  7.9 0.1 collective-permute-start.1
  8.0 0.5 collective-permute-start
  8.5 3.9 %norm.2 = (bf16[128,4096]{1,0:T(8,128)(2,1)}, bf16[32,128,128]{2,1,0:T(8,128)(2,1)}, f32[128,128]{1,0:T(8,128)}) custom-call(bf16[128,4096]{1,0:T(8,128)(2,1)} %refs_3_.1, f32[1,4096]{1,0:T(1,128)} %bitcast.6), custom_call_target="tpu_custom_call" | custom-call | flops 1100000000 | tf_op jit(solution)/shard_map/norm/pallas_call | solution.py:66
  12.4 0.1 pad_add_fusion.refs_2_.pos_ref
  12.5 3.2 %collective-permute-done.x_ref = bf16[128,4096]{1,0:T(8,128)(2,1)S(1)} collective-permute-done((bf16[128,4096]{1,0:T(8,128)(2,1)}, bf16[128,4096]{1,0:T(8,128)(2,1)S(1)}, u32[]{:S(2)}, u32[]{:S(2)}) %collective-permute-start) | collective-permute-done | bytes 1048608 | tf_op jit(solution)/shard_map/ppermute | solution.py:330
  15.7 1.0 copy-done.13
  16.7 3.8 %norm.3 = (bf16[128,4096]{1,0:T(8,128)(2,1)}, bf16[32,128,128]{2,1,0:T(8,128)(2,1)}, f32[128,128]{1,0:T(8,128)}) custom-call(bf16[128,4096]{1,0:T(8,128)(2,1)} %copy-done.13, f32[1,4096]{1,0:T(1,128)} %bitcast.7), custom_call_target="tpu_custom_call" | custom-call | flops 1100000000 | tf_op jit(solution)/shard_map/norm/pallas_call | solution.py:66
  20.5 0.0 collective-permute-done.1.refs_6_
  20.6 1.2 copy-done.2
  21.8 9.6 %grads.2 = (bf16[32,128,128]{2,1,0:T(8,128)(2,1)S(1)}, bf16[32,128,128]{2,1,0:T(8,128)(2,1)S(1)}, bf16[32,128,128]{2,1,0:T(8,128)(2,1)S(1)}, bf16[32,128,128]{2,1,0:T(8,128)(2,1)S(1)}) custom-call(s32[512]{0:T(512)S(1)} %copy-done.6, s32[512]{0:T(512)S(1)} %copy-done.7, s32[4]{0:T(128)S(1)} %pad_add_fusion.refs_2_.pos_ref, ...), custom_call_target="tpu_custom_call" | custom-call | flops 2200000000 | tf_op jit(solution)/shard_map/grads/pallas_call | solution.py:113
  31.4 2.9 %collective-permute-start.4 = (bf16[32,128,128]{2,1,0:T(8,128)(2,1)S(1)}, bf16[32,128,128]{2,1,0:T(8,128)(2,1)S(1)}, u32[]{:S(2)}, u32[]{:S(2)}) collective-permute-start(bf16[32,128,128]{2,1,0:T(8,128)(2,1)S(1)} %get-tuple-element.40.refs_7_), channel_id=1, source_target_pairs={{0,3},{1,0},{2,1},{3,2},{4,7},{5,4},{6,5},{7,6},{8,11},{9,8},{10,9... | collective-permute-start | bytes 3145736 | tf_op jit(solution)/shard_map/ppermute | solution.py:206
  34.4 2.3 %collective-permute-start.3 = (bf16[32,128,128]{2,1,0:T(8,128)(2,1)S(1)}, bf16[32,128,128]{2,1,0:T(8,128)(2,1)S(1)}, u32[]{:S(2)}, u32[]{:S(2)}) collective-permute-start(bf16[32,128,128]{2,1,0:T(8,128)(2,1)S(1)} %get-tuple-element.39), channel_id=1, source_target_pairs={{0,2},{1,3},{2,0},{3,1},{4,6},{5,7},{6,4},{7,5},{8,10},{9,11},{10,... | collective-permute-start | bytes 3145736 | tf_op jit(solution)/shard_map/ppermute | solution.py:206
  36.6 10.9 %grads.3 = (bf16[32,128,128]{2,1,0:T(8,128)(2,1)S(1)}, bf16[32,128,128]{2,1,0:T(8,128)(2,1)}, bf16[32,128,128]{2,1,0:T(8,128)(2,1)}, bf16[32,128,128]{2,1,0:T(8,128)(2,1)}) custom-call(s32[512]{0:T(512)S(1)} %copy-done.6, s32[512]{0:T(512)S(1)} %copy-done.7, s32[4]{0:T(128)S(1)} %pad_add_fusion.refs_2_.pos_ref, bf16[32,128,128]{2,1,0:T(8,128)(2,1)S(1)} %copy-done.1, ...), custom_call_target="tpu_custom_call" | custom-call | flops 2200000000 | tf_op jit(solution)/shard_map/grads/pallas_call | solution.py:113
  47.5 1.2 collective-permute-start.10
  48.7 0.8 collective-permute-start.8
  49.5 30.6 %collective-permute-done.4.refs_3_ = bf16[32,128,128]{2,1,0:T(8,128)(2,1)S(1)} collective-permute-done((bf16[32,128,128]{2,1,0:T(8,128)(2,1)S(1)}, bf16[32,128,128]{2,1,0:T(8,128)(2,1)S(1)}, u32[]{:S(2)}, u32[]{:S(2)}) %collective-permute-start.4) | collective-permute-done | bytes 1048608 | tf_op jit(solution)/shard_map/ppermute | solution.py:206
  80.2 3.9 %collective-permute-done.2.refs_1_ = bf16[32,128,128]{2,1,0:T(8,128)(2,1)S(1)} collective-permute-done((bf16[32,128,128]{2,1,0:T(8,128)(2,1)S(1)}, bf16[32,128,128]{2,1,0:T(8,128)(2,1)S(1)}, u32[]{:S(2)}, u32[]{:S(2)}) %collective-permute-start.2) | collective-permute-done | bytes 1048608 | tf_op jit(solution)/shard_map/ppermute | solution.py:206
  84.1 1.9 first_sum.2
  85.9 0.7 copy-done.9
  86.6 0.7 copy-done.11
  87.4 1.6 collective-permute-start.5
  88.9 1.2 copy-done.3
  90.2 1.2 copy-done.4
  91.4 37.9 %project.1 = (bf16[128,14336]{1,0:T(8,128)(2,1)}, bf16[128,4096]{1,0:T(8,128)(2,1)}, f32[32,128]{1,0:T(8,128)S(1)}) custom-call(s32[512]{0:T(512)S(1)} %copy-done.6, s32[512]{0:T(512)S(1)} %copy-done.7, bf16[512,128,128]{2,1,0:T(8,128)(2,1)} %all-gather.2.cloned.1.call-done.refs_2_, bf16[128,4096]{1,0:T(8,128)(2,1)S(1)} %copy-done.3, ...), custom_call_target="tpu_custom_call" | custom-call | flops 2200000000 | tf_op jit(solution)/shard_map/project/pallas_call | solution.py:183
  129.4 1.1 collective-permute-done.11.refs_5_
  130.5 2.8 %first_sum.3 = (bf16[9,128,128]{2,1,0:T(8,128)(2,1)S(1)}, bf16[9,128,128]{2,1,0:T(8,128)(2,1)S(1)}, bf16[9,128,128]{2,1,0:T(8,128)(2,1)S(1)}, bf16[9,128,128]{2,1,0:T(8,128)(2,1)S(1)}) custom-call(bf16[32,128,128]{2,1,0:T(8,128)(2,1)S(1)} %get-tuple-element.47.refs_0_, bf16[32,128,128]{2,1,0:T(8,128)(2,1)S(1)} %collective-permute-done.8.refs_1_, ...), custom_call_target="tpu_custom_call" | custom-call | flops 1100000000 | tf_op jit(solution)/shard_map/first_sum/pallas_call | solution.py:248
  133.4 1.6 collective-permute-start.12
  135.0 1.6 collective-permute-start.13
  136.6 2.4 %collective-permute-start.14 = (bf16[9,128,128]{2,1,0:T(8,128)(2,1)S(1)}, bf16[9,128,128]{2,1,0:T(8,128)(2,1)S(1)}, u32[]{:S(2)}, u32[]{:S(2)}) collective-permute-start(bf16[9,128,128]{2,1,0:T(8,128)(2,1)S(1)} %get-tuple-element.55), channel_id=1, source_target_pairs={{0,96},{32,0},{64,32},{96,64},{1,97},{33,1},{65,33},{97,65},{2,98}... | collective-permute-start | bytes 884744 | tf_op jit(solution)/shard_map/ppermute | solution.py:206
  138.9 0.7 collective-permute-start.6
  139.6 1.7 collective-permute-start.7
  141.3 14.4 %collective-permute-done.6.refs_2_ = bf16[8,128,128]{2,1,0:T(8,128)(2,1)S(1)} collective-permute-done((bf16[8,128,128]{2,1,0:T(8,128)(2,1)S(1)}, bf16[8,128,128]{2,1,0:T(8,128)(2,1)S(1)}, u32[]{:S(2)}, u32[]{:S(2)}) %collective-permute-start.6) | collective-permute-done | bytes 262176 | tf_op jit(solution)/shard_map/ppermute | solution.py:206
  155.6 6.3 %collective-permute-done.7.refs_3_ = bf16[8,128,128]{2,1,0:T(8,128)(2,1)S(1)} collective-permute-done((bf16[8,128,128]{2,1,0:T(8,128)(2,1)S(1)}, bf16[8,128,128]{2,1,0:T(8,128)(2,1)S(1)}, u32[]{:S(2)}, u32[]{:S(2)}) %collective-permute-start.7) | collective-permute-done | bytes 262176 | tf_op jit(solution)/shard_map/ppermute | solution.py:206
  161.9 1.2 second_sum.1
  163.2 2.0 %collective-permute-start.15 = (bf16[5,128,128]{2,1,0:T(8,128)(2,1)S(1)}, bf16[5,128,128]{2,1,0:T(8,128)(2,1)S(1)}, u32[]{:S(2)}, u32[]{:S(2)}) collective-permute-start(bf16[5,128,128]{2,1,0:T(8,128)(2,1)S(1)} %get-tuple-element.57), channel_id=1, source_target_pairs={{0,8},{8,16},{16,24},{24,0},{1,9},{9,17},{17,25},{25,1},{2,10},{10... | collective-permute-start | bytes 491528 | tf_op jit(solution)/shard_map/ppermute | solution.py:206
  165.1 3.5 %collective-permute-start.16 = (bf16[5,128,128]{2,1,0:T(8,128)(2,1)S(1)}, bf16[5,128,128]{2,1,0:T(8,128)(2,1)S(1)}, u32[]{:S(2)}, u32[]{:S(2)}) collective-permute-start(bf16[5,128,128]{2,1,0:T(8,128)(2,1)S(1)} %get-tuple-element.58), channel_id=1, source_target_pairs={{0,16},{8,24},{16,0},{24,8},{1,17},{9,25},{17,1},{25,9},{2,18},{10... | collective-permute-start | bytes 491528 | tf_op jit(solution)/shard_map/ppermute | solution.py:206
  168.6 1.1 collective-permute-start.17
  169.7 1.6 collective-permute-done.15.refs_1_
  171.3 3.9 %collective-permute-done.16.refs_2_ = bf16[5,128,128]{2,1,0:T(8,128)(2,1)S(1)} collective-permute-done((bf16[5,128,128]{2,1,0:T(8,128)(2,1)S(1)}, bf16[5,128,128]{2,1,0:T(8,128)(2,1)S(1)}, u32[]{:S(2)}, u32[]{:S(2)}) %collective-permute-start.16) | collective-permute-done | bytes 163872 | tf_op jit(solution)/shard_map/ppermute | solution.py:206
  175.2 0.1 third_sum.1.refs_0_
  175.3 0.9 collective-permute-start.18
  176.2 0.6 collective-permute-start.19
  176.8 2.1 %collective-permute-start.20 = (bf16[5,128,128]{2,1,0:T(8,128)(2,1)S(1)}, bf16[5,128,128]{2,1,0:T(8,128)(2,1)S(1)}, u32[]{:S(2)}, u32[]{:S(2)}) collective-permute-start(bf16[5,128,128]{2,1,0:T(8,128)(2,1)S(1)} %third_sum.1.refs_0_), channel_id=1, source_target_pairs={{0,3},{1,0},{2,1},{3,2},{4,7},{5,4},{6,5},{7,6},{8,11},{9,8},{10,9... | collective-permute-start | bytes 491528 | tf_op jit(solution)/shard_map/ppermute | solution.py:206
  178.9 5.3 %collective-permute-done.18.refs_1_ = bf16[5,128,128]{2,1,0:T(8,128)(2,1)S(1)} collective-permute-done((bf16[5,128,128]{2,1,0:T(8,128)(2,1)S(1)}, bf16[5,128,128]{2,1,0:T(8,128)(2,1)S(1)}, u32[]{:S(2)}, u32[]{:S(2)}) %collective-permute-start.18) | collective-permute-done | bytes 163872 | tf_op jit(solution)/shard_map/ppermute | solution.py:206
  184.3 0.6 collective-permute-done.20.refs_3_
  184.9 1.6 last_sum.1
  (36 shorter events, 0.1 us)
Async XLA Ops:
  7.2 81.8 %all-gather.2.cloned.1.call-start = ((), (), s32[]{:S(2)}) async-start(), calls=%async_computation | async-start | bytes 17301504 | tf_op jit(solution)/shard_map/all_gather | solution.py:328
  7.9 12.7 %collective-permute-start.1 = (bf16[128,14336]{1,0:T(8,128)(2,1)}, bf16[128,14336]{1,0:T(8,128)(2,1)}, u32[]{:S(2)}, u32[]{:S(2)}) collective-permute-start(bf16[128,14336]{1,0:T(8,128)(2,1)} %refs_5_.3), channel_id=1, source_target_pairs={{0,4},{4,0},{1,5},{5,1},{2,6},{6,2},{3,7},{7,3},{8,12},{12,8},{9,1... | collective-permute-start | bytes 11010056 | tf_op jit(solution)/shard_map/ppermute | solution.py:331
  8.0 7.7 %collective-permute-start = (bf16[128,4096]{1,0:T(8,128)(2,1)}, bf16[128,4096]{1,0:T(8,128)(2,1)S(1)}, u32[]{:S(2)}, u32[]{:S(2)}) collective-permute-start(bf16[128,4096]{1,0:T(8,128)(2,1)} %refs_3_.1), channel_id=1, source_target_pairs={{0,4},{4,0},{1,5},{5,1},{2,6},{6,2},{3,7},{7,3},{8,12},{12,8},{9,1... | collective-permute-start | bytes 3145736 | tf_op jit(solution)/shard_map/ppermute | solution.py:330
  8.5 12.1 %copy-start = (bf16[128,14336]{1,0:T(8,128)(2,1)S(1)}, bf16[128,14336]{1,0:T(8,128)(2,1)}, u32[]{:S(2)}) copy-start(bf16[128,14336]{1,0:T(8,128)(2,1)} %refs_5_.3) | copy-start | bytes 11010052
  8.5 12.1 %copy-start.6 = (s32[512]{0:T(512)S(1)}, s32[512]{0:T(512)}, u32[]{:S(2)}) copy-start(s32[512]{0:T(512)} %refs_0_.5) | copy-start | bytes 6148
  8.5 12.1 %copy-start.7 = (s32[512]{0:T(512)S(1)}, s32[512]{0:T(512)}, u32[]{:S(2)}) copy-start(s32[512]{0:T(512)} %refs_1_.5) | copy-start | bytes 6148
  12.4 8.1 %copy-start.1 = (bf16[32,128,128]{2,1,0:T(8,128)(2,1)S(1)}, bf16[32,128,128]{2,1,0:T(8,128)(2,1)}, u32[]{:S(2)}) copy-start(bf16[32,128,128]{2,1,0:T(8,128)(2,1)} %get-tuple-element.35.refs_3_) | copy-start | bytes 3145732
  15.7 1.0 copy-start.13
  20.6 1.2 copy-start.2
  31.4 48.7 %collective-permute-start.4 = (bf16[32,128,128]{2,1,0:T(8,128)(2,1)S(1)}, bf16[32,128,128]{2,1,0:T(8,128)(2,1)S(1)}, u32[]{:S(2)}, u32[]{:S(2)}) collective-permute-start(bf16[32,128,128]{2,1,0:T(8,128)(2,1)S(1)} %get-tuple-element.40.refs_7_), channel_id=1, source_target_pairs={{0,3},{1,0},{2,1},{3,2},{4,7},{5,4},{6,5},{7,6},{8,11},{9,8},{10,9... | collective-permute-start | bytes 3145736 | tf_op jit(solution)/shard_map/ppermute | solution.py:206
  34.4 49.7 %collective-permute-start.2 = (bf16[32,128,128]{2,1,0:T(8,128)(2,1)S(1)}, bf16[32,128,128]{2,1,0:T(8,128)(2,1)S(1)}, u32[]{:S(2)}, u32[]{:S(2)}) collective-permute-start(bf16[32,128,128]{2,1,0:T(8,128)(2,1)S(1)} %get-tuple-element.38), channel_id=1, source_target_pairs={{0,1},{1,2},{2,3},{3,0},{4,5},{5,6},{6,7},{7,4},{8,9},{9,10},{10,1... | collective-permute-start | bytes 3145736 | tf_op jit(solution)/shard_map/ppermute | solution.py:206
  34.4 49.7 %collective-permute-start.3 = (bf16[32,128,128]{2,1,0:T(8,128)(2,1)S(1)}, bf16[32,128,128]{2,1,0:T(8,128)(2,1)S(1)}, u32[]{:S(2)}, u32[]{:S(2)}) collective-permute-start(bf16[32,128,128]{2,1,0:T(8,128)(2,1)S(1)} %get-tuple-element.39), channel_id=1, source_target_pairs={{0,2},{1,3},{2,0},{3,1},{4,6},{5,7},{6,4},{7,5},{8,10},{9,11},{10,... | collective-permute-start | bytes 3145736 | tf_op jit(solution)/shard_map/ppermute | solution.py:206
  47.5 41.4 %copy-start.5 = (f32[128,128]{1,0:T(8,128)S(1)}, f32[128,128]{1,0:T(8,128)}, u32[]{:S(2)}) copy-start(f32[128,128]{1,0:T(8,128)} %get-tuple-element.34.refs_5_) | copy-start | bytes 196612
  47.5 41.4 %copy-start.8 = (f32[4096]{0:T(1024)S(1)}, f32[4096]{0:T(1024)}, u32[]{:S(2)}) copy-start(f32[4096]{0:T(1024)} %param.7) | copy-start | bytes 49156
  47.5 81.8 %collective-permute-start.10 = (bf16[32,128,128]{2,1,0:T(8,128)(2,1)}, bf16[32,128,128]{2,1,0:T(8,128)(2,1)S(1)}, u32[]{:S(2)}, u32[]{:S(2)}) collective-permute-start(bf16[32,128,128]{2,1,0:T(8,128)(2,1)} %get-tuple-element.50), channel_id=1, source_target_pairs={{0,3},{1,0},{2,1},{3,2},{4,7},{5,4},{6,5},{7,6},{8,11},{9,8},{10,9... | collective-permute-start | bytes 3145736 | tf_op jit(solution)/shard_map/ppermute | solution.py:206
  48.7 80.7 %collective-permute-start.8 = (bf16[32,128,128]{2,1,0:T(8,128)(2,1)}, bf16[32,128,128]{2,1,0:T(8,128)(2,1)S(1)}, u32[]{:S(2)}, u32[]{:S(2)}) collective-permute-start(bf16[32,128,128]{2,1,0:T(8,128)(2,1)} %get-tuple-element.48), channel_id=1, source_target_pairs={{0,1},{1,2},{2,3},{3,0},{4,5},{5,6},{6,7},{7,4},{8,9},{9,10},{10,1... | collective-permute-start | bytes 3145736 | tf_op jit(solution)/shard_map/ppermute | solution.py:206
  80.2 49.2 %collective-permute-start.9 = (bf16[32,128,128]{2,1,0:T(8,128)(2,1)}, bf16[32,128,128]{2,1,0:T(8,128)(2,1)}, u32[]{:S(2)}, u32[]{:S(2)}) collective-permute-start(bf16[32,128,128]{2,1,0:T(8,128)(2,1)} %get-tuple-element.49), channel_id=1, source_target_pairs={{0,2},{1,3},{2,0},{3,1},{4,6},{5,7},{6,4},{7,5},{8,10},{9,11},{10,... | collective-permute-start | bytes 3145736 | tf_op jit(solution)/shard_map/ppermute | solution.py:206
  85.9 0.7 copy-start.9
  86.6 0.7 copy-start.11
  87.4 52.2 %collective-permute-start.5 = (bf16[8,128,128]{2,1,0:T(8,128)(2,1)}, bf16[8,128,128]{2,1,0:T(8,128)(2,1)}, u32[]{:S(2)}, u32[]{:S(2)}) collective-permute-start(bf16[8,128,128]{2,1,0:T(8,128)(2,1)} %get-tuple-element.44), channel_id=1, source_target_pairs={{0,32},{32,64},{64,96},{96,0},{1,33},{33,65},{65,97},{97,1},{2,34}... | collective-permute-start | bytes 786440 | tf_op jit(solution)/shard_map/ppermute | solution.py:206
  88.9 1.2 copy-start.3
  90.2 1.2 copy-start.4
  129.3 9.6 %copy-start.12 = (bf16[8,128,128]{2,1,0:T(8,128)(2,1)S(1)}, bf16[8,128,128]{2,1,0:T(8,128)(2,1)}, u32[]{:S(2)}) copy-start(bf16[8,128,128]{2,1,0:T(8,128)(2,1)} %copy-done.11) | copy-start | bytes 786436
  129.3 10.3 %copy-start.10 = (bf16[8,128,128]{2,1,0:T(8,128)(2,1)S(1)}, bf16[8,128,128]{2,1,0:T(8,128)(2,1)}, u32[]{:S(2)}) copy-start(bf16[8,128,128]{2,1,0:T(8,128)(2,1)} %copy-done.9) | copy-start | bytes 786436
  129.3 1.2 collective-permute-start.11
  133.4 28.6 %collective-permute-start.12 = (bf16[9,128,128]{2,1,0:T(8,128)(2,1)S(1)}, bf16[9,128,128]{2,1,0:T(8,128)(2,1)S(1)}, u32[]{:S(2)}, u32[]{:S(2)}) collective-permute-start(bf16[9,128,128]{2,1,0:T(8,128)(2,1)S(1)} %get-tuple-element.53), channel_id=1, source_target_pairs={{0,32},{32,64},{64,96},{96,0},{1,33},{33,65},{65,97},{97,1},{2,34}... | collective-permute-start | bytes 884744 | tf_op jit(solution)/shard_map/ppermute | solution.py:206
  135.0 26.9 %collective-permute-start.13 = (bf16[9,128,128]{2,1,0:T(8,128)(2,1)S(1)}, bf16[9,128,128]{2,1,0:T(8,128)(2,1)S(1)}, u32[]{:S(2)}, u32[]{:S(2)}) collective-permute-start(bf16[9,128,128]{2,1,0:T(8,128)(2,1)S(1)} %get-tuple-element.54), channel_id=1, source_target_pairs={{0,64},{32,96},{64,0},{96,32},{1,65},{33,97},{65,1},{97,33},{2,66}... | collective-permute-start | bytes 884744 | tf_op jit(solution)/shard_map/ppermute | solution.py:206
  136.6 25.4 %collective-permute-start.14 = (bf16[9,128,128]{2,1,0:T(8,128)(2,1)S(1)}, bf16[9,128,128]{2,1,0:T(8,128)(2,1)S(1)}, u32[]{:S(2)}, u32[]{:S(2)}) collective-permute-start(bf16[9,128,128]{2,1,0:T(8,128)(2,1)S(1)} %get-tuple-element.55), channel_id=1, source_target_pairs={{0,96},{32,0},{64,32},{96,64},{1,97},{33,1},{65,33},{97,65},{2,98}... | collective-permute-start | bytes 884744 | tf_op jit(solution)/shard_map/ppermute | solution.py:206
  138.9 16.7 %collective-permute-start.6 = (bf16[8,128,128]{2,1,0:T(8,128)(2,1)S(1)}, bf16[8,128,128]{2,1,0:T(8,128)(2,1)S(1)}, u32[]{:S(2)}, u32[]{:S(2)}) collective-permute-start(bf16[8,128,128]{2,1,0:T(8,128)(2,1)S(1)} %copy-done.12), channel_id=1, source_target_pairs={{0,64},{32,96},{64,0},{96,32},{1,65},{33,97},{65,1},{97,33},{2,66}... | collective-permute-start | bytes 786440 | tf_op jit(solution)/shard_map/ppermute | solution.py:206
  139.6 22.3 %collective-permute-start.7 = (bf16[8,128,128]{2,1,0:T(8,128)(2,1)S(1)}, bf16[8,128,128]{2,1,0:T(8,128)(2,1)S(1)}, u32[]{:S(2)}, u32[]{:S(2)}) collective-permute-start(bf16[8,128,128]{2,1,0:T(8,128)(2,1)S(1)} %copy-done.10), channel_id=1, source_target_pairs={{0,96},{32,0},{64,32},{96,64},{1,97},{33,1},{65,33},{97,65},{2,98}... | collective-permute-start | bytes 786440 | tf_op jit(solution)/shard_map/ppermute | solution.py:206
  163.2 8.2 %collective-permute-start.15 = (bf16[5,128,128]{2,1,0:T(8,128)(2,1)S(1)}, bf16[5,128,128]{2,1,0:T(8,128)(2,1)S(1)}, u32[]{:S(2)}, u32[]{:S(2)}) collective-permute-start(bf16[5,128,128]{2,1,0:T(8,128)(2,1)S(1)} %get-tuple-element.57), channel_id=1, source_target_pairs={{0,8},{8,16},{16,24},{24,0},{1,9},{9,17},{17,25},{25,1},{2,10},{10... | collective-permute-start | bytes 491528 | tf_op jit(solution)/shard_map/ppermute | solution.py:206
  165.1 10.1 %collective-permute-start.16 = (bf16[5,128,128]{2,1,0:T(8,128)(2,1)S(1)}, bf16[5,128,128]{2,1,0:T(8,128)(2,1)S(1)}, u32[]{:S(2)}, u32[]{:S(2)}) collective-permute-start(bf16[5,128,128]{2,1,0:T(8,128)(2,1)S(1)} %get-tuple-element.58), channel_id=1, source_target_pairs={{0,16},{8,24},{16,0},{24,8},{1,17},{9,25},{17,1},{25,9},{2,18},{10... | collective-permute-start | bytes 491528 | tf_op jit(solution)/shard_map/ppermute | solution.py:206
  168.6 6.6 %collective-permute-start.17 = (bf16[5,128,128]{2,1,0:T(8,128)(2,1)S(1)}, bf16[5,128,128]{2,1,0:T(8,128)(2,1)S(1)}, u32[]{:S(2)}, u32[]{:S(2)}) collective-permute-start(bf16[5,128,128]{2,1,0:T(8,128)(2,1)S(1)} %get-tuple-element.59), channel_id=1, source_target_pairs={{0,24},{8,0},{16,8},{24,16},{1,25},{9,1},{17,9},{25,17},{2,26},{10... | collective-permute-start | bytes 491528 | tf_op jit(solution)/shard_map/ppermute | solution.py:206
  175.3 9.0 %collective-permute-start.18 = (bf16[5,128,128]{2,1,0:T(8,128)(2,1)S(1)}, bf16[5,128,128]{2,1,0:T(8,128)(2,1)S(1)}, u32[]{:S(2)}, u32[]{:S(2)}) collective-permute-start(bf16[5,128,128]{2,1,0:T(8,128)(2,1)S(1)} %third_sum.1.refs_0_), channel_id=1, source_target_pairs={{0,1},{1,2},{2,3},{3,0},{4,5},{5,6},{6,7},{7,4},{8,9},{9,10},{10,1... | collective-permute-start | bytes 491528 | tf_op jit(solution)/shard_map/ppermute | solution.py:206
  176.2 8.1 %collective-permute-start.19 = (bf16[5,128,128]{2,1,0:T(8,128)(2,1)S(1)}, bf16[5,128,128]{2,1,0:T(8,128)(2,1)S(1)}, u32[]{:S(2)}, u32[]{:S(2)}) collective-permute-start(bf16[5,128,128]{2,1,0:T(8,128)(2,1)S(1)} %third_sum.1.refs_0_), channel_id=1, source_target_pairs={{0,2},{1,3},{2,0},{3,1},{4,6},{5,7},{6,4},{7,5},{8,10},{9,11},{10,... | collective-permute-start | bytes 491528 | tf_op jit(solution)/shard_map/ppermute | solution.py:206
  176.8 8.1 %collective-permute-start.20 = (bf16[5,128,128]{2,1,0:T(8,128)(2,1)S(1)}, bf16[5,128,128]{2,1,0:T(8,128)(2,1)S(1)}, u32[]{:S(2)}, u32[]{:S(2)}) collective-permute-start(bf16[5,128,128]{2,1,0:T(8,128)(2,1)S(1)} %third_sum.1.refs_0_), channel_id=1, source_target_pairs={{0,3},{1,0},{2,1},{3,2},{4,7},{5,4},{6,5},{7,6},{8,11},{9,8},{10,9... | collective-permute-start | bytes 491528 | tf_op jit(solution)/shard_map/ppermute | solution.py:206
Sparse Core Ops, SparseCore 0:
  10.3 75.0 all-gather.1

commit v6 on v3

v6 whole, which is shorter than its diff:
```python
import jax
import jax.numpy as jnp
from jax import lax
from jax.experimental import pallas as pl
from jax.experimental.pallas import tpu as pltpu
from jax.sharding import Mesh, PartitionSpec as P

BF = jnp.bfloat16
F4 = jnp.float32
T = 128
ALL = ("y", "z", "c", "x")


def params(limit):
    return pltpu.CompilerParams(vmem_limit_bytes=limit * 1024 * 1024)


def cost(micros, nbytes):
    return pl.CostEstimate(flops=int(micros * 1.1e9), bytes_accessed=nbytes, transcendentals=0)


def whole(shape):
    zeros = (0,) * len(shape)
    return pl.BlockSpec(shape, lambda *_: zeros, pipeline_mode=pl.Buffered(1))


def dot(a, b):
    return jnp.dot(a, b, preferred_element_type=F4)


def dot_t(a, b):
    return lax.dot_general(a, b, (((1,), (1,)), ((), ())), preferred_element_type=F4)


ANY = pl.BlockSpec(memory_space=pl.ANY)


def cols_at(index):
    return pl.ds(pl.multiple_of(index * T, T), T)


def norm_kernel(x_ref, gain_ref, normed_ref, turned_ref, scale_ref):
    count, width = x_ref.shape
    blocks = width // T

    def squares(b, total):
        x = x_ref[:, cols_at(b)].astype(F4)
        return total + x * x

    total = lax.fori_loop(0, blocks, squares, jnp.zeros((count, T), F4), unroll=4)
    scale = lax.rsqrt(jnp.sum(total, axis=1, keepdims=True) / width + 1e-05)
    scale_ref[...] = jnp.broadcast_to(scale, (count, T))

    def fill(b, carry):
        x = x_ref[:, cols_at(b)].astype(F4)
        normed = (x * scale * gain_ref[:, cols_at(b)]).astype(BF)
        normed_ref[:, cols_at(b)] = normed
        turned_ref[b] = normed.T
        return carry

    lax.fori_loop(0, blocks, fill, 0, unroll=4)


def norm(x, gain):
    count, width = x.shape
    return pl.pallas_call(
        norm_kernel,
        out_shape=(
            jax.ShapeDtypeStruct((count, width), BF),
            jax.ShapeDtypeStruct((width // T, T, count), BF),
            jax.ShapeDtypeStruct((count, T), F4),
        ),
        compiler_params=params(56),
        cost_estimate=cost(1, 0),
        name="norm",
    )(x, gain)


def first_second(pos):
    y, z, c = pos[0], pos[1], pos[2]
    return jnp.where(c == 0, z, y), jnp.where(c == 0, y, z)


def owned_at(pos, first, second):
    first, second, c = lax.rem(first, 4), lax.rem(second, 4), pos[2]
    return jnp.where(c == 0, second * 4 + first, first * 4 + second) * 32 + c * 16


ORDER = (("x", "y", "z"), ("y", "z", "x"))


def listed(ahead, i, pos):
    y, z, c, x = pos[0], pos[1], pos[2], pos[3]
    one, two, three = ahead, i // 16, i // 4 % 4
    to_x = x + jnp.where(c == 0, one, three)
    to_y = y + jnp.where(c == 0, two, one)
    to_z = z + jnp.where(c == 0, three, two)
    return (lax.rem(to_y, 4) * 4 + lax.rem(to_z, 4)) * 32 + c * 16 + 4 * lax.rem(to_x, 4) + i % 4


STEP = 16


def grad_kernel(each, rows, cols, pos, turned_ref, turned_other_ref, own_ref, other_ref, *refs):
    at = pl.program_id(0)

    for ahead, out_ref in enumerate(refs[-4:]):

        @pl.when(at // each == ahead)
        def _(ahead=ahead, out_ref=out_ref):
            def one(k, carry):
                index = listed(ahead, (at - ahead * each) * STEP + k, pos)
                r, q = rows[index], cols[index]
                left = jnp.concatenate([turned_ref[r], turned_other_ref[r]], axis=1)
                right = jnp.concatenate([own_ref[:, cols_at(q)], other_ref[:, cols_at(q)]], axis=0)
                out_ref[k] = dot(left, right).astype(BF)
                return carry

            lax.fori_loop(0, STEP, one, 0, unroll=8)


def grads(rows, cols, pos, turned, turned_other, own, other, ties=()):
    piece = 64
    each = piece // STEP

    def out_spec(ahead):
        return pl.BlockSpec((STEP, T, T), lambda i, *_: (jnp.clip(i - ahead * each, 0, each - 1), 0, 0))

    return pl.pallas_call(
        lambda *refs: grad_kernel(each, *refs),
        out_shape=[jax.ShapeDtypeStruct((piece, T, T), BF)] * 4,
        grid_spec=pltpu.PrefetchScalarGridSpec(
            num_scalar_prefetch=3,
            grid=(4 * each,),
            in_specs=[whole(a.shape) for a in (turned, turned_other, own, other)] + [ANY] * len(ties),
            out_specs=[out_spec(ahead) for ahead in range(4)],
        ),
        compiler_params=params(40),
        cost_estimate=cost(2, 0),
        name="grads",
    )(rows, cols, pos, turned, turned_other, own, other, *ties)


def share_kernel(
    plan, rows, cols, pos, normed_ref, normed_other_ref, g_ref, g_other_ref, *refs
):
    tile_refs = refs[: len(plan)]
    shared_ref, out_acc, back_acc = refs[-3:]
    at = pl.program_id(0)
    count = normed_ref.shape[0]
    first, second = first_second(pos)

    @pl.when(at == 0)
    def _():
        out_acc[...] = jnp.zeros_like(out_acc)
        back_acc[...] = jnp.zeros_like(back_acc)

    for (behind, offset, start, each), tiles_ref in zip(plan, tile_refs):

        @pl.when((at >= start) & (at < start + each))
        def _(behind=behind, offset=offset, start=start, tiles_ref=tiles_ref):
            def one(k, carry):
                i = offset + (at - start) * 32 + k
                index = owned_at(pos, first + 4 - i // 16, second + 4 - behind) + i % 16
                r, q = cols_at(rows[index]), cols_at(cols[index])
                weight = tiles_ref[k]
                out = dot(jnp.concatenate([normed_ref[:, r], normed_other_ref[:, r]], axis=0), weight)
                back = dot_t(jnp.concatenate([g_ref[:, q], g_other_ref[:, q]], axis=0), weight)
                out_acc[:, q] += out
                back_acc[:, r] += back
                return carry

            lax.fori_loop(0, 32, one, 0, unroll=8)

    @pl.when(at == pl.num_programs(0) - 1)
    def _():
        width = back_acc.shape[1]
        for half, core in ((0, pos[2]), (1, 1 - pos[2])):
            part = slice(half * count, half * count + count)
            shared_ref[core, :, :width] = back_acc[part].astype(BF)
            shared_ref[core, :, width:] = out_acc[part].astype(BF)


def share(rows, cols, pos, blocks, normed, normed_other, g, g_other):
    plan, steps = [], 0
    for tiles, behind, offset in blocks:
        each = tiles.shape[0] // 32
        plan.append((behind, offset, steps, each))
        steps += each

    def tile_spec(start, each):
        return pl.BlockSpec((32, T, T), lambda i, *_: (jnp.clip(i - start, 0, each - 1), 0, 0))

    resident = (normed, normed_other, g, g_other)
    count = g.shape[0]
    shared = (2, count, normed.shape[1] + g.shape[1])
    return pl.pallas_call(
        lambda *refs: share_kernel(plan, *refs),
        out_shape=jax.ShapeDtypeStruct(shared, BF),
        grid_spec=pltpu.PrefetchScalarGridSpec(
            num_scalar_prefetch=3,
            grid=(steps,),
            in_specs=[whole(a.shape) for a in resident] + [tile_spec(start, each) for _, _, start, each in plan],
            out_specs=whole(shared),
            scratch_shapes=[pltpu.VMEM((2 * count, g.shape[1]), F4), pltpu.VMEM((2 * count, normed.shape[1]), F4)],
        ),
        compiler_params=params(56),
        cost_estimate=cost(2, 0),
        name="share",
    )(rows, cols, pos, *resident, *(tiles for tiles, _, _ in blocks))


def finish_kernel(x_ref, scale_ref, gain_ref, parts_ref, shared_ref, *refs):
    projected_ref, token_grad_ref, sums_ref, back_acc = refs[-4:]
    count, width = x_ref.shape
    blocks = width // T
    projected_ref[...] = (shared_ref[0].astype(F4) + shared_ref[1].astype(F4)).astype(BF)

    @pl.when(pl.program_id(0) == 0)
    def _():
        scale = scale_ref[...]

        def products(b, total):
            at = cols_at(b)
            x = x_ref[:, at].astype(F4)
            back = parts_ref[0, :, at].astype(F4) + parts_ref[1, :, at].astype(F4)
            back_acc[:, at] = back
            sums_ref[pl.ds(b, 1), :] = jnp.sum(back * x * scale, axis=0, keepdims=True)
            return total + x * gain_ref[:, at] * back

        total = lax.fori_loop(0, blocks, products, jnp.zeros((count, T), F4), unroll=2)
        inner = jnp.sum(total, axis=1, keepdims=True) / width
        cubed = scale * scale * scale * inner

        def finish(b, carry):
            at = cols_at(b)
            x = x_ref[:, at].astype(F4)
            token_grad_ref[:, at] = (scale * gain_ref[:, at] * back_acc[:, at] - x * cubed).astype(BF)
            return carry

        lax.fori_loop(0, blocks, finish, 0, unroll=2)


def finish(x, scale, gain, shared, ties=()):
    count, width = x.shape
    columns = shared.shape[2] - width
    chunk = columns // 7
    return pl.pallas_call(
        finish_kernel,
        out_shape=(
            jax.ShapeDtypeStruct((count, columns), BF),
            jax.ShapeDtypeStruct(x.shape, BF),
            jax.ShapeDtypeStruct((width // T, T), F4),
        ),
        grid=(7,),
        in_specs=[
            whole(x.shape),
            whole(scale.shape),
            whole(gain.shape),
            whole((2, count, width)),
            pl.BlockSpec((2, count, chunk), lambda i: (0, 0, i + width // chunk)),
        ]
        + [ANY] * len(ties),
        out_specs=[pl.BlockSpec((count, chunk), lambda i: (0, i)), whole(x.shape), whole((width // T, T))],
        scratch_shapes=[pltpu.VMEM(x.shape, F4)],
        compiler_params=params(40),
        cost_estimate=cost(2, 0),
        name="finish",
    )(x, scale, gain, shared, shared, *ties)


def joined(pieces, tie):
    each = pieces[0].shape[0]

    def kernel(*refs):
        for j in range(4):
            refs[-1][j] = refs[j][...]

    return pl.pallas_call(
        kernel,
        out_shape=jax.ShapeDtypeStruct((4, each, T, T), BF),
        grid=(4,),
        in_specs=[pl.BlockSpec((each // 4, T, T), lambda i: (i, 0, 0))] * 4 + [ANY],
        out_specs=pl.BlockSpec((4, each // 4, T, T), lambda i: (0, i, 0, 0)),
        compiler_params=params(32),
        cost_estimate=cost(1, 0),
        name="joined",
    )(*pieces, tie).reshape(4 * each, T, T)


def relayed(left, right, tie):
    half = left.shape[0] // 2

    def kernel(left_ref, right_ref, tie_ref, left_out, right_out):
        left_out[...] = left_ref[...]
        right_out[...] = right_ref[...]

    return pl.pallas_call(
        kernel,
        out_shape=[jax.ShapeDtypeStruct((half, T, T), BF)] * 2,
        grid=(2,),
        in_specs=[
            pl.BlockSpec((half // 2, T, T), lambda i: (i, 0, 0)),
            pl.BlockSpec((half // 2, T, T), lambda i: (2 + i, 0, 0)),
            ANY,
        ],
        out_specs=[pl.BlockSpec((half // 2, T, T), lambda i: (i, 0, 0))] * 2,
        compiler_params=params(32),
        cost_estimate=cost(1, 0),
        name="relayed",
    )(left, right, tie)


def ring(piece, axes, shift):
    if isinstance(axes, str):
        axes = (axes, axes)
    pairs = []
    for source in range(128):
        at = dict(y=source // 32, z=source // 8 % 4, c=source // 4 % 2, x=source % 4)
        axis = axes[at["c"]]
        to = dict(at, **{axis: (at[axis] + shift) % 4})
        pairs.append((source, to["y"] * 32 + to["z"] * 8 + to["c"] * 4 + to["x"]))
    return lax.ppermute(piece, ALL, pairs)


def exchange(pieces, axis):
    return [pieces[0]] + [ring(pieces[j], axis, j) for j in (1, 2, 3)]


def add_four(refs, i):
    a, b, c, d = (r[i].astype(F4) for r in refs)
    return (a + c) + (b + d)


def cut_sum(pieces, ties=()):
    each = pieces[0].shape[0] // 4

    def kernel(*refs):
        total = add_four(refs[:4], ...).astype(BF)
        for ahead, out in enumerate(refs[-4:]):

            @pl.when(pl.program_id(0) == ahead)
            def _(out=out):
                out[...] = total

    return pl.pallas_call(
        kernel,
        out_shape=[jax.ShapeDtypeStruct((each, T, T), BF)] * 4,
        grid=(4,),
        in_specs=[pl.BlockSpec((each, T, T), lambda i: (i, 0, 0))] * 4 + [ANY] * len(ties),
        out_specs=[whole((each, T, T))] * 4,
        compiler_params=params(32),
        cost_estimate=cost(1, 0),
        name="cut_sum",
    )(*pieces, *ties)


def join_sums(groups, ties=()):
    arrays = [a for group in groups for a in group]
    total = sum(group[0].shape[0] for group in groups)

    def kernel(*refs):
        at = 0
        for g, group in enumerate(groups):
            for i in range(group[0].shape[0]):
                refs[-1][at] = add_four(refs[4 * g : 4 * g + 4], i).astype(BF)
                at += 1

    return pl.pallas_call(
        kernel,
        out_shape=jax.ShapeDtypeStruct((total, T, T), BF),
        in_specs=[pl.BlockSpec(memory_space=pltpu.VMEM)] * len(arrays) + [ANY] * len(ties),
        compiler_params=params(32),
        cost_estimate=cost(1, 0),
        name="join_sums",
    )(*arrays, *ties)


def place(pieces, pos):
    def kernel(pos_ref, *refs):
        for back in range(4):
            source = lax.rem(pos_ref[3] + 4 - back, 4)
            for u in range(4):
                refs[-1][4 * source + u] = refs[back][u].astype(F4)

    return pl.pallas_call(
        kernel,
        out_shape=jax.ShapeDtypeStruct((16, T, T), F4),
        in_specs=[pl.BlockSpec(memory_space=pltpu.SMEM)] + [pl.BlockSpec(memory_space=pltpu.VMEM)] * 4,
        compiler_params=params(32),
        cost_estimate=cost(1, 0),
        name="place",
    )(pos, *pieces)


def shards(tokens, gain, tiles, rows, cols, cotangent):
    gain2 = gain.reshape(1, -1)
    pos = jnp.stack([lax.axis_index(a).astype(jnp.int32) for a in ("y", "z", "c", "x")])
    first, second = ("z", "y"), ("y", "z")
    one, two, three = (tuple(order[k] for order in ORDER) for k in range(3))
    swap = [(0, 1), (1, 0)]
    tokens_other = lax.ppermute(tokens, "c", swap)
    g_other = lax.ppermute(cotangent, "c", swap)
    normed, turned, scale = norm(tokens, gain2)
    normed_other, turned_other, _ = norm(tokens_other, gain2)
    line = joined(exchange([tiles] * 4, first), turned_other)
    left, right = ring(line, second, 1), ring(line, second, 3)
    part = grads(rows, cols, pos, turned, turned_other, cotangent, g_other)
    left_half, right_half = relayed(left, right, part[3])
    blocks = [
        (line, 0, 0),
        (left, 1, 0),
        (right, 3, 0),
        (ring(left_half, second, 1), 2, 0),
        (ring(right_half, second, 3), 2, 32),
    ]
    shared = share(rows, cols, pos, blocks, normed, normed_other, cotangent, g_other)
    shared = lax.all_to_all(shared, "c", 0, 0, tiled=True)
    mid = cut_sum(exchange(part, one), (shared,))
    projected, token_grad, sums = finish(tokens, scale, gain2, shared, (mid[0],))
    ends = cut_sum(exchange(mid, two), (sums,))
    sent = join_sums([exchange(ends, three)])
    tile_grad = place(exchange([sent] * 4, "x"), pos)
    sums = sums + lax.ppermute(sums, "c", swap)
    for axis in ("z", "y", "x"):
        own, right, opposite, left = exchange([sums] * 4, axis)
        sums = (own + opposite) + (right + left)
    return (projected, token_grad, tile_grad, sums.reshape(-1))


def solution(mesh):
    grid = Mesh(mesh.devices.reshape(4, 4, 2, 4), ALL)
    owners = ("y", "z", "c")
    placed = (P(ALL, None), P(), P(owners, None, None), P(), P(), P(ALL, None))
    return jax.shard_map(
        shards,
        mesh=grid,
        in_specs=placed,
        out_specs=(P(ALL, None), P(ALL, None), P(owners, None, None), P()),
        check_vma=False,
    )
```

time: 230 us -> 199 us (0.87)
  waiting for transfers between devices: 92.1 us -> 54.8 us
  between operations: 14.2 us -> 0.85 us
  blocking collectives: 0 us -> 13.3 us
  starting transfers between devices: 41.1 us -> 48.5 us
    ppermute x24 -> x28, waiting for transfers between devices: 87.4 us -> 53.6 us  [ring(): return lax.ppermute(piece, ALL, pairs)]
    all_to_all x0 -> x1, blocking collectives: none -> 13.3 us  [shards(): shared = lax.all_to_all(shared, 'c', 0, 0, tiled=True)]
    ppermute x24 -> x28, starting transfers between devices: 40.4 us -> 48 us  [ring(): return lax.ppermute(piece, ALL, pairs)]
    ppermute x1, waiting for transfers between devices: 2.85 us -> 0.05 us  [shards(): tokens_other = lax.ppermute(tokens, 'c', swap)]
    pallas_call x7 -> x9, Pallas kernels: 68.7 us -> 68 us  [the longest x1 32.6 us: share(): pl.pallas_call(lambda *refs: share_kernel(plan, *refs), out_shape=jax.Sha...]
  transfers between devices with their start and end apart: 28 -> 31, of which waited for: 9 -> 11; matrix products, arithmetic and copies ran while one was open for 1% -> 0% of each run, Pallas kernels for 32% -> 35%
where the time goes in v6:
time: 199 us; the launch traced here: 198 us
  Pallas kernels  75.7 us (38%)
  waiting for transfers between devices  54.8 us (28%)
  starting transfers between devices  48.5 us (24%)
  blocking collectives  13.3 us (7%)
  local copies, waits for them, and re-layouts  4.48 us (2%)
    ppermute x28, waiting for transfers between devices, ring(): return lax.ppermute(piece, ALL, pairs)  53.6 us
    ppermute x28, starting transfers between devices, ring(): return lax.ppermute(piece, ALL, pairs)  48 us
    pallas_call x1, Pallas kernels, share(): pl.pallas_call(lambda *refs: share_kernel(plan, *refs), out_shape=jax.Sha...  32.6 us
    pallas_call x1, Pallas kernels, grads(): pl.pallas_call(lambda *refs: grad_kernel(each, *refs), out_shape=[jax.Sha...  17.9 us
    all_to_all x1, blocking collectives, shards(): shared = lax.all_to_all(shared, 'c', 0, 0, tiled=True)  13.3 us
    pallas_call x2, Pallas kernels, norm(): pl.pallas_call(norm_kernel, out_shape=(jax.ShapeDtypeStruct((count, width...  7.76 us
    pallas_call x1, Pallas kernels, finish(): pl.pallas_call(finish_kernel, out_shape=(jax.ShapeDtypeStruct((count, col...  6.63 us
    pallas_call x2, Pallas kernels, cut_sum(): pl.pallas_call(kernel, out_shape=[jax.ShapeDtypeStruct((each, T, T), BF)]...  5.3 us
  transfers between devices with their start and end apart: 31, of which 11 were waited for; matrix products, arithmetic and copies ran while one was open for 0% of the time, Pallas kernels for 35%

profile of v6, /device:TPU:0, one launch (start us, length us, event | category | flops | bytes accessed | tf_op | source)
XLA Modules:
  0.0 198.4 jit_solution(6129480183467985955)
XLA Ops:
  0.7 0.5 collective-permute-start
  1.2 4.0 %collective-permute-start.3 = (bf16[16,128,128]{2,1,0:T(8,128)(2,1)}, bf16[16,128,128]{2,1,0:T(8,128)(2,1)S(1)}, u32[]{:S(2)}, u32[]{:S(2)}) collective-permute-start(bf16[16,128,128]{2,1,0:T(8,128)(2,1)} %refs_0_.3), channel_id=1, source_target_pairs={{0,16},{1,17},{2,18},{3,19},{4,68},{5,69},{6,70},{7,71},{8,24},{9,... | collective-permute-start | bytes 1572872 | tf_op jit(solution)/shard_map/ppermute | solution.py:323
  5.2 1.0 collective-permute-start.2
  6.2 2.2 %collective-permute-start.4 = (bf16[16,128,128]{2,1,0:T(8,128)(2,1)}, bf16[16,128,128]{2,1,0:T(8,128)(2,1)S(1)}, u32[]{:S(2)}, u32[]{:S(2)}) collective-permute-start(bf16[16,128,128]{2,1,0:T(8,128)(2,1)} %refs_0_.3), channel_id=1, source_target_pairs={{0,24},{1,25},{2,26},{3,27},{4,100},{5,101},{6,102},{7,103},{8,0},... | collective-permute-start | bytes 1572872 | tf_op jit(solution)/shard_map/ppermute | solution.py:323
  8.5 1.0 copy-done.17
  9.4 3.8 %norm.3 = (bf16[128,4096]{1,0:T(8,128)(2,1)}, bf16[32,128,128]{2,1,0:T(8,128)(2,1)}, f32[128,128]{1,0:T(8,128)}) custom-call(bf16[128,4096]{1,0:T(8,128)(2,1)} %copy-done.17, f32[1,4096]{1,0:T(1,128)} %bitcast.8), custom_call_target="tpu_custom_call" | custom-call | flops 1100000000 | tf_op jit(solution)/shard_map/norm/pallas_call | solution.py:66
  13.3 4.9 %collective-permute-done.2.refs_1_ = bf16[16,128,128]{2,1,0:T(8,128)(2,1)S(1)} collective-permute-done((bf16[16,128,128]{2,1,0:T(8,128)(2,1)}, bf16[16,128,128]{2,1,0:T(8,128)(2,1)S(1)}, u32[]{:S(2)}, u32[]{:S(2)}) %collective-permute-start.2) | collective-permute-done | bytes 524320 | tf_op jit(solution)/shard_map/ppermute | solution.py:323
  18.2 1.1 collective-permute-done.4.refs_3_
  19.2 1.2 copy-done.2
  20.5 1.8 joined.1
  22.3 3.0 %collective-permute-start.6 = (bf16[64,128,128]{2,1,0:T(8,128)(2,1)}, bf16[64,128,128]{2,1,0:T(8,128)(2,1)S(1)}, u32[]{:S(2)}, u32[]{:S(2)}) collective-permute-start(bf16[64,128,128]{2,1,0:T(8,128)(2,1)} %bitcast.5.refs_7_), channel_id=1, source_target_pairs={{0,96},{1,97},{2,98},{3,99},{4,28},{5,29},{6,30},{7,31},{8,104},{9... | collective-permute-start | bytes 6291464 | tf_op jit(solution)/shard_map/ppermute | solution.py:323
  25.3 3.9 %norm.2 = (bf16[128,4096]{1,0:T(8,128)(2,1)}, bf16[32,128,128]{2,1,0:T(8,128)(2,1)}, f32[128,128]{1,0:T(8,128)}) custom-call(bf16[128,4096]{1,0:T(8,128)(2,1)} %x_ref.3, f32[1,4096]{1,0:T(1,128)} %bitcast.9), custom_call_target="tpu_custom_call" | custom-call | flops 1100000000 | tf_op jit(solution)/shard_map/norm/pallas_call | solution.py:66
  29.4 1.2 copy-done.7
  30.6 17.9 %grads.1 = (bf16[64,128,128]{2,1,0:T(8,128)(2,1)S(1)}, bf16[64,128,128]{2,1,0:T(8,128)(2,1)}, bf16[64,128,128]{2,1,0:T(8,128)(2,1)}, bf16[64,128,128]{2,1,0:T(8,128)(2,1)}) custom-call(s32[512]{0:T(512)S(1)} %copy-done.11, s32[512]{0:T(512)S(1)} %copy-done.12, s32[4]{0:T(128)S(1)} %pad_add_fusion.refs_2_.pos_ref, bf16[32,128,128]{2,1,0:T(8,128)(2,1)S(1)} %copy-done.7, ...), custom_call_target="tpu_custom_call" | custom-call | flops 2200000000 | tf_op jit(solution)/shard_map/grads/pallas_call | solution.py:129
  48.5 1.5 collective-permute-start.9
  50.0 2.7 %collective-permute-start.10 = (bf16[64,128,128]{2,1,0:T(8,128)(2,1)}, bf16[64,128,128]{2,1,0:T(8,128)(2,1)}, u32[]{:S(2)}, u32[]{:S(2)}) collective-permute-start(bf16[64,128,128]{2,1,0:T(8,128)(2,1)} %get-tuple-element.36), channel_id=1, source_target_pairs={{0,2},{1,3},{2,0},{3,1},{4,68},{5,69},{6,70},{7,71},{8,10},{9,11},... | collective-permute-start | bytes 6291464 | tf_op jit(solution)/shard_map/ppermute | solution.py:323
  52.8 1.4 collective-permute-start.11
  54.2 2.1 %relayed.1 = (bf16[32,128,128]{2,1,0:T(8,128)(2,1)S(1)}, bf16[32,128,128]{2,1,0:T(8,128)(2,1)S(1)}) custom-call(bf16[64,128,128]{2,1,0:T(8,128)(2,1)} %collective-permute-done.5.left_ref.refs_8_, bf16[64,128,128]{2,1,0:T(8,128)(2,1)S(1)} %collective-permute-done.6.right_ref.refs_9_, bf16[64,128,128]{2,1,0:T(8,128)(2,1)} %get-tuple-element.31.tie_ref), custom_call_target="tpu_custom_call" | custom-call | flops 1100000000 | tf_op jit(solution)/shard_map/relayed/pallas_call | solution.py:298
  56.3 0.6 collective-permute-start.7
  56.9 2.7 %collective-permute-start.8 = (bf16[32,128,128]{2,1,0:T(8,128)(2,1)S(1)}, bf16[32,128,128]{2,1,0:T(8,128)(2,1)S(1)}, u32[]{:S(2)}, u32[]{:S(2)}) collective-permute-start(bf16[32,128,128]{2,1,0:T(8,128)(2,1)S(1)} %get-tuple-element.33), channel_id=1, source_target_pairs={{0,96},{1,97},{2,98},{3,99},{4,28},{5,29},{6,30},{7,31},{8,104},{9... | collective-permute-start | bytes 3145736 | tf_op jit(solution)/shard_map/ppermute | solution.py:323
  59.7 24.0 %collective-permute-done.7.refs_10_ = bf16[32,128,128]{2,1,0:T(8,128)(2,1)S(1)} collective-permute-done((bf16[32,128,128]{2,1,0:T(8,128)(2,1)S(1)}, bf16[32,128,128]{2,1,0:T(8,128)(2,1)S(1)}, u32[]{:S(2)}, u32[]{:S(2)}) %collective-permute-start.7) | collective-permute-done | bytes 1048608 | tf_op jit(solution)/shard_map/ppermute | solution.py:323
  83.7 13.0 %collective-permute-done.8.refs_11_ = bf16[32,128,128]{2,1,0:T(8,128)(2,1)S(1)} collective-permute-done((bf16[32,128,128]{2,1,0:T(8,128)(2,1)S(1)}, bf16[32,128,128]{2,1,0:T(8,128)(2,1)S(1)}, u32[]{:S(2)}, u32[]{:S(2)}) %collective-permute-start.8) | collective-permute-done | bytes 1048608 | tf_op jit(solution)/shard_map/ppermute | solution.py:323
  96.7 1.0 copy-done.16
  97.7 32.6 %share.1 = bf16[2,128,18432]{2,1,0:T(8,128)(2,1)} custom-call(s32[512]{0:T(512)} %refs_0_.5, s32[512]{0:T(512)} %refs_1_.3, s32[4]{0:T(128)} %copy-done.13, bf16[128,4096]{1,0:T(8,128)(2,1)} %get-tuple-element.27.refs_3_, bf16[128,4096]{1,0:T(8,128)(2,1)} %get-tuple-element.28.refs_4_, bf16[128,14336]{1,0:T(8,128)(2,1)} %refs_5_.3, ...), custom_call_target="tpu_custom_call" | custom-call | flops 2200000000 | tf_op jit(solution)/shard_map/share/pallas_call | solution.py:197
  130.3 13.3 %all_to_all.5.refs_4_.parts_ref.shared_ref = bf16[2,128,18432]{2,1,0:T(8,128)(2,1)S(1)} all-to-all(bf16[2,128,18432]{2,1,0:T(8,128)(2,1)} %share.1), channel_id=1, replica_groups=mesh['y'=4,'z'=4,'c'=2,'x'=4] {'c'}, dimensions={0} | all-to-all | bytes 18874368 | tf_op jit(solution)/shard_map/all_to_all | solution.py:418
  143.7 4.8 %cut_sum.2 = (bf16[16,128,128]{2,1,0:T(8,128)(2,1)S(1)}, bf16[16,128,128]{2,1,0:T(8,128)(2,1)S(1)}, bf16[16,128,128]{2,1,0:T(8,128)(2,1)S(1)}, bf16[16,128,128]{2,1,0:T(8,128)(2,1)S(1)}) custom-call(bf16[64,128,128]{2,1,0:T(8,128)(2,1)S(1)} %copy-done.5, bf16[64,128,128]{2,1,0:T(8,128)(2,1)} %collective-permute-done.9.refs_1_, ...), custom_call_target="tpu_custom_call" | custom-call | flops 1100000000 | tf_op jit(solution)/shard_map/cut_sum/pallas_call | solution.py:346
  148.4 1.9 collective-permute-start.12
  150.3 3.3 %collective-permute-start.13 = (bf16[16,128,128]{2,1,0:T(8,128)(2,1)S(1)}, bf16[16,128,128]{2,1,0:T(8,128)(2,1)S(1)}, u32[]{:S(2)}, u32[]{:S(2)}) collective-permute-start(bf16[16,128,128]{2,1,0:T(8,128)(2,1)S(1)} %get-tuple-element.41), channel_id=1, source_target_pairs={{0,64},{1,65},{2,66},{3,67},{4,20},{5,21},{6,22},{7,23},{8,72},{9,... | collective-permute-start | bytes 1572872 | tf_op jit(solution)/shard_map/ppermute | solution.py:323
  153.6 6.6 %finish.1 = (bf16[128,14336]{1,0:T(8,128)(2,1)}, bf16[128,4096]{1,0:T(8,128)(2,1)}, f32[32,128]{1,0:T(8,128)S(1)}) custom-call(bf16[128,4096]{1,0:T(8,128)(2,1)S(1)} %copy-done.6, f32[128,128]{1,0:T(8,128)S(1)} %copy-done.9, f32[1,4096]{1,0:T(1,128)S(1)} %bitcast.10, bf16[2,128,18432]{2,1,0:T(8,128)(2,1)S(1)} %all_to_all.5.refs_4_.parts_ref.shared_ref, ...), custom_call_target="tpu_custom_call" | custom-call | flops 2200000000 | tf_op jit(solution)/shard_map/finish/pallas_call | solution.py:248
  160.3 1.2 collective-permute-done.21
  161.5 3.0 %collective-permute-start.24 = (f32[32,128]{1,0:T(8,128)S(1)}, f32[32,128]{1,0:T(8,128)S(1)}, u32[]{:S(2)}, u32[]{:S(2)}) collective-permute-start(f32[32,128]{1,0:T(8,128)S(1)} %add.30), channel_id=1, source_target_pairs={{0,24},{1,25},{2,26},{3,27},{4,28},{5,29},{6,30},{7,31},{8,0},{9,1... | collective-permute-start | bytes 49160 | tf_op jit(solution)/shard_map/ppermute | solution.py:323
  164.4 1.4 collective-permute-done.24
  165.9 1.7 collective-permute-start.22
  167.6 1.8 collective-permute-done.23
  169.4 1.7 collective-permute-done.22
  171.1 1.9 collective-permute-start.27
  173.3 2.0 %collective-permute-start.25 = (f32[32,128]{1,0:T(8,128)S(1)}, f32[32,128]{1,0:T(8,128)S(1)}, u32[]{:S(2)}, u32[]{:S(2)}) collective-permute-start(f32[32,128]{1,0:T(8,128)S(1)} %add_add_fusion.1), channel_id=1, source_target_pairs={{0,64},{1,65},{2,66},{3,67},{4,68},{5,69},{6,70},{7,71},{8,72},{9,... | collective-permute-start | bytes 49160 | tf_op jit(solution)/shard_map/ppermute | solution.py:323
  175.3 0.5 cut_sum.3
  175.8 0.9 collective-permute-start.15
  176.7 4.1 %collective-permute-start.16 = (bf16[4,128,128]{2,1,0:T(8,128)(2,1)S(1)}, bf16[4,128,128]{2,1,0:T(8,128)(2,1)S(1)}, u32[]{:S(2)}, u32[]{:S(2)}) collective-permute-start(bf16[4,128,128]{2,1,0:T(8,128)(2,1)S(1)} %get-tuple-element.46), channel_id=1, source_target_pairs={{0,16},{1,17},{2,18},{3,19},{4,6},{5,7},{6,4},{7,5},{8,24},{9,25},... | collective-permute-start | bytes 393224 | tf_op jit(solution)/shard_map/ppermute | solution.py:323
  180.9 3.0 %collective-permute-start.30 = (f32[32,128]{1,0:T(8,128)S(1)}, f32[32,128]{1,0:T(8,128)S(1)}, u32[]{:S(2)}, u32[]{:S(2)}) collective-permute-start(f32[32,128]{1,0:T(8,128)S(1)} %add_add_fusion), channel_id=1, source_target_pairs={{0,3},{1,0},{2,1},{3,2},{4,7},{5,4},{6,5},{7,6},{8,11},{9,8},{10,9... | collective-permute-start | bytes 49160 | tf_op jit(solution)/shard_map/ppermute | solution.py:323
  183.9 2.3 %collective-permute-start.28 = (f32[32,128]{1,0:T(8,128)S(1)}, f32[32,128]{1,0:T(8,128)S(1)}, u32[]{:S(2)}, u32[]{:S(2)}) collective-permute-start(f32[32,128]{1,0:T(8,128)S(1)} %add_add_fusion), channel_id=1, source_target_pairs={{0,2},{1,3},{2,0},{3,1},{4,6},{5,7},{6,4},{7,5},{8,10},{9,11},{10,... | collective-permute-start | bytes 49160 | tf_op jit(solution)/shard_map/ppermute | solution.py:323
  186.3 2.6 %collective-permute-start.20 = (bf16[4,128,128]{2,1,0:T(8,128)(2,1)S(1)}, bf16[4,128,128]{2,1,0:T(8,128)(2,1)S(1)}, u32[]{:S(2)}, u32[]{:S(2)}) collective-permute-start(bf16[4,128,128]{2,1,0:T(8,128)(2,1)S(1)} %join_sums.1.refs_0_), channel_id=1, source_target_pairs={{0,3},{1,0},{2,1},{3,2},{4,7},{5,4},{6,5},{7,6},{8,11},{9,8},{10,9... | collective-permute-start | bytes 393224 | tf_op jit(solution)/shard_map/ppermute | solution.py:323
  188.9 1.3 collective-permute-start.19
  190.6 0.6 add_bitcast_fusion
  191.5 4.0 %collective-permute-done.19.refs_2_ = bf16[4,128,128]{2,1,0:T(8,128)(2,1)S(1)} collective-permute-done((bf16[4,128,128]{2,1,0:T(8,128)(2,1)S(1)}, bf16[4,128,128]{2,1,0:T(8,128)(2,1)S(1)}, u32[]{:S(2)}, u32[]{:S(2)}) %collective-permute-start.19) | collective-permute-done | bytes 131104 | tf_op jit(solution)/shard_map/ppermute | solution.py:323
  195.4 1.4 collective-permute-done.18.refs_1_
  196.8 1.6 place.1
  (67 shorter events, 1.3 us)
Async XLA Ops:
  0.6 18.6 %copy-start.8 = (bf16[16,128,128]{2,1,0:T(8,128)(2,1)S(1)}, bf16[16,128,128]{2,1,0:T(8,128)(2,1)}, u32[]{:S(2)}) copy-start(bf16[16,128,128]{2,1,0:T(8,128)(2,1)} %refs_0_.3) | copy-start | bytes 1572868
  0.6 28.7 %collective-permute-start.1 = (bf16[128,14336]{1,0:T(8,128)(2,1)}, bf16[128,14336]{1,0:T(8,128)(2,1)}, u32[]{:S(2)}, u32[]{:S(2)}) collective-permute-start(bf16[128,14336]{1,0:T(8,128)(2,1)} %refs_5_.3), channel_id=1, source_target_pairs={{0,4},{4,0},{1,5},{5,1},{2,6},{6,2},{3,7},{7,3},{8,12},{12,8},{9,1... | collective-permute-start | bytes 11010056 | tf_op jit(solution)/shard_map/ppermute | solution.py:403
  0.7 7.7 %collective-permute-start = (bf16[128,4096]{1,0:T(8,128)(2,1)}, bf16[128,4096]{1,0:T(8,128)(2,1)S(1)}, u32[]{:S(2)}, u32[]{:S(2)}) collective-permute-start(bf16[128,4096]{1,0:T(8,128)(2,1)} %x_ref.3), channel_id=1, source_target_pairs={{0,4},{4,0},{1,5},{5,1},{2,6},{6,2},{3,7},{7,3},{8,12},{12,8},{9,1... | collective-permute-start | bytes 3145736 | tf_op jit(solution)/shard_map/ppermute | solution.py:402
  1.2 12.1 %collective-permute-start.3 = (bf16[16,128,128]{2,1,0:T(8,128)(2,1)}, bf16[16,128,128]{2,1,0:T(8,128)(2,1)S(1)}, u32[]{:S(2)}, u32[]{:S(2)}) collective-permute-start(bf16[16,128,128]{2,1,0:T(8,128)(2,1)} %refs_0_.3), channel_id=1, source_target_pairs={{0,16},{1,17},{2,18},{3,19},{4,68},{5,69},{6,70},{7,71},{8,24},{9,... | collective-permute-start | bytes 1572872 | tf_op jit(solution)/shard_map/ppermute | solution.py:323
  5.2 13.0 %collective-permute-start.2 = (bf16[16,128,128]{2,1,0:T(8,128)(2,1)}, bf16[16,128,128]{2,1,0:T(8,128)(2,1)S(1)}, u32[]{:S(2)}, u32[]{:S(2)}) collective-permute-start(bf16[16,128,128]{2,1,0:T(8,128)(2,1)} %refs_0_.3), channel_id=1, source_target_pairs={{0,8},{1,9},{2,10},{3,11},{4,36},{5,37},{6,38},{7,39},{8,16},{9,17... | collective-permute-start | bytes 1572872 | tf_op jit(solution)/shard_map/ppermute | solution.py:323
  6.2 13.0 %collective-permute-start.4 = (bf16[16,128,128]{2,1,0:T(8,128)(2,1)}, bf16[16,128,128]{2,1,0:T(8,128)(2,1)S(1)}, u32[]{:S(2)}, u32[]{:S(2)}) collective-permute-start(bf16[16,128,128]{2,1,0:T(8,128)(2,1)} %refs_0_.3), channel_id=1, source_target_pairs={{0,24},{1,25},{2,26},{3,27},{4,100},{5,101},{6,102},{7,103},{8,0},... | collective-permute-start | bytes 1572872 | tf_op jit(solution)/shard_map/ppermute | solution.py:323
  19.2 1.2 copy-start.2
  20.5 8.9 %copy-start.3 = (bf16[32,128,128]{2,1,0:T(8,128)(2,1)S(1)}, bf16[32,128,128]{2,1,0:T(8,128)(2,1)}, u32[]{:S(2)}) copy-start(bf16[32,128,128]{2,1,0:T(8,128)(2,1)} %get-tuple-element.29.refs_4_) | copy-start | bytes 3145732
  22.3 7.0 %copy-start.11 = (s32[512]{0:T(512)S(1)}, s32[512]{0:T(512)}, u32[]{:S(2)}) copy-start(s32[512]{0:T(512)} %refs_0_.5) | copy-start | bytes 6148
  22.3 7.0 %copy-start.12 = (s32[512]{0:T(512)S(1)}, s32[512]{0:T(512)}, u32[]{:S(2)}) copy-start(s32[512]{0:T(512)} %refs_1_.3) | copy-start | bytes 6148
  22.3 31.9 %collective-permute-start.6 = (bf16[64,128,128]{2,1,0:T(8,128)(2,1)}, bf16[64,128,128]{2,1,0:T(8,128)(2,1)S(1)}, u32[]{:S(2)}, u32[]{:S(2)}) collective-permute-start(bf16[64,128,128]{2,1,0:T(8,128)(2,1)} %bitcast.5.refs_7_), channel_id=1, source_target_pairs={{0,96},{1,97},{2,98},{3,99},{4,28},{5,29},{6,30},{7,31},{8,104},{9... | collective-permute-start | bytes 6291464 | tf_op jit(solution)/shard_map/ppermute | solution.py:323
  25.3 28.9 %collective-permute-start.5 = (bf16[64,128,128]{2,1,0:T(8,128)(2,1)}, bf16[64,128,128]{2,1,0:T(8,128)(2,1)}, u32[]{:S(2)}, u32[]{:S(2)}) collective-permute-start(bf16[64,128,128]{2,1,0:T(8,128)(2,1)} %bitcast.5.refs_7_), channel_id=1, source_target_pairs={{0,32},{1,33},{2,34},{3,35},{4,12},{5,13},{6,14},{7,15},{8,40},{9,... | collective-permute-start | bytes 6291464 | tf_op jit(solution)/shard_map/ppermute | solution.py:323
  25.3 4.0 %copy-start = (bf16[128,14336]{1,0:T(8,128)(2,1)S(1)}, bf16[128,14336]{1,0:T(8,128)(2,1)}, u32[]{:S(2)}) copy-start(bf16[128,14336]{1,0:T(8,128)(2,1)} %refs_5_.3) | copy-start | bytes 11010052
  29.3 19.2 %copy-start.13 = (s32[4]{0:T(128)}, s32[4]{0:T(128)S(1)}, u32[]{:S(2)}) copy-start(s32[4]{0:T(128)S(1)} %pad_add_fusion.refs_2_.pos_ref) | copy-start | bytes 52
  29.4 1.2 copy-start.7
  48.5 7.7 %copy-start.4 = (bf16[64,128,128]{2,1,0:T(8,128)(2,1)}, bf16[64,128,128]{2,1,0:T(8,128)(2,1)S(1)}, u32[]{:S(2)}) copy-start(bf16[64,128,128]{2,1,0:T(8,128)(2,1)S(1)} %get-tuple-element.34.refs_0_) | copy-start | bytes 6291460
  48.5 95.1 %collective-permute-start.9 = (bf16[64,128,128]{2,1,0:T(8,128)(2,1)}, bf16[64,128,128]{2,1,0:T(8,128)(2,1)}, u32[]{:S(2)}, u32[]{:S(2)}) collective-permute-start(bf16[64,128,128]{2,1,0:T(8,128)(2,1)} %get-tuple-element.35), channel_id=1, source_target_pairs={{0,1},{1,2},{2,3},{3,0},{4,36},{5,37},{6,38},{7,39},{8,9},{9,10},{... | collective-permute-start | bytes 6291464 | tf_op jit(solution)/shard_map/ppermute | solution.py:323
  50.0 93.6 %collective-permute-start.10 = (bf16[64,128,128]{2,1,0:T(8,128)(2,1)}, bf16[64,128,128]{2,1,0:T(8,128)(2,1)}, u32[]{:S(2)}, u32[]{:S(2)}) collective-permute-start(bf16[64,128,128]{2,1,0:T(8,128)(2,1)} %get-tuple-element.36), channel_id=1, source_target_pairs={{0,2},{1,3},{2,0},{3,1},{4,68},{5,69},{6,70},{7,71},{8,10},{9,11},... | collective-permute-start | bytes 6291464 | tf_op jit(solution)/shard_map/ppermute | solution.py:323
  52.8 90.9 %collective-permute-start.11 = (bf16[64,128,128]{2,1,0:T(8,128)(2,1)}, bf16[64,128,128]{2,1,0:T(8,128)(2,1)}, u32[]{:S(2)}, u32[]{:S(2)}) collective-permute-start(bf16[64,128,128]{2,1,0:T(8,128)(2,1)} %get-tuple-element.31.tie_ref), channel_id=1, source_target_pairs={{0,3},{1,0},{2,1},{3,2},{4,100},{5,101},{6,102},{7,103},{8,11},{9,... | collective-permute-start | bytes 6291464 | tf_op jit(solution)/shard_map/ppermute | solution.py:323
  54.2 2.1 %copy-start.1 = (bf16[64,128,128]{2,1,0:T(8,128)(2,1)}, bf16[64,128,128]{2,1,0:T(8,128)(2,1)S(1)}, u32[]{:S(2)}) copy-start(bf16[64,128,128]{2,1,0:T(8,128)(2,1)S(1)} %collective-permute-done.6.right_ref.refs_9_) | copy-start | bytes 6291460
  56.3 27.4 %collective-permute-start.7 = (bf16[32,128,128]{2,1,0:T(8,128)(2,1)S(1)}, bf16[32,128,128]{2,1,0:T(8,128)(2,1)S(1)}, u32[]{:S(2)}, u32[]{:S(2)}) collective-permute-start(bf16[32,128,128]{2,1,0:T(8,128)(2,1)S(1)} %get-tuple-element.32), channel_id=1, source_target_pairs={{0,32},{1,33},{2,34},{3,35},{4,12},{5,13},{6,14},{7,15},{8,40},{9,... | collective-permute-start | bytes 3145736 | tf_op jit(solution)/shard_map/ppermute | solution.py:323
  56.9 39.8 %collective-permute-start.8 = (bf16[32,128,128]{2,1,0:T(8,128)(2,1)S(1)}, bf16[32,128,128]{2,1,0:T(8,128)(2,1)S(1)}, u32[]{:S(2)}, u32[]{:S(2)}) collective-permute-start(bf16[32,128,128]{2,1,0:T(8,128)(2,1)S(1)} %get-tuple-element.33), channel_id=1, source_target_pairs={{0,96},{1,97},{2,98},{3,99},{4,28},{5,29},{6,30},{7,31},{8,104},{9... | collective-permute-start | bytes 3145736 | tf_op jit(solution)/shard_map/ppermute | solution.py:323
  83.7 13.1 %copy-start.15 = (bf16[32,128,128]{2,1,0:T(8,128)(2,1)}, bf16[32,128,128]{2,1,0:T(8,128)(2,1)S(1)}, u32[]{:S(2)}) copy-start(bf16[32,128,128]{2,1,0:T(8,128)(2,1)S(1)} %collective-permute-done.7.refs_10_) | copy-start | bytes 3145732
  96.7 1.0 copy-start.16
  130.3 13.3 %copy-start.5 = (bf16[64,128,128]{2,1,0:T(8,128)(2,1)S(1)}, bf16[64,128,128]{2,1,0:T(8,128)(2,1)}, u32[]{:S(2)}) copy-start(bf16[64,128,128]{2,1,0:T(8,128)(2,1)} %copy-done.4) | copy-start | bytes 6291460
  143.6 10.0 %copy-start.6 = (bf16[128,4096]{1,0:T(8,128)(2,1)S(1)}, bf16[128,4096]{1,0:T(8,128)(2,1)}, u32[]{:S(2)}) copy-start(bf16[128,4096]{1,0:T(8,128)(2,1)} %x_ref.3) | copy-start | bytes 3145732
  143.6 10.0 %copy-start.9 = (f32[128,128]{1,0:T(8,128)S(1)}, f32[128,128]{1,0:T(8,128)}, u32[]{:S(2)}) copy-start(f32[128,128]{1,0:T(8,128)} %get-tuple-element.26.scale_ref) | copy-start | bytes 196612
  143.6 10.0 %copy-start.10 = (f32[4096]{0:T(1024)S(1)}, f32[4096]{0:T(1024)}, u32[]{:S(2)}) copy-start(f32[4096]{0:T(1024)} %param.7) | copy-start | bytes 49156
  148.4 24.9 %collective-permute-start.12 = (bf16[16,128,128]{2,1,0:T(8,128)(2,1)S(1)}, bf16[16,128,128]{2,1,0:T(8,128)(2,1)S(1)}, u32[]{:S(2)}, u32[]{:S(2)}) collective-permute-start(bf16[16,128,128]{2,1,0:T(8,128)(2,1)S(1)} %get-tuple-element.40), channel_id=1, source_target_pairs={{0,32},{1,33},{2,34},{3,35},{4,12},{5,13},{6,14},{7,15},{8,40},{9,... | collective-permute-start | bytes 1572872 | tf_op jit(solution)/shard_map/ppermute | solution.py:323
  150.3 24.9 %collective-permute-start.13 = (bf16[16,128,128]{2,1,0:T(8,128)(2,1)S(1)}, bf16[16,128,128]{2,1,0:T(8,128)(2,1)S(1)}, u32[]{:S(2)}, u32[]{:S(2)}) collective-permute-start(bf16[16,128,128]{2,1,0:T(8,128)(2,1)S(1)} %get-tuple-element.41), channel_id=1, source_target_pairs={{0,64},{1,65},{2,66},{3,67},{4,20},{5,21},{6,22},{7,23},{8,72},{9,... | collective-permute-start | bytes 1572872 | tf_op jit(solution)/shard_map/ppermute | solution.py:323
  153.6 21.6 %collective-permute-start.14 = (bf16[16,128,128]{2,1,0:T(8,128)(2,1)S(1)}, bf16[16,128,128]{2,1,0:T(8,128)(2,1)S(1)}, u32[]{:S(2)}, u32[]{:S(2)}) collective-permute-start(bf16[16,128,128]{2,1,0:T(8,128)(2,1)S(1)} %get-tuple-element.42), channel_id=1, source_target_pairs={{0,96},{1,97},{2,98},{3,99},{4,28},{5,29},{6,30},{7,31},{8,104},{9... | collective-permute-start | bytes 1572872 | tf_op jit(solution)/shard_map/ppermute | solution.py:323
  160.3 1.2 collective-permute-start.21
  161.5 4.4 %collective-permute-start.24 = (f32[32,128]{1,0:T(8,128)S(1)}, f32[32,128]{1,0:T(8,128)S(1)}, u32[]{:S(2)}, u32[]{:S(2)}) collective-permute-start(f32[32,128]{1,0:T(8,128)S(1)} %add.30), channel_id=1, source_target_pairs={{0,24},{1,25},{2,26},{3,27},{4,28},{5,29},{6,30},{7,31},{8,0},{9,1... | collective-permute-start | bytes 49160 | tf_op jit(solution)/shard_map/ppermute | solution.py:323
  164.4 5.0 %collective-permute-start.23 = (f32[32,128]{1,0:T(8,128)S(1)}, f32[32,128]{1,0:T(8,128)S(1)}, u32[]{:S(2)}, u32[]{:S(2)}) collective-permute-start(f32[32,128]{1,0:T(8,128)S(1)} %add.30), channel_id=1, source_target_pairs={{0,8},{1,9},{2,10},{3,11},{4,12},{5,13},{6,14},{7,15},{8,16},{9,17... | collective-permute-start | bytes 49160 | tf_op jit(solution)/shard_map/ppermute | solution.py:323
  165.9 5.2 %collective-permute-start.22 = (f32[32,128]{1,0:T(8,128)S(1)}, f32[32,128]{1,0:T(8,128)S(1)}, u32[]{:S(2)}, u32[]{:S(2)}) collective-permute-start(f32[32,128]{1,0:T(8,128)S(1)} %add.30), channel_id=1, source_target_pairs={{0,16},{1,17},{2,18},{3,19},{4,20},{5,21},{6,22},{7,23},{8,24},{9,... | collective-permute-start | bytes 49160 | tf_op jit(solution)/shard_map/ppermute | solution.py:323
  171.1 9.7 %collective-permute-start.27 = (f32[32,128]{1,0:T(8,128)S(1)}, f32[32,128]{1,0:T(8,128)S(1)}, u32[]{:S(2)}, u32[]{:S(2)}) collective-permute-start(f32[32,128]{1,0:T(8,128)S(1)} %add_add_fusion.1), channel_id=1, source_target_pairs={{0,96},{1,97},{2,98},{3,99},{4,100},{5,101},{6,102},{7,103},{8,104... | collective-permute-start | bytes 49160 | tf_op jit(solution)/shard_map/ppermute | solution.py:323
  173.0 7.8 %collective-permute-start.26 = (f32[32,128]{1,0:T(8,128)S(1)}, f32[32,128]{1,0:T(8,128)S(1)}, u32[]{:S(2)}, u32[]{:S(2)}) collective-permute-start(f32[32,128]{1,0:T(8,128)S(1)} %add_add_fusion.1), channel_id=1, source_target_pairs={{0,32},{1,33},{2,34},{3,35},{4,36},{5,37},{6,38},{7,39},{8,40},{9,... | collective-permute-start | bytes 49160 | tf_op jit(solution)/shard_map/ppermute | solution.py:323
  173.3 7.6 %collective-permute-start.25 = (f32[32,128]{1,0:T(8,128)S(1)}, f32[32,128]{1,0:T(8,128)S(1)}, u32[]{:S(2)}, u32[]{:S(2)}) collective-permute-start(f32[32,128]{1,0:T(8,128)S(1)} %add_add_fusion.1), channel_id=1, source_target_pairs={{0,64},{1,65},{2,66},{3,67},{4,68},{5,69},{6,70},{7,71},{8,72},{9,... | collective-permute-start | bytes 49160 | tf_op jit(solution)/shard_map/ppermute | solution.py:323
  175.8 8.1 %collective-permute-start.15 = (bf16[4,128,128]{2,1,0:T(8,128)(2,1)S(1)}, bf16[4,128,128]{2,1,0:T(8,128)(2,1)S(1)}, u32[]{:S(2)}, u32[]{:S(2)}) collective-permute-start(bf16[4,128,128]{2,1,0:T(8,128)(2,1)S(1)} %get-tuple-element.45), channel_id=1, source_target_pairs={{0,8},{1,9},{2,10},{3,11},{4,5},{5,6},{6,7},{7,4},{8,16},{9,17},{1... | collective-permute-start | bytes 393224 | tf_op jit(solution)/shard_map/ppermute | solution.py:323
  176.7 9.5 %collective-permute-start.16 = (bf16[4,128,128]{2,1,0:T(8,128)(2,1)S(1)}, bf16[4,128,128]{2,1,0:T(8,128)(2,1)S(1)}, u32[]{:S(2)}, u32[]{:S(2)}) collective-permute-start(bf16[4,128,128]{2,1,0:T(8,128)(2,1)S(1)} %get-tuple-element.46), channel_id=1, source_target_pairs={{0,16},{1,17},{2,18},{3,19},{4,6},{5,7},{6,4},{7,5},{8,24},{9,25},... | collective-permute-start | bytes 393224 | tf_op jit(solution)/shard_map/ppermute | solution.py:323
  180.9 5.4 %collective-permute-start.17 = (bf16[4,128,128]{2,1,0:T(8,128)(2,1)S(1)}, bf16[4,128,128]{2,1,0:T(8,128)(2,1)S(1)}, u32[]{:S(2)}, u32[]{:S(2)}) collective-permute-start(bf16[4,128,128]{2,1,0:T(8,128)(2,1)S(1)} %get-tuple-element.47), channel_id=1, source_target_pairs={{0,24},{1,25},{2,26},{3,27},{4,7},{5,4},{6,5},{7,6},{8,0},{9,1},{1... | collective-permute-start | bytes 393224 | tf_op jit(solution)/shard_map/ppermute | solution.py:323
  180.9 15.9 %copy-start.14 = (s32[4]{0:T(128)S(1)}, s32[4]{0:T(128)}, u32[]{:S(2)}) copy-start(s32[4]{0:T(128)} %copy-done.13) | copy-start | bytes 52
  180.9 9.4 %collective-permute-start.30 = (f32[32,128]{1,0:T(8,128)S(1)}, f32[32,128]{1,0:T(8,128)S(1)}, u32[]{:S(2)}, u32[]{:S(2)}) collective-permute-start(f32[32,128]{1,0:T(8,128)S(1)} %add_add_fusion), channel_id=1, source_target_pairs={{0,3},{1,0},{2,1},{3,2},{4,7},{5,4},{6,5},{7,6},{8,11},{9,8},{10,9... | collective-permute-start | bytes 49160 | tf_op jit(solution)/shard_map/ppermute | solution.py:323
  183.9 6.7 %collective-permute-start.29 = (f32[32,128]{1,0:T(8,128)S(1)}, f32[32,128]{1,0:T(8,128)S(1)}, u32[]{:S(2)}, u32[]{:S(2)}) collective-permute-start(f32[32,128]{1,0:T(8,128)S(1)} %add_add_fusion), channel_id=1, source_target_pairs={{0,1},{1,2},{2,3},{3,0},{4,5},{5,6},{6,7},{7,4},{8,9},{9,10},{10,1... | collective-permute-start | bytes 49160 | tf_op jit(solution)/shard_map/ppermute | solution.py:323
  183.9 6.7 %collective-permute-start.28 = (f32[32,128]{1,0:T(8,128)S(1)}, f32[32,128]{1,0:T(8,128)S(1)}, u32[]{:S(2)}, u32[]{:S(2)}) collective-permute-start(f32[32,128]{1,0:T(8,128)S(1)} %add_add_fusion), channel_id=1, source_target_pairs={{0,2},{1,3},{2,0},{3,1},{4,6},{5,7},{6,4},{7,5},{8,10},{9,11},{10,... | collective-permute-start | bytes 49160 | tf_op jit(solution)/shard_map/ppermute | solution.py:323
  186.3 5.1 %collective-permute-start.20 = (bf16[4,128,128]{2,1,0:T(8,128)(2,1)S(1)}, bf16[4,128,128]{2,1,0:T(8,128)(2,1)S(1)}, u32[]{:S(2)}, u32[]{:S(2)}) collective-permute-start(bf16[4,128,128]{2,1,0:T(8,128)(2,1)S(1)} %join_sums.1.refs_0_), channel_id=1, source_target_pairs={{0,3},{1,0},{2,1},{3,2},{4,7},{5,4},{6,5},{7,6},{8,11},{9,8},{10,9... | collective-permute-start | bytes 393224 | tf_op jit(solution)/shard_map/ppermute | solution.py:323
  188.9 6.5 %collective-permute-start.19 = (bf16[4,128,128]{2,1,0:T(8,128)(2,1)S(1)}, bf16[4,128,128]{2,1,0:T(8,128)(2,1)S(1)}, u32[]{:S(2)}, u32[]{:S(2)}) collective-permute-start(bf16[4,128,128]{2,1,0:T(8,128)(2,1)S(1)} %join_sums.1.refs_0_), channel_id=1, source_target_pairs={{0,2},{1,3},{2,0},{3,1},{4,6},{5,7},{6,4},{7,5},{8,10},{9,11},{10,... | collective-permute-start | bytes 393224 | tf_op jit(solution)/shard_map/ppermute | solution.py:323
  190.3 6.6 %collective-permute-start.18 = (bf16[4,128,128]{2,1,0:T(8,128)(2,1)S(1)}, bf16[4,128,128]{2,1,0:T(8,128)(2,1)S(1)}, u32[]{:S(2)}, u32[]{:S(2)}) collective-permute-start(bf16[4,128,128]{2,1,0:T(8,128)(2,1)S(1)} %join_sums.1.refs_0_), channel_id=1, source_target_pairs={{0,1},{1,2},{2,3},{3,0},{4,5},{5,6},{6,7},{7,4},{8,9},{9,10},{10,1... | collective-permute-start | bytes 393224 | tf_op jit(solution)/shard_map/ppermute | solution.py:323
  (1 other events, 1.0 us)

commit v7 on v5

v7 whole, which is shorter than its diff:
```python
import jax
import jax.numpy as jnp
from jax import lax
from jax.experimental import pallas as pl
from jax.experimental.pallas import tpu as pltpu
from jax.sharding import Mesh, PartitionSpec as P

BF = jnp.bfloat16
F4 = jnp.float32
T = 128
ALL = ("y", "z", "c", "x")


def params(limit):
    return pltpu.CompilerParams(vmem_limit_bytes=limit * 1024 * 1024)


def cost(micros, nbytes):
    return pl.CostEstimate(flops=int(micros * 1.1e9), bytes_accessed=nbytes, transcendentals=0)


def whole(shape):
    zeros = (0,) * len(shape)
    return pl.BlockSpec(shape, lambda *_: zeros, pipeline_mode=pl.Buffered(1))


def dot(a, b):
    return jnp.dot(a, b, preferred_element_type=F4)


def dot_t(a, b):
    return lax.dot_general(a, b, (((1,), (1,)), ((), ())), preferred_element_type=F4)


ANY = pl.BlockSpec(memory_space=pl.ANY)


def cols_at(index):
    return pl.ds(pl.multiple_of(index * T, T), T)


def norm_kernel(x_ref, gain_ref, normed_ref, turned_ref, scale_ref):
    count, width = x_ref.shape
    blocks = width // T

    def squares(b, total):
        x = x_ref[:, cols_at(b)].astype(F4)
        return total + x * x

    total = lax.fori_loop(0, blocks, squares, jnp.zeros((count, T), F4), unroll=4)
    scale = lax.rsqrt(jnp.sum(total, axis=1, keepdims=True) / width + 1e-05)
    scale_ref[...] = jnp.broadcast_to(scale, (count, T))

    def fill(b, carry):
        x = x_ref[:, cols_at(b)].astype(F4)
        normed = (x * scale * gain_ref[:, cols_at(b)]).astype(BF)
        normed_ref[:, cols_at(b)] = normed
        turned_ref[b] = normed.T
        return carry

    lax.fori_loop(0, blocks, fill, 0, unroll=4)


def norm(x, gain):
    count, width = x.shape
    return pl.pallas_call(
        norm_kernel,
        out_shape=(
            jax.ShapeDtypeStruct((count, width), BF),
            jax.ShapeDtypeStruct((width // T, T, count), BF),
            jax.ShapeDtypeStruct((count, T), F4),
        ),
        compiler_params=params(56),
        cost_estimate=cost(1, 0),
        name="norm",
    )(x, gain)


def owned_at(pos, core, to_first, to_second):
    to_z = jnp.where(core == 0, to_first, to_second)
    to_y = jnp.where(core == 0, to_second, to_first)
    return (lax.rem(pos[0] + to_y, 4) * 4 + lax.rem(pos[1] + to_z, 4)) * 32 + core * 16


ORDER = (("x", "y", "z"), ("y", "z", "x"))


def listed(ahead, i, pos):
    y, z, c, x = pos[0], pos[1], pos[2], pos[3]
    one, two, three = ahead, i // 16, i // 4 % 4
    to_x = x + jnp.where(c == 0, one, three)
    to_y = y + jnp.where(c == 0, two, one)
    to_z = z + jnp.where(c == 0, three, two)
    return (lax.rem(to_y, 4) * 4 + lax.rem(to_z, 4)) * 32 + c * 16 + 4 * lax.rem(to_x, 4) + i % 4


STEP = 16


def grad_kernel(aheads, each, rows, cols, pos, turned_ref, turned_other_ref, own_ref, other_ref, *refs):
    at = pl.program_id(0)

    for k, (ahead, out_ref) in enumerate(zip(aheads, refs[-len(aheads) :])):

        @pl.when(at // each == k)
        def _(k=k, ahead=ahead, out_ref=out_ref):
            def one(t, carry):
                index = listed(ahead, (at - k * each) * STEP + t, pos)
                r, q = rows[index], cols[index]
                left = jnp.concatenate([turned_ref[r], turned_other_ref[r]], axis=1)
                right = jnp.concatenate([own_ref[:, cols_at(q)], other_ref[:, cols_at(q)]], axis=0)
                out_ref[t] = dot(left, right).astype(BF)
                return carry

            lax.fori_loop(0, STEP, one, 0, unroll=8)


def grads(aheads, rows, cols, pos, turned, turned_other, own, other, carried=(), ties=()):
    piece = 64
    each = piece // STEP

    def out_spec(k):
        return pl.BlockSpec((STEP, T, T), lambda i, *_: (jnp.clip(i - k * each, 0, each - 1), 0, 0))

    resident = (turned, turned_other, own, other)
    return pl.pallas_call(
        lambda *refs: grad_kernel(aheads, each, *refs),
        out_shape=[jax.ShapeDtypeStruct(a.shape, a.dtype) for a in carried]
        + [jax.ShapeDtypeStruct((piece, T, T), BF)] * len(aheads),
        grid_spec=pltpu.PrefetchScalarGridSpec(
            num_scalar_prefetch=3,
            grid=(len(aheads) * each,),
            in_specs=[whole(a.shape) for a in resident] + [ANY] * (len(carried) + len(ties)),
            out_specs=[ANY] * len(carried) + [out_spec(k) for k in range(len(aheads))],
        ),
        input_output_aliases={7 + k: k for k in range(len(carried))},
        compiler_params=params(40),
        cost_estimate=cost(2, 0),
        name="grads",
    )(rows, cols, pos, *resident, *carried, *ties)


def project_kernel(plan, rows, cols, pos, x_ref, normed_ref, scale_ref, gain_ref, g_ref, *refs):
    projected_ref, token_grad_ref, sums_ref, out_acc, back_acc = refs[-5:]
    s = pl.program_id(0)
    count, width = x_ref.shape
    blocks = width // T

    @pl.when(s == 0)
    def _():
        out_acc[...] = jnp.zeros_like(out_acc)
        back_acc[...] = jnp.zeros_like(back_acc)

    for (other, behind, offset, start, each), tiles_ref in zip(plan, refs):

        @pl.when((s >= start) & (s < start + each))
        def _(other=other, behind=behind, offset=offset, start=start, tiles_ref=tiles_ref):
            core = 1 - pos[2] if other else pos[2]

            def one(k, carry):
                i = offset + (s - start) * 32 + k
                index = owned_at(pos, core, 4 - i // 16, 4 - behind) + i % 16
                r, q = cols_at(rows[index]), cols_at(cols[index])
                weight = tiles_ref[k]
                out_acc[:, q] += dot(normed_ref[:, r], weight)
                back_acc[:, r] += dot_t(g_ref[:, q], weight)
                return carry

            lax.fori_loop(0, 32, one, 0, unroll=8)

    @pl.when(s == pl.num_programs(0) - 1)
    def _():
        scale = scale_ref[...]

        def products(b, total):
            at = cols_at(b)
            x = x_ref[:, at].astype(F4)
            back = back_acc[:, at]
            sums_ref[pl.ds(b, 1), :] = jnp.sum(back * x * scale, axis=0, keepdims=True)
            return total + x * gain_ref[:, at] * back

        total = lax.fori_loop(0, blocks, products, jnp.zeros((count, T), F4), unroll=2)
        inner = jnp.sum(total, axis=1, keepdims=True) / width
        cubed = scale * scale * scale * inner

        def finish(b, carry):
            at = cols_at(b)
            x = x_ref[:, at].astype(F4)
            token_grad_ref[:, at] = (scale * gain_ref[:, at] * back_acc[:, at] - x * cubed).astype(BF)
            return carry

        lax.fori_loop(0, blocks, finish, 0, unroll=2)

        def write(b, carry):
            projected_ref[:, cols_at(b)] = out_acc[:, cols_at(b)].astype(BF)
            return carry

        lax.fori_loop(0, g_ref.shape[1] // T, write, 0, unroll=4)


def project(rows, cols, pos, arrays, x, normed, scale, gain, g):
    plan, steps = [], 0
    for tiles, other, behind, offset in arrays:
        each = tiles.shape[0] // 32
        plan.append((other, behind, offset, steps, each))
        steps += each

    def tile_spec(start, each):
        return pl.BlockSpec((32, T, T), lambda i, *_: (jnp.clip(i - start, 0, each - 1), 0, 0))

    resident = (x, normed, scale, gain, g)
    sums = (x.shape[1] // T, T)
    return pl.pallas_call(
        lambda *refs: project_kernel(plan, *refs),
        out_shape=(
            jax.ShapeDtypeStruct(g.shape, BF),
            jax.ShapeDtypeStruct(x.shape, BF),
            jax.ShapeDtypeStruct(sums, F4),
        ),
        grid_spec=pltpu.PrefetchScalarGridSpec(
            num_scalar_prefetch=3,
            grid=(steps,),
            in_specs=[whole(a.shape) for a in resident] + [tile_spec(p[3], p[4]) for p in plan],
            out_specs=[whole(g.shape), whole(x.shape), whole(sums)],
            scratch_shapes=[pltpu.VMEM(g.shape, F4), pltpu.VMEM(x.shape, F4)],
        ),
        compiler_params=params(54),
        cost_estimate=cost(2, 0),
        name="project",
    )(rows, cols, pos, *resident, *(a[0] for a in arrays))


def joined(pieces, tie):
    each = pieces[0].shape[0]

    def kernel(*refs):
        for j in range(4):
            refs[-1][j] = refs[j][...]

    return pl.pallas_call(
        kernel,
        out_shape=jax.ShapeDtypeStruct((4, each, T, T), BF),
        grid=(4,),
        in_specs=[pl.BlockSpec((each // 4, T, T), lambda i: (i, 0, 0))] * 4 + [ANY],
        out_specs=pl.BlockSpec((4, each // 4, T, T), lambda i: (0, i, 0, 0)),
        compiler_params=params(32),
        cost_estimate=cost(1, 0),
        name="joined",
    )(*pieces, tie).reshape(4 * each, T, T)


def held(values, tie):
    return pl.pallas_call(
        lambda *refs: None,
        out_shape=[jax.ShapeDtypeStruct(a.shape, a.dtype) for a in values],
        in_specs=[ANY] * (len(values) + 1),
        out_specs=[ANY] * len(values),
        input_output_aliases={k: k for k in range(len(values))},
        cost_estimate=cost(1, 0),
        name="held",
    )(*values, tie)


def relayed(left, right, tie):
    half = left.shape[0] // 2

    def kernel(left_ref, right_ref, tie_ref, left_out, right_out):
        left_out[...] = left_ref[...]
        right_out[...] = right_ref[...]

    return pl.pallas_call(
        kernel,
        out_shape=[jax.ShapeDtypeStruct((half, T, T), BF)] * 2,
        grid=(2,),
        in_specs=[
            pl.BlockSpec((half // 2, T, T), lambda i: (i, 0, 0)),
            pl.BlockSpec((half // 2, T, T), lambda i: (2 + i, 0, 0)),
            ANY,
        ],
        out_specs=[pl.BlockSpec((half // 2, T, T), lambda i: (i, 0, 0))] * 2,
        compiler_params=params(32),
        cost_estimate=cost(1, 0),
        name="relayed",
    )(left, right, tie)


def ring(piece, axes, shift):
    if isinstance(axes, str):
        axes = (axes, axes)
    pairs = []
    for source in range(128):
        at = dict(y=source // 32, z=source // 8 % 4, c=source // 4 % 2, x=source % 4)
        axis = axes[at["c"]]
        to = dict(at, **{axis: (at[axis] + shift) % 4})
        pairs.append((source, to["y"] * 32 + to["z"] * 8 + to["c"] * 4 + to["x"]))
    return lax.ppermute(piece, ALL, pairs)


def exchange(pieces, axis):
    return [pieces[0]] + [ring(pieces[j], axis, j) for j in (1, 2, 3)]


def add_four(refs, i):
    a, b, c, d = (r[i].astype(F4) for r in refs)
    return (a + c) + (b + d)


def put_sums(ref, i, value):
    rows = value.shape[0]
    for part in range(3):
        rounded = value.astype(BF)
        ref[i, part * rows : (part + 1) * rows] = rounded
        value = value - rounded.astype(F4)
    ref[i, 3 * rows :] = jnp.zeros((T - 3 * rows, T), BF)


def get_sums(ref, i, rows):
    low, mid, high = (ref[i, part * rows : (part + 1) * rows].astype(F4) for part in (2, 1, 0))
    return (low + mid) + high


def add_sums(refs, i, rows):
    a, b, c, d = (get_sums(r, i, rows) for r in refs)
    return (a + c) + (b + d)


def cut_sum(pieces, sums):
    each = pieces[0].shape[0] // 4

    def kernel(*refs):
        total = add_four(refs[:4], ...).astype(BF)
        for ahead, out in enumerate(refs[-4:]):

            @pl.when(pl.program_id(0) == ahead)
            def _(out=out):
                out[:each] = total
                put_sums(out, each, refs[4][...] + refs[5][...])

    return pl.pallas_call(
        kernel,
        out_shape=[jax.ShapeDtypeStruct((each + 1, T, T), BF)] * 4,
        grid=(4,),
        in_specs=[pl.BlockSpec((each, T, T), lambda i: (i, 0, 0))] * 4 + [whole(a.shape) for a in sums],
        out_specs=[whole((each + 1, T, T))] * 4,
        compiler_params=params(32),
        cost_estimate=cost(1, 0),
        name="cut_sum",
    )(*pieces, *sums)


def next_sum(pieces, rows, cuts):
    each = (pieces[0].shape[0] - 1) // cuts

    def kernel(*refs):
        sums = add_sums(refs[:4], cuts * each, rows)
        for ahead, out in enumerate(refs[4:]):
            for i in range(each):
                out[i] = add_four(refs[:4], ahead * each + i).astype(BF)
            put_sums(out, each, sums)

    return pl.pallas_call(
        kernel,
        out_shape=[jax.ShapeDtypeStruct((each + 1, T, T), BF)] * cuts,
        in_specs=[pl.BlockSpec(memory_space=pltpu.VMEM)] * 4,
        compiler_params=params(32),
        cost_estimate=cost(1, 0),
        name="next_sum",
    )(*pieces)


def place(pieces, pos, rows):
    def kernel(pos_ref, *refs):
        out_ref, sums_ref = refs[4:]
        for back in range(4):
            source = lax.rem(pos_ref[3] + 4 - back, 4)
            for u in range(4):
                out_ref[4 * source + u] = refs[back][u].astype(F4)
        sums_ref[...] = add_sums(refs[:4], 4, rows)

    return pl.pallas_call(
        kernel,
        out_shape=(jax.ShapeDtypeStruct((16, T, T), F4), jax.ShapeDtypeStruct((rows, T), F4)),
        in_specs=[pl.BlockSpec(memory_space=pltpu.SMEM)] + [pl.BlockSpec(memory_space=pltpu.VMEM)] * 4,
        compiler_params=params(32),
        cost_estimate=cost(1, 0),
        name="place",
    )(pos, *pieces)


def shards(tokens, gain, tiles, rows, cols, cotangent):
    gain2 = gain.reshape(1, -1)
    pos = jnp.stack([lax.axis_index(a).astype(jnp.int32) for a in ("y", "z", "c", "x")])
    first, second = ("z", "y"), ("y", "z")
    one, two, three = (tuple(order[k] for order in ORDER) for k in range(3))

    def other_core(value):
        return lax.ppermute(value, "c", [(0, 1), (1, 0)])

    tokens_other, g_other = other_core(tokens), other_core(cotangent)
    normed, turned, scale = norm(tokens, gain2)
    _, turned_other, _ = norm(tokens_other, gain2)
    line = joined(exchange([tiles] * 4, first), turned_other)
    left, right = ring(line, second, 1), ring(line, second, 3)
    operands = (rows, cols, pos, turned, turned_other, cotangent, g_other)
    part0, part2 = grads((0, 2), *operands)
    left_half, right_half = relayed(left, right, part0)
    left, right = held((left, right), left_half)
    part0, part2, part1, part3 = grads((1, 3), *operands, (part0, part2), (left_half,))
    far0, far1 = held((ring(left_half, second, 1), ring(right_half, second, 3)), part3)
    blocks = [(line, 0, 0), (left, 1, 0), (right, 3, 0), (far0, 2, 0), (far1, 2, 32)]
    arrays = [(block, False, *where) for block, *where in blocks]
    arrays += [(other_core(block), True, *where) for block, *where in blocks]
    projected, token_grad, sums = project(rows, cols, pos, arrays, tokens, normed, scale, gain2, cotangent)
    count = sums.shape[0]
    mid = cut_sum(exchange([part0, part1, part2, part3], one), (sums, other_core(sums)))
    ends = next_sum(exchange(mid, two), count, 4)
    (sent,) = next_sum(exchange(ends, three), count, 1)
    tile_grad, sums = place(exchange([sent] * 4, "x"), pos, count)
    sums = jnp.where(pos[2] == 0, sums, other_core(sums))
    return (projected, token_grad, tile_grad, sums.reshape(-1))


def solution(mesh):
    grid = Mesh(mesh.devices.reshape(4, 4, 2, 4), ALL)
    owners = ("y", "z", "c")
    placed = (P(ALL, None), P(), P(owners, None, None), P(), P(), P(ALL, None))
    return jax.shard_map(
        shards,
        mesh=grid,
        in_specs=placed,
        out_specs=(P(ALL, None), P(ALL, None), P(owners, None, None), P()),
        check_vma=False,
    )
```

time: 195 us -> 178 us (0.913)
  waiting for transfers between devices: 71.7 us -> 50.8 us
  between operations: 14.2 us -> 0.83 us
  local copies, waits for them, and re-layouts: 6.09 us -> 12.3 us
  starting transfers between devices: 27.5 us -> 32.9 us
  Pallas kernels: 73.8 us -> 79 us
    ppermute x21 -> x28, waiting for transfers between devices: 71 us -> 50.8 us  [the longest x19 44.9 us: ring(): return lax.ppermute(piece, ALL, pairs)]
    unnamed x28 -> x48, local copies, waits for them, and re-layouts: 6.09 us -> 12.3 us
    ppermute x21 -> x28, starting transfers between devices: 27.5 us -> 32.9 us  [the longest x19 30.8 us: ring(): return lax.ppermute(piece, ALL, pairs)]
    pallas_call x8 -> x11, Pallas kernels: 66 us -> 71.3 us  [the longest x1 42.6 us: project(): pl.pallas_call(lambda *refs: project_kernel(plan, *refs), out_shape=(jax....]
  transfers between devices with their start and end apart: 22 -> 28, of which waited for: 10 -> 17; matrix products, arithmetic and copies ran while one was open for 0% -> 0% of each run, Pallas kernels for 37% -> 41%
where the time goes in v7:
time: 178 us; the launch traced here: 177 us
  Pallas kernels  79 us (44%)
  waiting for transfers between devices  50.8 us (29%)
  starting transfers between devices  32.9 us (18%)
  local copies, waits for them, and re-layouts  12.3 us (7%)
    ppermute x19, waiting for transfers between devices, ring(): return lax.ppermute(piece, ALL, pairs)  44.9 us
    pallas_call x1, Pallas kernels, project(): pl.pallas_call(lambda *refs: project_kernel(plan, *refs), out_shape=(jax....  42.6 us
    ppermute x19, starting transfers between devices, ring(): return lax.ppermute(piece, ALL, pairs)  30.8 us
    pallas_call x2, Pallas kernels, grads(): pl.pallas_call(lambda *refs: grad_kernel(aheads, each, *refs), out_shape=...  19.6 us
    unnamed x48, local copies, waits for them, and re-layouts  12.3 us
    pallas_call x2, Pallas kernels, norm(): pl.pallas_call(norm_kernel, out_shape=(jax.ShapeDtypeStruct((count, width...  7.7 us
    ppermute x9, waiting for transfers between devices, other_core(): return lax.ppermute(value, 'c', [(0, 1), (1, 0)])  5.9 us
    pallas_call x1, Pallas kernels, cut_sum(): pl.pallas_call(kernel, out_shape=[jax.ShapeDtypeStruct((each + 1, T, T),...  3.96 us
  transfers between devices with their start and end apart: 28, of which 17 were waited for; matrix products, arithmetic and copies ran while one was open for 0% of the time, Pallas kernels for 41%

profile of v7, /device:TPU:0, one launch (start us, length us, event | category | flops | bytes accessed | tf_op | source)
XLA Modules:
  0.0 176.6 jit_solution(115313725788329369)
XLA Ops:
  1.2 4.0 %collective-permute-start.1 = (bf16[16,128,128]{2,1,0:T(8,128)(2,1)}, bf16[16,128,128]{2,1,0:T(8,128)(2,1)S(1)}, u32[]{:S(2)}, u32[]{:S(2)}) collective-permute-start(bf16[16,128,128]{2,1,0:T(8,128)(2,1)} %refs_0_.4), channel_id=1, source_target_pairs={{0,16},{1,17},{2,18},{3,19},{4,68},{5,69},{6,70},{7,71},{8,24},{9,... | collective-permute-start | bytes 1572872 | tf_op jit(solution)/shard_map/ppermute | solution.py:296
  5.2 1.0 collective-permute-start
  6.2 2.2 %collective-permute-start.2 = (bf16[16,128,128]{2,1,0:T(8,128)(2,1)}, bf16[16,128,128]{2,1,0:T(8,128)(2,1)S(1)}, u32[]{:S(2)}, u32[]{:S(2)}) collective-permute-start(bf16[16,128,128]{2,1,0:T(8,128)(2,1)} %refs_0_.4), channel_id=1, source_target_pairs={{0,24},{1,25},{2,26},{3,27},{4,100},{5,101},{6,102},{7,103},{8,0},... | collective-permute-start | bytes 1572872 | tf_op jit(solution)/shard_map/ppermute | solution.py:296
  8.5 1.0 copy-done.23
  9.4 3.8 %norm.3 = (bf16[128,4096]{1,0:T(8,128)(2,1)}, bf16[32,128,128]{2,1,0:T(8,128)(2,1)}, f32[128,128]{1,0:T(8,128)}) custom-call(bf16[128,4096]{1,0:T(8,128)(2,1)} %copy-done.23, f32[1,4096]{1,0:T(1,128)} %bitcast.8), custom_call_target="tpu_custom_call" | custom-call | flops 1100000000 | tf_op jit(solution)/shard_map/norm/pallas_call | solution.py:66
  13.2 5.0 %collective-permute-done.refs_1_ = bf16[16,128,128]{2,1,0:T(8,128)(2,1)S(1)} collective-permute-done((bf16[16,128,128]{2,1,0:T(8,128)(2,1)}, bf16[16,128,128]{2,1,0:T(8,128)(2,1)S(1)}, u32[]{:S(2)}, u32[]{:S(2)}) %collective-permute-start) | collective-permute-done | bytes 524320 | tf_op jit(solution)/shard_map/ppermute | solution.py:296
  18.2 1.1 collective-permute-done.2.refs_3_
  19.2 1.2 copy-done.4
  20.5 1.9 %joined.1 = bf16[4,16,128,128]{3,2,1,0:T(8,128)(2,1)} custom-call(bf16[16,128,128]{2,1,0:T(8,128)(2,1)S(1)} %copy-done.11, bf16[16,128,128]{2,1,0:T(8,128)(2,1)S(1)} %collective-permute-done.refs_1_, bf16[16,128,128]{2,1,0:T(8,128)(2,1)S(1)} %collective-permute-done.1.refs_2_, bf16[16,128,128]{2,1,0:T(8,128)(2,1)S(1)} %collective-permute-done.2.refs_3_, ...), custom_call_target="tpu_custom_call" | custom-call | flops 1100000000 | tf_op jit(solution)/shard_map/joined/pallas_call | solution.py:240
  22.4 3.0 %collective-permute-start.5 = (bf16[64,128,128]{2,1,0:T(8,128)(2,1)}, bf16[64,128,128]{2,1,0:T(8,128)(2,1)S(1)}, u32[]{:S(2)}, u32[]{:S(2)}) collective-permute-start(bf16[64,128,128]{2,1,0:T(8,128)(2,1)} %bitcast.5.refs_8_), channel_id=1, source_target_pairs={{0,96},{1,97},{2,98},{3,99},{4,28},{5,29},{6,30},{7,31},{8,104},{9... | collective-permute-start | bytes 6291464 | tf_op jit(solution)/shard_map/ppermute | solution.py:296
  25.4 3.9 %norm.2 = (bf16[128,4096]{1,0:T(8,128)(2,1)}, bf16[32,128,128]{2,1,0:T(8,128)(2,1)}, f32[128,128]{1,0:T(8,128)}) custom-call(bf16[128,4096]{1,0:T(8,128)(2,1)} %refs_3_.1, f32[1,4096]{1,0:T(1,128)} %bitcast.9), custom_call_target="tpu_custom_call" | custom-call | flops 1100000000 | tf_op jit(solution)/shard_map/norm/pallas_call | solution.py:66
  29.4 1.2 copy-done.7
  30.7 9.2 %grads.2 = (bf16[64,128,128]{2,1,0:T(8,128)(2,1)S(1)}, bf16[64,128,128]{2,1,0:T(8,128)(2,1)S(1)}) custom-call(s32[512]{0:T(512)S(1)} %copy-done.12, s32[512]{0:T(512)S(1)} %copy-done.13, s32[4]{0:T(128)S(1)} %pad_add_fusion.refs_2_.pos_ref, bf16[32,128,128]{2,1,0:T(8,128)(2,1)S(1)} %copy-done.7, bf16[32,128,128]{2,1,0:T(8,128)(2,1)S(1)} %copy-done.5, ...), custom_call_target="tpu_custom_call" | custom-call | flops 2200000000 | tf_op jit(solution)/shard_map/grads/pallas_call | solution.py:126
  39.9 9.4 %collective-permute-done.5.right_ref.refs_1_ = bf16[64,128,128]{2,1,0:T(8,128)(2,1)S(1)} collective-permute-done((bf16[64,128,128]{2,1,0:T(8,128)(2,1)}, bf16[64,128,128]{2,1,0:T(8,128)(2,1)S(1)}, u32[]{:S(2)}, u32[]{:S(2)}) %collective-permute-start.5) | collective-permute-done | bytes 2097184 | tf_op jit(solution)/shard_map/ppermute | solution.py:296
  49.3 3.7 %collective-permute-done.4.left_ref.refs_0_ = bf16[64,128,128]{2,1,0:T(8,128)(2,1)} collective-permute-done((bf16[64,128,128]{2,1,0:T(8,128)(2,1)}, bf16[64,128,128]{2,1,0:T(8,128)(2,1)}, u32[]{:S(2)}, u32[]{:S(2)}) %collective-permute-start.4) | collective-permute-done | bytes 2097184 | tf_op jit(solution)/shard_map/ppermute | solution.py:296
  52.9 1.3 relayed.1
  55.0 1.4 collective-permute-start.7
  56.4 10.4 %grads.3 = (bf16[64,128,128]{2,1,0:T(8,128)(2,1)S(1)}, bf16[64,128,128]{2,1,0:T(8,128)(2,1)S(1)}, bf16[64,128,128]{2,1,0:T(8,128)(2,1)S(1)}, bf16[64,128,128]{2,1,0:T(8,128)(2,1)S(1)}) custom-call(s32[512]{0:T(512)S(1)} %copy-done.12, s32[512]{0:T(512)S(1)} %copy-done.13, ...), custom_call_target="tpu_custom_call", output_to_operand_aliasing={{0}: (7, {}), {1}: (8, {})} | custom-call | flops 2200000000 | tf_op jit(solution)/shard_map/grads/pallas_call | solution.py:126
  66.8 1.4 copy-done.2
  68.1 1.3 copy-done.8
  69.4 1.4 copy-done.10
  70.8 1.4 copy-done.17
  72.3 1.0 copy-done.19
  74.6 1.5 collective-permute-start.14
  76.1 1.9 %collective-permute-done.12.refs_16_ = bf16[32,128,128]{2,1,0:T(8,128)(2,1)S(1)} collective-permute-done((bf16[32,128,128]{2,1,0:T(8,128)(2,1)}, bf16[32,128,128]{2,1,0:T(8,128)(2,1)S(1)}, u32[]{:S(2)}, u32[]{:S(2)}) %collective-permute-start.12) | collective-permute-done | bytes 1048608 | tf_op jit(solution)/shard_map/ppermute | solution.py:397
  78.0 3.0 %collective-permute-start.15 = (bf16[64,128,128]{2,1,0:T(8,128)(2,1)S(1)}, bf16[64,128,128]{2,1,0:T(8,128)(2,1)S(1)}, u32[]{:S(2)}, u32[]{:S(2)}) collective-permute-start(bf16[64,128,128]{2,1,0:T(8,128)(2,1)S(1)} %copy-done.9), channel_id=1, source_target_pairs={{0,2},{1,3},{2,0},{3,1},{4,68},{5,69},{6,70},{7,71},{8,10},{9,11},... | collective-permute-start | bytes 6291464 | tf_op jit(solution)/shard_map/ppermute | solution.py:296
  81.0 1.3 collective-permute-start.16
  82.3 1.7 collective-permute-done.11.refs_15_
  84.1 1.4 copy-done.21
  85.4 42.6 %project.1 = (bf16[128,14336]{1,0:T(8,128)(2,1)}, bf16[128,4096]{1,0:T(8,128)(2,1)}, f32[32,128]{1,0:T(8,128)}) custom-call(s32[512]{0:T(512)} %refs_0_.7, s32[512]{0:T(512)} %refs_1_.5, s32[4]{0:T(128)} %copy-done.15, bf16[128,4096]{1,0:T(8,128)(2,1)} %refs_3_.1, bf16[128,4096]{1,0:T(8,128)(2,1)} %get-tuple-element.33.refs_4_, ...), custom_call_target="tpu_custom_call" | custom-call | flops 2200000000 | tf_op jit(solution)/shard_map/project/pallas_call | solution.py:213
  128.5 1.0 collective-permute-done.17.refs_5_
  130.3 4.0 %cut_sum.1 = (bf16[17,128,128]{2,1,0:T(8,128)(2,1)S(1)}, bf16[17,128,128]{2,1,0:T(8,128)(2,1)S(1)}, bf16[17,128,128]{2,1,0:T(8,128)(2,1)S(1)}, bf16[17,128,128]{2,1,0:T(8,128)(2,1)S(1)}) custom-call(bf16[64,128,128]{2,1,0:T(8,128)(2,1)S(1)} %copy-done.3, bf16[64,128,128]{2,1,0:T(8,128)(2,1)S(1)} %collective-permute-done.14.refs_1_, ...), custom_call_target="tpu_custom_call" | custom-call | flops 1100000000 | tf_op jit(solution)/shard_map/cut_sum/pallas_call | solution.py:339
  134.4 3.3 %collective-permute-start.19 = (bf16[17,128,128]{2,1,0:T(8,128)(2,1)S(1)}, bf16[17,128,128]{2,1,0:T(8,128)(2,1)S(1)}, u32[]{:S(2)}, u32[]{:S(2)}) collective-permute-start(bf16[17,128,128]{2,1,0:T(8,128)(2,1)S(1)} %get-tuple-element.54), channel_id=1, source_target_pairs={{0,64},{1,65},{2,66},{3,67},{4,20},{5,21},{6,22},{7,23},{8,72},{9,... | collective-permute-start | bytes 1671176 | tf_op jit(solution)/shard_map/ppermute | solution.py:296
  137.7 7.4 %collective-permute-done.18.refs_1_ = bf16[17,128,128]{2,1,0:T(8,128)(2,1)S(1)} collective-permute-done((bf16[17,128,128]{2,1,0:T(8,128)(2,1)S(1)}, bf16[17,128,128]{2,1,0:T(8,128)(2,1)S(1)}, u32[]{:S(2)}, u32[]{:S(2)}) %collective-permute-start.18) | collective-permute-done | bytes 557088 | tf_op jit(solution)/shard_map/ppermute | solution.py:296
  145.1 6.1 %collective-permute-done.19.refs_2_ = bf16[17,128,128]{2,1,0:T(8,128)(2,1)S(1)} collective-permute-done((bf16[17,128,128]{2,1,0:T(8,128)(2,1)S(1)}, bf16[17,128,128]{2,1,0:T(8,128)(2,1)S(1)}, u32[]{:S(2)}, u32[]{:S(2)}) %collective-permute-start.19) | collective-permute-done | bytes 557088 | tf_op jit(solution)/shard_map/ppermute | solution.py:296
  151.2 0.8 collective-permute-done.20.refs_3_
  152.2 1.1 collective-permute-start.21
  153.3 3.1 %collective-permute-start.22 = (bf16[5,128,128]{2,1,0:T(8,128)(2,1)S(1)}, bf16[5,128,128]{2,1,0:T(8,128)(2,1)S(1)}, u32[]{:S(2)}, u32[]{:S(2)}) collective-permute-start(bf16[5,128,128]{2,1,0:T(8,128)(2,1)S(1)} %get-tuple-element.58), channel_id=1, source_target_pairs={{0,16},{1,17},{2,18},{3,19},{4,6},{5,7},{6,4},{7,5},{8,24},{9,25},... | collective-permute-start | bytes 491528 | tf_op jit(solution)/shard_map/ppermute | solution.py:296
  157.0 1.8 %collective-permute-done.21.refs_1_ = bf16[5,128,128]{2,1,0:T(8,128)(2,1)S(1)} collective-permute-done((bf16[5,128,128]{2,1,0:T(8,128)(2,1)S(1)}, bf16[5,128,128]{2,1,0:T(8,128)(2,1)S(1)}, u32[]{:S(2)}, u32[]{:S(2)}) %collective-permute-start.21) | collective-permute-done | bytes 163872 | tf_op jit(solution)/shard_map/ppermute | solution.py:296
  158.8 2.6 %collective-permute-done.22.refs_2_ = bf16[5,128,128]{2,1,0:T(8,128)(2,1)S(1)} collective-permute-done((bf16[5,128,128]{2,1,0:T(8,128)(2,1)S(1)}, bf16[5,128,128]{2,1,0:T(8,128)(2,1)S(1)}, u32[]{:S(2)}, u32[]{:S(2)}) %collective-permute-start.22) | collective-permute-done | bytes 163872 | tf_op jit(solution)/shard_map/ppermute | solution.py:296
  161.8 2.8 %collective-permute-start.26 = (bf16[5,128,128]{2,1,0:T(8,128)(2,1)S(1)}, bf16[5,128,128]{2,1,0:T(8,128)(2,1)S(1)}, u32[]{:S(2)}, u32[]{:S(2)}) collective-permute-start(bf16[5,128,128]{2,1,0:T(8,128)(2,1)S(1)} %next_sum.3.refs_0_), channel_id=1, source_target_pairs={{0,3},{1,0},{2,1},{3,2},{4,7},{5,4},{6,5},{7,6},{8,11},{9,8},{10,9... | collective-permute-start | bytes 491528 | tf_op jit(solution)/shard_map/ppermute | solution.py:296
  164.7 0.8 collective-permute-start.25
  165.5 0.9 collective-permute-start.24
  166.4 3.1 %collective-permute-done.26.refs_3_ = bf16[5,128,128]{2,1,0:T(8,128)(2,1)S(1)} collective-permute-done((bf16[5,128,128]{2,1,0:T(8,128)(2,1)S(1)}, bf16[5,128,128]{2,1,0:T(8,128)(2,1)S(1)}, u32[]{:S(2)}, u32[]{:S(2)}) %collective-permute-start.26) | collective-permute-done | bytes 163872 | tf_op jit(solution)/shard_map/ppermute | solution.py:296
  169.5 2.1 %collective-permute-done.25.refs_2_ = bf16[5,128,128]{2,1,0:T(8,128)(2,1)S(1)} collective-permute-done((bf16[5,128,128]{2,1,0:T(8,128)(2,1)S(1)}, bf16[5,128,128]{2,1,0:T(8,128)(2,1)S(1)}, u32[]{:S(2)}, u32[]{:S(2)}) %collective-permute-start.25) | collective-permute-done | bytes 163872 | tf_op jit(solution)/shard_map/ppermute | solution.py:296
  171.6 1.7 collective-permute-done.24.refs_1_
  173.2 1.6 place.1
  174.8 1.2 collective-permute-done.27
  (71 shorter events, 5.9 us)
Async XLA Ops:
  0.6 18.6 %copy-start.11 = (bf16[16,128,128]{2,1,0:T(8,128)(2,1)S(1)}, bf16[16,128,128]{2,1,0:T(8,128)(2,1)}, u32[]{:S(2)}) copy-start(bf16[16,128,128]{2,1,0:T(8,128)(2,1)} %refs_0_.4) | copy-start | bytes 1572868
  0.6 28.8 %collective-permute-start.6 = (bf16[128,14336]{1,0:T(8,128)(2,1)}, bf16[128,14336]{1,0:T(8,128)(2,1)}, u32[]{:S(2)}, u32[]{:S(2)}) collective-permute-start(bf16[128,14336]{1,0:T(8,128)(2,1)} %refs_7_.1), channel_id=1, source_target_pairs={{0,4},{4,0},{1,5},{5,1},{2,6},{6,2},{3,7},{7,3},{8,12},{12,8},{9,1... | collective-permute-start | bytes 11010056 | tf_op jit(solution)/shard_map/ppermute | solution.py:397
  0.7 7.7 %collective-permute-start.3 = (bf16[128,4096]{1,0:T(8,128)(2,1)}, bf16[128,4096]{1,0:T(8,128)(2,1)S(1)}, u32[]{:S(2)}, u32[]{:S(2)}) collective-permute-start(bf16[128,4096]{1,0:T(8,128)(2,1)} %refs_3_.1), channel_id=1, source_target_pairs={{0,4},{4,0},{1,5},{5,1},{2,6},{6,2},{3,7},{7,3},{8,12},{12,8},{9,1... | collective-permute-start | bytes 3145736 | tf_op jit(solution)/shard_map/ppermute | solution.py:397
  1.2 12.0 %collective-permute-start.1 = (bf16[16,128,128]{2,1,0:T(8,128)(2,1)}, bf16[16,128,128]{2,1,0:T(8,128)(2,1)S(1)}, u32[]{:S(2)}, u32[]{:S(2)}) collective-permute-start(bf16[16,128,128]{2,1,0:T(8,128)(2,1)} %refs_0_.4), channel_id=1, source_target_pairs={{0,16},{1,17},{2,18},{3,19},{4,68},{5,69},{6,70},{7,71},{8,24},{9,... | collective-permute-start | bytes 1572872 | tf_op jit(solution)/shard_map/ppermute | solution.py:296
  5.2 13.0 %collective-permute-start = (bf16[16,128,128]{2,1,0:T(8,128)(2,1)}, bf16[16,128,128]{2,1,0:T(8,128)(2,1)S(1)}, u32[]{:S(2)}, u32[]{:S(2)}) collective-permute-start(bf16[16,128,128]{2,1,0:T(8,128)(2,1)} %refs_0_.4), channel_id=1, source_target_pairs={{0,8},{1,9},{2,10},{3,11},{4,36},{5,37},{6,38},{7,39},{8,16},{9,17... | collective-permute-start | bytes 1572872 | tf_op jit(solution)/shard_map/ppermute | solution.py:296
  6.2 13.0 %collective-permute-start.2 = (bf16[16,128,128]{2,1,0:T(8,128)(2,1)}, bf16[16,128,128]{2,1,0:T(8,128)(2,1)S(1)}, u32[]{:S(2)}, u32[]{:S(2)}) collective-permute-start(bf16[16,128,128]{2,1,0:T(8,128)(2,1)} %refs_0_.4), channel_id=1, source_target_pairs={{0,24},{1,25},{2,26},{3,27},{4,100},{5,101},{6,102},{7,103},{8,0},... | collective-permute-start | bytes 1572872 | tf_op jit(solution)/shard_map/ppermute | solution.py:296
  20.5 8.9 %copy-start.5 = (bf16[32,128,128]{2,1,0:T(8,128)(2,1)S(1)}, bf16[32,128,128]{2,1,0:T(8,128)(2,1)}, u32[]{:S(2)}) copy-start(bf16[32,128,128]{2,1,0:T(8,128)(2,1)} %get-tuple-element.35.refs_4_) | copy-start | bytes 3145732
  22.4 7.0 %copy-start.12 = (s32[512]{0:T(512)S(1)}, s32[512]{0:T(512)}, u32[]{:S(2)}) copy-start(s32[512]{0:T(512)} %refs_0_.7) | copy-start | bytes 6148
  22.4 7.0 %copy-start.13 = (s32[512]{0:T(512)S(1)}, s32[512]{0:T(512)}, u32[]{:S(2)}) copy-start(s32[512]{0:T(512)} %refs_1_.5) | copy-start | bytes 6148
  22.4 26.9 %collective-permute-start.5 = (bf16[64,128,128]{2,1,0:T(8,128)(2,1)}, bf16[64,128,128]{2,1,0:T(8,128)(2,1)S(1)}, u32[]{:S(2)}, u32[]{:S(2)}) collective-permute-start(bf16[64,128,128]{2,1,0:T(8,128)(2,1)} %bitcast.5.refs_8_), channel_id=1, source_target_pairs={{0,96},{1,97},{2,98},{3,99},{4,28},{5,29},{6,30},{7,31},{8,104},{9... | collective-permute-start | bytes 6291464 | tf_op jit(solution)/shard_map/ppermute | solution.py:296
  25.4 27.6 %collective-permute-start.4 = (bf16[64,128,128]{2,1,0:T(8,128)(2,1)}, bf16[64,128,128]{2,1,0:T(8,128)(2,1)}, u32[]{:S(2)}, u32[]{:S(2)}) collective-permute-start(bf16[64,128,128]{2,1,0:T(8,128)(2,1)} %bitcast.5.refs_8_), channel_id=1, source_target_pairs={{0,32},{1,33},{2,34},{3,35},{4,12},{5,13},{6,14},{7,15},{8,40},{9,... | collective-permute-start | bytes 6291464 | tf_op jit(solution)/shard_map/ppermute | solution.py:296
  25.4 4.0 %copy-start = (bf16[128,14336]{1,0:T(8,128)(2,1)S(1)}, bf16[128,14336]{1,0:T(8,128)(2,1)}, u32[]{:S(2)}) copy-start(bf16[128,14336]{1,0:T(8,128)(2,1)} %refs_7_.1) | copy-start | bytes 11010052
  29.4 27.0 %copy-start.15 = (s32[4]{0:T(128)}, s32[4]{0:T(128)S(1)}, u32[]{:S(2)}) copy-start(s32[4]{0:T(128)S(1)} %pad_add_fusion.refs_2_.pos_ref) | copy-start | bytes 52
  29.4 1.2 copy-start.7
  49.3 5.0 %copy-start.1 = (bf16[64,128,128]{2,1,0:T(8,128)(2,1)}, bf16[64,128,128]{2,1,0:T(8,128)(2,1)S(1)}, u32[]{:S(2)}) copy-start(bf16[64,128,128]{2,1,0:T(8,128)(2,1)S(1)} %collective-permute-done.5.right_ref.refs_1_) | copy-start | bytes 6291460
  54.3 12.5 %copy-start.6 = (bf16[32,128,128]{2,1,0:T(8,128)(2,1)}, bf16[32,128,128]{2,1,0:T(8,128)(2,1)S(1)}, u32[]{:S(2)}) copy-start(bf16[32,128,128]{2,1,0:T(8,128)(2,1)S(1)} %get-tuple-element.38.refs_2_.refs_9_) | copy-start | bytes 3145732
  54.3 18.0 %collective-permute-start.8 = (bf16[32,128,128]{2,1,0:T(8,128)(2,1)S(1)}, bf16[32,128,128]{2,1,0:T(8,128)(2,1)S(1)}, u32[]{:S(2)}, u32[]{:S(2)}) collective-permute-start(bf16[32,128,128]{2,1,0:T(8,128)(2,1)S(1)} %get-tuple-element.41), channel_id=1, source_target_pairs={{0,96},{1,97},{2,98},{3,99},{4,28},{5,29},{6,30},{7,31},{8,104},{9... | collective-permute-start | bytes 3145736 | tf_op jit(solution)/shard_map/ppermute | solution.py:296
  55.0 17.3 %collective-permute-start.7 = (bf16[32,128,128]{2,1,0:T(8,128)(2,1)S(1)}, bf16[32,128,128]{2,1,0:T(8,128)(2,1)S(1)}, u32[]{:S(2)}, u32[]{:S(2)}) collective-permute-start(bf16[32,128,128]{2,1,0:T(8,128)(2,1)S(1)} %get-tuple-element.38.refs_2_.refs_9_), channel_id=1, source_target_pairs={{0,32},{1,33},{2,34},{3,35},{4,12},{5,13},{6,14},{7,15},{8,40},{9,... | collective-permute-start | bytes 3145736 | tf_op jit(solution)/shard_map/ppermute | solution.py:296
  56.4 18.2 %collective-permute-start.9 = (bf16[64,128,128]{2,1,0:T(8,128)(2,1)}, bf16[64,128,128]{2,1,0:T(8,128)(2,1)}, u32[]{:S(2)}, u32[]{:S(2)}) collective-permute-start(bf16[64,128,128]{2,1,0:T(8,128)(2,1)} %bitcast.5.refs_8_), channel_id=1, source_target_pairs={{0,4},{4,0},{1,5},{5,1},{2,6},{6,2},{3,7},{7,3},{8,12},{12,8},{9,1... | collective-permute-start | bytes 6291464 | tf_op jit(solution)/shard_map/ppermute | solution.py:397
  66.8 1.4 copy-start.2
  68.1 1.3 copy-start.8
  69.4 1.4 copy-start.10
  70.8 1.4 copy-start.17
  72.2 1.3 copy-start.18
  73.6 4.4 %collective-permute-start.12 = (bf16[32,128,128]{2,1,0:T(8,128)(2,1)}, bf16[32,128,128]{2,1,0:T(8,128)(2,1)S(1)}, u32[]{:S(2)}, u32[]{:S(2)}) collective-permute-start(bf16[32,128,128]{2,1,0:T(8,128)(2,1)} %get-tuple-element.44.refs_11_), channel_id=1, source_target_pairs={{0,4},{4,0},{1,5},{5,1},{2,6},{6,2},{3,7},{7,3},{8,12},{12,8},{9,1... | collective-permute-start | bytes 3145736 | tf_op jit(solution)/shard_map/ppermute | solution.py:397
  74.1 3.9 %copy-start.9 = (bf16[64,128,128]{2,1,0:T(8,128)(2,1)S(1)}, bf16[64,128,128]{2,1,0:T(8,128)(2,1)}, u32[]{:S(2)}) copy-start(bf16[64,128,128]{2,1,0:T(8,128)(2,1)} %copy-done.8) | copy-start | bytes 6291460
  74.1 6.9 %collective-permute-start.13 = (bf16[32,128,128]{2,1,0:T(8,128)(2,1)}, bf16[32,128,128]{2,1,0:T(8,128)(2,1)}, u32[]{:S(2)}, u32[]{:S(2)}) collective-permute-start(bf16[32,128,128]{2,1,0:T(8,128)(2,1)} %get-tuple-element.45.refs_12_), channel_id=1, source_target_pairs={{0,4},{4,0},{1,5},{5,1},{2,6},{6,2},{3,7},{7,3},{8,12},{12,8},{9,1... | collective-permute-start | bytes 3145736 | tf_op jit(solution)/shard_map/ppermute | solution.py:397
  74.1 8.2 %collective-permute-start.10 = (bf16[64,128,128]{2,1,0:T(8,128)(2,1)}, bf16[64,128,128]{2,1,0:T(8,128)(2,1)S(1)}, u32[]{:S(2)}, u32[]{:S(2)}) collective-permute-start(bf16[64,128,128]{2,1,0:T(8,128)(2,1)} %get-tuple-element.39.refs_9_), channel_id=1, source_target_pairs={{0,4},{4,0},{1,5},{5,1},{2,6},{6,2},{3,7},{7,3},{8,12},{12,8},{9,1... | collective-permute-start | bytes 6291464 | tf_op jit(solution)/shard_map/ppermute | solution.py:397
  74.6 9.5 %collective-permute-start.11 = (bf16[64,128,128]{2,1,0:T(8,128)(2,1)}, bf16[64,128,128]{2,1,0:T(8,128)(2,1)S(1)}, u32[]{:S(2)}, u32[]{:S(2)}) collective-permute-start(bf16[64,128,128]{2,1,0:T(8,128)(2,1)} %get-tuple-element.40.refs_10_), channel_id=1, source_target_pairs={{0,4},{4,0},{1,5},{5,1},{2,6},{6,2},{3,7},{7,3},{8,12},{12,8},{9,1... | collective-permute-start | bytes 6291464 | tf_op jit(solution)/shard_map/ppermute | solution.py:397
  74.6 54.0 %collective-permute-start.14 = (bf16[64,128,128]{2,1,0:T(8,128)(2,1)}, bf16[64,128,128]{2,1,0:T(8,128)(2,1)S(1)}, u32[]{:S(2)}, u32[]{:S(2)}) collective-permute-start(bf16[64,128,128]{2,1,0:T(8,128)(2,1)} %copy-done.17), channel_id=1, source_target_pairs={{0,1},{1,2},{2,3},{3,0},{4,36},{5,37},{6,38},{7,39},{8,9},{9,10},{... | collective-permute-start | bytes 6291464 | tf_op jit(solution)/shard_map/ppermute | solution.py:296
  78.0 7.5 %copy-start.22 = (bf16[32,128,128]{2,1,0:T(8,128)(2,1)}, bf16[32,128,128]{2,1,0:T(8,128)(2,1)S(1)}, u32[]{:S(2)}) copy-start(bf16[32,128,128]{2,1,0:T(8,128)(2,1)S(1)} %collective-permute-done.12.refs_16_) | copy-start | bytes 3145732
  78.0 50.6 %collective-permute-start.15 = (bf16[64,128,128]{2,1,0:T(8,128)(2,1)S(1)}, bf16[64,128,128]{2,1,0:T(8,128)(2,1)S(1)}, u32[]{:S(2)}, u32[]{:S(2)}) collective-permute-start(bf16[64,128,128]{2,1,0:T(8,128)(2,1)S(1)} %copy-done.9), channel_id=1, source_target_pairs={{0,2},{1,3},{2,0},{3,1},{4,68},{5,69},{6,70},{7,71},{8,10},{9,11},... | collective-permute-start | bytes 6291464 | tf_op jit(solution)/shard_map/ppermute | solution.py:296
  81.0 47.6 %collective-permute-start.16 = (bf16[64,128,128]{2,1,0:T(8,128)(2,1)}, bf16[64,128,128]{2,1,0:T(8,128)(2,1)}, u32[]{:S(2)}, u32[]{:S(2)}) collective-permute-start(bf16[64,128,128]{2,1,0:T(8,128)(2,1)} %copy-done.10), channel_id=1, source_target_pairs={{0,3},{1,0},{2,1},{3,2},{4,100},{5,101},{6,102},{7,103},{8,11},{9,... | collective-permute-start | bytes 6291464 | tf_op jit(solution)/shard_map/ppermute | solution.py:296
  82.3 1.7 copy-start.20
  84.1 1.4 copy-start.21
  85.4 44.2 %copy-start.3 = (bf16[64,128,128]{2,1,0:T(8,128)(2,1)S(1)}, bf16[64,128,128]{2,1,0:T(8,128)(2,1)}, u32[]{:S(2)}) copy-start(bf16[64,128,128]{2,1,0:T(8,128)(2,1)} %copy-done.2) | copy-start | bytes 6291460
  128.1 1.5 collective-permute-start.17
  134.3 10.8 %collective-permute-start.18 = (bf16[17,128,128]{2,1,0:T(8,128)(2,1)S(1)}, bf16[17,128,128]{2,1,0:T(8,128)(2,1)S(1)}, u32[]{:S(2)}, u32[]{:S(2)}) collective-permute-start(bf16[17,128,128]{2,1,0:T(8,128)(2,1)S(1)} %get-tuple-element.53), channel_id=1, source_target_pairs={{0,32},{1,33},{2,34},{3,35},{4,12},{5,13},{6,14},{7,15},{8,40},{9,... | collective-permute-start | bytes 1671176 | tf_op jit(solution)/shard_map/ppermute | solution.py:296
  134.4 16.8 %collective-permute-start.19 = (bf16[17,128,128]{2,1,0:T(8,128)(2,1)S(1)}, bf16[17,128,128]{2,1,0:T(8,128)(2,1)S(1)}, u32[]{:S(2)}, u32[]{:S(2)}) collective-permute-start(bf16[17,128,128]{2,1,0:T(8,128)(2,1)S(1)} %get-tuple-element.54), channel_id=1, source_target_pairs={{0,64},{1,65},{2,66},{3,67},{4,20},{5,21},{6,22},{7,23},{8,72},{9,... | collective-permute-start | bytes 1671176 | tf_op jit(solution)/shard_map/ppermute | solution.py:296
  137.7 14.3 %collective-permute-start.20 = (bf16[17,128,128]{2,1,0:T(8,128)(2,1)S(1)}, bf16[17,128,128]{2,1,0:T(8,128)(2,1)S(1)}, u32[]{:S(2)}, u32[]{:S(2)}) collective-permute-start(bf16[17,128,128]{2,1,0:T(8,128)(2,1)S(1)} %get-tuple-element.55), channel_id=1, source_target_pairs={{0,96},{1,97},{2,98},{3,99},{4,28},{5,29},{6,30},{7,31},{8,104},{9... | collective-permute-start | bytes 1671176 | tf_op jit(solution)/shard_map/ppermute | solution.py:296
  152.2 21.0 %copy-start.16 = (s32[4]{0:T(128)S(1)}, s32[4]{0:T(128)}, u32[]{:S(2)}) copy-start(s32[4]{0:T(128)} %copy-done.15) | copy-start | bytes 52
  152.2 6.6 %collective-permute-start.21 = (bf16[5,128,128]{2,1,0:T(8,128)(2,1)S(1)}, bf16[5,128,128]{2,1,0:T(8,128)(2,1)S(1)}, u32[]{:S(2)}, u32[]{:S(2)}) collective-permute-start(bf16[5,128,128]{2,1,0:T(8,128)(2,1)S(1)} %get-tuple-element.57), channel_id=1, source_target_pairs={{0,8},{1,9},{2,10},{3,11},{4,5},{5,6},{6,7},{7,4},{8,16},{9,17},{1... | collective-permute-start | bytes 491528 | tf_op jit(solution)/shard_map/ppermute | solution.py:296
  153.3 8.1 %collective-permute-start.22 = (bf16[5,128,128]{2,1,0:T(8,128)(2,1)S(1)}, bf16[5,128,128]{2,1,0:T(8,128)(2,1)S(1)}, u32[]{:S(2)}, u32[]{:S(2)}) collective-permute-start(bf16[5,128,128]{2,1,0:T(8,128)(2,1)S(1)} %get-tuple-element.58), channel_id=1, source_target_pairs={{0,16},{1,17},{2,18},{3,19},{4,6},{5,7},{6,4},{7,5},{8,24},{9,25},... | collective-permute-start | bytes 491528 | tf_op jit(solution)/shard_map/ppermute | solution.py:296
  156.4 5.3 %collective-permute-start.23 = (bf16[5,128,128]{2,1,0:T(8,128)(2,1)S(1)}, bf16[5,128,128]{2,1,0:T(8,128)(2,1)S(1)}, u32[]{:S(2)}, u32[]{:S(2)}) collective-permute-start(bf16[5,128,128]{2,1,0:T(8,128)(2,1)S(1)} %get-tuple-element.59), channel_id=1, source_target_pairs={{0,24},{1,25},{2,26},{3,27},{4,7},{5,4},{6,5},{7,6},{8,0},{9,1},{1... | collective-permute-start | bytes 491528 | tf_op jit(solution)/shard_map/ppermute | solution.py:296
  161.8 7.6 %collective-permute-start.26 = (bf16[5,128,128]{2,1,0:T(8,128)(2,1)S(1)}, bf16[5,128,128]{2,1,0:T(8,128)(2,1)S(1)}, u32[]{:S(2)}, u32[]{:S(2)}) collective-permute-start(bf16[5,128,128]{2,1,0:T(8,128)(2,1)S(1)} %next_sum.3.refs_0_), channel_id=1, source_target_pairs={{0,3},{1,0},{2,1},{3,2},{4,7},{5,4},{6,5},{7,6},{8,11},{9,8},{10,9... | collective-permute-start | bytes 491528 | tf_op jit(solution)/shard_map/ppermute | solution.py:296
  164.7 6.9 %collective-permute-start.25 = (bf16[5,128,128]{2,1,0:T(8,128)(2,1)S(1)}, bf16[5,128,128]{2,1,0:T(8,128)(2,1)S(1)}, u32[]{:S(2)}, u32[]{:S(2)}) collective-permute-start(bf16[5,128,128]{2,1,0:T(8,128)(2,1)S(1)} %next_sum.3.refs_0_), channel_id=1, source_target_pairs={{0,2},{1,3},{2,0},{3,1},{4,6},{5,7},{6,4},{7,5},{8,10},{9,11},{10,... | collective-permute-start | bytes 491528 | tf_op jit(solution)/shard_map/ppermute | solution.py:296
  165.5 7.8 %collective-permute-start.24 = (bf16[5,128,128]{2,1,0:T(8,128)(2,1)S(1)}, bf16[5,128,128]{2,1,0:T(8,128)(2,1)S(1)}, u32[]{:S(2)}, u32[]{:S(2)}) collective-permute-start(bf16[5,128,128]{2,1,0:T(8,128)(2,1)S(1)} %next_sum.3.refs_0_), channel_id=1, source_target_pairs={{0,1},{1,2},{2,3},{3,0},{4,5},{5,6},{6,7},{7,4},{8,9},{9,10},{10,1... | collective-permute-start | bytes 491528 | tf_op jit(solution)/shard_map/ppermute | solution.py:296
  174.8 1.2 collective-permute-start.27
  (4 other events, 3.9 us)

commit v8 on v7

--- a/solution.py
+++ b/solution.py
@@ -70,7 +70,7 @@
             jax.ShapeDtypeStruct((width // T, T, count), BF),
             jax.ShapeDtypeStruct((count, T), F4),
         ),
-        compiler_params=params(56),
+        compiler_params=params(60),
         cost_estimate=cost(1, 0),
         name="norm",
     )(x, gain)
@@ -134,39 +134,50 @@
             out_specs=[ANY] * len(carried) + [out_spec(k) for k in range(len(aheads))],
         ),
         input_output_aliases={7 + k: k for k in range(len(carried))},
-        compiler_params=params(40),
+        compiler_params=params(60),
         cost_estimate=cost(2, 0),
         name="grads",
     )(rows, cols, pos, *resident, *carried, *ties)
 
 
-def project_kernel(plan, rows, cols, pos, x_ref, normed_ref, scale_ref, gain_ref, g_ref, *refs):
-    projected_ref, token_grad_ref, sums_ref, out_acc, back_acc = refs[-5:]
+def project_kernel(sources, rows, cols, pos, x_ref, normed_ref, scale_ref, gain_ref, g_ref, *refs):
+    projected_ref, token_grad_ref, sums_ref, out_acc, back_acc, held_ref, sem = refs[-7:]
     s = pl.program_id(0)
     count, width = x_ref.shape
     blocks = width // T
+    slot = lax.rem(s, 2)
+
+    def fetch(k):
+        array, offset = sources[k]
+        pltpu.make_async_copy(refs[array].at[pl.ds(offset, 32)], held_ref.at[k % 2], sem.at[k % 2]).start()
 
     @pl.when(s == 0)
     def _():
+        fetch(0)
         out_acc[...] = jnp.zeros_like(out_acc)
         back_acc[...] = jnp.zeros_like(back_acc)
 
-    for (other, behind, offset, start, each), tiles_ref in zip(plan, refs):
-
-        @pl.when((s >= start) & (s < start + each))
-        def _(other=other, behind=behind, offset=offset, start=start, tiles_ref=tiles_ref):
-            core = 1 - pos[2] if other else pos[2]
-
-            def one(k, carry):
-                i = offset + (s - start) * 32 + k
-                index = owned_at(pos, core, 4 - i // 16, 4 - behind) + i % 16
-                r, q = cols_at(rows[index]), cols_at(cols[index])
-                weight = tiles_ref[k]
-                out_acc[:, q] += dot(normed_ref[:, r], weight)
-                back_acc[:, r] += dot_t(g_ref[:, q], weight)
-                return carry
-
-            lax.fori_loop(0, 32, one, 0, unroll=8)
+    for k in range(1, len(sources)):
+
+        @pl.when(s == k - 1)
+        def _(k=k):
+            fetch(k)
+
+    pltpu.make_async_copy(refs[0].at[pl.ds(0, 32)], held_ref.at[slot], sem.at[slot]).wait()
+    core = jnp.where(s < 8, pos[2], 1 - pos[2])
+    pair = lax.rem(s, 8) // 2
+    behind = jnp.where(pair < 2, pair, 5 - pair)
+
+    def one(k, carry):
+        i = lax.rem(s, 2) * 32 + k
+        index = owned_at(pos, core, 4 - i // 16, 4 - behind) + i % 16
+        r, q = cols_at(rows[index]), cols_at(cols[index])
+        weight = held_ref[slot, k]
+        out_acc[:, q] += dot(normed_ref[:, r], weight)
+        back_acc[:, r] += dot_t(g_ref[:, q], weight)
+        return carry
+
+    lax.fori_loop(0, 32, one, 0, unroll=8)
 
     @pl.when(s == pl.num_programs(0) - 1)
     def _():
@@ -199,19 +210,11 @@
 
 
 def project(rows, cols, pos, arrays, x, normed, scale, gain, g):
-    plan, steps = [], 0
-    for tiles, other, behind, offset in arrays:
-        each = tiles.shape[0] // 32
-        plan.append((other, behind, offset, steps, each))
-        steps += each
-
-    def tile_spec(start, each):
-        return pl.BlockSpec((32, T, T), lambda i, *_: (jnp.clip(i - start, 0, each - 1), 0, 0))
-
+    sources = [(k, offset) for k, tiles in enumerate(arrays) for offset in range(0, tiles.shape[0], 32)]
     resident = (x, normed, scale, gain, g)
     sums = (x.shape[1] // T, T)
     return pl.pallas_call(
-        lambda *refs: project_kernel(plan, *refs),
+        lambda *refs: project_kernel(sources, *refs),
         out_shape=(
             jax.ShapeDtypeStruct(g.shape, BF),
             jax.ShapeDtypeStruct(x.shape, BF),
@@ -219,15 +222,20 @@
         ),
         grid_spec=pltpu.PrefetchScalarGridSpec(
             num_scalar_prefetch=3,
-            grid=(steps,),
-            in_specs=[whole(a.shape) for a in resident] + [tile_spec(p[3], p[4]) for p in plan],
+            grid=(len(sources),),
+            in_specs=[whole(a.shape) for a in resident] + [ANY] * len(arrays),
             out_specs=[whole(g.shape), whole(x.shape), whole(sums)],
-            scratch_shapes=[pltpu.VMEM(g.shape, F4), pltpu.VMEM(x.shape, F4)],
+            scratch_shapes=[
+                pltpu.VMEM(g.shape, F4),
+                pltpu.VMEM(x.shape, F4),
+                pltpu.VMEM((2, 32, T, T), BF),
+                pltpu.SemaphoreType.DMA((2,)),
+            ],
         ),
-        compiler_params=params(54),
+        compiler_params=params(60),
         cost_estimate=cost(2, 0),
         name="project",
-    )(rows, cols, pos, *resident, *(a[0] for a in arrays))
+    )(rows, cols, pos, *resident, *arrays)
 
 
 def joined(pieces, tie):
@@ -249,16 +257,16 @@
     )(*pieces, tie).reshape(4 * each, T, T)
 
 
-def held(values, tie):
+def held(values, *ties):
     return pl.pallas_call(
         lambda *refs: None,
         out_shape=[jax.ShapeDtypeStruct(a.shape, a.dtype) for a in values],
-        in_specs=[ANY] * (len(values) + 1),
+        in_specs=[ANY] * (len(values) + len(ties)),
         out_specs=[ANY] * len(values),
         input_output_aliases={k: k for k in range(len(values))},
         cost_estimate=cost(1, 0),
         name="held",
-    )(*values, tie)
+    )(*values, *ties)
 
 
 def relayed(left, right, tie):
@@ -278,7 +286,7 @@
             ANY,
         ],
         out_specs=[pl.BlockSpec((half // 2, T, T), lambda i: (i, 0, 0))] * 2,
-        compiler_params=params(32),
+        compiler_params=params(60),
         cost_estimate=cost(1, 0),
         name="relayed",
     )(left, right, tie)
@@ -362,7 +370,7 @@
         kernel,
         out_shape=[jax.ShapeDtypeStruct((each + 1, T, T), BF)] * cuts,
         in_specs=[pl.BlockSpec(memory_space=pltpu.VMEM)] * 4,
-        compiler_params=params(32),
+        compiler_params=params(16),
         cost_estimate=cost(1, 0),
         name="next_sum",
     )(*pieces)
@@ -381,7 +389,7 @@
         kernel,
         out_shape=(jax.ShapeDtypeStruct((16, T, T), F4), jax.ShapeDtypeStruct((rows, T), F4)),
         in_specs=[pl.BlockSpec(memory_space=pltpu.SMEM)] + [pl.BlockSpec(memory_space=pltpu.VMEM)] * 4,
-        compiler_params=params(32),
+        compiler_params=params(16),
         cost_estimate=cost(1, 0),
         name="place",
     )(pos, *pieces)
@@ -402,14 +410,14 @@
     line = joined(exchange([tiles] * 4, first), turned_other)
     left, right = ring(line, second, 1), ring(line, second, 3)
     operands = (rows, cols, pos, turned, turned_other, cotangent, g_other)
-    part0, part2 = grads((0, 2), *operands)
+    part0, part2, part1 = grads((0, 2, 1), *operands)
     left_half, right_half = relayed(left, right, part0)
     left, right = held((left, right), left_half)
-    part0, part2, part1, part3 = grads((1, 3), *operands, (part0, part2), (left_half,))
-    far0, far1 = held((ring(left_half, second, 1), ring(right_half, second, 3)), part3)
-    blocks = [(line, 0, 0), (left, 1, 0), (right, 3, 0), (far0, 2, 0), (far1, 2, 32)]
-    arrays = [(block, False, *where) for block, *where in blocks]
-    arrays += [(other_core(block), True, *where) for block, *where in blocks]
+    part0, part2, part1, part3 = grads((3,), *operands, (part0, part2, part1), (left_half,))
+    near = [line, left, right]
+    swapped = [other_core(block) for block in near]
+    far = held((ring(left_half, second, 1), ring(right_half, second, 3)), part3, *swapped)
+    arrays = near + list(far) + swapped + [other_core(block) for block in far]
     projected, token_grad, sums = project(rows, cols, pos, arrays, tokens, normed, scale, gain2, cotangent)
     count = sums.shape[0]
     mid = cut_sum(exchange([part0, part1, part2, part3], one), (sums, other_core(sums)))

time: 178 us -> 170 us (0.955)
  local copies, waits for them, and re-layouts: 12.3 us -> 5.73 us
  waiting for transfers between devices: 50.8 us -> 44.6 us
  starting transfers between devices: 32.9 us -> 36.2 us
    unnamed x48 -> x24, local copies, waits for them, and re-layouts: 12.3 us -> 5.73 us
    ppermute x19, waiting for transfers between devices: 44.9 us -> 38.9 us  [ring(): return lax.ppermute(piece, ALL, pairs)]
    pallas_call x2, Pallas kernels: 19.6 us -> 24.9 us  [grads(): pl.pallas_call(lambda *refs: grad_kernel(aheads, each, *refs), out_shape=...]
    pallas_call x1, Pallas kernels: 42.6 us -> 37.5 us  [project(): pl.pallas_call(lambda *refs: project_kernel(sources, *refs), out_shape=(j...]
    ppermute x19, starting transfers between devices: 30.8 us -> 34.3 us  [ring(): return lax.ppermute(piece, ALL, pairs)]
  transfers between devices with their start and end apart: 28 -> 28, of which waited for: 17 -> 17; matrix products, arithmetic and copies ran while one was open for 0% -> 0% of each run, Pallas kernels for 41% -> 43%
where the time goes in v8:
time: 170 us; the launch traced here: 168 us
  Pallas kernels  79.6 us (47%)
  waiting for transfers between devices  44.6 us (26%)
  starting transfers between devices  36.2 us (21%)
  local copies, waits for them, and re-layouts  5.73 us (3%)
    ppermute x19, waiting for transfers between devices, ring(): return lax.ppermute(piece, ALL, pairs)  38.9 us
    pallas_call x1, Pallas kernels, project(): pl.pallas_call(lambda *refs: project_kernel(sources, *refs), out_shape=(j...  37.5 us
    ppermute x19, starting transfers between devices, ring(): return lax.ppermute(piece, ALL, pairs)  34.3 us
    pallas_call x2, Pallas kernels, grads(): pl.pallas_call(lambda *refs: grad_kernel(aheads, each, *refs), out_shape=...  24.9 us
    pallas_call x2, Pallas kernels, norm(): pl.pallas_call(norm_kernel, out_shape=(jax.ShapeDtypeStruct((count, width...  7.57 us
    unnamed x24, local copies, waits for them, and re-layouts  5.73 us
    ppermute x9, waiting for transfers between devices, other_core(): return lax.ppermute(value, 'c', [(0, 1), (1, 0)])  5.7 us
    pallas_call x1, Pallas kernels, cut_sum(): pl.pallas_call(kernel, out_shape=[jax.ShapeDtypeStruct((each + 1, T, T),...  4.7 us
  transfers between devices with their start and end apart: 28, of which 17 were waited for; matrix products, arithmetic and copies ran while one was open for 0% of the time, Pallas kernels for 43%

profile of v8, /device:TPU:0, one launch (start us, length us, event | category | flops | bytes accessed | tf_op | source)
XLA Modules:
  0.0 168.0 jit_solution(14194001105334765770)
XLA Ops:
  1.2 2.0 %collective-permute-start = (bf16[16,128,128]{2,1,0:T(8,128)(2,1)}, bf16[16,128,128]{2,1,0:T(8,128)(2,1)S(1)}, u32[]{:S(2)}, u32[]{:S(2)}) collective-permute-start(bf16[16,128,128]{2,1,0:T(8,128)(2,1)} %refs_0_.4), channel_id=1, source_target_pairs={{0,8},{1,9},{2,10},{3,11},{4,36},{5,37},{6,38},{7,39},{8,16},{9,17... | collective-permute-start | bytes 1572872 | tf_op jit(solution)/shard_map/ppermute | solution.py:304
  3.2 3.6 %collective-permute-start.1 = (bf16[16,128,128]{2,1,0:T(8,128)(2,1)}, bf16[16,128,128]{2,1,0:T(8,128)(2,1)S(1)}, u32[]{:S(2)}, u32[]{:S(2)}) collective-permute-start(bf16[16,128,128]{2,1,0:T(8,128)(2,1)} %refs_0_.4), channel_id=1, source_target_pairs={{0,16},{1,17},{2,18},{3,19},{4,68},{5,69},{6,70},{7,71},{8,24},{9,... | collective-permute-start | bytes 1572872 | tf_op jit(solution)/shard_map/ppermute | solution.py:304
  6.8 1.0 collective-permute-start.2
  7.8 0.7 collective-permute-done.3.x_ref
  8.5 1.0 copy-done.11
  9.4 3.8 %norm.3 = (bf16[128,4096]{1,0:T(8,128)(2,1)}, bf16[32,128,128]{2,1,0:T(8,128)(2,1)}, f32[128,128]{1,0:T(8,128)}) custom-call(bf16[128,4096]{1,0:T(8,128)(2,1)} %copy-done.11, f32[1,4096]{1,0:T(1,128)} %bitcast.12), custom_call_target="tpu_custom_call" | custom-call | flops 1100000000 | tf_op jit(solution)/shard_map/norm/pallas_call | solution.py:66
  13.2 6.6 %collective-permute-done.1.refs_2_ = bf16[16,128,128]{2,1,0:T(8,128)(2,1)S(1)} collective-permute-done((bf16[16,128,128]{2,1,0:T(8,128)(2,1)}, bf16[16,128,128]{2,1,0:T(8,128)(2,1)S(1)}, u32[]{:S(2)}, u32[]{:S(2)}) %collective-permute-start.1) | collective-permute-done | bytes 524320 | tf_op jit(solution)/shard_map/ppermute | solution.py:304
  19.8 0.8 copy-done.4
  20.6 1.2 copy-done.1
  21.8 1.0 copy-done.5
  23.2 1.6 collective-permute-start.4
  24.9 1.7 collective-permute-start.5
  26.5 3.8 %norm.2 = (bf16[128,4096]{1,0:T(8,128)(2,1)}, bf16[32,128,128]{2,1,0:T(8,128)(2,1)}, f32[128,128]{1,0:T(8,128)}) custom-call(bf16[128,4096]{1,0:T(8,128)(2,1)} %refs_3_.1, f32[1,4096]{1,0:T(1,128)} %bitcast.13), custom_call_target="tpu_custom_call" | custom-call | flops 1100000000 | tf_op jit(solution)/shard_map/norm/pallas_call | solution.py:66
  30.3 0.6 pad_add_fusion.refs_2_.pos_ref
  30.9 16.3 %grads.2 = (bf16[64,128,128]{2,1,0:T(8,128)(2,1)}, bf16[64,128,128]{2,1,0:T(8,128)(2,1)}, bf16[64,128,128]{2,1,0:T(8,128)(2,1)}) custom-call(s32[512]{0:T(512)} %refs_0_.7, s32[512]{0:T(512)} %refs_1_.5, s32[4]{0:T(128)} %pad_add_fusion.refs_2_.pos_ref, bf16[32,128,128]{2,1,0:T(8,128)(2,1)} %get-tuple-element.37.refs_3_, ...), custom_call_target="tpu_custom_call" | custom-call | flops 2200000000 | tf_op jit(solution)/shard_map/grads/pallas_call | solution.py:126
  47.1 3.5 %collective-permute-done.4.left_ref.refs_0_ = bf16[64,128,128]{2,1,0:T(8,128)(2,1)} collective-permute-done((bf16[64,128,128]{2,1,0:T(8,128)(2,1)S(1)}, bf16[64,128,128]{2,1,0:T(8,128)(2,1)}, u32[]{:S(2)}, u32[]{:S(2)}) %collective-permute-start.4) | collective-permute-done | bytes 2097184 | tf_op jit(solution)/shard_map/ppermute | solution.py:304
  51.0 2.6 %relayed.1 = (bf16[32,128,128]{2,1,0:T(8,128)(2,1)}, bf16[32,128,128]{2,1,0:T(8,128)(2,1)}) custom-call(bf16[64,128,128]{2,1,0:T(8,128)(2,1)} %collective-permute-done.4.left_ref.refs_0_, bf16[64,128,128]{2,1,0:T(8,128)(2,1)} %collective-permute-done.5.right_ref.refs_1_, bf16[64,128,128]{2,1,0:T(8,128)(2,1)} %get-tuple-element.38.tie_ref.refs_7_), custom_call_target="tpu_custom_call" | custom-call | flops 1100000000 | tf_op jit(solution)/shard_map/relayed/pallas_call | solution.py:279
  53.6 0.5 collective-permute-start.11
  54.1 1.6 collective-permute-start.7
  55.7 1.7 collective-permute-start.8
  57.3 8.6 %grads.3 = (bf16[64,128,128]{2,1,0:T(8,128)(2,1)}, bf16[64,128,128]{2,1,0:T(8,128)(2,1)}, bf16[64,128,128]{2,1,0:T(8,128)(2,1)}, bf16[64,128,128]{2,1,0:T(8,128)(2,1)}) custom-call(s32[512]{0:T(512)} %refs_0_.7, s32[512]{0:T(512)} %refs_1_.5, s32[4]{0:T(128)} %pad_add_fusion.refs_2_.pos_ref, ...), custom_call_target="tpu_custom_call", output_to_operand_aliasing={{0}: (7, {}), {1}: (8, {}), {2}: (9, {})} | custom-call | flops 2200000000 | tf_op jit(solution)/shard_map/grads/pallas_call | solution.py:126
  65.9 1.5 collective-permute-start.14
  67.4 3.6 %collective-permute-done.7.refs_0_ = bf16[32,128,128]{2,1,0:T(8,128)(2,1)S(1)} collective-permute-done((bf16[32,128,128]{2,1,0:T(8,128)(2,1)}, bf16[32,128,128]{2,1,0:T(8,128)(2,1)S(1)}, u32[]{:S(2)}, u32[]{:S(2)}) %collective-permute-start.7) | collective-permute-done | bytes 1048608 | tf_op jit(solution)/shard_map/ppermute | solution.py:304
  71.1 3.0 %collective-permute-start.15 = (bf16[64,128,128]{2,1,0:T(8,128)(2,1)}, bf16[64,128,128]{2,1,0:T(8,128)(2,1)}, u32[]{:S(2)}, u32[]{:S(2)}) collective-permute-start(bf16[64,128,128]{2,1,0:T(8,128)(2,1)} %get-tuple-element.52), channel_id=1, source_target_pairs={{0,2},{1,3},{2,0},{3,1},{4,68},{5,69},{6,70},{7,71},{8,10},{9,11},... | collective-permute-start | bytes 6291464 | tf_op jit(solution)/shard_map/ppermute | solution.py:304
  74.1 1.1 collective-permute-start.16
  75.9 2.4 %collective-permute-done.12.refs_16_ = bf16[32,128,128]{2,1,0:T(8,128)(2,1)S(1)} collective-permute-done((bf16[32,128,128]{2,1,0:T(8,128)(2,1)}, bf16[32,128,128]{2,1,0:T(8,128)(2,1)S(1)}, u32[]{:S(2)}, u32[]{:S(2)}) %collective-permute-start.12) | collective-permute-done | bytes 1048608 | tf_op jit(solution)/shard_map/ppermute | solution.py:405
  78.2 1.5 collective-permute-done.13.refs_17_
  79.7 1.0 copy-done.10
  80.7 37.5 %project.1 = (bf16[128,14336]{1,0:T(8,128)(2,1)}, bf16[128,4096]{1,0:T(8,128)(2,1)}, f32[32,128]{1,0:T(8,128)}) custom-call(s32[512]{0:T(512)} %refs_0_.7, s32[512]{0:T(512)} %refs_1_.5, s32[4]{0:T(128)} %pad_add_fusion.refs_2_.pos_ref, bf16[128,4096]{1,0:T(8,128)(2,1)} %refs_3_.1, bf16[128,4096]{1,0:T(8,128)(2,1)} %get-tuple-element.34.refs_4_, ...), custom_call_target="tpu_custom_call" | custom-call | flops 2200000000 | tf_op jit(solution)/shard_map/project/pallas_call | solution.py:216
  118.4 3.1 %collective-permute-done.16.refs_3_ = bf16[64,128,128]{2,1,0:T(8,128)(2,1)} collective-permute-done((bf16[64,128,128]{2,1,0:T(8,128)(2,1)}, bf16[64,128,128]{2,1,0:T(8,128)(2,1)}, u32[]{:S(2)}, u32[]{:S(2)}) %collective-permute-start.16) | collective-permute-done | bytes 2097184 | tf_op jit(solution)/shard_map/ppermute | solution.py:304
  121.5 0.7 copy-done.6
  122.3 4.7 %cut_sum.1 = (bf16[17,128,128]{2,1,0:T(8,128)(2,1)S(1)}, bf16[17,128,128]{2,1,0:T(8,128)(2,1)S(1)}, bf16[17,128,128]{2,1,0:T(8,128)(2,1)S(1)}, bf16[17,128,128]{2,1,0:T(8,128)(2,1)S(1)}) custom-call(bf16[64,128,128]{2,1,0:T(8,128)(2,1)S(1)} %copy-done, bf16[64,128,128]{2,1,0:T(8,128)(2,1)} %collective-permute-done.14.refs_1_, ...), custom_call_target="tpu_custom_call" | custom-call | flops 1100000000 | tf_op jit(solution)/shard_map/cut_sum/pallas_call | solution.py:347
  127.4 2.8 %collective-permute-start.19 = (bf16[17,128,128]{2,1,0:T(8,128)(2,1)S(1)}, bf16[17,128,128]{2,1,0:T(8,128)(2,1)S(1)}, u32[]{:S(2)}, u32[]{:S(2)}) collective-permute-start(bf16[17,128,128]{2,1,0:T(8,128)(2,1)S(1)} %get-tuple-element.56), channel_id=1, source_target_pairs={{0,64},{1,65},{2,66},{3,67},{4,20},{5,21},{6,22},{7,23},{8,72},{9,... | collective-permute-start | bytes 1671176 | tf_op jit(solution)/shard_map/ppermute | solution.py:304
  130.2 1.2 collective-permute-start.20
  131.3 12.4 %collective-permute-done.18.refs_1_ = bf16[17,128,128]{2,1,0:T(8,128)(2,1)S(1)} collective-permute-done((bf16[17,128,128]{2,1,0:T(8,128)(2,1)S(1)}, bf16[17,128,128]{2,1,0:T(8,128)(2,1)S(1)}, u32[]{:S(2)}, u32[]{:S(2)}) %collective-permute-start.18) | collective-permute-done | bytes 557088 | tf_op jit(solution)/shard_map/ppermute | solution.py:304
  143.7 0.9 collective-permute-done.20.refs_3_
  145.0 2.7 %collective-permute-start.21 = (bf16[5,128,128]{2,1,0:T(8,128)(2,1)S(1)}, bf16[5,128,128]{2,1,0:T(8,128)(2,1)S(1)}, u32[]{:S(2)}, u32[]{:S(2)}) collective-permute-start(bf16[5,128,128]{2,1,0:T(8,128)(2,1)S(1)} %get-tuple-element.59), channel_id=1, source_target_pairs={{0,8},{1,9},{2,10},{3,11},{4,5},{5,6},{6,7},{7,4},{8,16},{9,17},{1... | collective-permute-start | bytes 491528 | tf_op jit(solution)/shard_map/ppermute | solution.py:304
  147.7 2.1 %collective-permute-start.22 = (bf16[5,128,128]{2,1,0:T(8,128)(2,1)S(1)}, bf16[5,128,128]{2,1,0:T(8,128)(2,1)S(1)}, u32[]{:S(2)}, u32[]{:S(2)}) collective-permute-start(bf16[5,128,128]{2,1,0:T(8,128)(2,1)S(1)} %get-tuple-element.60), channel_id=1, source_target_pairs={{0,16},{1,17},{2,18},{3,19},{4,6},{5,7},{6,4},{7,5},{8,24},{9,25},... | collective-permute-start | bytes 491528 | tf_op jit(solution)/shard_map/ppermute | solution.py:304
  149.8 1.6 collective-permute-start.23
  151.6 3.2 %collective-permute-done.22.refs_2_ = bf16[5,128,128]{2,1,0:T(8,128)(2,1)S(1)} collective-permute-done((bf16[5,128,128]{2,1,0:T(8,128)(2,1)S(1)}, bf16[5,128,128]{2,1,0:T(8,128)(2,1)S(1)}, u32[]{:S(2)}, u32[]{:S(2)}) %collective-permute-start.22) | collective-permute-done | bytes 163872 | tf_op jit(solution)/shard_map/ppermute | solution.py:304
  155.2 1.4 collective-permute-start.24
  156.6 2.7 %collective-permute-start.25 = (bf16[5,128,128]{2,1,0:T(8,128)(2,1)S(1)}, bf16[5,128,128]{2,1,0:T(8,128)(2,1)S(1)}, u32[]{:S(2)}, u32[]{:S(2)}) collective-permute-start(bf16[5,128,128]{2,1,0:T(8,128)(2,1)S(1)} %next_sum.3.refs_0_), channel_id=1, source_target_pairs={{0,2},{1,3},{2,0},{3,1},{4,6},{5,7},{6,4},{7,5},{8,10},{9,11},{10,... | collective-permute-start | bytes 491528 | tf_op jit(solution)/shard_map/ppermute | solution.py:304
  159.3 0.5 collective-permute-start.26
  159.9 1.9 %collective-permute-done.24.refs_1_ = bf16[5,128,128]{2,1,0:T(8,128)(2,1)S(1)} collective-permute-done((bf16[5,128,128]{2,1,0:T(8,128)(2,1)S(1)}, bf16[5,128,128]{2,1,0:T(8,128)(2,1)S(1)}, u32[]{:S(2)}, u32[]{:S(2)}) %collective-permute-start.24) | collective-permute-done | bytes 163872 | tf_op jit(solution)/shard_map/ppermute | solution.py:304
  161.8 2.6 %collective-permute-done.25.refs_2_ = bf16[5,128,128]{2,1,0:T(8,128)(2,1)S(1)} collective-permute-done((bf16[5,128,128]{2,1,0:T(8,128)(2,1)S(1)}, bf16[5,128,128]{2,1,0:T(8,128)(2,1)S(1)}, u32[]{:S(2)}, u32[]{:S(2)}) %collective-permute-start.25) | collective-permute-done | bytes 163872 | tf_op jit(solution)/shard_map/ppermute | solution.py:304
  164.7 1.6 place.1
  166.2 1.2 collective-permute-done.27
  167.4 0.6 select_bitcast_fusion
  (47 shorter events, 3.7 us)
Async XLA Ops:
  0.6 20.0 %copy-start.3 = (bf16[16,128,128]{2,1,0:T(8,128)(2,1)S(1)}, bf16[16,128,128]{2,1,0:T(8,128)(2,1)}, u32[]{:S(2)}) copy-start(bf16[16,128,128]{2,1,0:T(8,128)(2,1)} %refs_0_.4) | copy-start | bytes 1572868
  0.6 30.2 %collective-permute-start.6 = (bf16[128,14336]{1,0:T(8,128)(2,1)}, bf16[128,14336]{1,0:T(8,128)(2,1)}, u32[]{:S(2)}, u32[]{:S(2)}) collective-permute-start(bf16[128,14336]{1,0:T(8,128)(2,1)} %refs_7_.1), channel_id=1, source_target_pairs={{0,4},{4,0},{1,5},{5,1},{2,6},{6,2},{3,7},{7,3},{8,12},{12,8},{9,1... | collective-permute-start | bytes 11010056 | tf_op jit(solution)/shard_map/ppermute | solution.py:405
  0.7 7.7 %collective-permute-start.3 = (bf16[128,4096]{1,0:T(8,128)(2,1)}, bf16[128,4096]{1,0:T(8,128)(2,1)S(1)}, u32[]{:S(2)}, u32[]{:S(2)}) collective-permute-start(bf16[128,4096]{1,0:T(8,128)(2,1)} %refs_3_.1), channel_id=1, source_target_pairs={{0,4},{4,0},{1,5},{5,1},{2,6},{6,2},{3,7},{7,3},{8,12},{12,8},{9,1... | collective-permute-start | bytes 3145736 | tf_op jit(solution)/shard_map/ppermute | solution.py:405
  1.2 12.0 %collective-permute-start = (bf16[16,128,128]{2,1,0:T(8,128)(2,1)}, bf16[16,128,128]{2,1,0:T(8,128)(2,1)S(1)}, u32[]{:S(2)}, u32[]{:S(2)}) collective-permute-start(bf16[16,128,128]{2,1,0:T(8,128)(2,1)} %refs_0_.4), channel_id=1, source_target_pairs={{0,8},{1,9},{2,10},{3,11},{4,36},{5,37},{6,38},{7,39},{8,16},{9,17... | collective-permute-start | bytes 1572872 | tf_op jit(solution)/shard_map/ppermute | solution.py:304
  3.2 16.6 %collective-permute-start.1 = (bf16[16,128,128]{2,1,0:T(8,128)(2,1)}, bf16[16,128,128]{2,1,0:T(8,128)(2,1)S(1)}, u32[]{:S(2)}, u32[]{:S(2)}) collective-permute-start(bf16[16,128,128]{2,1,0:T(8,128)(2,1)} %refs_0_.4), channel_id=1, source_target_pairs={{0,16},{1,17},{2,18},{3,19},{4,68},{5,69},{6,70},{7,71},{8,24},{9,... | collective-permute-start | bytes 1572872 | tf_op jit(solution)/shard_map/ppermute | solution.py:304
  6.8 13.0 %collective-permute-start.2 = (bf16[16,128,128]{2,1,0:T(8,128)(2,1)}, bf16[16,128,128]{2,1,0:T(8,128)(2,1)S(1)}, u32[]{:S(2)}, u32[]{:S(2)}) collective-permute-start(bf16[16,128,128]{2,1,0:T(8,128)(2,1)} %refs_0_.4), channel_id=1, source_target_pairs={{0,24},{1,25},{2,26},{3,27},{4,100},{5,101},{6,102},{7,103},{8,0},... | collective-permute-start | bytes 1572872 | tf_op jit(solution)/shard_map/ppermute | solution.py:304
  8.5 1.0 copy-start.11
  19.8 0.8 copy-start.4
  20.6 1.2 copy-start.1
  21.8 1.0 copy-start.5
  23.2 23.9 %copy-start.2 = (bf16[4,16,128,128]{3,2,1,0:T(8,128)(2,1)}, bf16[4,16,128,128]{3,2,1,0:T(8,128)(2,1)S(1)}, u32[]{:S(2)}) copy-start(bf16[4,16,128,128]{3,2,1,0:T(8,128)(2,1)S(1)} %joined.1) | copy-start | bytes 6291460
  23.2 27.4 %collective-permute-start.4 = (bf16[64,128,128]{2,1,0:T(8,128)(2,1)S(1)}, bf16[64,128,128]{2,1,0:T(8,128)(2,1)}, u32[]{:S(2)}, u32[]{:S(2)}) collective-permute-start(bf16[64,128,128]{2,1,0:T(8,128)(2,1)S(1)} %bitcast.8), channel_id=1, source_target_pairs={{0,32},{1,33},{2,34},{3,35},{4,12},{5,13},{6,14},{7,15},{8,40},{9,... | collective-permute-start | bytes 6291464 | tf_op jit(solution)/shard_map/ppermute | solution.py:304
  24.9 26.1 %collective-permute-start.5 = (bf16[64,128,128]{2,1,0:T(8,128)(2,1)S(1)}, bf16[64,128,128]{2,1,0:T(8,128)(2,1)}, u32[]{:S(2)}, u32[]{:S(2)}) collective-permute-start(bf16[64,128,128]{2,1,0:T(8,128)(2,1)S(1)} %bitcast.9), channel_id=1, source_target_pairs={{0,96},{1,97},{2,98},{3,99},{4,28},{5,29},{6,30},{7,31},{8,104},{9... | collective-permute-start | bytes 6291464 | tf_op jit(solution)/shard_map/ppermute | solution.py:304
  26.5 39.4 %collective-permute-start.9 = (bf16[64,128,128]{2,1,0:T(8,128)(2,1)S(1)}, bf16[64,128,128]{2,1,0:T(8,128)(2,1)}, u32[]{:S(2)}, u32[]{:S(2)}) collective-permute-start(bf16[64,128,128]{2,1,0:T(8,128)(2,1)S(1)} %bitcast.10), channel_id=1, source_target_pairs={{0,4},{4,0},{1,5},{5,1},{2,6},{6,2},{3,7},{7,3},{8,12},{12,8},{9,1... | collective-permute-start | bytes 6291464 | tf_op jit(solution)/shard_map/ppermute | solution.py:405
  53.6 21.7 %collective-permute-start.10 = (bf16[64,128,128]{2,1,0:T(8,128)(2,1)}, bf16[64,128,128]{2,1,0:T(8,128)(2,1)}, u32[]{:S(2)}, u32[]{:S(2)}) collective-permute-start(bf16[64,128,128]{2,1,0:T(8,128)(2,1)} %get-tuple-element.40.refs_9_), channel_id=1, source_target_pairs={{0,4},{4,0},{1,5},{5,1},{2,6},{6,2},{3,7},{7,3},{8,12},{12,8},{9,1... | collective-permute-start | bytes 6291464 | tf_op jit(solution)/shard_map/ppermute | solution.py:405
  53.6 21.7 %collective-permute-start.11 = (bf16[64,128,128]{2,1,0:T(8,128)(2,1)}, bf16[64,128,128]{2,1,0:T(8,128)(2,1)}, u32[]{:S(2)}, u32[]{:S(2)}) collective-permute-start(bf16[64,128,128]{2,1,0:T(8,128)(2,1)} %get-tuple-element.41.refs_10_), channel_id=1, source_target_pairs={{0,4},{4,0},{1,5},{5,1},{2,6},{6,2},{3,7},{7,3},{8,12},{12,8},{9,1... | collective-permute-start | bytes 6291464 | tf_op jit(solution)/shard_map/ppermute | solution.py:405
  54.1 17.0 %collective-permute-start.7 = (bf16[32,128,128]{2,1,0:T(8,128)(2,1)}, bf16[32,128,128]{2,1,0:T(8,128)(2,1)S(1)}, u32[]{:S(2)}, u32[]{:S(2)}) collective-permute-start(bf16[32,128,128]{2,1,0:T(8,128)(2,1)} %get-tuple-element.39.refs_2_.refs_10_), channel_id=1, source_target_pairs={{0,32},{1,33},{2,34},{3,35},{4,12},{5,13},{6,14},{7,15},{8,40},{9,... | collective-permute-start | bytes 3145736 | tf_op jit(solution)/shard_map/ppermute | solution.py:304
  55.7 18.4 %collective-permute-start.8 = (bf16[32,128,128]{2,1,0:T(8,128)(2,1)}, bf16[32,128,128]{2,1,0:T(8,128)(2,1)}, u32[]{:S(2)}, u32[]{:S(2)}) collective-permute-start(bf16[32,128,128]{2,1,0:T(8,128)(2,1)} %get-tuple-element.42), channel_id=1, source_target_pairs={{0,96},{1,97},{2,98},{3,99},{4,28},{5,29},{6,30},{7,31},{8,104},{9... | collective-permute-start | bytes 3145736 | tf_op jit(solution)/shard_map/ppermute | solution.py:304
  65.9 52.5 %collective-permute-start.14 = (bf16[64,128,128]{2,1,0:T(8,128)(2,1)}, bf16[64,128,128]{2,1,0:T(8,128)(2,1)}, u32[]{:S(2)}, u32[]{:S(2)}) collective-permute-start(bf16[64,128,128]{2,1,0:T(8,128)(2,1)} %get-tuple-element.51), channel_id=1, source_target_pairs={{0,1},{1,2},{2,3},{3,0},{4,36},{5,37},{6,38},{7,39},{8,9},{9,10},{... | collective-permute-start | bytes 6291464 | tf_op jit(solution)/shard_map/ppermute | solution.py:304
  71.1 4.2 %copy-start.8 = (bf16[32,128,128]{2,1,0:T(8,128)(2,1)}, bf16[32,128,128]{2,1,0:T(8,128)(2,1)S(1)}, u32[]{:S(2)}) copy-start(bf16[32,128,128]{2,1,0:T(8,128)(2,1)S(1)} %collective-permute-done.7.refs_0_) | copy-start | bytes 3145732
  71.1 47.4 %collective-permute-start.15 = (bf16[64,128,128]{2,1,0:T(8,128)(2,1)}, bf16[64,128,128]{2,1,0:T(8,128)(2,1)}, u32[]{:S(2)}, u32[]{:S(2)}) collective-permute-start(bf16[64,128,128]{2,1,0:T(8,128)(2,1)} %get-tuple-element.52), channel_id=1, source_target_pairs={{0,2},{1,3},{2,0},{3,1},{4,68},{5,69},{6,70},{7,71},{8,10},{9,11},... | collective-permute-start | bytes 6291464 | tf_op jit(solution)/shard_map/ppermute | solution.py:304
  74.1 47.4 %collective-permute-start.16 = (bf16[64,128,128]{2,1,0:T(8,128)(2,1)}, bf16[64,128,128]{2,1,0:T(8,128)(2,1)}, u32[]{:S(2)}, u32[]{:S(2)}) collective-permute-start(bf16[64,128,128]{2,1,0:T(8,128)(2,1)} %get-tuple-element.45.refs_2_), channel_id=1, source_target_pairs={{0,3},{1,0},{2,1},{3,2},{4,100},{5,101},{6,102},{7,103},{8,11},{9,... | collective-permute-start | bytes 6291464 | tf_op jit(solution)/shard_map/ppermute | solution.py:304
  75.3 3.0 %collective-permute-start.12 = (bf16[32,128,128]{2,1,0:T(8,128)(2,1)}, bf16[32,128,128]{2,1,0:T(8,128)(2,1)S(1)}, u32[]{:S(2)}, u32[]{:S(2)}) collective-permute-start(bf16[32,128,128]{2,1,0:T(8,128)(2,1)} %get-tuple-element.46.refs_11_), channel_id=1, source_target_pairs={{0,4},{4,0},{1,5},{5,1},{2,6},{6,2},{3,7},{7,3},{8,12},{12,8},{9,1... | collective-permute-start | bytes 3145736 | tf_op jit(solution)/shard_map/ppermute | solution.py:405
  75.4 4.4 %collective-permute-start.13 = (bf16[32,128,128]{2,1,0:T(8,128)(2,1)}, bf16[32,128,128]{2,1,0:T(8,128)(2,1)S(1)}, u32[]{:S(2)}, u32[]{:S(2)}) collective-permute-start(bf16[32,128,128]{2,1,0:T(8,128)(2,1)} %get-tuple-element.47.refs_12_), channel_id=1, source_target_pairs={{0,4},{4,0},{1,5},{5,1},{2,6},{6,2},{3,7},{7,3},{8,12},{12,8},{9,1... | collective-permute-start | bytes 3145736 | tf_op jit(solution)/shard_map/ppermute | solution.py:405
  78.2 2.5 %copy-start.9 = (bf16[32,128,128]{2,1,0:T(8,128)(2,1)}, bf16[32,128,128]{2,1,0:T(8,128)(2,1)S(1)}, u32[]{:S(2)}) copy-start(bf16[32,128,128]{2,1,0:T(8,128)(2,1)S(1)} %collective-permute-done.12.refs_16_) | copy-start | bytes 3145732
  79.7 1.0 copy-start.10
  80.7 40.9 %copy-start = (bf16[64,128,128]{2,1,0:T(8,128)(2,1)S(1)}, bf16[64,128,128]{2,1,0:T(8,128)(2,1)}, u32[]{:S(2)}) copy-start(bf16[64,128,128]{2,1,0:T(8,128)(2,1)} %get-tuple-element.50.refs_0_) | copy-start | bytes 6291460
  118.2 3.3 %collective-permute-start.17 = (f32[32,128]{1,0:T(8,128)}, f32[32,128]{1,0:T(8,128)S(1)}, u32[]{:S(2)}, u32[]{:S(2)}) collective-permute-start(f32[32,128]{1,0:T(8,128)} %get-tuple-element.53.refs_4_), channel_id=1, source_target_pairs={{0,4},{4,0},{1,5},{5,1},{2,6},{6,2},{3,7},{7,3},{8,12},{12,8},{9,1... | collective-permute-start | bytes 49160 | tf_op jit(solution)/shard_map/ppermute | solution.py:405
  121.5 0.7 copy-start.6
  127.0 16.8 %collective-permute-start.18 = (bf16[17,128,128]{2,1,0:T(8,128)(2,1)S(1)}, bf16[17,128,128]{2,1,0:T(8,128)(2,1)S(1)}, u32[]{:S(2)}, u32[]{:S(2)}) collective-permute-start(bf16[17,128,128]{2,1,0:T(8,128)(2,1)S(1)} %get-tuple-element.55), channel_id=1, source_target_pairs={{0,32},{1,33},{2,34},{3,35},{4,12},{5,13},{6,14},{7,15},{8,40},{9,... | collective-permute-start | bytes 1671176 | tf_op jit(solution)/shard_map/ppermute | solution.py:304
  127.4 16.4 %collective-permute-start.19 = (bf16[17,128,128]{2,1,0:T(8,128)(2,1)S(1)}, bf16[17,128,128]{2,1,0:T(8,128)(2,1)S(1)}, u32[]{:S(2)}, u32[]{:S(2)}) collective-permute-start(bf16[17,128,128]{2,1,0:T(8,128)(2,1)S(1)} %get-tuple-element.56), channel_id=1, source_target_pairs={{0,64},{1,65},{2,66},{3,67},{4,20},{5,21},{6,22},{7,23},{8,72},{9,... | collective-permute-start | bytes 1671176 | tf_op jit(solution)/shard_map/ppermute | solution.py:304
  130.2 14.5 %collective-permute-start.20 = (bf16[17,128,128]{2,1,0:T(8,128)(2,1)S(1)}, bf16[17,128,128]{2,1,0:T(8,128)(2,1)S(1)}, u32[]{:S(2)}, u32[]{:S(2)}) collective-permute-start(bf16[17,128,128]{2,1,0:T(8,128)(2,1)S(1)} %get-tuple-element.57), channel_id=1, source_target_pairs={{0,96},{1,97},{2,98},{3,99},{4,28},{5,29},{6,30},{7,31},{8,104},{9... | collective-permute-start | bytes 1671176 | tf_op jit(solution)/shard_map/ppermute | solution.py:304
  144.9 19.7 %copy-start.7 = (s32[4]{0:T(128)S(1)}, s32[4]{0:T(128)}, u32[]{:S(2)}) copy-start(s32[4]{0:T(128)} %pad_add_fusion.refs_2_.pos_ref) | copy-start | bytes 52
  145.0 6.6 %collective-permute-start.21 = (bf16[5,128,128]{2,1,0:T(8,128)(2,1)S(1)}, bf16[5,128,128]{2,1,0:T(8,128)(2,1)S(1)}, u32[]{:S(2)}, u32[]{:S(2)}) collective-permute-start(bf16[5,128,128]{2,1,0:T(8,128)(2,1)S(1)} %get-tuple-element.59), channel_id=1, source_target_pairs={{0,8},{1,9},{2,10},{3,11},{4,5},{5,6},{6,7},{7,4},{8,16},{9,17},{1... | collective-permute-start | bytes 491528 | tf_op jit(solution)/shard_map/ppermute | solution.py:304
  147.7 7.2 %collective-permute-start.22 = (bf16[5,128,128]{2,1,0:T(8,128)(2,1)S(1)}, bf16[5,128,128]{2,1,0:T(8,128)(2,1)S(1)}, u32[]{:S(2)}, u32[]{:S(2)}) collective-permute-start(bf16[5,128,128]{2,1,0:T(8,128)(2,1)S(1)} %get-tuple-element.60), channel_id=1, source_target_pairs={{0,16},{1,17},{2,18},{3,19},{4,6},{5,7},{6,4},{7,5},{8,24},{9,25},... | collective-permute-start | bytes 491528 | tf_op jit(solution)/shard_map/ppermute | solution.py:304
  149.8 5.3 %collective-permute-start.23 = (bf16[5,128,128]{2,1,0:T(8,128)(2,1)S(1)}, bf16[5,128,128]{2,1,0:T(8,128)(2,1)S(1)}, u32[]{:S(2)}, u32[]{:S(2)}) collective-permute-start(bf16[5,128,128]{2,1,0:T(8,128)(2,1)S(1)} %get-tuple-element.61), channel_id=1, source_target_pairs={{0,24},{1,25},{2,26},{3,27},{4,7},{5,4},{6,5},{7,6},{8,0},{9,1},{1... | collective-permute-start | bytes 491528 | tf_op jit(solution)/shard_map/ppermute | solution.py:304
  155.2 6.6 %collective-permute-start.24 = (bf16[5,128,128]{2,1,0:T(8,128)(2,1)S(1)}, bf16[5,128,128]{2,1,0:T(8,128)(2,1)S(1)}, u32[]{:S(2)}, u32[]{:S(2)}) collective-permute-start(bf16[5,128,128]{2,1,0:T(8,128)(2,1)S(1)} %next_sum.3.refs_0_), channel_id=1, source_target_pairs={{0,1},{1,2},{2,3},{3,0},{4,5},{5,6},{6,7},{7,4},{8,9},{9,10},{10,1... | collective-permute-start | bytes 491528 | tf_op jit(solution)/shard_map/ppermute | solution.py:304
  156.6 7.8 %collective-permute-start.25 = (bf16[5,128,128]{2,1,0:T(8,128)(2,1)S(1)}, bf16[5,128,128]{2,1,0:T(8,128)(2,1)S(1)}, u32[]{:S(2)}, u32[]{:S(2)}) collective-permute-start(bf16[5,128,128]{2,1,0:T(8,128)(2,1)S(1)} %next_sum.3.refs_0_), channel_id=1, source_target_pairs={{0,2},{1,3},{2,0},{3,1},{4,6},{5,7},{6,4},{7,5},{8,10},{9,11},{10,... | collective-permute-start | bytes 491528 | tf_op jit(solution)/shard_map/ppermute | solution.py:304
  159.3 5.3 %collective-permute-start.26 = (bf16[5,128,128]{2,1,0:T(8,128)(2,1)S(1)}, bf16[5,128,128]{2,1,0:T(8,128)(2,1)S(1)}, u32[]{:S(2)}, u32[]{:S(2)}) collective-permute-start(bf16[5,128,128]{2,1,0:T(8,128)(2,1)S(1)} %next_sum.3.refs_0_), channel_id=1, source_target_pairs={{0,3},{1,0},{2,1},{3,2},{4,7},{5,4},{6,5},{7,6},{8,11},{9,8},{10,9... | collective-permute-start | bytes 491528 | tf_op jit(solution)/shard_map/ppermute | solution.py:304
  166.2 1.2 collective-permute-start.27

commit v9 on v8

--- a/solution.py
+++ b/solution.py
@@ -238,23 +238,34 @@
     )(rows, cols, pos, *resident, *arrays)
 
 
-def joined(pieces, tie):
+def moved(plan, shapes, values, ties, name):
+    def kernel(*refs):
+        outs, sem = refs[-1 - len(shapes) : -1], refs[-1]
+        copies = [
+            pltpu.make_async_copy(refs[v].at[pl.ds(i, n)], outs[o].at[pl.ds(j, n)], sem.at[k])
+            for k, (v, i, o, j, n) in enumerate(plan)
+        ]
+        for copy in copies:
+            copy.start()
+        for copy in copies:
+            copy.wait()
+
+    return pl.pallas_call(
+        kernel,
+        out_shape=[jax.ShapeDtypeStruct(shape, BF) for shape in shapes],
+        in_specs=[ANY] * (len(values) + len(ties)),
+        out_specs=[ANY] * len(shapes),
+        scratch_shapes=[pltpu.SemaphoreType.DMA((len(plan),))],
+        compiler_params=params(60),
+        cost_estimate=cost(1, 0),
+        name=name,
+    )(*values, *ties)
+
+
+def joined(pieces, *ties):
     each = pieces[0].shape[0]
-
-    def kernel(*refs):
-        for j in range(4):
-            refs[-1][j] = refs[j][...]
-
-    return pl.pallas_call(
-        kernel,
-        out_shape=jax.ShapeDtypeStruct((4, each, T, T), BF),
-        grid=(4,),
-        in_specs=[pl.BlockSpec((each // 4, T, T), lambda i: (i, 0, 0))] * 4 + [ANY],
-        out_specs=pl.BlockSpec((4, each // 4, T, T), lambda i: (0, i, 0, 0)),
-        compiler_params=params(32),
-        cost_estimate=cost(1, 0),
-        name="joined",
-    )(*pieces, tie).reshape(4 * each, T, T)
+    plan = [(j, 0, 0, j * each, each) for j in range(4)]
+    return moved(plan, [(4 * each, T, T)], pieces, ties, "joined")[0]
 
 
 def held(values, *ties):
@@ -271,25 +282,8 @@
 
 def relayed(left, right, tie):
     half = left.shape[0] // 2
-
-    def kernel(left_ref, right_ref, tie_ref, left_out, right_out):
-        left_out[...] = left_ref[...]
-        right_out[...] = right_ref[...]
-
-    return pl.pallas_call(
-        kernel,
-        out_shape=[jax.ShapeDtypeStruct((half, T, T), BF)] * 2,
-        grid=(2,),
-        in_specs=[
-            pl.BlockSpec((half // 2, T, T), lambda i: (i, 0, 0)),
-            pl.BlockSpec((half // 2, T, T), lambda i: (2 + i, 0, 0)),
-            ANY,
-        ],
-        out_specs=[pl.BlockSpec((half // 2, T, T), lambda i: (i, 0, 0))] * 2,
-        compiler_params=params(60),
-        cost_estimate=cost(1, 0),
-        name="relayed",
-    )(left, right, tie)
+    plan = [(0, 0, 0, 0, half), (1, half, 1, 0, half)]
+    return moved(plan, [(half, T, T)] * 2, (left, right), (tie,), "relayed")
 
 
 def ring(piece, axes, shift):
@@ -407,16 +401,16 @@
     tokens_other, g_other = other_core(tokens), other_core(cotangent)
     normed, turned, scale = norm(tokens, gain2)
     _, turned_other, _ = norm(tokens_other, gain2)
-    line = joined(exchange([tiles] * 4, first), turned_other)
+    line = joined(exchange([tiles] * 4, first), turned, turned_other)
     left, right = ring(line, second, 1), ring(line, second, 3)
     operands = (rows, cols, pos, turned, turned_other, cotangent, g_other)
-    part0, part2, part1 = grads((0, 2, 1), *operands)
-    left_half, right_half = relayed(left, right, part0)
+    parts = grads((0, 2, 1, 3), *operands)
+    left_half, right_half = relayed(left, right, parts[0])
     left, right = held((left, right), left_half)
-    part0, part2, part1, part3 = grads((3,), *operands, (part0, part2, part1), (left_half,))
+    part0, part2, part1, part3 = held(parts, left_half)
     near = [line, left, right]
     swapped = [other_core(block) for block in near]
-    far = held((ring(left_half, second, 1), ring(right_half, second, 3)), part3, *swapped)
+    far = held((ring(left_half, second, 1), ring(right_half, second, 3)), *swapped)
     arrays = near + list(far) + swapped + [other_core(block) for block in far]
     projected, token_grad, sums = project(rows, cols, pos, arrays, tokens, normed, scale, gain2, cotangent)
     count = sums.shape[0]

time: 170 us -> 306 us (1.80)
  Pallas kernels: 79.6 us -> 201 us
  waiting for transfers between devices: 44.6 us -> 63.4 us
  starting transfers between devices: 36.2 us -> 32.5 us
    pallas_call x2, Pallas kernels: 2.91 us -> 129 us  [moved(): pl.pallas_call(kernel, out_shape=[jax.ShapeDtypeStruct(shape, BF) for sha...]
    ppermute x19, waiting for transfers between devices: 38.9 us -> 57.1 us  [ring(): return lax.ppermute(piece, ALL, pairs)]
    pallas_call x2 -> x1, Pallas kernels: 24.9 us -> 20.4 us  [grads(): pl.pallas_call(lambda *refs: grad_kernel(aheads, each, *refs), out_shape=...]
    ppermute x19, starting transfers between devices: 34.3 us -> 30.6 us  [ring(): return lax.ppermute(piece, ALL, pairs)]
  transfers between devices with their start and end apart: 28 -> 28, of which waited for: 17 -> 18; matrix products, arithmetic and copies ran while one was open for 0% -> 0% of each run, Pallas kernels for 43% -> 64%
where the time goes in v9:
time: 306 us; the launch traced here: 304 us
  Pallas kernels  201 us (66%)
  waiting for transfers between devices  63.4 us (21%)
  starting transfers between devices  32.5 us (11%)
  local copies, waits for them, and re-layouts  4.87 us (2%)
    pallas_call x2, Pallas kernels, moved(): pl.pallas_call(kernel, out_shape=[jax.ShapeDtypeStruct(shape, BF) for sha...  129 us
    ppermute x19, waiting for transfers between devices, ring(): return lax.ppermute(piece, ALL, pairs)  57.1 us
    pallas_call x1, Pallas kernels, project(): pl.pallas_call(lambda *refs: project_kernel(sources, *refs), out_shape=(j...  37.5 us
    ppermute x19, starting transfers between devices, ring(): return lax.ppermute(piece, ALL, pairs)  30.6 us
    pallas_call x1, Pallas kernels, grads(): pl.pallas_call(lambda *refs: grad_kernel(aheads, each, *refs), out_shape=...  20.4 us
    pallas_call x2, Pallas kernels, norm(): pl.pallas_call(norm_kernel, out_shape=(jax.ShapeDtypeStruct((count, width...  7.57 us
    ppermute x9, waiting for transfers between devices, other_core(): return lax.ppermute(value, 'c', [(0, 1), (1, 0)])  6.29 us
  transfers between devices with their start and end apart: 28, of which 18 were waited for; matrix products, arithmetic and copies ran while one was open for 0% of the time, Pallas kernels for 64%

profile of v9, /device:TPU:0, one launch (start us, length us, event | category | flops | bytes accessed | tf_op | source)
XLA Modules:
  0.0 304.2 jit_solution(10793989864868407901)
XLA Ops:
  1.2 4.0 %collective-permute-start.1 = (bf16[16,128,128]{2,1,0:T(8,128)(2,1)}, bf16[16,128,128]{2,1,0:T(8,128)(2,1)S(1)}, u32[]{:S(2)}, u32[]{:S(2)}) collective-permute-start(bf16[16,128,128]{2,1,0:T(8,128)(2,1)} %refs_0_.3), channel_id=1, source_target_pairs={{0,16},{1,17},{2,18},{3,19},{4,68},{5,69},{6,70},{7,71},{8,24},{9,... | collective-permute-start | bytes 1572872 | tf_op jit(solution)/shard_map/ppermute | solution.py:298
  5.2 1.0 collective-permute-start
  6.2 2.2 collective-permute-start.2
  8.4 3.8 %norm.2 = (bf16[128,4096]{1,0:T(8,128)(2,1)}, bf16[32,128,128]{2,1,0:T(8,128)(2,1)}, f32[128,128]{1,0:T(8,128)}) custom-call(bf16[128,4096]{1,0:T(8,128)(2,1)} %refs_3_.1, f32[1,4096]{1,0:T(1,128)} %bitcast.7), custom_call_target="tpu_custom_call" | custom-call | flops 1100000000 | tf_op jit(solution)/shard_map/norm/pallas_call | solution.py:66
  12.2 1.0 copy-done.11
  13.2 3.8 %norm.3 = (bf16[128,4096]{1,0:T(8,128)(2,1)}, bf16[32,128,128]{2,1,0:T(8,128)(2,1)}, f32[128,128]{1,0:T(8,128)}) custom-call(bf16[128,4096]{1,0:T(8,128)(2,1)} %copy-done.11, f32[1,4096]{1,0:T(1,128)} %bitcast.8), custom_call_target="tpu_custom_call" | custom-call | flops 1100000000 | tf_op jit(solution)/shard_map/norm/pallas_call | solution.py:66
  17.0 1.2 collective-permute-done.refs_1_
  18.2 1.1 collective-permute-done.2.refs_3_
  19.2 0.8 copy-done.10
  20.0 64.7 %joined.1.refs_8_ = bf16[64,128,128]{2,1,0:T(8,128)(2,1)} custom-call(bf16[16,128,128]{2,1,0:T(8,128)(2,1)} %refs_0_.3, bf16[16,128,128]{2,1,0:T(8,128)(2,1)} %copy-done.9, bf16[16,128,128]{2,1,0:T(8,128)(2,1)} %copy-done.8, bf16[16,128,128]{2,1,0:T(8,128)(2,1)} %copy-done.10, bf16[32,128,128]{2,1,0:T(8,128)(2,1)} %get-tuple-element.37.refs_4_.refs_3_, ...), custom_call_target="tpu_custom_call" | custom-call | flops 1100000000 | tf_op jit(solution)/shard_map/joined/pallas_call | solution.py:253
  84.7 3.1 %collective-permute-start.5 = (bf16[64,128,128]{2,1,0:T(8,128)(2,1)}, bf16[64,128,128]{2,1,0:T(8,128)(2,1)S(1)}, u32[]{:S(2)}, u32[]{:S(2)}) collective-permute-start(bf16[64,128,128]{2,1,0:T(8,128)(2,1)} %joined.1.refs_8_), channel_id=1, source_target_pairs={{0,96},{1,97},{2,98},{3,99},{4,28},{5,29},{6,30},{7,31},{8,104},{9... | collective-permute-start | bytes 6291464 | tf_op jit(solution)/shard_map/ppermute | solution.py:298
  87.8 0.6 pad_add_fusion.refs_2_.pos_ref
  88.4 20.4 %grads.1 = (bf16[64,128,128]{2,1,0:T(8,128)(2,1)}, bf16[64,128,128]{2,1,0:T(8,128)(2,1)}, bf16[64,128,128]{2,1,0:T(8,128)(2,1)}, bf16[64,128,128]{2,1,0:T(8,128)(2,1)}) custom-call(s32[512]{0:T(512)} %refs_0_.5, s32[512]{0:T(512)} %refs_1_.3, s32[4]{0:T(128)} %pad_add_fusion.refs_2_.pos_ref, bf16[32,128,128]{2,1,0:T(8,128)(2,1)} %get-tuple-element.37.refs_4_.refs_3_, ...), custom_call_target="tpu_custom_call" | custom-call | flops 2200000000 | tf_op jit(solution)/shard_map/grads/pallas_call | solution.py:126
  108.8 2.9 collective-permute-done.5.refs_1_
  111.6 3.7 %collective-permute-done.4.refs_0_ = bf16[64,128,128]{2,1,0:T(8,128)(2,1)} collective-permute-done((bf16[64,128,128]{2,1,0:T(8,128)(2,1)}, bf16[64,128,128]{2,1,0:T(8,128)(2,1)}, u32[]{:S(2)}, u32[]{:S(2)}) %collective-permute-start.4) | collective-permute-done | bytes 2097184 | tf_op jit(solution)/shard_map/ppermute | solution.py:298
  115.3 64.6 %relayed.1 = (bf16[32,128,128]{2,1,0:T(8,128)(2,1)}, bf16[32,128,128]{2,1,0:T(8,128)(2,1)}) custom-call(bf16[64,128,128]{2,1,0:T(8,128)(2,1)} %collective-permute-done.4.refs_0_, bf16[64,128,128]{2,1,0:T(8,128)(2,1)} %copy-done.3, bf16[64,128,128]{2,1,0:T(8,128)(2,1)} %get-tuple-element.39.refs_2_.refs_0_), custom_call_target="tpu_custom_call" | custom-call | flops 1100000000 | tf_op jit(solution)/shard_map/relayed/pallas_call | solution.py:253
  180.6 1.2 collective-permute-start.8
  181.8 0.8 collective-permute-start.7
  182.6 1.5 collective-permute-start.14
  184.1 11.6 %collective-permute-done.8.refs_1_ = bf16[32,128,128]{2,1,0:T(8,128)(2,1)} collective-permute-done((bf16[32,128,128]{2,1,0:T(8,128)(2,1)}, bf16[32,128,128]{2,1,0:T(8,128)(2,1)}, u32[]{:S(2)}, u32[]{:S(2)}) %collective-permute-start.8) | collective-permute-done | bytes 1048608 | tf_op jit(solution)/shard_map/ppermute | solution.py:298
  195.7 3.0 collective-permute-start.15
  198.7 9.9 %collective-permute-done.7.refs_0_ = bf16[32,128,128]{2,1,0:T(8,128)(2,1)} collective-permute-done((bf16[32,128,128]{2,1,0:T(8,128)(2,1)S(1)}, bf16[32,128,128]{2,1,0:T(8,128)(2,1)}, u32[]{:S(2)}, u32[]{:S(2)}) %collective-permute-start.7) | collective-permute-done | bytes 1048608 | tf_op jit(solution)/shard_map/ppermute | solution.py:298
  208.7 2.8 collective-permute-start.16
  211.4 1.4 copy-done.4
  213.3 2.4 collective-permute-done.12.refs_16_
  215.7 1.5 collective-permute-done.13.refs_17_
  217.2 1.0 copy-done.7
  218.2 37.5 %project.1 = (bf16[128,14336]{1,0:T(8,128)(2,1)}, bf16[128,4096]{1,0:T(8,128)(2,1)}, f32[32,128]{1,0:T(8,128)}) custom-call(s32[512]{0:T(512)} %refs_0_.5, s32[512]{0:T(512)} %refs_1_.3, s32[4]{0:T(128)} %pad_add_fusion.refs_2_.pos_ref, bf16[128,4096]{1,0:T(8,128)(2,1)} %refs_3_.1, bf16[128,4096]{1,0:T(8,128)(2,1)} %get-tuple-element.35.refs_4_, ...), custom_call_target="tpu_custom_call" | custom-call | flops 2200000000 | tf_op jit(solution)/shard_map/project/pallas_call | solution.py:216
  255.9 1.2 collective-permute-done.17.refs_5_
  257.2 0.7 copy-done.1
  257.9 4.7 %cut_sum.1 = (bf16[17,128,128]{2,1,0:T(8,128)(2,1)S(1)}, bf16[17,128,128]{2,1,0:T(8,128)(2,1)S(1)}, bf16[17,128,128]{2,1,0:T(8,128)(2,1)S(1)}, bf16[17,128,128]{2,1,0:T(8,128)(2,1)S(1)}) custom-call(bf16[64,128,128]{2,1,0:T(8,128)(2,1)S(1)} %copy-done, bf16[64,128,128]{2,1,0:T(8,128)(2,1)} %collective-permute-done.14.refs_1_, ...), custom_call_target="tpu_custom_call" | custom-call | flops 1100000000 | tf_op jit(solution)/shard_map/cut_sum/pallas_call | solution.py:341
  262.8 0.8 collective-permute-start.19
  263.6 2.3 collective-permute-start.20
  265.9 13.5 %collective-permute-done.18.refs_1_ = bf16[17,128,128]{2,1,0:T(8,128)(2,1)S(1)} collective-permute-done((bf16[17,128,128]{2,1,0:T(8,128)(2,1)S(1)}, bf16[17,128,128]{2,1,0:T(8,128)(2,1)S(1)}, u32[]{:S(2)}, u32[]{:S(2)}) %collective-permute-start.18) | collective-permute-done | bytes 557088 | tf_op jit(solution)/shard_map/ppermute | solution.py:298
  279.4 0.9 collective-permute-done.20.refs_3_
  280.6 1.7 collective-permute-start.21
  282.3 2.2 collective-permute-start.22
  284.5 1.6 collective-permute-start.23
  286.0 1.2 collective-permute-done.21.refs_1_
  287.2 2.3 collective-permute-done.22.refs_2_
  289.9 0.9 collective-permute-start.26
  291.3 0.9 collective-permute-start.24
  292.2 5.2 %collective-permute-done.26.refs_3_ = bf16[5,128,128]{2,1,0:T(8,128)(2,1)S(1)} collective-permute-done((bf16[5,128,128]{2,1,0:T(8,128)(2,1)S(1)}, bf16[5,128,128]{2,1,0:T(8,128)(2,1)S(1)}, u32[]{:S(2)}, u32[]{:S(2)}) %collective-permute-start.26) | collective-permute-done | bytes 163872 | tf_op jit(solution)/shard_map/ppermute | solution.py:298
  297.4 2.0 collective-permute-done.25.refs_2_
  299.4 1.4 collective-permute-done.24.refs_1_
  300.8 1.6 place.1
  302.4 1.2 collective-permute-done.27
  303.6 0.6 select_bitcast_fusion
  (47 shorter events, 3.3 us)
Async XLA Ops:
  0.6 87.8 %collective-permute-start.6 = (bf16[128,14336]{1,0:T(8,128)(2,1)}, bf16[128,14336]{1,0:T(8,128)(2,1)}, u32[]{:S(2)}, u32[]{:S(2)}) collective-permute-start(bf16[128,14336]{1,0:T(8,128)(2,1)} %refs_7_.1), channel_id=1, source_target_pairs={{0,4},{4,0},{1,5},{5,1},{2,6},{6,2},{3,7},{7,3},{8,12},{12,8},{9,1... | collective-permute-start | bytes 11010056 | tf_op jit(solution)/shard_map/ppermute | solution.py:399
  0.7 11.5 %collective-permute-start.3 = (bf16[128,4096]{1,0:T(8,128)(2,1)}, bf16[128,4096]{1,0:T(8,128)(2,1)S(1)}, u32[]{:S(2)}, u32[]{:S(2)}) collective-permute-start(bf16[128,4096]{1,0:T(8,128)(2,1)} %refs_3_.1), channel_id=1, source_target_pairs={{0,4},{4,0},{1,5},{5,1},{2,6},{6,2},{3,7},{7,3},{8,12},{12,8},{9,1... | collective-permute-start | bytes 3145736 | tf_op jit(solution)/shard_map/ppermute | solution.py:399
  1.2 15.7 %collective-permute-start.1 = (bf16[16,128,128]{2,1,0:T(8,128)(2,1)}, bf16[16,128,128]{2,1,0:T(8,128)(2,1)S(1)}, u32[]{:S(2)}, u32[]{:S(2)}) collective-permute-start(bf16[16,128,128]{2,1,0:T(8,128)(2,1)} %refs_0_.3), channel_id=1, source_target_pairs={{0,16},{1,17},{2,18},{3,19},{4,68},{5,69},{6,70},{7,71},{8,24},{9,... | collective-permute-start | bytes 1572872 | tf_op jit(solution)/shard_map/ppermute | solution.py:298
  5.2 13.0 %collective-permute-start = (bf16[16,128,128]{2,1,0:T(8,128)(2,1)}, bf16[16,128,128]{2,1,0:T(8,128)(2,1)S(1)}, u32[]{:S(2)}, u32[]{:S(2)}) collective-permute-start(bf16[16,128,128]{2,1,0:T(8,128)(2,1)} %refs_0_.3), channel_id=1, source_target_pairs={{0,8},{1,9},{2,10},{3,11},{4,36},{5,37},{6,38},{7,39},{8,16},{9,17... | collective-permute-start | bytes 1572872 | tf_op jit(solution)/shard_map/ppermute | solution.py:298
  6.2 13.0 %collective-permute-start.2 = (bf16[16,128,128]{2,1,0:T(8,128)(2,1)}, bf16[16,128,128]{2,1,0:T(8,128)(2,1)S(1)}, u32[]{:S(2)}, u32[]{:S(2)}) collective-permute-start(bf16[16,128,128]{2,1,0:T(8,128)(2,1)} %refs_0_.3), channel_id=1, source_target_pairs={{0,24},{1,25},{2,26},{3,27},{4,100},{5,101},{6,102},{7,103},{8,0},... | collective-permute-start | bytes 1572872 | tf_op jit(solution)/shard_map/ppermute | solution.py:298
  12.2 1.0 copy-start.11
  17.0 2.3 copy-start.8
  18.2 1.1 copy-start.9
  19.2 0.8 copy-start.10
  84.7 27.0 %collective-permute-start.5 = (bf16[64,128,128]{2,1,0:T(8,128)(2,1)}, bf16[64,128,128]{2,1,0:T(8,128)(2,1)S(1)}, u32[]{:S(2)}, u32[]{:S(2)}) collective-permute-start(bf16[64,128,128]{2,1,0:T(8,128)(2,1)} %joined.1.refs_8_), channel_id=1, source_target_pairs={{0,96},{1,97},{2,98},{3,99},{4,28},{5,29},{6,30},{7,31},{8,104},{9... | collective-permute-start | bytes 6291464 | tf_op jit(solution)/shard_map/ppermute | solution.py:298
  87.8 27.6 %collective-permute-start.4 = (bf16[64,128,128]{2,1,0:T(8,128)(2,1)}, bf16[64,128,128]{2,1,0:T(8,128)(2,1)}, u32[]{:S(2)}, u32[]{:S(2)}) collective-permute-start(bf16[64,128,128]{2,1,0:T(8,128)(2,1)} %joined.1.refs_8_), channel_id=1, source_target_pairs={{0,32},{1,33},{2,34},{3,35},{4,12},{5,13},{6,14},{7,15},{8,40},{9,... | collective-permute-start | bytes 6291464 | tf_op jit(solution)/shard_map/ppermute | solution.py:298
  87.8 94.9 %collective-permute-start.9 = (bf16[64,128,128]{2,1,0:T(8,128)(2,1)}, bf16[64,128,128]{2,1,0:T(8,128)(2,1)}, u32[]{:S(2)}, u32[]{:S(2)}) collective-permute-start(bf16[64,128,128]{2,1,0:T(8,128)(2,1)} %joined.1.refs_8_), channel_id=1, source_target_pairs={{0,4},{4,0},{1,5},{5,1},{2,6},{6,2},{3,7},{7,3},{8,12},{12,8},{9,1... | collective-permute-start | bytes 6291464 | tf_op jit(solution)/shard_map/ppermute | solution.py:399
  111.6 3.7 %copy-start.3 = (bf16[64,128,128]{2,1,0:T(8,128)(2,1)}, bf16[64,128,128]{2,1,0:T(8,128)(2,1)S(1)}, u32[]{:S(2)}) copy-start(bf16[64,128,128]{2,1,0:T(8,128)(2,1)S(1)} %collective-permute-done.5.refs_1_) | copy-start | bytes 6291460
  180.0 1.8 copy-start.5
  180.0 31.4 %collective-permute-start.10 = (bf16[64,128,128]{2,1,0:T(8,128)(2,1)}, bf16[64,128,128]{2,1,0:T(8,128)(2,1)S(1)}, u32[]{:S(2)}, u32[]{:S(2)}) collective-permute-start(bf16[64,128,128]{2,1,0:T(8,128)(2,1)} %get-tuple-element.41.refs_9_), channel_id=1, source_target_pairs={{0,4},{4,0},{1,5},{5,1},{2,6},{6,2},{3,7},{7,3},{8,12},{12,8},{9,1... | collective-permute-start | bytes 6291464 | tf_op jit(solution)/shard_map/ppermute | solution.py:399
  180.1 31.3 %collective-permute-start.11 = (bf16[64,128,128]{2,1,0:T(8,128)(2,1)}, bf16[64,128,128]{2,1,0:T(8,128)(2,1)}, u32[]{:S(2)}, u32[]{:S(2)}) collective-permute-start(bf16[64,128,128]{2,1,0:T(8,128)(2,1)} %get-tuple-element.42.refs_10_), channel_id=1, source_target_pairs={{0,4},{4,0},{1,5},{5,1},{2,6},{6,2},{3,7},{7,3},{8,12},{12,8},{9,1... | collective-permute-start | bytes 6291464 | tf_op jit(solution)/shard_map/ppermute | solution.py:399
  180.6 15.1 %collective-permute-start.8 = (bf16[32,128,128]{2,1,0:T(8,128)(2,1)}, bf16[32,128,128]{2,1,0:T(8,128)(2,1)}, u32[]{:S(2)}, u32[]{:S(2)}) collective-permute-start(bf16[32,128,128]{2,1,0:T(8,128)(2,1)} %get-tuple-element.43), channel_id=1, source_target_pairs={{0,96},{1,97},{2,98},{3,99},{4,28},{5,29},{6,30},{7,31},{8,104},{9... | collective-permute-start | bytes 3145736 | tf_op jit(solution)/shard_map/ppermute | solution.py:298
  181.8 26.9 %collective-permute-start.7 = (bf16[32,128,128]{2,1,0:T(8,128)(2,1)S(1)}, bf16[32,128,128]{2,1,0:T(8,128)(2,1)}, u32[]{:S(2)}, u32[]{:S(2)}) collective-permute-start(bf16[32,128,128]{2,1,0:T(8,128)(2,1)S(1)} %copy-done.5), channel_id=1, source_target_pairs={{0,32},{1,33},{2,34},{3,35},{4,12},{5,13},{6,14},{7,15},{8,40},{9,... | collective-permute-start | bytes 3145736 | tf_op jit(solution)/shard_map/ppermute | solution.py:298
  182.6 73.3 %collective-permute-start.14 = (bf16[64,128,128]{2,1,0:T(8,128)(2,1)}, bf16[64,128,128]{2,1,0:T(8,128)(2,1)}, u32[]{:S(2)}, u32[]{:S(2)}) collective-permute-start(bf16[64,128,128]{2,1,0:T(8,128)(2,1)} %get-tuple-element.52), channel_id=1, source_target_pairs={{0,1},{1,2},{2,3},{3,0},{4,36},{5,37},{6,38},{7,39},{8,9},{9,10},{... | collective-permute-start | bytes 6291464 | tf_op jit(solution)/shard_map/ppermute | solution.py:298
  195.7 60.2 %collective-permute-start.15 = (bf16[64,128,128]{2,1,0:T(8,128)(2,1)}, bf16[64,128,128]{2,1,0:T(8,128)(2,1)}, u32[]{:S(2)}, u32[]{:S(2)}) collective-permute-start(bf16[64,128,128]{2,1,0:T(8,128)(2,1)} %get-tuple-element.53), channel_id=1, source_target_pairs={{0,2},{1,3},{2,0},{3,1},{4,68},{5,69},{6,70},{7,71},{8,10},{9,11},... | collective-permute-start | bytes 6291464 | tf_op jit(solution)/shard_map/ppermute | solution.py:298
  208.7 47.3 %collective-permute-start.16 = (bf16[64,128,128]{2,1,0:T(8,128)(2,1)}, bf16[64,128,128]{2,1,0:T(8,128)(2,1)}, u32[]{:S(2)}, u32[]{:S(2)}) collective-permute-start(bf16[64,128,128]{2,1,0:T(8,128)(2,1)} %get-tuple-element.54), channel_id=1, source_target_pairs={{0,3},{1,0},{2,1},{3,2},{4,100},{5,101},{6,102},{7,103},{8,11},{9,... | collective-permute-start | bytes 6291464 | tf_op jit(solution)/shard_map/ppermute | solution.py:298
  211.4 1.4 copy-start.4
  212.8 2.9 collective-permute-start.12
  212.8 4.4 %collective-permute-start.13 = (bf16[32,128,128]{2,1,0:T(8,128)(2,1)}, bf16[32,128,128]{2,1,0:T(8,128)(2,1)S(1)}, u32[]{:S(2)}, u32[]{:S(2)}) collective-permute-start(bf16[32,128,128]{2,1,0:T(8,128)(2,1)} %get-tuple-element.45.refs_12_), channel_id=1, source_target_pairs={{0,4},{4,0},{1,5},{5,1},{2,6},{6,2},{3,7},{7,3},{8,12},{12,8},{9,1... | collective-permute-start | bytes 3145736 | tf_op jit(solution)/shard_map/ppermute | solution.py:399
  215.7 2.5 copy-start.6
  217.2 1.0 copy-start.7
  218.2 39.0 %copy-start = (bf16[64,128,128]{2,1,0:T(8,128)(2,1)S(1)}, bf16[64,128,128]{2,1,0:T(8,128)(2,1)}, u32[]{:S(2)}) copy-start(bf16[64,128,128]{2,1,0:T(8,128)(2,1)} %get-tuple-element.51.refs_0_) | copy-start | bytes 6291460
  255.7 1.5 collective-permute-start.17
  257.2 0.7 copy-start.1
  262.6 16.8 %collective-permute-start.18 = (bf16[17,128,128]{2,1,0:T(8,128)(2,1)S(1)}, bf16[17,128,128]{2,1,0:T(8,128)(2,1)S(1)}, u32[]{:S(2)}, u32[]{:S(2)}) collective-permute-start(bf16[17,128,128]{2,1,0:T(8,128)(2,1)S(1)} %get-tuple-element.57), channel_id=1, source_target_pairs={{0,32},{1,33},{2,34},{3,35},{4,12},{5,13},{6,14},{7,15},{8,40},{9,... | collective-permute-start | bytes 1671176 | tf_op jit(solution)/shard_map/ppermute | solution.py:298
  262.8 16.6 %collective-permute-start.19 = (bf16[17,128,128]{2,1,0:T(8,128)(2,1)S(1)}, bf16[17,128,128]{2,1,0:T(8,128)(2,1)S(1)}, u32[]{:S(2)}, u32[]{:S(2)}) collective-permute-start(bf16[17,128,128]{2,1,0:T(8,128)(2,1)S(1)} %get-tuple-element.58), channel_id=1, source_target_pairs={{0,64},{1,65},{2,66},{3,67},{4,20},{5,21},{6,22},{7,23},{8,72},{9,... | collective-permute-start | bytes 1671176 | tf_op jit(solution)/shard_map/ppermute | solution.py:298
  263.6 16.7 %collective-permute-start.20 = (bf16[17,128,128]{2,1,0:T(8,128)(2,1)S(1)}, bf16[17,128,128]{2,1,0:T(8,128)(2,1)S(1)}, u32[]{:S(2)}, u32[]{:S(2)}) collective-permute-start(bf16[17,128,128]{2,1,0:T(8,128)(2,1)S(1)} %get-tuple-element.59), channel_id=1, source_target_pairs={{0,96},{1,97},{2,98},{3,99},{4,28},{5,29},{6,30},{7,31},{8,104},{9... | collective-permute-start | bytes 1671176 | tf_op jit(solution)/shard_map/ppermute | solution.py:298
  280.6 20.2 %copy-start.2 = (s32[4]{0:T(128)S(1)}, s32[4]{0:T(128)}, u32[]{:S(2)}) copy-start(s32[4]{0:T(128)} %pad_add_fusion.refs_2_.pos_ref) | copy-start | bytes 52
  280.6 6.6 %collective-permute-start.21 = (bf16[5,128,128]{2,1,0:T(8,128)(2,1)S(1)}, bf16[5,128,128]{2,1,0:T(8,128)(2,1)S(1)}, u32[]{:S(2)}, u32[]{:S(2)}) collective-permute-start(bf16[5,128,128]{2,1,0:T(8,128)(2,1)S(1)} %get-tuple-element.61), channel_id=1, source_target_pairs={{0,8},{1,9},{2,10},{3,11},{4,5},{5,6},{6,7},{7,4},{8,16},{9,17},{1... | collective-permute-start | bytes 491528 | tf_op jit(solution)/shard_map/ppermute | solution.py:298
  282.3 7.2 %collective-permute-start.22 = (bf16[5,128,128]{2,1,0:T(8,128)(2,1)S(1)}, bf16[5,128,128]{2,1,0:T(8,128)(2,1)S(1)}, u32[]{:S(2)}, u32[]{:S(2)}) collective-permute-start(bf16[5,128,128]{2,1,0:T(8,128)(2,1)S(1)} %get-tuple-element.62), channel_id=1, source_target_pairs={{0,16},{1,17},{2,18},{3,19},{4,6},{5,7},{6,4},{7,5},{8,24},{9,25},... | collective-permute-start | bytes 491528 | tf_op jit(solution)/shard_map/ppermute | solution.py:298
  284.5 5.3 %collective-permute-start.23 = (bf16[5,128,128]{2,1,0:T(8,128)(2,1)S(1)}, bf16[5,128,128]{2,1,0:T(8,128)(2,1)S(1)}, u32[]{:S(2)}, u32[]{:S(2)}) collective-permute-start(bf16[5,128,128]{2,1,0:T(8,128)(2,1)S(1)} %get-tuple-element.63), channel_id=1, source_target_pairs={{0,24},{1,25},{2,26},{3,27},{4,7},{5,4},{6,5},{7,6},{8,0},{9,1},{1... | collective-permute-start | bytes 491528 | tf_op jit(solution)/shard_map/ppermute | solution.py:298
  289.9 7.5 %collective-permute-start.26 = (bf16[5,128,128]{2,1,0:T(8,128)(2,1)S(1)}, bf16[5,128,128]{2,1,0:T(8,128)(2,1)S(1)}, u32[]{:S(2)}, u32[]{:S(2)}) collective-permute-start(bf16[5,128,128]{2,1,0:T(8,128)(2,1)S(1)} %next_sum.3.refs_0_), channel_id=1, source_target_pairs={{0,3},{1,0},{2,1},{3,2},{4,7},{5,4},{6,5},{7,6},{8,11},{9,8},{10,9... | collective-permute-start | bytes 491528 | tf_op jit(solution)/shard_map/ppermute | solution.py:298
  290.8 8.6 %collective-permute-start.25 = (bf16[5,128,128]{2,1,0:T(8,128)(2,1)S(1)}, bf16[5,128,128]{2,1,0:T(8,128)(2,1)S(1)}, u32[]{:S(2)}, u32[]{:S(2)}) collective-permute-start(bf16[5,128,128]{2,1,0:T(8,128)(2,1)S(1)} %next_sum.3.refs_0_), channel_id=1, source_target_pairs={{0,2},{1,3},{2,0},{3,1},{4,6},{5,7},{6,4},{7,5},{8,10},{9,11},{10,... | collective-permute-start | bytes 491528 | tf_op jit(solution)/shard_map/ppermute | solution.py:298
  291.3 9.5 %collective-permute-start.24 = (bf16[5,128,128]{2,1,0:T(8,128)(2,1)S(1)}, bf16[5,128,128]{2,1,0:T(8,128)(2,1)S(1)}, u32[]{:S(2)}, u32[]{:S(2)}) collective-permute-start(bf16[5,128,128]{2,1,0:T(8,128)(2,1)S(1)} %next_sum.3.refs_0_), channel_id=1, source_target_pairs={{0,1},{1,2},{2,3},{3,0},{4,5},{5,6},{6,7},{7,4},{8,9},{9,10},{10,1... | collective-permute-start | bytes 491528 | tf_op jit(solution)/shard_map/ppermute | solution.py:298
  302.4 1.2 collective-permute-start.27

commit v10 on v8

--- a/solution.py
+++ b/solution.py
@@ -70,7 +70,7 @@
             jax.ShapeDtypeStruct((width // T, T, count), BF),
             jax.ShapeDtypeStruct((count, T), F4),
         ),
-        compiler_params=params(60),
+        compiler_params=params(16),
         cost_estimate=cost(1, 0),
         name="norm",
     )(x, gain)
@@ -112,7 +112,7 @@
                 out_ref[t] = dot(left, right).astype(BF)
                 return carry
 
-            lax.fori_loop(0, STEP, one, 0, unroll=8)
+            lax.fori_loop(0, STEP, one, 0, unroll=16)
 
 
 def grads(aheads, rows, cols, pos, turned, turned_other, own, other, carried=(), ties=()):
@@ -177,7 +177,7 @@
         back_acc[:, r] += dot_t(g_ref[:, q], weight)
         return carry
 
-    lax.fori_loop(0, 32, one, 0, unroll=8)
+    lax.fori_loop(0, 32, one, 0, unroll=32)
 
     @pl.when(s == pl.num_programs(0) - 1)
     def _():
@@ -238,23 +238,21 @@
     )(rows, cols, pos, *resident, *arrays)
 
 
-def joined(pieces, tie):
+def joined(pieces, *ties):
     each = pieces[0].shape[0]
 
     def kernel(*refs):
         for j in range(4):
-            refs[-1][j] = refs[j][...]
+            refs[-1][j * each : (j + 1) * each] = refs[j][...]
 
     return pl.pallas_call(
         kernel,
-        out_shape=jax.ShapeDtypeStruct((4, each, T, T), BF),
-        grid=(4,),
-        in_specs=[pl.BlockSpec((each // 4, T, T), lambda i: (i, 0, 0))] * 4 + [ANY],
-        out_specs=pl.BlockSpec((4, each // 4, T, T), lambda i: (0, i, 0, 0)),
-        compiler_params=params(32),
+        out_shape=jax.ShapeDtypeStruct((4 * each, T, T), BF),
+        in_specs=[pl.BlockSpec(memory_space=pltpu.VMEM)] * 4 + [ANY] * len(ties),
+        compiler_params=params(16),
         cost_estimate=cost(1, 0),
         name="joined",
-    )(*pieces, tie).reshape(4 * each, T, T)
+    )(*pieces, *ties)
 
 
 def held(values, *ties):
@@ -407,7 +405,7 @@
     tokens_other, g_other = other_core(tokens), other_core(cotangent)
     normed, turned, scale = norm(tokens, gain2)
     _, turned_other, _ = norm(tokens_other, gain2)
-    line = joined(exchange([tiles] * 4, first), turned_other)
+    line = joined(exchange([tiles] * 4, first), turned, turned_other)
     left, right = ring(line, second, 1), ring(line, second, 3)
     operands = (rows, cols, pos, turned, turned_other, cotangent, g_other)
     part0, part2, part1 = grads((0, 2, 1), *operands)
@@ -417,6 +415,7 @@
     near = [line, left, right]
     swapped = [other_core(block) for block in near]
     far = held((ring(left_half, second, 1), ring(right_half, second, 3)), part3, *swapped)
+    part0, part2, part1, part3 = held((part0, part2, part1, part3), far[0])
     arrays = near + list(far) + swapped + [other_core(block) for block in far]
     projected, token_grad, sums = project(rows, cols, pos, arrays, tokens, normed, scale, gain2, cotangent)
     count = sums.shape[0]

time: 170 us -> 170 us (level)
  Pallas kernels: 79.6 us -> 68.6 us
  waiting for transfers between devices: 44.6 us -> 52.7 us
  local copies, waits for them, and re-layouts: 5.73 us -> 8.28 us
    ppermute x19, waiting for transfers between devices: 38.9 us -> 46.6 us  [ring(): return lax.ppermute(piece, ALL, pairs)]
    pallas_call x1, Pallas kernels: 37.5 us -> 32 us  [project(): pl.pallas_call(lambda *refs: project_kernel(sources, *refs), out_shape=(j...]
    pallas_call x2, Pallas kernels: 7.57 us -> 3.53 us  [norm(): pl.pallas_call(norm_kernel, out_shape=(jax.ShapeDtypeStruct((count, width...]
    pallas_call x2, Pallas kernels: 24.9 us -> 22.2 us  [grads(): pl.pallas_call(lambda *refs: grad_kernel(aheads, each, *refs), out_shape=...]
    unnamed x24 -> x38, local copies, waits for them, and re-layouts: 5.73 us -> 8.28 us
  transfers between devices with their start and end apart: 28 -> 28, of which waited for: 17 -> 18; matrix products, arithmetic and copies ran while one was open for 0% -> 0% of each run, Pallas kernels for 43% -> 37%
where the time goes in v10:
time: 170 us; the launch traced here: 169 us
  Pallas kernels  68.6 us (40%)
  waiting for transfers between devices  52.7 us (31%)
  starting transfers between devices  37 us (22%)
  local copies, waits for them, and re-layouts  8.28 us (5%)
    ppermute x19, waiting for transfers between devices, ring(): return lax.ppermute(piece, ALL, pairs)  46.6 us
    ppermute x19, starting transfers between devices, ring(): return lax.ppermute(piece, ALL, pairs)  35 us
    pallas_call x1, Pallas kernels, project(): pl.pallas_call(lambda *refs: project_kernel(sources, *refs), out_shape=(j...  32 us
    pallas_call x2, Pallas kernels, grads(): pl.pallas_call(lambda *refs: grad_kernel(aheads, each, *refs), out_shape=...  22.2 us
    unnamed x38, local copies, waits for them, and re-layouts  8.28 us
    ppermute x9, waiting for transfers between devices, other_core(): return lax.ppermute(value, 'c', [(0, 1), (1, 0)])  6.09 us
    pallas_call x1, Pallas kernels, cut_sum(): pl.pallas_call(kernel, out_shape=[jax.ShapeDtypeStruct((each + 1, T, T),...  4.7 us
    pallas_call x2, Pallas kernels, norm(): pl.pallas_call(norm_kernel, out_shape=(jax.ShapeDtypeStruct((count, width...  3.53 us
  transfers between devices with their start and end apart: 28, of which 18 were waited for; matrix products, arithmetic and copies ran while one was open for 0% of the time, Pallas kernels for 37%

profile of v10, /device:TPU:0, one launch (start us, length us, event | category | flops | bytes accessed | tf_op | source)
XLA Modules:
  0.0 168.6 jit_solution(6815546432059497340)
XLA Ops:
  1.2 2.0 %collective-permute-start = (bf16[16,128,128]{2,1,0:T(8,128)(2,1)}, bf16[16,128,128]{2,1,0:T(8,128)(2,1)S(1)}, u32[]{:S(2)}, u32[]{:S(2)}) collective-permute-start(bf16[16,128,128]{2,1,0:T(8,128)(2,1)} %refs_0_.4), channel_id=1, source_target_pairs={{0,8},{1,9},{2,10},{3,11},{4,36},{5,37},{6,38},{7,39},{8,16},{9,17... | collective-permute-start | bytes 1572872 | tf_op jit(solution)/shard_map/ppermute | solution.py:302
  3.2 3.6 %collective-permute-start.1 = (bf16[16,128,128]{2,1,0:T(8,128)(2,1)}, bf16[16,128,128]{2,1,0:T(8,128)(2,1)S(1)}, u32[]{:S(2)}, u32[]{:S(2)}) collective-permute-start(bf16[16,128,128]{2,1,0:T(8,128)(2,1)} %refs_0_.4), channel_id=1, source_target_pairs={{0,16},{1,17},{2,18},{3,19},{4,68},{5,69},{6,70},{7,71},{8,24},{9,... | collective-permute-start | bytes 1572872 | tf_op jit(solution)/shard_map/ppermute | solution.py:302
  6.8 1.0 collective-permute-start.2
  7.8 1.2 copy-done.3
  9.0 0.7 copy-done.7
  9.8 1.3 norm.2
  11.1 1.0 copy-done.4
  12.7 2.2 %norm.3 = (bf16[128,4096]{1,0:T(8,128)(2,1)}, bf16[32,128,128]{2,1,0:T(8,128)(2,1)S(1)}, f32[128,128]{1,0:T(8,128)}) custom-call(bf16[128,4096]{1,0:T(8,128)(2,1)S(1)} %collective-permute-done.3.x_ref, f32[1,4096]{1,0:T(1,128)S(1)} %bitcast.9), custom_call_target="tpu_custom_call" | custom-call | flops 1100000000 | tf_op jit(solution)/shard_map/norm/pallas_call | solution.py:66
  14.9 4.9 %collective-permute-done.1.refs_2_ = bf16[16,128,128]{2,1,0:T(8,128)(2,1)S(1)} collective-permute-done((bf16[16,128,128]{2,1,0:T(8,128)(2,1)}, bf16[16,128,128]{2,1,0:T(8,128)(2,1)S(1)}, u32[]{:S(2)}, u32[]{:S(2)}) %collective-permute-start.1) | collective-permute-done | bytes 524320 | tf_op jit(solution)/shard_map/ppermute | solution.py:302
  19.8 1.5 joined.1.refs_8_
  21.3 1.6 collective-permute-start.4
  22.9 1.7 collective-permute-start.5
  25.2 14.2 %grads.2 = (bf16[64,128,128]{2,1,0:T(8,128)(2,1)}, bf16[64,128,128]{2,1,0:T(8,128)(2,1)}, bf16[64,128,128]{2,1,0:T(8,128)(2,1)}) custom-call(s32[512]{0:T(512)} %refs_0_.7, s32[512]{0:T(512)} %refs_1_.5, s32[4]{0:T(128)} %pad_add_fusion.refs_2_.pos_ref, bf16[32,128,128]{2,1,0:T(8,128)(2,1)} %copy-done.1, bf16[32,128,128]{2,1,0:T(8,128)(2,1)} %copy-done.2, ...), custom_call_target="tpu_custom_call" | custom-call | flops 2200000000 | tf_op jit(solution)/shard_map/grads/pallas_call | solution.py:126
  39.4 9.5 %collective-permute-done.4.left_ref.refs_0_ = bf16[64,128,128]{2,1,0:T(8,128)(2,1)} collective-permute-done((bf16[64,128,128]{2,1,0:T(8,128)(2,1)}, bf16[64,128,128]{2,1,0:T(8,128)(2,1)}, u32[]{:S(2)}, u32[]{:S(2)}) %collective-permute-start.4) | collective-permute-done | bytes 2097184 | tf_op jit(solution)/shard_map/ppermute | solution.py:302
  49.1 1.3 copy-done.11
  50.4 2.7 %relayed.1 = (bf16[32,128,128]{2,1,0:T(8,128)(2,1)}, bf16[32,128,128]{2,1,0:T(8,128)(2,1)}) custom-call(bf16[64,128,128]{2,1,0:T(8,128)(2,1)} %collective-permute-done.4.left_ref.refs_0_, bf16[64,128,128]{2,1,0:T(8,128)(2,1)} %copy-done.11, bf16[64,128,128]{2,1,0:T(8,128)(2,1)} %get-tuple-element.42.tie_ref.refs_7_), custom_call_target="tpu_custom_call" | custom-call | flops 1100000000 | tf_op jit(solution)/shard_map/relayed/pallas_call | solution.py:277
  54.3 1.6 collective-permute-start.7
  55.9 1.7 collective-permute-start.8
  57.6 8.0 %grads.3 = (bf16[64,128,128]{2,1,0:T(8,128)(2,1)}, bf16[64,128,128]{2,1,0:T(8,128)(2,1)}, bf16[64,128,128]{2,1,0:T(8,128)(2,1)}, bf16[64,128,128]{2,1,0:T(8,128)(2,1)}) custom-call(s32[512]{0:T(512)} %refs_0_.7, s32[512]{0:T(512)} %refs_1_.5, s32[4]{0:T(128)} %pad_add_fusion.refs_2_.pos_ref, ...), custom_call_target="tpu_custom_call", output_to_operand_aliasing={{0}: (7, {}), {1}: (8, {}), {2}: (9, {})} | custom-call | flops 2200000000 | tf_op jit(solution)/shard_map/grads/pallas_call | solution.py:126
  65.6 4.7 %collective-permute-done.7.refs_0_ = bf16[32,128,128]{2,1,0:T(8,128)(2,1)S(1)} collective-permute-done((bf16[32,128,128]{2,1,0:T(8,128)(2,1)S(1)}, bf16[32,128,128]{2,1,0:T(8,128)(2,1)S(1)}, u32[]{:S(2)}, u32[]{:S(2)}) %collective-permute-start.7) | collective-permute-done | bytes 1048608 | tf_op jit(solution)/shard_map/ppermute | solution.py:302
  71.9 1.5 collective-permute-start.14
  73.4 2.7 %collective-permute-start.15 = (bf16[64,128,128]{2,1,0:T(8,128)(2,1)}, bf16[64,128,128]{2,1,0:T(8,128)(2,1)}, u32[]{:S(2)}, u32[]{:S(2)}) collective-permute-start(bf16[64,128,128]{2,1,0:T(8,128)(2,1)} %get-tuple-element.59), channel_id=1, source_target_pairs={{0,2},{1,3},{2,0},{3,1},{4,68},{5,69},{6,70},{7,71},{8,10},{9,11},... | collective-permute-start | bytes 6291464 | tf_op jit(solution)/shard_map/ppermute | solution.py:302
  76.1 1.4 collective-permute-start.16
  78.1 2.1 %collective-permute-done.12.refs_16_ = bf16[32,128,128]{2,1,0:T(8,128)(2,1)S(1)} collective-permute-done((bf16[32,128,128]{2,1,0:T(8,128)(2,1)S(1)}, bf16[32,128,128]{2,1,0:T(8,128)(2,1)S(1)}, u32[]{:S(2)}, u32[]{:S(2)}) %collective-permute-start.12) | collective-permute-done | bytes 1048608 | tf_op jit(solution)/shard_map/ppermute | solution.py:403
  80.2 1.5 collective-permute-done.13.refs_17_
  81.7 1.0 copy-done.18
  82.7 32.0 %project.1 = (bf16[128,14336]{1,0:T(8,128)(2,1)}, bf16[128,4096]{1,0:T(8,128)(2,1)}, f32[32,128]{1,0:T(8,128)}) custom-call(s32[512]{0:T(512)} %refs_0_.7, s32[512]{0:T(512)} %refs_1_.5, s32[4]{0:T(128)} %pad_add_fusion.refs_2_.pos_ref, bf16[128,4096]{1,0:T(8,128)(2,1)} %refs_3_.1, bf16[128,4096]{1,0:T(8,128)(2,1)} %copy-done.4, f32[128,128]{1,0:T(8,128)} %copy-done.6, ...), custom_call_target="tpu_custom_call" | custom-call | flops 2200000000 | tf_op jit(solution)/shard_map/project/pallas_call | solution.py:216
  115.1 1.3 collective-permute-done.17.refs_5_
  116.4 6.5 %collective-permute-done.15.refs_2_ = bf16[64,128,128]{2,1,0:T(8,128)(2,1)} collective-permute-done((bf16[64,128,128]{2,1,0:T(8,128)(2,1)}, bf16[64,128,128]{2,1,0:T(8,128)(2,1)}, u32[]{:S(2)}, u32[]{:S(2)}) %collective-permute-start.15) | collective-permute-done | bytes 2097184 | tf_op jit(solution)/shard_map/ppermute | solution.py:302
  122.9 0.7 copy-done.9
  123.7 4.7 %cut_sum.1 = (bf16[17,128,128]{2,1,0:T(8,128)(2,1)S(1)}, bf16[17,128,128]{2,1,0:T(8,128)(2,1)S(1)}, bf16[17,128,128]{2,1,0:T(8,128)(2,1)S(1)}, bf16[17,128,128]{2,1,0:T(8,128)(2,1)S(1)}) custom-call(bf16[64,128,128]{2,1,0:T(8,128)(2,1)S(1)} %copy-done, bf16[64,128,128]{2,1,0:T(8,128)(2,1)} %collective-permute-done.14.refs_1_, ...), custom_call_target="tpu_custom_call" | custom-call | flops 1100000000 | tf_op jit(solution)/shard_map/cut_sum/pallas_call | solution.py:345
  128.4 1.4 collective-permute-start.18
  129.7 3.1 %collective-permute-start.19 = (bf16[17,128,128]{2,1,0:T(8,128)(2,1)S(1)}, bf16[17,128,128]{2,1,0:T(8,128)(2,1)S(1)}, u32[]{:S(2)}, u32[]{:S(2)}) collective-permute-start(bf16[17,128,128]{2,1,0:T(8,128)(2,1)S(1)} %get-tuple-element.64), channel_id=1, source_target_pairs={{0,64},{1,65},{2,66},{3,67},{4,20},{5,21},{6,22},{7,23},{8,72},{9,... | collective-permute-start | bytes 1671176 | tf_op jit(solution)/shard_map/ppermute | solution.py:302
  132.8 1.1 collective-permute-start.20
  133.8 5.4 %collective-permute-done.18.refs_1_ = bf16[17,128,128]{2,1,0:T(8,128)(2,1)S(1)} collective-permute-done((bf16[17,128,128]{2,1,0:T(8,128)(2,1)S(1)}, bf16[17,128,128]{2,1,0:T(8,128)(2,1)S(1)}, u32[]{:S(2)}, u32[]{:S(2)}) %collective-permute-start.18) | collective-permute-done | bytes 557088 | tf_op jit(solution)/shard_map/ppermute | solution.py:302
  139.2 7.1 %collective-permute-done.19.refs_2_ = bf16[17,128,128]{2,1,0:T(8,128)(2,1)S(1)} collective-permute-done((bf16[17,128,128]{2,1,0:T(8,128)(2,1)S(1)}, bf16[17,128,128]{2,1,0:T(8,128)(2,1)S(1)}, u32[]{:S(2)}, u32[]{:S(2)}) %collective-permute-start.19) | collective-permute-done | bytes 557088 | tf_op jit(solution)/shard_map/ppermute | solution.py:302
  146.6 1.5 collective-permute-start.21
  148.0 2.1 %collective-permute-start.22 = (bf16[5,128,128]{2,1,0:T(8,128)(2,1)S(1)}, bf16[5,128,128]{2,1,0:T(8,128)(2,1)S(1)}, u32[]{:S(2)}, u32[]{:S(2)}) collective-permute-start(bf16[5,128,128]{2,1,0:T(8,128)(2,1)S(1)} %get-tuple-element.68), channel_id=1, source_target_pairs={{0,16},{1,17},{2,18},{3,19},{4,6},{5,7},{6,4},{7,5},{8,24},{9,25},... | collective-permute-start | bytes 491528 | tf_op jit(solution)/shard_map/ppermute | solution.py:302
  150.2 1.6 collective-permute-start.23
  151.8 1.4 collective-permute-done.21.refs_1_
  153.2 2.0 %collective-permute-done.22.refs_2_ = bf16[5,128,128]{2,1,0:T(8,128)(2,1)S(1)} collective-permute-done((bf16[5,128,128]{2,1,0:T(8,128)(2,1)S(1)}, bf16[5,128,128]{2,1,0:T(8,128)(2,1)S(1)}, u32[]{:S(2)}, u32[]{:S(2)}) %collective-permute-start.22) | collective-permute-done | bytes 163872 | tf_op jit(solution)/shard_map/ppermute | solution.py:302
  155.9 2.0 %collective-permute-start.24 = (bf16[5,128,128]{2,1,0:T(8,128)(2,1)S(1)}, bf16[5,128,128]{2,1,0:T(8,128)(2,1)S(1)}, u32[]{:S(2)}, u32[]{:S(2)}) collective-permute-start(bf16[5,128,128]{2,1,0:T(8,128)(2,1)S(1)} %next_sum.3.refs_0_), channel_id=1, source_target_pairs={{0,1},{1,2},{2,3},{3,0},{4,5},{5,6},{6,7},{7,4},{8,9},{9,10},{10,1... | collective-permute-start | bytes 491528 | tf_op jit(solution)/shard_map/ppermute | solution.py:302
  157.8 2.1 %collective-permute-start.25 = (bf16[5,128,128]{2,1,0:T(8,128)(2,1)S(1)}, bf16[5,128,128]{2,1,0:T(8,128)(2,1)S(1)}, u32[]{:S(2)}, u32[]{:S(2)}) collective-permute-start(bf16[5,128,128]{2,1,0:T(8,128)(2,1)S(1)} %next_sum.3.refs_0_), channel_id=1, source_target_pairs={{0,2},{1,3},{2,0},{3,1},{4,6},{5,7},{6,4},{7,5},{8,10},{9,11},{10,... | collective-permute-start | bytes 491528 | tf_op jit(solution)/shard_map/ppermute | solution.py:302
  159.9 1.6 collective-permute-start.26
  161.5 1.0 collective-permute-done.24.refs_1_
  162.5 2.5 %collective-permute-done.25.refs_2_ = bf16[5,128,128]{2,1,0:T(8,128)(2,1)S(1)} collective-permute-done((bf16[5,128,128]{2,1,0:T(8,128)(2,1)S(1)}, bf16[5,128,128]{2,1,0:T(8,128)(2,1)S(1)}, u32[]{:S(2)}, u32[]{:S(2)}) %collective-permute-start.25) | collective-permute-done | bytes 163872 | tf_op jit(solution)/shard_map/ppermute | solution.py:302
  165.2 1.6 place.1
  166.8 1.2 collective-permute-done.27
  (62 shorter events, 7.7 us)
Async XLA Ops:
  0.6 24.6 %collective-permute-start.6 = (bf16[128,14336]{1,0:T(8,128)(2,1)}, bf16[128,14336]{1,0:T(8,128)(2,1)}, u32[]{:S(2)}, u32[]{:S(2)}) collective-permute-start(bf16[128,14336]{1,0:T(8,128)(2,1)} %refs_7_.1), channel_id=1, source_target_pairs={{0,4},{4,0},{1,5},{5,1},{2,6},{6,2},{3,7},{7,3},{8,12},{12,8},{9,1... | collective-permute-start | bytes 11010056 | tf_op jit(solution)/shard_map/ppermute | solution.py:403
  0.7 12.0 %collective-permute-start.3 = (bf16[128,4096]{1,0:T(8,128)(2,1)}, bf16[128,4096]{1,0:T(8,128)(2,1)S(1)}, u32[]{:S(2)}, u32[]{:S(2)}) collective-permute-start(bf16[128,4096]{1,0:T(8,128)(2,1)} %refs_3_.1), channel_id=1, source_target_pairs={{0,4},{4,0},{1,5},{5,1},{2,6},{6,2},{3,7},{7,3},{8,12},{12,8},{9,1... | collective-permute-start | bytes 3145736 | tf_op jit(solution)/shard_map/ppermute | solution.py:403
  1.2 13.7 %collective-permute-start = (bf16[16,128,128]{2,1,0:T(8,128)(2,1)}, bf16[16,128,128]{2,1,0:T(8,128)(2,1)S(1)}, u32[]{:S(2)}, u32[]{:S(2)}) collective-permute-start(bf16[16,128,128]{2,1,0:T(8,128)(2,1)} %refs_0_.4), channel_id=1, source_target_pairs={{0,8},{1,9},{2,10},{3,11},{4,36},{5,37},{6,38},{7,39},{8,16},{9,17... | collective-permute-start | bytes 1572872 | tf_op jit(solution)/shard_map/ppermute | solution.py:302
  3.2 16.6 %collective-permute-start.1 = (bf16[16,128,128]{2,1,0:T(8,128)(2,1)}, bf16[16,128,128]{2,1,0:T(8,128)(2,1)S(1)}, u32[]{:S(2)}, u32[]{:S(2)}) collective-permute-start(bf16[16,128,128]{2,1,0:T(8,128)(2,1)} %refs_0_.4), channel_id=1, source_target_pairs={{0,16},{1,17},{2,18},{3,19},{4,68},{5,69},{6,70},{7,71},{8,24},{9,... | collective-permute-start | bytes 1572872 | tf_op jit(solution)/shard_map/ppermute | solution.py:302
  6.8 13.0 %collective-permute-start.2 = (bf16[16,128,128]{2,1,0:T(8,128)(2,1)}, bf16[16,128,128]{2,1,0:T(8,128)(2,1)S(1)}, u32[]{:S(2)}, u32[]{:S(2)}) collective-permute-start(bf16[16,128,128]{2,1,0:T(8,128)(2,1)} %refs_0_.4), channel_id=1, source_target_pairs={{0,24},{1,25},{2,26},{3,27},{4,100},{5,101},{6,102},{7,103},{8,0},... | collective-permute-start | bytes 1572872 | tf_op jit(solution)/shard_map/ppermute | solution.py:302
  7.8 1.2 copy-start.3
  9.0 0.7 copy-start.7
  9.8 2.9 %copy-start.8 = (f32[4096]{0:T(1024)S(1)}, f32[4096]{0:T(1024)}, u32[]{:S(2)}) copy-start(f32[4096]{0:T(1024)} %param.7) | copy-start | bytes 49156
  11.1 1.0 copy-start.4
  12.0 0.6 copy-start.6
  12.7 8.6 %copy-start.1 = (bf16[32,128,128]{2,1,0:T(8,128)(2,1)}, bf16[32,128,128]{2,1,0:T(8,128)(2,1)S(1)}, u32[]{:S(2)}) copy-start(bf16[32,128,128]{2,1,0:T(8,128)(2,1)S(1)} %get-tuple-element.40.refs_4_.refs_3_) | copy-start | bytes 3145732
  12.7 7.1 %copy-start.5 = (bf16[16,128,128]{2,1,0:T(8,128)(2,1)S(1)}, bf16[16,128,128]{2,1,0:T(8,128)(2,1)}, u32[]{:S(2)}) copy-start(bf16[16,128,128]{2,1,0:T(8,128)(2,1)} %refs_0_.4) | copy-start | bytes 1572868
  14.9 6.4 %copy-start.2 = (bf16[32,128,128]{2,1,0:T(8,128)(2,1)}, bf16[32,128,128]{2,1,0:T(8,128)(2,1)S(1)}, u32[]{:S(2)}) copy-start(bf16[32,128,128]{2,1,0:T(8,128)(2,1)S(1)} %get-tuple-element.41.refs_5_.refs_4_) | copy-start | bytes 3145732
  21.3 27.6 %collective-permute-start.4 = (bf16[64,128,128]{2,1,0:T(8,128)(2,1)}, bf16[64,128,128]{2,1,0:T(8,128)(2,1)}, u32[]{:S(2)}, u32[]{:S(2)}) collective-permute-start(bf16[64,128,128]{2,1,0:T(8,128)(2,1)} %joined.1.refs_8_), channel_id=1, source_target_pairs={{0,32},{1,33},{2,34},{3,35},{4,12},{5,13},{6,14},{7,15},{8,40},{9,... | collective-permute-start | bytes 6291464 | tf_op jit(solution)/shard_map/ppermute | solution.py:302
  22.9 26.2 %collective-permute-start.5 = (bf16[64,128,128]{2,1,0:T(8,128)(2,1)}, bf16[64,128,128]{2,1,0:T(8,128)(2,1)S(1)}, u32[]{:S(2)}, u32[]{:S(2)}) collective-permute-start(bf16[64,128,128]{2,1,0:T(8,128)(2,1)} %joined.1.refs_8_), channel_id=1, source_target_pairs={{0,96},{1,97},{2,98},{3,99},{4,28},{5,29},{6,30},{7,31},{8,104},{9... | collective-permute-start | bytes 6291464 | tf_op jit(solution)/shard_map/ppermute | solution.py:302
  25.2 40.4 %collective-permute-start.9 = (bf16[64,128,128]{2,1,0:T(8,128)(2,1)}, bf16[64,128,128]{2,1,0:T(8,128)(2,1)}, u32[]{:S(2)}, u32[]{:S(2)}) collective-permute-start(bf16[64,128,128]{2,1,0:T(8,128)(2,1)} %joined.1.refs_8_), channel_id=1, source_target_pairs={{0,4},{4,0},{1,5},{5,1},{2,6},{6,2},{3,7},{7,3},{8,12},{12,8},{9,1... | collective-permute-start | bytes 6291464 | tf_op jit(solution)/shard_map/ppermute | solution.py:403
  49.1 1.3 copy-start.11
  53.1 1.2 copy-start.14
  53.1 17.8 %collective-permute-start.10 = (bf16[64,128,128]{2,1,0:T(8,128)(2,1)}, bf16[64,128,128]{2,1,0:T(8,128)(2,1)}, u32[]{:S(2)}, u32[]{:S(2)}) collective-permute-start(bf16[64,128,128]{2,1,0:T(8,128)(2,1)} %get-tuple-element.44.refs_9_), channel_id=1, source_target_pairs={{0,4},{4,0},{1,5},{5,1},{2,6},{6,2},{3,7},{7,3},{8,12},{12,8},{9,1... | collective-permute-start | bytes 6291464 | tf_op jit(solution)/shard_map/ppermute | solution.py:403
  53.1 17.8 %collective-permute-start.11 = (bf16[64,128,128]{2,1,0:T(8,128)(2,1)}, bf16[64,128,128]{2,1,0:T(8,128)(2,1)}, u32[]{:S(2)}, u32[]{:S(2)}) collective-permute-start(bf16[64,128,128]{2,1,0:T(8,128)(2,1)} %get-tuple-element.45.refs_10_), channel_id=1, source_target_pairs={{0,4},{4,0},{1,5},{5,1},{2,6},{6,2},{3,7},{7,3},{8,12},{12,8},{9,1... | collective-permute-start | bytes 6291464 | tf_op jit(solution)/shard_map/ppermute | solution.py:403
  54.3 16.0 %collective-permute-start.7 = (bf16[32,128,128]{2,1,0:T(8,128)(2,1)S(1)}, bf16[32,128,128]{2,1,0:T(8,128)(2,1)S(1)}, u32[]{:S(2)}, u32[]{:S(2)}) collective-permute-start(bf16[32,128,128]{2,1,0:T(8,128)(2,1)S(1)} %copy-done.14), channel_id=1, source_target_pairs={{0,32},{1,33},{2,34},{3,35},{4,12},{5,13},{6,14},{7,15},{8,40},{9,... | collective-permute-start | bytes 3145736 | tf_op jit(solution)/shard_map/ppermute | solution.py:302
  55.9 15.0 %collective-permute-start.8 = (bf16[32,128,128]{2,1,0:T(8,128)(2,1)}, bf16[32,128,128]{2,1,0:T(8,128)(2,1)S(1)}, u32[]{:S(2)}, u32[]{:S(2)}) collective-permute-start(bf16[32,128,128]{2,1,0:T(8,128)(2,1)} %get-tuple-element.46), channel_id=1, source_target_pairs={{0,96},{1,97},{2,98},{3,99},{4,28},{5,29},{6,30},{7,31},{8,104},{9... | collective-permute-start | bytes 3145736 | tf_op jit(solution)/shard_map/ppermute | solution.py:302
  70.3 1.0 copy-start.12
  70.9 1.0 copy-start.15
  71.9 5.7 %copy-start.13 = (bf16[32,128,128]{2,1,0:T(8,128)(2,1)S(1)}, bf16[32,128,128]{2,1,0:T(8,128)(2,1)}, u32[]{:S(2)}) copy-start(bf16[32,128,128]{2,1,0:T(8,128)(2,1)} %get-tuple-element.50.refs_11_.refs_4_) | copy-start | bytes 3145732
  71.9 5.7 %copy-start.16 = (bf16[32,128,128]{2,1,0:T(8,128)(2,1)S(1)}, bf16[32,128,128]{2,1,0:T(8,128)(2,1)}, u32[]{:S(2)}) copy-start(bf16[32,128,128]{2,1,0:T(8,128)(2,1)} %get-tuple-element.51.refs_12_) | copy-start | bytes 3145732
  71.9 44.5 %collective-permute-start.14 = (bf16[64,128,128]{2,1,0:T(8,128)(2,1)}, bf16[64,128,128]{2,1,0:T(8,128)(2,1)}, u32[]{:S(2)}, u32[]{:S(2)}) collective-permute-start(bf16[64,128,128]{2,1,0:T(8,128)(2,1)} %get-tuple-element.58), channel_id=1, source_target_pairs={{0,1},{1,2},{2,3},{3,0},{4,36},{5,37},{6,38},{7,39},{8,9},{9,10},{... | collective-permute-start | bytes 6291464 | tf_op jit(solution)/shard_map/ppermute | solution.py:302
  73.4 49.5 %collective-permute-start.15 = (bf16[64,128,128]{2,1,0:T(8,128)(2,1)}, bf16[64,128,128]{2,1,0:T(8,128)(2,1)}, u32[]{:S(2)}, u32[]{:S(2)}) collective-permute-start(bf16[64,128,128]{2,1,0:T(8,128)(2,1)} %get-tuple-element.59), channel_id=1, source_target_pairs={{0,2},{1,3},{2,0},{3,1},{4,68},{5,69},{6,70},{7,71},{8,10},{9,11},... | collective-permute-start | bytes 6291464 | tf_op jit(solution)/shard_map/ppermute | solution.py:302
  76.1 46.8 %collective-permute-start.16 = (bf16[64,128,128]{2,1,0:T(8,128)(2,1)}, bf16[64,128,128]{2,1,0:T(8,128)(2,1)}, u32[]{:S(2)}, u32[]{:S(2)}) collective-permute-start(bf16[64,128,128]{2,1,0:T(8,128)(2,1)} %get-tuple-element.60), channel_id=1, source_target_pairs={{0,3},{1,0},{2,1},{3,2},{4,100},{5,101},{6,102},{7,103},{8,11},{9,... | collective-permute-start | bytes 6291464 | tf_op jit(solution)/shard_map/ppermute | solution.py:302
  77.6 2.7 %collective-permute-start.12 = (bf16[32,128,128]{2,1,0:T(8,128)(2,1)S(1)}, bf16[32,128,128]{2,1,0:T(8,128)(2,1)S(1)}, u32[]{:S(2)}, u32[]{:S(2)}) collective-permute-start(bf16[32,128,128]{2,1,0:T(8,128)(2,1)S(1)} %copy-done.13), channel_id=1, source_target_pairs={{0,4},{4,0},{1,5},{5,1},{2,6},{6,2},{3,7},{7,3},{8,12},{12,8},{9,1... | collective-permute-start | bytes 3145736 | tf_op jit(solution)/shard_map/ppermute | solution.py:403
  77.6 4.2 %collective-permute-start.13 = (bf16[32,128,128]{2,1,0:T(8,128)(2,1)S(1)}, bf16[32,128,128]{2,1,0:T(8,128)(2,1)S(1)}, u32[]{:S(2)}, u32[]{:S(2)}) collective-permute-start(bf16[32,128,128]{2,1,0:T(8,128)(2,1)S(1)} %copy-done.16), channel_id=1, source_target_pairs={{0,4},{4,0},{1,5},{5,1},{2,6},{6,2},{3,7},{7,3},{8,12},{12,8},{9,1... | collective-permute-start | bytes 3145736 | tf_op jit(solution)/shard_map/ppermute | solution.py:403
  80.2 1.5 copy-start.17
  81.7 1.0 copy-start.18
  82.7 40.2 %copy-start = (bf16[64,128,128]{2,1,0:T(8,128)(2,1)S(1)}, bf16[64,128,128]{2,1,0:T(8,128)(2,1)}, u32[]{:S(2)}) copy-start(bf16[64,128,128]{2,1,0:T(8,128)(2,1)} %get-tuple-element.57.refs_0_) | copy-start | bytes 6291460
  114.7 1.7 collective-permute-start.17
  122.9 0.7 copy-start.9
  128.4 10.8 %collective-permute-start.18 = (bf16[17,128,128]{2,1,0:T(8,128)(2,1)S(1)}, bf16[17,128,128]{2,1,0:T(8,128)(2,1)S(1)}, u32[]{:S(2)}, u32[]{:S(2)}) collective-permute-start(bf16[17,128,128]{2,1,0:T(8,128)(2,1)S(1)} %get-tuple-element.63), channel_id=1, source_target_pairs={{0,32},{1,33},{2,34},{3,35},{4,12},{5,13},{6,14},{7,15},{8,40},{9,... | collective-permute-start | bytes 1671176 | tf_op jit(solution)/shard_map/ppermute | solution.py:302
  129.7 16.5 %collective-permute-start.19 = (bf16[17,128,128]{2,1,0:T(8,128)(2,1)S(1)}, bf16[17,128,128]{2,1,0:T(8,128)(2,1)S(1)}, u32[]{:S(2)}, u32[]{:S(2)}) collective-permute-start(bf16[17,128,128]{2,1,0:T(8,128)(2,1)S(1)} %get-tuple-element.64), channel_id=1, source_target_pairs={{0,64},{1,65},{2,66},{3,67},{4,20},{5,21},{6,22},{7,23},{8,72},{9,... | collective-permute-start | bytes 1671176 | tf_op jit(solution)/shard_map/ppermute | solution.py:302
  132.8 13.5 %collective-permute-start.20 = (bf16[17,128,128]{2,1,0:T(8,128)(2,1)S(1)}, bf16[17,128,128]{2,1,0:T(8,128)(2,1)S(1)}, u32[]{:S(2)}, u32[]{:S(2)}) collective-permute-start(bf16[17,128,128]{2,1,0:T(8,128)(2,1)S(1)} %get-tuple-element.65), channel_id=1, source_target_pairs={{0,96},{1,97},{2,98},{3,99},{4,28},{5,29},{6,30},{7,31},{8,104},{9... | collective-permute-start | bytes 1671176 | tf_op jit(solution)/shard_map/ppermute | solution.py:302
  146.5 18.7 %copy-start.10 = (s32[4]{0:T(128)S(1)}, s32[4]{0:T(128)}, u32[]{:S(2)}) copy-start(s32[4]{0:T(128)} %pad_add_fusion.refs_2_.pos_ref) | copy-start | bytes 52
  146.6 6.6 %collective-permute-start.21 = (bf16[5,128,128]{2,1,0:T(8,128)(2,1)S(1)}, bf16[5,128,128]{2,1,0:T(8,128)(2,1)S(1)}, u32[]{:S(2)}, u32[]{:S(2)}) collective-permute-start(bf16[5,128,128]{2,1,0:T(8,128)(2,1)S(1)} %get-tuple-element.67), channel_id=1, source_target_pairs={{0,8},{1,9},{2,10},{3,11},{4,5},{5,6},{6,7},{7,4},{8,16},{9,17},{1... | collective-permute-start | bytes 491528 | tf_op jit(solution)/shard_map/ppermute | solution.py:302
  148.0 7.2 %collective-permute-start.22 = (bf16[5,128,128]{2,1,0:T(8,128)(2,1)S(1)}, bf16[5,128,128]{2,1,0:T(8,128)(2,1)S(1)}, u32[]{:S(2)}, u32[]{:S(2)}) collective-permute-start(bf16[5,128,128]{2,1,0:T(8,128)(2,1)S(1)} %get-tuple-element.68), channel_id=1, source_target_pairs={{0,16},{1,17},{2,18},{3,19},{4,6},{5,7},{6,4},{7,5},{8,24},{9,25},... | collective-permute-start | bytes 491528 | tf_op jit(solution)/shard_map/ppermute | solution.py:302
  150.2 5.6 %collective-permute-start.23 = (bf16[5,128,128]{2,1,0:T(8,128)(2,1)S(1)}, bf16[5,128,128]{2,1,0:T(8,128)(2,1)S(1)}, u32[]{:S(2)}, u32[]{:S(2)}) collective-permute-start(bf16[5,128,128]{2,1,0:T(8,128)(2,1)S(1)} %get-tuple-element.69), channel_id=1, source_target_pairs={{0,24},{1,25},{2,26},{3,27},{4,7},{5,4},{6,5},{7,6},{8,0},{9,1},{1... | collective-permute-start | bytes 491528 | tf_op jit(solution)/shard_map/ppermute | solution.py:302
  155.9 6.6 %collective-permute-start.24 = (bf16[5,128,128]{2,1,0:T(8,128)(2,1)S(1)}, bf16[5,128,128]{2,1,0:T(8,128)(2,1)S(1)}, u32[]{:S(2)}, u32[]{:S(2)}) collective-permute-start(bf16[5,128,128]{2,1,0:T(8,128)(2,1)S(1)} %next_sum.3.refs_0_), channel_id=1, source_target_pairs={{0,1},{1,2},{2,3},{3,0},{4,5},{5,6},{6,7},{7,4},{8,9},{9,10},{10,1... | collective-permute-start | bytes 491528 | tf_op jit(solution)/shard_map/ppermute | solution.py:302
  157.8 7.2 %collective-permute-start.25 = (bf16[5,128,128]{2,1,0:T(8,128)(2,1)S(1)}, bf16[5,128,128]{2,1,0:T(8,128)(2,1)S(1)}, u32[]{:S(2)}, u32[]{:S(2)}) collective-permute-start(bf16[5,128,128]{2,1,0:T(8,128)(2,1)S(1)} %next_sum.3.refs_0_), channel_id=1, source_target_pairs={{0,2},{1,3},{2,0},{3,1},{4,6},{5,7},{6,4},{7,5},{8,10},{9,11},{10,... | collective-permute-start | bytes 491528 | tf_op jit(solution)/shard_map/ppermute | solution.py:302
  159.9 5.3 %collective-permute-start.26 = (bf16[5,128,128]{2,1,0:T(8,128)(2,1)S(1)}, bf16[5,128,128]{2,1,0:T(8,128)(2,1)S(1)}, u32[]{:S(2)}, u32[]{:S(2)}) collective-permute-start(bf16[5,128,128]{2,1,0:T(8,128)(2,1)S(1)} %next_sum.3.refs_0_), channel_id=1, source_target_pairs={{0,3},{1,0},{2,1},{3,2},{4,7},{5,4},{6,5},{7,6},{8,11},{9,8},{10,9... | collective-permute-start | bytes 491528 | tf_op jit(solution)/shard_map/ppermute | solution.py:302
  166.8 1.2 collective-permute-start.27

commit v11 on v10

--- a/solution.py
+++ b/solution.py
@@ -267,10 +267,11 @@
     )(*values, *ties)
 
 
-def relayed(left, right, tie):
+def relayed(left, right, *ties):
     half = left.shape[0] // 2
 
-    def kernel(left_ref, right_ref, tie_ref, left_out, right_out):
+    def kernel(left_ref, right_ref, *refs):
+        left_out, right_out = refs[-2:]
         left_out[...] = left_ref[...]
         right_out[...] = right_ref[...]
 
@@ -281,13 +282,13 @@
         in_specs=[
             pl.BlockSpec((half // 2, T, T), lambda i: (i, 0, 0)),
             pl.BlockSpec((half // 2, T, T), lambda i: (2 + i, 0, 0)),
-            ANY,
-        ],
+        ]
+        + [ANY] * len(ties),
         out_specs=[pl.BlockSpec((half // 2, T, T), lambda i: (i, 0, 0))] * 2,
         compiler_params=params(60),
         cost_estimate=cost(1, 0),
         name="relayed",
-    )(left, right, tie)
+    )(left, right, *ties)
 
 
 def ring(piece, axes, shift):
@@ -409,13 +410,14 @@
     left, right = ring(line, second, 1), ring(line, second, 3)
     operands = (rows, cols, pos, turned, turned_other, cotangent, g_other)
     part0, part2, part1 = grads((0, 2, 1), *operands)
-    left_half, right_half = relayed(left, right, part0)
+    line_swapped = other_core(line)
+    left_half, right_half = relayed(left, right, part0, line_swapped)
     left, right = held((left, right), left_half)
-    part0, part2, part1, part3 = grads((3,), *operands, (part0, part2, part1), (left_half,))
+    part2, part1 = held((part2, part1), left_half)
+    (part3,) = grads((3,), *operands, (), (left_half,))
     near = [line, left, right]
-    swapped = [other_core(block) for block in near]
+    swapped = [line_swapped, other_core(left), other_core(right)]
     far = held((ring(left_half, second, 1), ring(right_half, second, 3)), part3, *swapped)
-    part0, part2, part1, part3 = held((part0, part2, part1, part3), far[0])
     arrays = near + list(far) + swapped + [other_core(block) for block in far]
     projected, token_grad, sums = project(rows, cols, pos, arrays, tokens, normed, scale, gain2, cotangent)
     count = sums.shape[0]

time: 170 us -> 174 us (1.024)
  waiting for transfers between devices: 52.7 us -> 63.9 us
  starting transfers between devices: 37 us -> 32.4 us
  local copies, waits for them, and re-layouts: 8.28 us -> 6.02 us
    ppermute x19, waiting for transfers between devices: 46.6 us -> 57.6 us  [ring(): return lax.ppermute(piece, ALL, pairs)]
    ppermute x19, starting transfers between devices: 35 us -> 30.3 us  [ring(): return lax.ppermute(piece, ALL, pairs)]
    unnamed x38 -> x32, local copies, waits for them, and re-layouts: 8.28 us -> 6.02 us
  transfers between devices with their start and end apart: 28 -> 28, of which waited for: 18 -> 18; matrix products, arithmetic and copies ran while one was open for 0% -> 0% of each run, Pallas kernels for 37% -> 34%
where the time goes in v11:
time: 174 us; the launch traced here: 173 us
  Pallas kernels  68.6 us (39%)
  waiting for transfers between devices  63.9 us (37%)
  starting transfers between devices  32.4 us (19%)
  local copies, waits for them, and re-layouts  6.02 us (3%)
    ppermute x19, waiting for transfers between devices, ring(): return lax.ppermute(piece, ALL, pairs)  57.6 us
    pallas_call x1, Pallas kernels, project(): pl.pallas_call(lambda *refs: project_kernel(sources, *refs), out_shape=(j...  31.9 us
    ppermute x19, starting transfers between devices, ring(): return lax.ppermute(piece, ALL, pairs)  30.3 us
    pallas_call x2, Pallas kernels, grads(): pl.pallas_call(lambda *refs: grad_kernel(aheads, each, *refs), out_shape=...  22.3 us
    ppermute x9, waiting for transfers between devices, other_core(): return lax.ppermute(value, 'c', [(0, 1), (1, 0)])  6.29 us
    unnamed x32, local copies, waits for them, and re-layouts  6.02 us
    pallas_call x1, Pallas kernels, cut_sum(): pl.pallas_call(kernel, out_shape=[jax.ShapeDtypeStruct((each + 1, T, T),...  4.7 us
    pallas_call x2, Pallas kernels, norm(): pl.pallas_call(norm_kernel, out_shape=(jax.ShapeDtypeStruct((count, width...  3.53 us
  transfers between devices with their start and end apart: 28, of which 18 were waited for; matrix products, arithmetic and copies ran while one was open for 0% of the time, Pallas kernels for 34%

profile of v11, /device:TPU:0, one launch (start us, length us, event | category | flops | bytes accessed | tf_op | source)
XLA Modules:
  0.0 172.9 jit_solution(1113485579733888769)
XLA Ops:
  1.2 4.0 %collective-permute-start.1 = (bf16[16,128,128]{2,1,0:T(8,128)(2,1)}, bf16[16,128,128]{2,1,0:T(8,128)(2,1)S(1)}, u32[]{:S(2)}, u32[]{:S(2)}) collective-permute-start(bf16[16,128,128]{2,1,0:T(8,128)(2,1)} %refs_0_.4), channel_id=1, source_target_pairs={{0,16},{1,17},{2,18},{3,19},{4,68},{5,69},{6,70},{7,71},{8,24},{9,... | collective-permute-start | bytes 1572872 | tf_op jit(solution)/shard_map/ppermute | solution.py:303
  5.2 1.0 collective-permute-start
  6.2 2.2 %collective-permute-start.2 = (bf16[16,128,128]{2,1,0:T(8,128)(2,1)}, bf16[16,128,128]{2,1,0:T(8,128)(2,1)S(1)}, u32[]{:S(2)}, u32[]{:S(2)}) collective-permute-start(bf16[16,128,128]{2,1,0:T(8,128)(2,1)} %refs_0_.4), channel_id=1, source_target_pairs={{0,24},{1,25},{2,26},{3,27},{4,100},{5,101},{6,102},{7,103},{8,0},... | collective-permute-start | bytes 1572872 | tf_op jit(solution)/shard_map/ppermute | solution.py:303
  8.4 1.2 copy-done.3
  9.6 0.7 copy-done.7
  10.4 1.3 norm.2
  11.7 1.0 copy-done.4
  12.7 2.2 %norm.3 = (bf16[128,4096]{1,0:T(8,128)(2,1)}, bf16[32,128,128]{2,1,0:T(8,128)(2,1)S(1)}, f32[128,128]{1,0:T(8,128)}) custom-call(bf16[128,4096]{1,0:T(8,128)(2,1)S(1)} %collective-permute-done.3.x_ref, f32[1,4096]{1,0:T(1,128)S(1)} %bitcast.9), custom_call_target="tpu_custom_call" | custom-call | flops 1100000000 | tf_op jit(solution)/shard_map/norm/pallas_call | solution.py:66
  14.9 3.3 %collective-permute-done.refs_1_ = bf16[16,128,128]{2,1,0:T(8,128)(2,1)S(1)} collective-permute-done((bf16[16,128,128]{2,1,0:T(8,128)(2,1)}, bf16[16,128,128]{2,1,0:T(8,128)(2,1)S(1)}, u32[]{:S(2)}, u32[]{:S(2)}) %collective-permute-start) | collective-permute-done | bytes 524320 | tf_op jit(solution)/shard_map/ppermute | solution.py:303
  18.2 1.1 collective-permute-done.2.refs_3_
  19.2 1.5 joined.1.refs_8_
  20.8 3.1 %collective-permute-start.5 = (bf16[64,128,128]{2,1,0:T(8,128)(2,1)}, bf16[64,128,128]{2,1,0:T(8,128)(2,1)S(1)}, u32[]{:S(2)}, u32[]{:S(2)}) collective-permute-start(bf16[64,128,128]{2,1,0:T(8,128)(2,1)} %joined.1.refs_8_), channel_id=1, source_target_pairs={{0,96},{1,97},{2,98},{3,99},{4,28},{5,29},{6,30},{7,31},{8,104},{9... | collective-permute-start | bytes 6291464 | tf_op jit(solution)/shard_map/ppermute | solution.py:303
  24.6 14.3 %grads.2 = (bf16[64,128,128]{2,1,0:T(8,128)(2,1)}, bf16[64,128,128]{2,1,0:T(8,128)(2,1)}, bf16[64,128,128]{2,1,0:T(8,128)(2,1)}) custom-call(s32[512]{0:T(512)} %refs_0_.7, s32[512]{0:T(512)} %refs_1_.5, s32[4]{0:T(128)} %pad_add_fusion.refs_2_.pos_ref, bf16[32,128,128]{2,1,0:T(8,128)(2,1)} %copy-done, bf16[32,128,128]{2,1,0:T(8,128)(2,1)} %copy-done.1, ...), custom_call_target="tpu_custom_call" | custom-call | flops 2200000000 | tf_op jit(solution)/shard_map/grads/pallas_call | solution.py:126
  38.9 8.9 %collective-permute-done.5.right_ref.refs_1_ = bf16[64,128,128]{2,1,0:T(8,128)(2,1)S(1)} collective-permute-done((bf16[64,128,128]{2,1,0:T(8,128)(2,1)}, bf16[64,128,128]{2,1,0:T(8,128)(2,1)S(1)}, u32[]{:S(2)}, u32[]{:S(2)}) %collective-permute-start.5) | collective-permute-done | bytes 2097184 | tf_op jit(solution)/shard_map/ppermute | solution.py:303
  47.8 3.7 %collective-permute-done.4.left_ref.refs_0_ = bf16[64,128,128]{2,1,0:T(8,128)(2,1)} collective-permute-done((bf16[64,128,128]{2,1,0:T(8,128)(2,1)}, bf16[64,128,128]{2,1,0:T(8,128)(2,1)}, u32[]{:S(2)}, u32[]{:S(2)}) %collective-permute-start.4) | collective-permute-done | bytes 2097184 | tf_op jit(solution)/shard_map/ppermute | solution.py:303
  51.5 2.6 %relayed.1 = (bf16[32,128,128]{2,1,0:T(8,128)(2,1)}, bf16[32,128,128]{2,1,0:T(8,128)(2,1)}) custom-call(bf16[64,128,128]{2,1,0:T(8,128)(2,1)} %collective-permute-done.4.left_ref.refs_0_, bf16[64,128,128]{2,1,0:T(8,128)(2,1)} %copy-done.11, bf16[64,128,128]{2,1,0:T(8,128)(2,1)} %get-tuple-element.36.refs_0_, ...), custom_call_target="tpu_custom_call" | custom-call | flops 1100000000 | tf_op jit(solution)/shard_map/relayed/pallas_call | solution.py:278
  54.6 1.2 collective-permute-start.9
  55.8 0.8 collective-permute-start.8
  56.6 1.5 collective-permute-start.14
  58.1 8.1 %grads.3.refs_2_ = bf16[64,128,128]{2,1,0:T(8,128)(2,1)} custom-call(s32[512]{0:T(512)} %refs_0_.7, s32[512]{0:T(512)} %refs_1_.5, s32[4]{0:T(128)} %pad_add_fusion.refs_2_.pos_ref, bf16[32,128,128]{2,1,0:T(8,128)(2,1)} %copy-done, bf16[32,128,128]{2,1,0:T(8,128)(2,1)} %copy-done.1, bf16[128,14336]{1,0:T(8,128)(2,1)} %refs_7_.1, ...), custom_call_target="tpu_custom_call" | custom-call | flops 2200000000 | tf_op jit(solution)/shard_map/grads/pallas_call | solution.py:126
  66.2 3.5 %collective-permute-done.9.refs_1_ = bf16[32,128,128]{2,1,0:T(8,128)(2,1)} collective-permute-done((bf16[32,128,128]{2,1,0:T(8,128)(2,1)}, bf16[32,128,128]{2,1,0:T(8,128)(2,1)}, u32[]{:S(2)}, u32[]{:S(2)}) %collective-permute-start.9) | collective-permute-done | bytes 1048608 | tf_op jit(solution)/shard_map/ppermute | solution.py:303
  69.7 3.0 %collective-permute-start.15 = (bf16[64,128,128]{2,1,0:T(8,128)(2,1)}, bf16[64,128,128]{2,1,0:T(8,128)(2,1)}, u32[]{:S(2)}, u32[]{:S(2)}) collective-permute-start(bf16[64,128,128]{2,1,0:T(8,128)(2,1)} %get-tuple-element.48), channel_id=1, source_target_pairs={{0,2},{1,3},{2,0},{3,1},{4,68},{5,69},{6,70},{7,71},{8,10},{9,11},... | collective-permute-start | bytes 6291464 | tf_op jit(solution)/shard_map/ppermute | solution.py:303
  72.7 10.1 %collective-permute-done.8.refs_0_ = bf16[32,128,128]{2,1,0:T(8,128)(2,1)} collective-permute-done((bf16[32,128,128]{2,1,0:T(8,128)(2,1)S(1)}, bf16[32,128,128]{2,1,0:T(8,128)(2,1)}, u32[]{:S(2)}, u32[]{:S(2)}) %collective-permute-start.8) | collective-permute-done | bytes 1048608 | tf_op jit(solution)/shard_map/ppermute | solution.py:303
  82.8 2.8 %collective-permute-start.16 = (bf16[64,128,128]{2,1,0:T(8,128)(2,1)}, bf16[64,128,128]{2,1,0:T(8,128)(2,1)}, u32[]{:S(2)}, u32[]{:S(2)}) collective-permute-start(bf16[64,128,128]{2,1,0:T(8,128)(2,1)} %grads.3.refs_2_), channel_id=1, source_target_pairs={{0,3},{1,0},{2,1},{3,2},{4,100},{5,101},{6,102},{7,103},{8,11},{9,... | collective-permute-start | bytes 6291464 | tf_op jit(solution)/shard_map/ppermute | solution.py:303
  85.5 1.4 copy-done.13
  87.4 2.4 %collective-permute-done.12.refs_16_ = bf16[32,128,128]{2,1,0:T(8,128)(2,1)S(1)} collective-permute-done((bf16[32,128,128]{2,1,0:T(8,128)(2,1)}, bf16[32,128,128]{2,1,0:T(8,128)(2,1)S(1)}, u32[]{:S(2)}, u32[]{:S(2)}) %collective-permute-start.12) | collective-permute-done | bytes 1048608 | tf_op jit(solution)/shard_map/ppermute | solution.py:404
  89.8 1.5 collective-permute-done.13.refs_17_
  91.3 1.0 copy-done.15
  92.3 31.9 %project.1 = (bf16[128,14336]{1,0:T(8,128)(2,1)}, bf16[128,4096]{1,0:T(8,128)(2,1)}, f32[32,128]{1,0:T(8,128)}) custom-call(s32[512]{0:T(512)} %refs_0_.7, s32[512]{0:T(512)} %refs_1_.5, s32[4]{0:T(128)} %pad_add_fusion.refs_2_.pos_ref, bf16[128,4096]{1,0:T(8,128)(2,1)} %refs_3_.1, bf16[128,4096]{1,0:T(8,128)(2,1)} %copy-done.4, f32[128,128]{1,0:T(8,128)} %copy-done.6, ...), custom_call_target="tpu_custom_call" | custom-call | flops 2200000000 | tf_op jit(solution)/shard_map/project/pallas_call | solution.py:216
  124.6 1.2 collective-permute-done.17.refs_5_
  125.9 0.7 copy-done.9
  126.6 4.7 %cut_sum.1 = (bf16[17,128,128]{2,1,0:T(8,128)(2,1)S(1)}, bf16[17,128,128]{2,1,0:T(8,128)(2,1)S(1)}, bf16[17,128,128]{2,1,0:T(8,128)(2,1)S(1)}, bf16[17,128,128]{2,1,0:T(8,128)(2,1)S(1)}) custom-call(bf16[64,128,128]{2,1,0:T(8,128)(2,1)S(1)} %copy-done.2, bf16[64,128,128]{2,1,0:T(8,128)(2,1)} %collective-permute-done.14.refs_1_, ...), custom_call_target="tpu_custom_call" | custom-call | flops 1100000000 | tf_op jit(solution)/shard_map/cut_sum/pallas_call | solution.py:346
  131.4 0.9 collective-permute-start.19
  132.3 2.3 %collective-permute-start.20 = (bf16[17,128,128]{2,1,0:T(8,128)(2,1)S(1)}, bf16[17,128,128]{2,1,0:T(8,128)(2,1)S(1)}, u32[]{:S(2)}, u32[]{:S(2)}) collective-permute-start(bf16[17,128,128]{2,1,0:T(8,128)(2,1)S(1)} %get-tuple-element.53), channel_id=1, source_target_pairs={{0,96},{1,97},{2,98},{3,99},{4,28},{5,29},{6,30},{7,31},{8,104},{9... | collective-permute-start | bytes 1671176 | tf_op jit(solution)/shard_map/ppermute | solution.py:303
  134.6 13.5 %collective-permute-done.18.refs_1_ = bf16[17,128,128]{2,1,0:T(8,128)(2,1)S(1)} collective-permute-done((bf16[17,128,128]{2,1,0:T(8,128)(2,1)S(1)}, bf16[17,128,128]{2,1,0:T(8,128)(2,1)S(1)}, u32[]{:S(2)}, u32[]{:S(2)}) %collective-permute-start.18) | collective-permute-done | bytes 557088 | tf_op jit(solution)/shard_map/ppermute | solution.py:303
  148.1 0.9 collective-permute-done.20.refs_3_
  149.3 1.4 collective-permute-start.21
  150.7 2.4 %collective-permute-start.22 = (bf16[5,128,128]{2,1,0:T(8,128)(2,1)S(1)}, bf16[5,128,128]{2,1,0:T(8,128)(2,1)S(1)}, u32[]{:S(2)}, u32[]{:S(2)}) collective-permute-start(bf16[5,128,128]{2,1,0:T(8,128)(2,1)S(1)} %get-tuple-element.56), channel_id=1, source_target_pairs={{0,16},{1,17},{2,18},{3,19},{4,6},{5,7},{6,4},{7,5},{8,24},{9,25},... | collective-permute-start | bytes 491528 | tf_op jit(solution)/shard_map/ppermute | solution.py:303
  153.1 1.4 collective-permute-start.23
  154.4 1.5 collective-permute-done.21.refs_1_
  155.9 2.2 %collective-permute-done.22.refs_2_ = bf16[5,128,128]{2,1,0:T(8,128)(2,1)S(1)} collective-permute-done((bf16[5,128,128]{2,1,0:T(8,128)(2,1)S(1)}, bf16[5,128,128]{2,1,0:T(8,128)(2,1)S(1)}, u32[]{:S(2)}, u32[]{:S(2)}) %collective-permute-start.22) | collective-permute-done | bytes 163872 | tf_op jit(solution)/shard_map/ppermute | solution.py:303
  158.6 0.9 collective-permute-start.26
  160.0 0.9 collective-permute-start.24
  160.9 5.2 %collective-permute-done.26.refs_3_ = bf16[5,128,128]{2,1,0:T(8,128)(2,1)S(1)} collective-permute-done((bf16[5,128,128]{2,1,0:T(8,128)(2,1)S(1)}, bf16[5,128,128]{2,1,0:T(8,128)(2,1)S(1)}, u32[]{:S(2)}, u32[]{:S(2)}) %collective-permute-start.26) | collective-permute-done | bytes 163872 | tf_op jit(solution)/shard_map/ppermute | solution.py:303
  166.1 2.0 %collective-permute-done.25.refs_2_ = bf16[5,128,128]{2,1,0:T(8,128)(2,1)S(1)} collective-permute-done((bf16[5,128,128]{2,1,0:T(8,128)(2,1)S(1)}, bf16[5,128,128]{2,1,0:T(8,128)(2,1)S(1)}, u32[]{:S(2)}, u32[]{:S(2)}) %collective-permute-start.25) | collective-permute-done | bytes 163872 | tf_op jit(solution)/shard_map/ppermute | solution.py:303
  168.1 1.4 collective-permute-done.24.refs_1_
  169.5 1.6 place.1
  171.1 1.2 collective-permute-done.27
  (56 shorter events, 4.8 us)
Async XLA Ops:
  0.6 24.0 %collective-permute-start.6 = (bf16[128,14336]{1,0:T(8,128)(2,1)}, bf16[128,14336]{1,0:T(8,128)(2,1)}, u32[]{:S(2)}, u32[]{:S(2)}) collective-permute-start(bf16[128,14336]{1,0:T(8,128)(2,1)} %refs_7_.1), channel_id=1, source_target_pairs={{0,4},{4,0},{1,5},{5,1},{2,6},{6,2},{3,7},{7,3},{8,12},{12,8},{9,1... | collective-permute-start | bytes 11010056 | tf_op jit(solution)/shard_map/ppermute | solution.py:404
  0.7 11.9 %collective-permute-start.3 = (bf16[128,4096]{1,0:T(8,128)(2,1)}, bf16[128,4096]{1,0:T(8,128)(2,1)S(1)}, u32[]{:S(2)}, u32[]{:S(2)}) collective-permute-start(bf16[128,4096]{1,0:T(8,128)(2,1)} %refs_3_.1), channel_id=1, source_target_pairs={{0,4},{4,0},{1,5},{5,1},{2,6},{6,2},{3,7},{7,3},{8,12},{12,8},{9,1... | collective-permute-start | bytes 3145736 | tf_op jit(solution)/shard_map/ppermute | solution.py:404
  1.2 13.7 %collective-permute-start.1 = (bf16[16,128,128]{2,1,0:T(8,128)(2,1)}, bf16[16,128,128]{2,1,0:T(8,128)(2,1)S(1)}, u32[]{:S(2)}, u32[]{:S(2)}) collective-permute-start(bf16[16,128,128]{2,1,0:T(8,128)(2,1)} %refs_0_.4), channel_id=1, source_target_pairs={{0,16},{1,17},{2,18},{3,19},{4,68},{5,69},{6,70},{7,71},{8,24},{9,... | collective-permute-start | bytes 1572872 | tf_op jit(solution)/shard_map/ppermute | solution.py:303
  5.2 13.0 %collective-permute-start = (bf16[16,128,128]{2,1,0:T(8,128)(2,1)}, bf16[16,128,128]{2,1,0:T(8,128)(2,1)S(1)}, u32[]{:S(2)}, u32[]{:S(2)}) collective-permute-start(bf16[16,128,128]{2,1,0:T(8,128)(2,1)} %refs_0_.4), channel_id=1, source_target_pairs={{0,8},{1,9},{2,10},{3,11},{4,36},{5,37},{6,38},{7,39},{8,16},{9,17... | collective-permute-start | bytes 1572872 | tf_op jit(solution)/shard_map/ppermute | solution.py:303
  6.2 13.0 %collective-permute-start.2 = (bf16[16,128,128]{2,1,0:T(8,128)(2,1)}, bf16[16,128,128]{2,1,0:T(8,128)(2,1)S(1)}, u32[]{:S(2)}, u32[]{:S(2)}) collective-permute-start(bf16[16,128,128]{2,1,0:T(8,128)(2,1)} %refs_0_.4), channel_id=1, source_target_pairs={{0,24},{1,25},{2,26},{3,27},{4,100},{5,101},{6,102},{7,103},{8,0},... | collective-permute-start | bytes 1572872 | tf_op jit(solution)/shard_map/ppermute | solution.py:303
  8.4 1.2 copy-start.3
  9.6 0.7 copy-start.7
  10.4 2.3 %copy-start.8 = (f32[4096]{0:T(1024)S(1)}, f32[4096]{0:T(1024)}, u32[]{:S(2)}) copy-start(f32[4096]{0:T(1024)} %param.7) | copy-start | bytes 49156
  11.7 1.0 copy-start.4
  12.6 8.1 %copy-start = (bf16[32,128,128]{2,1,0:T(8,128)(2,1)}, bf16[32,128,128]{2,1,0:T(8,128)(2,1)S(1)}, u32[]{:S(2)}) copy-start(bf16[32,128,128]{2,1,0:T(8,128)(2,1)S(1)} %get-tuple-element.34.refs_4_.refs_3_) | copy-start | bytes 3145732
  12.6 8.1 %copy-start.6 = (f32[128,128]{1,0:T(8,128)}, f32[128,128]{1,0:T(8,128)S(1)}, u32[]{:S(2)}) copy-start(f32[128,128]{1,0:T(8,128)S(1)} %get-tuple-element.33.refs_5_) | copy-start | bytes 196612
  12.6 6.6 %copy-start.5 = (bf16[16,128,128]{2,1,0:T(8,128)(2,1)S(1)}, bf16[16,128,128]{2,1,0:T(8,128)(2,1)}, u32[]{:S(2)}) copy-start(bf16[16,128,128]{2,1,0:T(8,128)(2,1)} %refs_0_.4) | copy-start | bytes 1572868
  14.9 5.8 %copy-start.1 = (bf16[32,128,128]{2,1,0:T(8,128)(2,1)}, bf16[32,128,128]{2,1,0:T(8,128)(2,1)S(1)}, u32[]{:S(2)}) copy-start(bf16[32,128,128]{2,1,0:T(8,128)(2,1)S(1)} %get-tuple-element.35.refs_5_.refs_4_) | copy-start | bytes 3145732
  20.7 18.1 %collective-permute-start.7 = (bf16[64,128,128]{2,1,0:T(8,128)(2,1)}, bf16[64,128,128]{2,1,0:T(8,128)(2,1)}, u32[]{:S(2)}, u32[]{:S(2)}) collective-permute-start(bf16[64,128,128]{2,1,0:T(8,128)(2,1)} %joined.1.refs_8_), channel_id=1, source_target_pairs={{0,4},{4,0},{1,5},{5,1},{2,6},{6,2},{3,7},{7,3},{8,12},{12,8},{9,1... | collective-permute-start | bytes 6291464 | tf_op jit(solution)/shard_map/ppermute | solution.py:404
  20.8 27.0 %collective-permute-start.5 = (bf16[64,128,128]{2,1,0:T(8,128)(2,1)}, bf16[64,128,128]{2,1,0:T(8,128)(2,1)S(1)}, u32[]{:S(2)}, u32[]{:S(2)}) collective-permute-start(bf16[64,128,128]{2,1,0:T(8,128)(2,1)} %joined.1.refs_8_), channel_id=1, source_target_pairs={{0,96},{1,97},{2,98},{3,99},{4,28},{5,29},{6,30},{7,31},{8,104},{9... | collective-permute-start | bytes 6291464 | tf_op jit(solution)/shard_map/ppermute | solution.py:303
  23.9 27.6 %collective-permute-start.4 = (bf16[64,128,128]{2,1,0:T(8,128)(2,1)}, bf16[64,128,128]{2,1,0:T(8,128)(2,1)}, u32[]{:S(2)}, u32[]{:S(2)}) collective-permute-start(bf16[64,128,128]{2,1,0:T(8,128)(2,1)} %joined.1.refs_8_), channel_id=1, source_target_pairs={{0,32},{1,33},{2,34},{3,35},{4,12},{5,13},{6,14},{7,15},{8,40},{9,... | collective-permute-start | bytes 6291464 | tf_op jit(solution)/shard_map/ppermute | solution.py:303
  47.8 3.7 %copy-start.11 = (bf16[64,128,128]{2,1,0:T(8,128)(2,1)}, bf16[64,128,128]{2,1,0:T(8,128)(2,1)S(1)}, u32[]{:S(2)}) copy-start(bf16[64,128,128]{2,1,0:T(8,128)(2,1)S(1)} %collective-permute-done.5.right_ref.refs_1_) | copy-start | bytes 6291460
  54.1 1.7 %copy-start.12 = (bf16[32,128,128]{2,1,0:T(8,128)(2,1)S(1)}, bf16[32,128,128]{2,1,0:T(8,128)(2,1)}, u32[]{:S(2)}) copy-start(bf16[32,128,128]{2,1,0:T(8,128)(2,1)} %get-tuple-element.37.refs_2_.refs_7_) | copy-start | bytes 3145732
  54.1 31.5 %collective-permute-start.10 = (bf16[64,128,128]{2,1,0:T(8,128)(2,1)}, bf16[64,128,128]{2,1,0:T(8,128)(2,1)S(1)}, u32[]{:S(2)}, u32[]{:S(2)}) collective-permute-start(bf16[64,128,128]{2,1,0:T(8,128)(2,1)} %get-tuple-element.38.refs_9_), channel_id=1, source_target_pairs={{0,4},{4,0},{1,5},{5,1},{2,6},{6,2},{3,7},{7,3},{8,12},{12,8},{9,1... | collective-permute-start | bytes 6291464 | tf_op jit(solution)/shard_map/ppermute | solution.py:404
  54.1 31.5 %collective-permute-start.11 = (bf16[64,128,128]{2,1,0:T(8,128)(2,1)}, bf16[64,128,128]{2,1,0:T(8,128)(2,1)}, u32[]{:S(2)}, u32[]{:S(2)}) collective-permute-start(bf16[64,128,128]{2,1,0:T(8,128)(2,1)} %get-tuple-element.39.refs_10_), channel_id=1, source_target_pairs={{0,4},{4,0},{1,5},{5,1},{2,6},{6,2},{3,7},{7,3},{8,12},{12,8},{9,1... | collective-permute-start | bytes 6291464 | tf_op jit(solution)/shard_map/ppermute | solution.py:404
  54.6 15.1 %collective-permute-start.9 = (bf16[32,128,128]{2,1,0:T(8,128)(2,1)}, bf16[32,128,128]{2,1,0:T(8,128)(2,1)}, u32[]{:S(2)}, u32[]{:S(2)}) collective-permute-start(bf16[32,128,128]{2,1,0:T(8,128)(2,1)} %get-tuple-element.40), channel_id=1, source_target_pairs={{0,96},{1,97},{2,98},{3,99},{4,28},{5,29},{6,30},{7,31},{8,104},{9... | collective-permute-start | bytes 3145736 | tf_op jit(solution)/shard_map/ppermute | solution.py:303
  55.8 27.0 %collective-permute-start.8 = (bf16[32,128,128]{2,1,0:T(8,128)(2,1)S(1)}, bf16[32,128,128]{2,1,0:T(8,128)(2,1)}, u32[]{:S(2)}, u32[]{:S(2)}) collective-permute-start(bf16[32,128,128]{2,1,0:T(8,128)(2,1)S(1)} %copy-done.12), channel_id=1, source_target_pairs={{0,32},{1,33},{2,34},{3,35},{4,12},{5,13},{6,14},{7,15},{8,40},{9,... | collective-permute-start | bytes 3145736 | tf_op jit(solution)/shard_map/ppermute | solution.py:303
  56.6 68.0 %collective-permute-start.14 = (bf16[64,128,128]{2,1,0:T(8,128)(2,1)}, bf16[64,128,128]{2,1,0:T(8,128)(2,1)}, u32[]{:S(2)}, u32[]{:S(2)}) collective-permute-start(bf16[64,128,128]{2,1,0:T(8,128)(2,1)} %get-tuple-element.47), channel_id=1, source_target_pairs={{0,1},{1,2},{2,3},{3,0},{4,36},{5,37},{6,38},{7,39},{8,9},{9,10},{... | collective-permute-start | bytes 6291464 | tf_op jit(solution)/shard_map/ppermute | solution.py:303
  69.7 54.9 %collective-permute-start.15 = (bf16[64,128,128]{2,1,0:T(8,128)(2,1)}, bf16[64,128,128]{2,1,0:T(8,128)(2,1)}, u32[]{:S(2)}, u32[]{:S(2)}) collective-permute-start(bf16[64,128,128]{2,1,0:T(8,128)(2,1)} %get-tuple-element.48), channel_id=1, source_target_pairs={{0,2},{1,3},{2,0},{3,1},{4,68},{5,69},{6,70},{7,71},{8,10},{9,11},... | collective-permute-start | bytes 6291464 | tf_op jit(solution)/shard_map/ppermute | solution.py:303
  82.8 41.9 %collective-permute-start.16 = (bf16[64,128,128]{2,1,0:T(8,128)(2,1)}, bf16[64,128,128]{2,1,0:T(8,128)(2,1)}, u32[]{:S(2)}, u32[]{:S(2)}) collective-permute-start(bf16[64,128,128]{2,1,0:T(8,128)(2,1)} %grads.3.refs_2_), channel_id=1, source_target_pairs={{0,3},{1,0},{2,1},{3,2},{4,100},{5,101},{6,102},{7,103},{8,11},{9,... | collective-permute-start | bytes 6291464 | tf_op jit(solution)/shard_map/ppermute | solution.py:303
  85.5 1.4 copy-start.13
  86.9 2.9 %collective-permute-start.12 = (bf16[32,128,128]{2,1,0:T(8,128)(2,1)}, bf16[32,128,128]{2,1,0:T(8,128)(2,1)S(1)}, u32[]{:S(2)}, u32[]{:S(2)}) collective-permute-start(bf16[32,128,128]{2,1,0:T(8,128)(2,1)} %get-tuple-element.41.refs_11_), channel_id=1, source_target_pairs={{0,4},{4,0},{1,5},{5,1},{2,6},{6,2},{3,7},{7,3},{8,12},{12,8},{9,1... | collective-permute-start | bytes 3145736 | tf_op jit(solution)/shard_map/ppermute | solution.py:404
  86.9 4.4 %collective-permute-start.13 = (bf16[32,128,128]{2,1,0:T(8,128)(2,1)}, bf16[32,128,128]{2,1,0:T(8,128)(2,1)S(1)}, u32[]{:S(2)}, u32[]{:S(2)}) collective-permute-start(bf16[32,128,128]{2,1,0:T(8,128)(2,1)} %get-tuple-element.42.refs_12_), channel_id=1, source_target_pairs={{0,4},{4,0},{1,5},{5,1},{2,6},{6,2},{3,7},{7,3},{8,12},{12,8},{9,1... | collective-permute-start | bytes 3145736 | tf_op jit(solution)/shard_map/ppermute | solution.py:404
  89.8 2.5 %copy-start.14 = (bf16[32,128,128]{2,1,0:T(8,128)(2,1)}, bf16[32,128,128]{2,1,0:T(8,128)(2,1)S(1)}, u32[]{:S(2)}) copy-start(bf16[32,128,128]{2,1,0:T(8,128)(2,1)S(1)} %collective-permute-done.12.refs_16_) | copy-start | bytes 3145732
  91.3 1.0 copy-start.15
  92.3 33.6 %copy-start.2 = (bf16[64,128,128]{2,1,0:T(8,128)(2,1)S(1)}, bf16[64,128,128]{2,1,0:T(8,128)(2,1)}, u32[]{:S(2)}) copy-start(bf16[64,128,128]{2,1,0:T(8,128)(2,1)} %get-tuple-element.36.refs_0_) | copy-start | bytes 6291460
  124.2 1.7 collective-permute-start.17
  125.9 0.7 copy-start.9
  131.3 16.8 %collective-permute-start.18 = (bf16[17,128,128]{2,1,0:T(8,128)(2,1)S(1)}, bf16[17,128,128]{2,1,0:T(8,128)(2,1)S(1)}, u32[]{:S(2)}, u32[]{:S(2)}) collective-permute-start(bf16[17,128,128]{2,1,0:T(8,128)(2,1)S(1)} %get-tuple-element.51), channel_id=1, source_target_pairs={{0,32},{1,33},{2,34},{3,35},{4,12},{5,13},{6,14},{7,15},{8,40},{9,... | collective-permute-start | bytes 1671176 | tf_op jit(solution)/shard_map/ppermute | solution.py:303
  131.4 16.7 %collective-permute-start.19 = (bf16[17,128,128]{2,1,0:T(8,128)(2,1)S(1)}, bf16[17,128,128]{2,1,0:T(8,128)(2,1)S(1)}, u32[]{:S(2)}, u32[]{:S(2)}) collective-permute-start(bf16[17,128,128]{2,1,0:T(8,128)(2,1)S(1)} %get-tuple-element.52), channel_id=1, source_target_pairs={{0,64},{1,65},{2,66},{3,67},{4,20},{5,21},{6,22},{7,23},{8,72},{9,... | collective-permute-start | bytes 1671176 | tf_op jit(solution)/shard_map/ppermute | solution.py:303
  132.3 16.7 %collective-permute-start.20 = (bf16[17,128,128]{2,1,0:T(8,128)(2,1)S(1)}, bf16[17,128,128]{2,1,0:T(8,128)(2,1)S(1)}, u32[]{:S(2)}, u32[]{:S(2)}) collective-permute-start(bf16[17,128,128]{2,1,0:T(8,128)(2,1)S(1)} %get-tuple-element.53), channel_id=1, source_target_pairs={{0,96},{1,97},{2,98},{3,99},{4,28},{5,29},{6,30},{7,31},{8,104},{9... | collective-permute-start | bytes 1671176 | tf_op jit(solution)/shard_map/ppermute | solution.py:303
  149.3 20.2 %copy-start.10 = (s32[4]{0:T(128)S(1)}, s32[4]{0:T(128)}, u32[]{:S(2)}) copy-start(s32[4]{0:T(128)} %pad_add_fusion.refs_2_.pos_ref) | copy-start | bytes 52
  149.3 6.6 %collective-permute-start.21 = (bf16[5,128,128]{2,1,0:T(8,128)(2,1)S(1)}, bf16[5,128,128]{2,1,0:T(8,128)(2,1)S(1)}, u32[]{:S(2)}, u32[]{:S(2)}) collective-permute-start(bf16[5,128,128]{2,1,0:T(8,128)(2,1)S(1)} %get-tuple-element.55), channel_id=1, source_target_pairs={{0,8},{1,9},{2,10},{3,11},{4,5},{5,6},{6,7},{7,4},{8,16},{9,17},{1... | collective-permute-start | bytes 491528 | tf_op jit(solution)/shard_map/ppermute | solution.py:303
  150.7 7.5 %collective-permute-start.22 = (bf16[5,128,128]{2,1,0:T(8,128)(2,1)S(1)}, bf16[5,128,128]{2,1,0:T(8,128)(2,1)S(1)}, u32[]{:S(2)}, u32[]{:S(2)}) collective-permute-start(bf16[5,128,128]{2,1,0:T(8,128)(2,1)S(1)} %get-tuple-element.56), channel_id=1, source_target_pairs={{0,16},{1,17},{2,18},{3,19},{4,6},{5,7},{6,4},{7,5},{8,24},{9,25},... | collective-permute-start | bytes 491528 | tf_op jit(solution)/shard_map/ppermute | solution.py:303
  153.1 5.4 %collective-permute-start.23 = (bf16[5,128,128]{2,1,0:T(8,128)(2,1)S(1)}, bf16[5,128,128]{2,1,0:T(8,128)(2,1)S(1)}, u32[]{:S(2)}, u32[]{:S(2)}) collective-permute-start(bf16[5,128,128]{2,1,0:T(8,128)(2,1)S(1)} %get-tuple-element.57), channel_id=1, source_target_pairs={{0,24},{1,25},{2,26},{3,27},{4,7},{5,4},{6,5},{7,6},{8,0},{9,1},{1... | collective-permute-start | bytes 491528 | tf_op jit(solution)/shard_map/ppermute | solution.py:303
  158.6 7.5 %collective-permute-start.26 = (bf16[5,128,128]{2,1,0:T(8,128)(2,1)S(1)}, bf16[5,128,128]{2,1,0:T(8,128)(2,1)S(1)}, u32[]{:S(2)}, u32[]{:S(2)}) collective-permute-start(bf16[5,128,128]{2,1,0:T(8,128)(2,1)S(1)} %next_sum.3.refs_0_), channel_id=1, source_target_pairs={{0,3},{1,0},{2,1},{3,2},{4,7},{5,4},{6,5},{7,6},{8,11},{9,8},{10,9... | collective-permute-start | bytes 491528 | tf_op jit(solution)/shard_map/ppermute | solution.py:303
  159.5 8.6 %collective-permute-start.25 = (bf16[5,128,128]{2,1,0:T(8,128)(2,1)S(1)}, bf16[5,128,128]{2,1,0:T(8,128)(2,1)S(1)}, u32[]{:S(2)}, u32[]{:S(2)}) collective-permute-start(bf16[5,128,128]{2,1,0:T(8,128)(2,1)S(1)} %next_sum.3.refs_0_), channel_id=1, source_target_pairs={{0,2},{1,3},{2,0},{3,1},{4,6},{5,7},{6,4},{7,5},{8,10},{9,11},{10,... | collective-permute-start | bytes 491528 | tf_op jit(solution)/shard_map/ppermute | solution.py:303
  160.0 9.5 %collective-permute-start.24 = (bf16[5,128,128]{2,1,0:T(8,128)(2,1)S(1)}, bf16[5,128,128]{2,1,0:T(8,128)(2,1)S(1)}, u32[]{:S(2)}, u32[]{:S(2)}) collective-permute-start(bf16[5,128,128]{2,1,0:T(8,128)(2,1)S(1)} %next_sum.3.refs_0_), channel_id=1, source_target_pairs={{0,1},{1,2},{2,3},{3,0},{4,5},{5,6},{6,7},{7,4},{8,9},{9,10},{10,1... | collective-permute-start | bytes 491528 | tf_op jit(solution)/shard_map/ppermute | solution.py:303
  171.1 1.2 collective-permute-start.27

commit v12 on v10

--- a/solution.py
+++ b/solution.py
@@ -415,7 +415,6 @@
     near = [line, left, right]
     swapped = [other_core(block) for block in near]
     far = held((ring(left_half, second, 1), ring(right_half, second, 3)), part3, *swapped)
-    part0, part2, part1, part3 = held((part0, part2, part1, part3), far[0])
     arrays = near + list(far) + swapped + [other_core(block) for block in far]
     projected, token_grad, sums = project(rows, cols, pos, arrays, tokens, normed, scale, gain2, cotangent)
     count = sums.shape[0]

time: 170 us -> 170 us (level)
    unnamed x38 -> x32, local copies, waits for them, and re-layouts: 8.28 us -> 7.97 us
where the time goes in v12:
time: 170 us; the launch traced here: 168 us
  Pallas kernels  68.5 us (40%)
  waiting for transfers between devices  53.2 us (31%)
  starting transfers between devices  36.2 us (21%)
  local copies, waits for them, and re-layouts  7.97 us (5%)
    ppermute x19, waiting for transfers between devices, ring(): return lax.ppermute(piece, ALL, pairs)  48.2 us
    ppermute x19, starting transfers between devices, ring(): return lax.ppermute(piece, ALL, pairs)  34.2 us
    pallas_call x1, Pallas kernels, project(): pl.pallas_call(lambda *refs: project_kernel(sources, *refs), out_shape=(j...  32 us
    pallas_call x2, Pallas kernels, grads(): pl.pallas_call(lambda *refs: grad_kernel(aheads, each, *refs), out_shape=...  22.3 us
    unnamed x32, local copies, waits for them, and re-layouts  7.97 us
    ppermute x9, waiting for transfers between devices, other_core(): return lax.ppermute(value, 'c', [(0, 1), (1, 0)])  5.05 us
    pallas_call x1, Pallas kernels, cut_sum(): pl.pallas_call(kernel, out_shape=[jax.ShapeDtypeStruct((each + 1, T, T),...  4.7 us
    pallas_call x2, Pallas kernels, norm(): pl.pallas_call(norm_kernel, out_shape=(jax.ShapeDtypeStruct((count, width...  3.53 us
  transfers between devices with their start and end apart: 28, of which 18 were waited for; matrix products, arithmetic and copies ran while one was open for 0% of the time, Pallas kernels for 37%

profile of v12, /device:TPU:0, one launch (start us, length us, event | category | flops | bytes accessed | tf_op | source)
XLA Modules:
  0.0 168.0 jit_solution(18379569099483446189)
XLA Ops:
  1.2 2.0 %collective-permute-start = (bf16[16,128,128]{2,1,0:T(8,128)(2,1)}, bf16[16,128,128]{2,1,0:T(8,128)(2,1)S(1)}, u32[]{:S(2)}, u32[]{:S(2)}) collective-permute-start(bf16[16,128,128]{2,1,0:T(8,128)(2,1)} %refs_0_.4), channel_id=1, source_target_pairs={{0,8},{1,9},{2,10},{3,11},{4,36},{5,37},{6,38},{7,39},{8,16},{9,17... | collective-permute-start | bytes 1572872 | tf_op jit(solution)/shard_map/ppermute | solution.py:302
  3.2 3.6 %collective-permute-start.1 = (bf16[16,128,128]{2,1,0:T(8,128)(2,1)}, bf16[16,128,128]{2,1,0:T(8,128)(2,1)S(1)}, u32[]{:S(2)}, u32[]{:S(2)}) collective-permute-start(bf16[16,128,128]{2,1,0:T(8,128)(2,1)} %refs_0_.4), channel_id=1, source_target_pairs={{0,16},{1,17},{2,18},{3,19},{4,68},{5,69},{6,70},{7,71},{8,24},{9,... | collective-permute-start | bytes 1572872 | tf_op jit(solution)/shard_map/ppermute | solution.py:302
  6.8 1.0 collective-permute-start.2
  7.8 1.2 copy-done.3
  9.0 0.7 copy-done.7
  9.8 1.3 norm.2
  11.1 1.0 copy-done.4
  12.7 2.2 %norm.3 = (bf16[128,4096]{1,0:T(8,128)(2,1)}, bf16[32,128,128]{2,1,0:T(8,128)(2,1)S(1)}, f32[128,128]{1,0:T(8,128)}) custom-call(bf16[128,4096]{1,0:T(8,128)(2,1)S(1)} %collective-permute-done.3.x_ref, f32[1,4096]{1,0:T(1,128)S(1)} %bitcast.9), custom_call_target="tpu_custom_call" | custom-call | flops 1100000000 | tf_op jit(solution)/shard_map/norm/pallas_call | solution.py:66
  14.9 4.9 %collective-permute-done.1.refs_2_ = bf16[16,128,128]{2,1,0:T(8,128)(2,1)S(1)} collective-permute-done((bf16[16,128,128]{2,1,0:T(8,128)(2,1)}, bf16[16,128,128]{2,1,0:T(8,128)(2,1)S(1)}, u32[]{:S(2)}, u32[]{:S(2)}) %collective-permute-start.1) | collective-permute-done | bytes 524320 | tf_op jit(solution)/shard_map/ppermute | solution.py:302
  19.8 1.5 joined.1.refs_8_
  21.3 1.6 collective-permute-start.4
  22.9 1.7 collective-permute-start.5
  24.5 0.7 pad_add_fusion.refs_2_.pos_ref
  25.2 14.2 %grads.2 = (bf16[64,128,128]{2,1,0:T(8,128)(2,1)}, bf16[64,128,128]{2,1,0:T(8,128)(2,1)}, bf16[64,128,128]{2,1,0:T(8,128)(2,1)}) custom-call(s32[512]{0:T(512)} %refs_0_.7, s32[512]{0:T(512)} %refs_1_.5, s32[4]{0:T(128)} %pad_add_fusion.refs_2_.pos_ref, bf16[32,128,128]{2,1,0:T(8,128)(2,1)} %copy-done.1, bf16[32,128,128]{2,1,0:T(8,128)(2,1)} %copy-done.2, ...), custom_call_target="tpu_custom_call" | custom-call | flops 2200000000 | tf_op jit(solution)/shard_map/grads/pallas_call | solution.py:126
  39.4 9.5 %collective-permute-done.4.left_ref.refs_0_ = bf16[64,128,128]{2,1,0:T(8,128)(2,1)} collective-permute-done((bf16[64,128,128]{2,1,0:T(8,128)(2,1)}, bf16[64,128,128]{2,1,0:T(8,128)(2,1)}, u32[]{:S(2)}, u32[]{:S(2)}) %collective-permute-start.4) | collective-permute-done | bytes 2097184 | tf_op jit(solution)/shard_map/ppermute | solution.py:302
  49.1 1.3 copy-done.11
  50.4 2.6 %relayed.1 = (bf16[32,128,128]{2,1,0:T(8,128)(2,1)}, bf16[32,128,128]{2,1,0:T(8,128)(2,1)}) custom-call(bf16[64,128,128]{2,1,0:T(8,128)(2,1)} %collective-permute-done.4.left_ref.refs_0_, bf16[64,128,128]{2,1,0:T(8,128)(2,1)} %copy-done.11, bf16[64,128,128]{2,1,0:T(8,128)(2,1)} %get-tuple-element.38.tie_ref.refs_7_), custom_call_target="tpu_custom_call" | custom-call | flops 1100000000 | tf_op jit(solution)/shard_map/relayed/pallas_call | solution.py:277
  53.5 1.6 collective-permute-start.7
  55.1 1.7 collective-permute-start.8
  56.8 8.1 %grads.3 = (bf16[64,128,128]{2,1,0:T(8,128)(2,1)}, bf16[64,128,128]{2,1,0:T(8,128)(2,1)}, bf16[64,128,128]{2,1,0:T(8,128)(2,1)}, bf16[64,128,128]{2,1,0:T(8,128)(2,1)}) custom-call(s32[512]{0:T(512)} %refs_0_.7, s32[512]{0:T(512)} %refs_1_.5, s32[4]{0:T(128)} %pad_add_fusion.refs_2_.pos_ref, ...), custom_call_target="tpu_custom_call", output_to_operand_aliasing={{0}: (7, {}), {1}: (8, {}), {2}: (9, {})} | custom-call | flops 2200000000 | tf_op jit(solution)/shard_map/grads/pallas_call | solution.py:126
  64.9 1.5 collective-permute-start.14
  66.4 4.6 %collective-permute-done.7.refs_0_ = bf16[32,128,128]{2,1,0:T(8,128)(2,1)S(1)} collective-permute-done((bf16[32,128,128]{2,1,0:T(8,128)(2,1)}, bf16[32,128,128]{2,1,0:T(8,128)(2,1)S(1)}, u32[]{:S(2)}, u32[]{:S(2)}) %collective-permute-start.7) | collective-permute-done | bytes 1048608 | tf_op jit(solution)/shard_map/ppermute | solution.py:302
  71.0 3.0 %collective-permute-start.15 = (bf16[64,128,128]{2,1,0:T(8,128)(2,1)}, bf16[64,128,128]{2,1,0:T(8,128)(2,1)}, u32[]{:S(2)}, u32[]{:S(2)}) collective-permute-start(bf16[64,128,128]{2,1,0:T(8,128)(2,1)} %get-tuple-element.52), channel_id=1, source_target_pairs={{0,2},{1,3},{2,0},{3,1},{4,68},{5,69},{6,70},{7,71},{8,10},{9,11},... | collective-permute-start | bytes 6291464 | tf_op jit(solution)/shard_map/ppermute | solution.py:302
  74.1 1.1 collective-permute-start.16
  75.2 1.4 copy-done.12
  77.1 2.4 %collective-permute-done.12.refs_16_ = bf16[32,128,128]{2,1,0:T(8,128)(2,1)S(1)} collective-permute-done((bf16[32,128,128]{2,1,0:T(8,128)(2,1)}, bf16[32,128,128]{2,1,0:T(8,128)(2,1)S(1)}, u32[]{:S(2)}, u32[]{:S(2)}) %collective-permute-start.12) | collective-permute-done | bytes 1048608 | tf_op jit(solution)/shard_map/ppermute | solution.py:403
  79.5 1.5 collective-permute-done.13.refs_17_
  81.0 1.0 copy-done.15
  82.0 32.0 %project.1 = (bf16[128,14336]{1,0:T(8,128)(2,1)}, bf16[128,4096]{1,0:T(8,128)(2,1)}, f32[32,128]{1,0:T(8,128)}) custom-call(s32[512]{0:T(512)} %refs_0_.7, s32[512]{0:T(512)} %refs_1_.5, s32[4]{0:T(128)} %pad_add_fusion.refs_2_.pos_ref, bf16[128,4096]{1,0:T(8,128)(2,1)} %refs_3_.1, bf16[128,4096]{1,0:T(8,128)(2,1)} %copy-done.4, f32[128,128]{1,0:T(8,128)} %copy-done.6, ...), custom_call_target="tpu_custom_call" | custom-call | flops 2200000000 | tf_op jit(solution)/shard_map/project/pallas_call | solution.py:216
  114.3 1.6 collective-permute-done.15.refs_2_
  115.9 5.6 %collective-permute-done.16.refs_3_ = bf16[64,128,128]{2,1,0:T(8,128)(2,1)} collective-permute-done((bf16[64,128,128]{2,1,0:T(8,128)(2,1)}, bf16[64,128,128]{2,1,0:T(8,128)(2,1)}, u32[]{:S(2)}, u32[]{:S(2)}) %collective-permute-start.16) | collective-permute-done | bytes 2097184 | tf_op jit(solution)/shard_map/ppermute | solution.py:302
  121.5 0.7 copy-done.9
  122.2 4.7 %cut_sum.1 = (bf16[17,128,128]{2,1,0:T(8,128)(2,1)S(1)}, bf16[17,128,128]{2,1,0:T(8,128)(2,1)S(1)}, bf16[17,128,128]{2,1,0:T(8,128)(2,1)S(1)}, bf16[17,128,128]{2,1,0:T(8,128)(2,1)S(1)}) custom-call(bf16[64,128,128]{2,1,0:T(8,128)(2,1)S(1)} %copy-done, bf16[64,128,128]{2,1,0:T(8,128)(2,1)} %collective-permute-done.14.refs_1_, ...), custom_call_target="tpu_custom_call" | custom-call | flops 1100000000 | tf_op jit(solution)/shard_map/cut_sum/pallas_call | solution.py:345
  127.4 2.8 %collective-permute-start.19 = (bf16[17,128,128]{2,1,0:T(8,128)(2,1)S(1)}, bf16[17,128,128]{2,1,0:T(8,128)(2,1)S(1)}, u32[]{:S(2)}, u32[]{:S(2)}) collective-permute-start(bf16[17,128,128]{2,1,0:T(8,128)(2,1)S(1)} %get-tuple-element.56), channel_id=1, source_target_pairs={{0,64},{1,65},{2,66},{3,67},{4,20},{5,21},{6,22},{7,23},{8,72},{9,... | collective-permute-start | bytes 1671176 | tf_op jit(solution)/shard_map/ppermute | solution.py:302
  130.1 1.2 collective-permute-start.20
  131.3 6.4 %collective-permute-done.18.refs_1_ = bf16[17,128,128]{2,1,0:T(8,128)(2,1)S(1)} collective-permute-done((bf16[17,128,128]{2,1,0:T(8,128)(2,1)S(1)}, bf16[17,128,128]{2,1,0:T(8,128)(2,1)S(1)}, u32[]{:S(2)}, u32[]{:S(2)}) %collective-permute-start.18) | collective-permute-done | bytes 557088 | tf_op jit(solution)/shard_map/ppermute | solution.py:302
  137.7 6.0 %collective-permute-done.19.refs_2_ = bf16[17,128,128]{2,1,0:T(8,128)(2,1)S(1)} collective-permute-done((bf16[17,128,128]{2,1,0:T(8,128)(2,1)S(1)}, bf16[17,128,128]{2,1,0:T(8,128)(2,1)S(1)}, u32[]{:S(2)}, u32[]{:S(2)}) %collective-permute-start.19) | collective-permute-done | bytes 557088 | tf_op jit(solution)/shard_map/ppermute | solution.py:302
  143.7 0.9 collective-permute-done.20.refs_3_
  144.9 2.7 %collective-permute-start.21 = (bf16[5,128,128]{2,1,0:T(8,128)(2,1)S(1)}, bf16[5,128,128]{2,1,0:T(8,128)(2,1)S(1)}, u32[]{:S(2)}, u32[]{:S(2)}) collective-permute-start(bf16[5,128,128]{2,1,0:T(8,128)(2,1)S(1)} %get-tuple-element.59), channel_id=1, source_target_pairs={{0,8},{1,9},{2,10},{3,11},{4,5},{5,6},{6,7},{7,4},{8,16},{9,17},{1... | collective-permute-start | bytes 491528 | tf_op jit(solution)/shard_map/ppermute | solution.py:302
  147.6 2.1 %collective-permute-start.22 = (bf16[5,128,128]{2,1,0:T(8,128)(2,1)S(1)}, bf16[5,128,128]{2,1,0:T(8,128)(2,1)S(1)}, u32[]{:S(2)}, u32[]{:S(2)}) collective-permute-start(bf16[5,128,128]{2,1,0:T(8,128)(2,1)S(1)} %get-tuple-element.60), channel_id=1, source_target_pairs={{0,16},{1,17},{2,18},{3,19},{4,6},{5,7},{6,4},{7,5},{8,24},{9,25},... | collective-permute-start | bytes 491528 | tf_op jit(solution)/shard_map/ppermute | solution.py:302
  149.7 1.6 collective-permute-start.23
  151.6 3.2 %collective-permute-done.22.refs_2_ = bf16[5,128,128]{2,1,0:T(8,128)(2,1)S(1)} collective-permute-done((bf16[5,128,128]{2,1,0:T(8,128)(2,1)S(1)}, bf16[5,128,128]{2,1,0:T(8,128)(2,1)S(1)}, u32[]{:S(2)}, u32[]{:S(2)}) %collective-permute-start.22) | collective-permute-done | bytes 163872 | tf_op jit(solution)/shard_map/ppermute | solution.py:302
  155.1 1.4 collective-permute-start.24
  156.6 2.7 %collective-permute-start.25 = (bf16[5,128,128]{2,1,0:T(8,128)(2,1)S(1)}, bf16[5,128,128]{2,1,0:T(8,128)(2,1)S(1)}, u32[]{:S(2)}, u32[]{:S(2)}) collective-permute-start(bf16[5,128,128]{2,1,0:T(8,128)(2,1)S(1)} %next_sum.3.refs_0_), channel_id=1, source_target_pairs={{0,2},{1,3},{2,0},{3,1},{4,6},{5,7},{6,4},{7,5},{8,10},{9,11},{10,... | collective-permute-start | bytes 491528 | tf_op jit(solution)/shard_map/ppermute | solution.py:302
  159.8 1.9 %collective-permute-done.24.refs_1_ = bf16[5,128,128]{2,1,0:T(8,128)(2,1)S(1)} collective-permute-done((bf16[5,128,128]{2,1,0:T(8,128)(2,1)S(1)}, bf16[5,128,128]{2,1,0:T(8,128)(2,1)S(1)}, u32[]{:S(2)}, u32[]{:S(2)}) %collective-permute-start.24) | collective-permute-done | bytes 163872 | tf_op jit(solution)/shard_map/ppermute | solution.py:302
  161.7 2.6 %collective-permute-done.25.refs_2_ = bf16[5,128,128]{2,1,0:T(8,128)(2,1)S(1)} collective-permute-done((bf16[5,128,128]{2,1,0:T(8,128)(2,1)S(1)}, bf16[5,128,128]{2,1,0:T(8,128)(2,1)S(1)}, u32[]{:S(2)}, u32[]{:S(2)}) %collective-permute-start.25) | collective-permute-done | bytes 163872 | tf_op jit(solution)/shard_map/ppermute | solution.py:302
  164.6 1.6 place.1
  166.2 1.2 collective-permute-done.27
  (55 shorter events, 5.7 us)
Async XLA Ops:
  0.6 24.6 %collective-permute-start.6 = (bf16[128,14336]{1,0:T(8,128)(2,1)}, bf16[128,14336]{1,0:T(8,128)(2,1)}, u32[]{:S(2)}, u32[]{:S(2)}) collective-permute-start(bf16[128,14336]{1,0:T(8,128)(2,1)} %refs_7_.1), channel_id=1, source_target_pairs={{0,4},{4,0},{1,5},{5,1},{2,6},{6,2},{3,7},{7,3},{8,12},{12,8},{9,1... | collective-permute-start | bytes 11010056 | tf_op jit(solution)/shard_map/ppermute | solution.py:403
  0.7 12.0 %collective-permute-start.3 = (bf16[128,4096]{1,0:T(8,128)(2,1)}, bf16[128,4096]{1,0:T(8,128)(2,1)S(1)}, u32[]{:S(2)}, u32[]{:S(2)}) collective-permute-start(bf16[128,4096]{1,0:T(8,128)(2,1)} %refs_3_.1), channel_id=1, source_target_pairs={{0,4},{4,0},{1,5},{5,1},{2,6},{6,2},{3,7},{7,3},{8,12},{12,8},{9,1... | collective-permute-start | bytes 3145736 | tf_op jit(solution)/shard_map/ppermute | solution.py:403
  1.2 13.7 %collective-permute-start = (bf16[16,128,128]{2,1,0:T(8,128)(2,1)}, bf16[16,128,128]{2,1,0:T(8,128)(2,1)S(1)}, u32[]{:S(2)}, u32[]{:S(2)}) collective-permute-start(bf16[16,128,128]{2,1,0:T(8,128)(2,1)} %refs_0_.4), channel_id=1, source_target_pairs={{0,8},{1,9},{2,10},{3,11},{4,36},{5,37},{6,38},{7,39},{8,16},{9,17... | collective-permute-start | bytes 1572872 | tf_op jit(solution)/shard_map/ppermute | solution.py:302
  3.2 16.6 %collective-permute-start.1 = (bf16[16,128,128]{2,1,0:T(8,128)(2,1)}, bf16[16,128,128]{2,1,0:T(8,128)(2,1)S(1)}, u32[]{:S(2)}, u32[]{:S(2)}) collective-permute-start(bf16[16,128,128]{2,1,0:T(8,128)(2,1)} %refs_0_.4), channel_id=1, source_target_pairs={{0,16},{1,17},{2,18},{3,19},{4,68},{5,69},{6,70},{7,71},{8,24},{9,... | collective-permute-start | bytes 1572872 | tf_op jit(solution)/shard_map/ppermute | solution.py:302
  6.8 13.0 %collective-permute-start.2 = (bf16[16,128,128]{2,1,0:T(8,128)(2,1)}, bf16[16,128,128]{2,1,0:T(8,128)(2,1)S(1)}, u32[]{:S(2)}, u32[]{:S(2)}) collective-permute-start(bf16[16,128,128]{2,1,0:T(8,128)(2,1)} %refs_0_.4), channel_id=1, source_target_pairs={{0,24},{1,25},{2,26},{3,27},{4,100},{5,101},{6,102},{7,103},{8,0},... | collective-permute-start | bytes 1572872 | tf_op jit(solution)/shard_map/ppermute | solution.py:302
  7.8 1.2 copy-start.3
  9.0 0.7 copy-start.7
  9.8 2.9 %copy-start.8 = (f32[4096]{0:T(1024)S(1)}, f32[4096]{0:T(1024)}, u32[]{:S(2)}) copy-start(f32[4096]{0:T(1024)} %param.7) | copy-start | bytes 49156
  11.1 1.0 copy-start.4
  12.0 0.6 copy-start.6
  12.7 8.6 %copy-start.1 = (bf16[32,128,128]{2,1,0:T(8,128)(2,1)}, bf16[32,128,128]{2,1,0:T(8,128)(2,1)S(1)}, u32[]{:S(2)}) copy-start(bf16[32,128,128]{2,1,0:T(8,128)(2,1)S(1)} %get-tuple-element.36.refs_4_.refs_3_) | copy-start | bytes 3145732
  12.7 7.1 %copy-start.5 = (bf16[16,128,128]{2,1,0:T(8,128)(2,1)S(1)}, bf16[16,128,128]{2,1,0:T(8,128)(2,1)}, u32[]{:S(2)}) copy-start(bf16[16,128,128]{2,1,0:T(8,128)(2,1)} %refs_0_.4) | copy-start | bytes 1572868
  14.9 6.4 %copy-start.2 = (bf16[32,128,128]{2,1,0:T(8,128)(2,1)}, bf16[32,128,128]{2,1,0:T(8,128)(2,1)S(1)}, u32[]{:S(2)}) copy-start(bf16[32,128,128]{2,1,0:T(8,128)(2,1)S(1)} %get-tuple-element.37.refs_5_.refs_4_) | copy-start | bytes 3145732
  21.3 27.6 %collective-permute-start.4 = (bf16[64,128,128]{2,1,0:T(8,128)(2,1)}, bf16[64,128,128]{2,1,0:T(8,128)(2,1)}, u32[]{:S(2)}, u32[]{:S(2)}) collective-permute-start(bf16[64,128,128]{2,1,0:T(8,128)(2,1)} %joined.1.refs_8_), channel_id=1, source_target_pairs={{0,32},{1,33},{2,34},{3,35},{4,12},{5,13},{6,14},{7,15},{8,40},{9,... | collective-permute-start | bytes 6291464 | tf_op jit(solution)/shard_map/ppermute | solution.py:302
  22.9 26.2 %collective-permute-start.5 = (bf16[64,128,128]{2,1,0:T(8,128)(2,1)}, bf16[64,128,128]{2,1,0:T(8,128)(2,1)S(1)}, u32[]{:S(2)}, u32[]{:S(2)}) collective-permute-start(bf16[64,128,128]{2,1,0:T(8,128)(2,1)} %joined.1.refs_8_), channel_id=1, source_target_pairs={{0,96},{1,97},{2,98},{3,99},{4,28},{5,29},{6,30},{7,31},{8,104},{9... | collective-permute-start | bytes 6291464 | tf_op jit(solution)/shard_map/ppermute | solution.py:302
  24.5 40.4 %collective-permute-start.9 = (bf16[64,128,128]{2,1,0:T(8,128)(2,1)}, bf16[64,128,128]{2,1,0:T(8,128)(2,1)}, u32[]{:S(2)}, u32[]{:S(2)}) collective-permute-start(bf16[64,128,128]{2,1,0:T(8,128)(2,1)} %joined.1.refs_8_), channel_id=1, source_target_pairs={{0,4},{4,0},{1,5},{5,1},{2,6},{6,2},{3,7},{7,3},{8,12},{12,8},{9,1... | collective-permute-start | bytes 6291464 | tf_op jit(solution)/shard_map/ppermute | solution.py:403
  49.1 1.3 copy-start.11
  53.0 22.2 %collective-permute-start.10 = (bf16[64,128,128]{2,1,0:T(8,128)(2,1)}, bf16[64,128,128]{2,1,0:T(8,128)(2,1)S(1)}, u32[]{:S(2)}, u32[]{:S(2)}) collective-permute-start(bf16[64,128,128]{2,1,0:T(8,128)(2,1)} %get-tuple-element.40.refs_9_), channel_id=1, source_target_pairs={{0,4},{4,0},{1,5},{5,1},{2,6},{6,2},{3,7},{7,3},{8,12},{12,8},{9,1... | collective-permute-start | bytes 6291464 | tf_op jit(solution)/shard_map/ppermute | solution.py:403
  53.0 22.2 %collective-permute-start.11 = (bf16[64,128,128]{2,1,0:T(8,128)(2,1)}, bf16[64,128,128]{2,1,0:T(8,128)(2,1)}, u32[]{:S(2)}, u32[]{:S(2)}) collective-permute-start(bf16[64,128,128]{2,1,0:T(8,128)(2,1)} %get-tuple-element.41.refs_10_), channel_id=1, source_target_pairs={{0,4},{4,0},{1,5},{5,1},{2,6},{6,2},{3,7},{7,3},{8,12},{12,8},{9,1... | collective-permute-start | bytes 6291464 | tf_op jit(solution)/shard_map/ppermute | solution.py:403
  53.5 17.5 %collective-permute-start.7 = (bf16[32,128,128]{2,1,0:T(8,128)(2,1)}, bf16[32,128,128]{2,1,0:T(8,128)(2,1)S(1)}, u32[]{:S(2)}, u32[]{:S(2)}) collective-permute-start(bf16[32,128,128]{2,1,0:T(8,128)(2,1)} %get-tuple-element.39.refs_2_.refs_10_), channel_id=1, source_target_pairs={{0,32},{1,33},{2,34},{3,35},{4,12},{5,13},{6,14},{7,15},{8,40},{9,... | collective-permute-start | bytes 3145736 | tf_op jit(solution)/shard_map/ppermute | solution.py:302
  55.1 18.9 %collective-permute-start.8 = (bf16[32,128,128]{2,1,0:T(8,128)(2,1)}, bf16[32,128,128]{2,1,0:T(8,128)(2,1)}, u32[]{:S(2)}, u32[]{:S(2)}) collective-permute-start(bf16[32,128,128]{2,1,0:T(8,128)(2,1)} %get-tuple-element.42), channel_id=1, source_target_pairs={{0,96},{1,97},{2,98},{3,99},{4,28},{5,29},{6,30},{7,31},{8,104},{9... | collective-permute-start | bytes 3145736 | tf_op jit(solution)/shard_map/ppermute | solution.py:302
  64.9 49.4 %collective-permute-start.14 = (bf16[64,128,128]{2,1,0:T(8,128)(2,1)}, bf16[64,128,128]{2,1,0:T(8,128)(2,1)}, u32[]{:S(2)}, u32[]{:S(2)}) collective-permute-start(bf16[64,128,128]{2,1,0:T(8,128)(2,1)} %get-tuple-element.51), channel_id=1, source_target_pairs={{0,1},{1,2},{2,3},{3,0},{4,36},{5,37},{6,38},{7,39},{8,9},{9,10},{... | collective-permute-start | bytes 6291464 | tf_op jit(solution)/shard_map/ppermute | solution.py:302
  71.0 4.2 %copy-start.13 = (bf16[32,128,128]{2,1,0:T(8,128)(2,1)}, bf16[32,128,128]{2,1,0:T(8,128)(2,1)S(1)}, u32[]{:S(2)}) copy-start(bf16[32,128,128]{2,1,0:T(8,128)(2,1)S(1)} %collective-permute-done.7.refs_0_) | copy-start | bytes 3145732
  71.0 44.9 %collective-permute-start.15 = (bf16[64,128,128]{2,1,0:T(8,128)(2,1)}, bf16[64,128,128]{2,1,0:T(8,128)(2,1)}, u32[]{:S(2)}, u32[]{:S(2)}) collective-permute-start(bf16[64,128,128]{2,1,0:T(8,128)(2,1)} %get-tuple-element.52), channel_id=1, source_target_pairs={{0,2},{1,3},{2,0},{3,1},{4,68},{5,69},{6,70},{7,71},{8,10},{9,11},... | collective-permute-start | bytes 6291464 | tf_op jit(solution)/shard_map/ppermute | solution.py:302
  74.1 47.4 %collective-permute-start.16 = (bf16[64,128,128]{2,1,0:T(8,128)(2,1)}, bf16[64,128,128]{2,1,0:T(8,128)(2,1)}, u32[]{:S(2)}, u32[]{:S(2)}) collective-permute-start(bf16[64,128,128]{2,1,0:T(8,128)(2,1)} %get-tuple-element.45.refs_2_), channel_id=1, source_target_pairs={{0,3},{1,0},{2,1},{3,2},{4,100},{5,101},{6,102},{7,103},{8,11},{9,... | collective-permute-start | bytes 6291464 | tf_op jit(solution)/shard_map/ppermute | solution.py:302
  75.2 1.4 copy-start.12
  76.6 2.9 %collective-permute-start.12 = (bf16[32,128,128]{2,1,0:T(8,128)(2,1)}, bf16[32,128,128]{2,1,0:T(8,128)(2,1)S(1)}, u32[]{:S(2)}, u32[]{:S(2)}) collective-permute-start(bf16[32,128,128]{2,1,0:T(8,128)(2,1)} %get-tuple-element.46.refs_11_), channel_id=1, source_target_pairs={{0,4},{4,0},{1,5},{5,1},{2,6},{6,2},{3,7},{7,3},{8,12},{12,8},{9,1... | collective-permute-start | bytes 3145736 | tf_op jit(solution)/shard_map/ppermute | solution.py:403
  76.6 4.4 %collective-permute-start.13 = (bf16[32,128,128]{2,1,0:T(8,128)(2,1)}, bf16[32,128,128]{2,1,0:T(8,128)(2,1)S(1)}, u32[]{:S(2)}, u32[]{:S(2)}) collective-permute-start(bf16[32,128,128]{2,1,0:T(8,128)(2,1)} %get-tuple-element.47.refs_12_), channel_id=1, source_target_pairs={{0,4},{4,0},{1,5},{5,1},{2,6},{6,2},{3,7},{7,3},{8,12},{12,8},{9,1... | collective-permute-start | bytes 3145736 | tf_op jit(solution)/shard_map/ppermute | solution.py:403
  79.5 2.5 %copy-start.14 = (bf16[32,128,128]{2,1,0:T(8,128)(2,1)}, bf16[32,128,128]{2,1,0:T(8,128)(2,1)S(1)}, u32[]{:S(2)}) copy-start(bf16[32,128,128]{2,1,0:T(8,128)(2,1)S(1)} %collective-permute-done.12.refs_16_) | copy-start | bytes 3145732
  81.0 1.0 copy-start.15
  81.9 39.5 %copy-start = (bf16[64,128,128]{2,1,0:T(8,128)(2,1)S(1)}, bf16[64,128,128]{2,1,0:T(8,128)(2,1)}, u32[]{:S(2)}) copy-start(bf16[64,128,128]{2,1,0:T(8,128)(2,1)} %get-tuple-element.50.refs_0_) | copy-start | bytes 6291460
  113.9 7.6 %collective-permute-start.17 = (f32[32,128]{1,0:T(8,128)}, f32[32,128]{1,0:T(8,128)S(1)}, u32[]{:S(2)}, u32[]{:S(2)}) collective-permute-start(f32[32,128]{1,0:T(8,128)} %get-tuple-element.53.refs_4_), channel_id=1, source_target_pairs={{0,4},{4,0},{1,5},{5,1},{2,6},{6,2},{3,7},{7,3},{8,12},{12,8},{9,1... | collective-permute-start | bytes 49160 | tf_op jit(solution)/shard_map/ppermute | solution.py:403
  121.5 0.7 copy-start.9
  126.9 10.8 %collective-permute-start.18 = (bf16[17,128,128]{2,1,0:T(8,128)(2,1)S(1)}, bf16[17,128,128]{2,1,0:T(8,128)(2,1)S(1)}, u32[]{:S(2)}, u32[]{:S(2)}) collective-permute-start(bf16[17,128,128]{2,1,0:T(8,128)(2,1)S(1)} %get-tuple-element.55), channel_id=1, source_target_pairs={{0,32},{1,33},{2,34},{3,35},{4,12},{5,13},{6,14},{7,15},{8,40},{9,... | collective-permute-start | bytes 1671176 | tf_op jit(solution)/shard_map/ppermute | solution.py:302
  127.4 16.4 %collective-permute-start.19 = (bf16[17,128,128]{2,1,0:T(8,128)(2,1)S(1)}, bf16[17,128,128]{2,1,0:T(8,128)(2,1)S(1)}, u32[]{:S(2)}, u32[]{:S(2)}) collective-permute-start(bf16[17,128,128]{2,1,0:T(8,128)(2,1)S(1)} %get-tuple-element.56), channel_id=1, source_target_pairs={{0,64},{1,65},{2,66},{3,67},{4,20},{5,21},{6,22},{7,23},{8,72},{9,... | collective-permute-start | bytes 1671176 | tf_op jit(solution)/shard_map/ppermute | solution.py:302
  130.1 14.5 %collective-permute-start.20 = (bf16[17,128,128]{2,1,0:T(8,128)(2,1)S(1)}, bf16[17,128,128]{2,1,0:T(8,128)(2,1)S(1)}, u32[]{:S(2)}, u32[]{:S(2)}) collective-permute-start(bf16[17,128,128]{2,1,0:T(8,128)(2,1)S(1)} %get-tuple-element.57), channel_id=1, source_target_pairs={{0,96},{1,97},{2,98},{3,99},{4,28},{5,29},{6,30},{7,31},{8,104},{9... | collective-permute-start | bytes 1671176 | tf_op jit(solution)/shard_map/ppermute | solution.py:302
  144.9 19.7 %copy-start.10 = (s32[4]{0:T(128)S(1)}, s32[4]{0:T(128)}, u32[]{:S(2)}) copy-start(s32[4]{0:T(128)} %pad_add_fusion.refs_2_.pos_ref) | copy-start | bytes 52
  144.9 6.6 %collective-permute-start.21 = (bf16[5,128,128]{2,1,0:T(8,128)(2,1)S(1)}, bf16[5,128,128]{2,1,0:T(8,128)(2,1)S(1)}, u32[]{:S(2)}, u32[]{:S(2)}) collective-permute-start(bf16[5,128,128]{2,1,0:T(8,128)(2,1)S(1)} %get-tuple-element.59), channel_id=1, source_target_pairs={{0,8},{1,9},{2,10},{3,11},{4,5},{5,6},{6,7},{7,4},{8,16},{9,17},{1... | collective-permute-start | bytes 491528 | tf_op jit(solution)/shard_map/ppermute | solution.py:302
  147.6 7.2 %collective-permute-start.22 = (bf16[5,128,128]{2,1,0:T(8,128)(2,1)S(1)}, bf16[5,128,128]{2,1,0:T(8,128)(2,1)S(1)}, u32[]{:S(2)}, u32[]{:S(2)}) collective-permute-start(bf16[5,128,128]{2,1,0:T(8,128)(2,1)S(1)} %get-tuple-element.60), channel_id=1, source_target_pairs={{0,16},{1,17},{2,18},{3,19},{4,6},{5,7},{6,4},{7,5},{8,24},{9,25},... | collective-permute-start | bytes 491528 | tf_op jit(solution)/shard_map/ppermute | solution.py:302
  149.7 5.3 %collective-permute-start.23 = (bf16[5,128,128]{2,1,0:T(8,128)(2,1)S(1)}, bf16[5,128,128]{2,1,0:T(8,128)(2,1)S(1)}, u32[]{:S(2)}, u32[]{:S(2)}) collective-permute-start(bf16[5,128,128]{2,1,0:T(8,128)(2,1)S(1)} %get-tuple-element.61), channel_id=1, source_target_pairs={{0,24},{1,25},{2,26},{3,27},{4,7},{5,4},{6,5},{7,6},{8,0},{9,1},{1... | collective-permute-start | bytes 491528 | tf_op jit(solution)/shard_map/ppermute | solution.py:302
  155.1 6.6 %collective-permute-start.24 = (bf16[5,128,128]{2,1,0:T(8,128)(2,1)S(1)}, bf16[5,128,128]{2,1,0:T(8,128)(2,1)S(1)}, u32[]{:S(2)}, u32[]{:S(2)}) collective-permute-start(bf16[5,128,128]{2,1,0:T(8,128)(2,1)S(1)} %next_sum.3.refs_0_), channel_id=1, source_target_pairs={{0,1},{1,2},{2,3},{3,0},{4,5},{5,6},{6,7},{7,4},{8,9},{9,10},{10,1... | collective-permute-start | bytes 491528 | tf_op jit(solution)/shard_map/ppermute | solution.py:302
  156.6 7.8 %collective-permute-start.25 = (bf16[5,128,128]{2,1,0:T(8,128)(2,1)S(1)}, bf16[5,128,128]{2,1,0:T(8,128)(2,1)S(1)}, u32[]{:S(2)}, u32[]{:S(2)}) collective-permute-start(bf16[5,128,128]{2,1,0:T(8,128)(2,1)S(1)} %next_sum.3.refs_0_), channel_id=1, source_target_pairs={{0,2},{1,3},{2,0},{3,1},{4,6},{5,7},{6,4},{7,5},{8,10},{9,11},{10,... | collective-permute-start | bytes 491528 | tf_op jit(solution)/shard_map/ppermute | solution.py:302
  159.3 5.3 %collective-permute-start.26 = (bf16[5,128,128]{2,1,0:T(8,128)(2,1)S(1)}, bf16[5,128,128]{2,1,0:T(8,128)(2,1)S(1)}, u32[]{:S(2)}, u32[]{:S(2)}) collective-permute-start(bf16[5,128,128]{2,1,0:T(8,128)(2,1)S(1)} %next_sum.3.refs_0_), channel_id=1, source_target_pairs={{0,3},{1,0},{2,1},{3,2},{4,7},{5,4},{6,5},{7,6},{8,11},{9,8},{10,9... | collective-permute-start | bytes 491528 | tf_op jit(solution)/shard_map/ppermute | solution.py:302
  166.2 1.2 collective-permute-start.27

commit v13 on v12

--- a/solution.py
+++ b/solution.py
@@ -303,12 +303,12 @@
 
 
 def exchange(pieces, axis):
-    return [pieces[0]] + [ring(pieces[j], axis, j) for j in (1, 2, 3)]
+    return [pieces[0]] + [ring(pieces[j], axis, j) for j in (2, 1, 3)]
 
 
 def add_four(refs, i):
     a, b, c, d = (r[i].astype(F4) for r in refs)
-    return (a + c) + (b + d)
+    return (a + b) + (c + d)
 
 
 def put_sums(ref, i, value):
@@ -327,7 +327,7 @@
 
 def add_sums(refs, i, rows):
     a, b, c, d = (get_sums(r, i, rows) for r in refs)
-    return (a + c) + (b + d)
+    return (a + b) + (c + d)
 
 
 def cut_sum(pieces, sums):
@@ -377,10 +377,10 @@
 def place(pieces, pos, rows):
     def kernel(pos_ref, *refs):
         out_ref, sums_ref = refs[4:]
-        for back in range(4):
+        for k, back in enumerate((0, 2, 1, 3)):
             source = lax.rem(pos_ref[3] + 4 - back, 4)
             for u in range(4):
-                out_ref[4 * source + u] = refs[back][u].astype(F4)
+                out_ref[4 * source + u] = refs[k][u].astype(F4)
         sums_ref[...] = add_sums(refs[:4], 4, rows)
 
     return pl.pallas_call(
@@ -405,7 +405,8 @@
     tokens_other, g_other = other_core(tokens), other_core(cotangent)
     normed, turned, scale = norm(tokens, gain2)
     _, turned_other, _ = norm(tokens_other, gain2)
-    line = joined(exchange([tiles] * 4, first), turned, turned_other)
+    own, opposite, behind, ahead = exchange([tiles] * 4, first)
+    line = joined([own, behind, opposite, ahead], turned, turned_other)
     left, right = ring(line, second, 1), ring(line, second, 3)
     operands = (rows, cols, pos, turned, turned_other, cotangent, g_other)
     part0, part2, part1 = grads((0, 2, 1), *operands)

time: 170 us -> 182 us (1.071)
  starting transfers between devices: 36.2 us -> 55.8 us
  waiting for transfers between devices: 53.2 us -> 45.8 us
    ppermute x19, starting transfers between devices: 34.2 us -> 53.8 us  [ring(): return lax.ppermute(piece, ALL, pairs)]
    ppermute x19, waiting for transfers between devices: 48.2 us -> 40.8 us  [ring(): return lax.ppermute(piece, ALL, pairs)]
  transfers between devices with their start and end apart: 28 -> 28, of which waited for: 18 -> 15; matrix products, arithmetic and copies ran while one was open for 0% -> 0% of each run, Pallas kernels for 37% -> 34%
where the time goes in v13:
time: 182 us; the launch traced here: 180 us
  Pallas kernels  68.6 us (38%)
  starting transfers between devices  55.8 us (31%)
  waiting for transfers between devices  45.8 us (25%)
  local copies, waits for them, and re-layouts  7.97 us (4%)
    ppermute x19, starting transfers between devices, ring(): return lax.ppermute(piece, ALL, pairs)  53.8 us
    ppermute x19, waiting for transfers between devices, ring(): return lax.ppermute(piece, ALL, pairs)  40.8 us
    pallas_call x1, Pallas kernels, project(): pl.pallas_call(lambda *refs: project_kernel(sources, *refs), out_shape=(j...  32 us
    pallas_call x2, Pallas kernels, grads(): pl.pallas_call(lambda *refs: grad_kernel(aheads, each, *refs), out_shape=...  22.3 us
    unnamed x32, local copies, waits for them, and re-layouts  7.97 us
    ppermute x9, waiting for transfers between devices, other_core(): return lax.ppermute(value, 'c', [(0, 1), (1, 0)])  5.05 us
    pallas_call x1, Pallas kernels, cut_sum(): pl.pallas_call(kernel, out_shape=[jax.ShapeDtypeStruct((each + 1, T, T),...  4.7 us
  transfers between devices with their start and end apart: 28, of which 15 were waited for; matrix products, arithmetic and copies ran while one was open for 0% of the time, Pallas kernels for 34%

profile of v13, /device:TPU:0, one launch (start us, length us, event | category | flops | bytes accessed | tf_op | source)
XLA Modules:
  0.0 180.2 jit_solution(3133089533465415306)
XLA Ops:
  1.2 2.0 %collective-permute-start = (bf16[16,128,128]{2,1,0:T(8,128)(2,1)}, bf16[16,128,128]{2,1,0:T(8,128)(2,1)S(1)}, u32[]{:S(2)}, u32[]{:S(2)}) collective-permute-start(bf16[16,128,128]{2,1,0:T(8,128)(2,1)} %refs_0_.4), channel_id=1, source_target_pairs={{0,8},{1,9},{2,10},{3,11},{4,36},{5,37},{6,38},{7,39},{8,16},{9,17... | collective-permute-start | bytes 1572872 | tf_op jit(solution)/shard_map/ppermute | solution.py:302
  3.2 3.6 %collective-permute-start.1 = (bf16[16,128,128]{2,1,0:T(8,128)(2,1)}, bf16[16,128,128]{2,1,0:T(8,128)(2,1)S(1)}, u32[]{:S(2)}, u32[]{:S(2)}) collective-permute-start(bf16[16,128,128]{2,1,0:T(8,128)(2,1)} %refs_0_.4), channel_id=1, source_target_pairs={{0,16},{1,17},{2,18},{3,19},{4,68},{5,69},{6,70},{7,71},{8,24},{9,... | collective-permute-start | bytes 1572872 | tf_op jit(solution)/shard_map/ppermute | solution.py:302
  6.8 1.0 collective-permute-start.2
  7.8 1.2 copy-done.3
  9.0 0.7 copy-done.7
  9.8 1.3 norm.2
  11.1 1.0 copy-done.4
  12.0 0.6 copy-done.6
  12.7 2.2 %norm.3 = (bf16[128,4096]{1,0:T(8,128)(2,1)}, bf16[32,128,128]{2,1,0:T(8,128)(2,1)S(1)}, f32[128,128]{1,0:T(8,128)}) custom-call(bf16[128,4096]{1,0:T(8,128)(2,1)S(1)} %collective-permute-done.3.x_ref, f32[1,4096]{1,0:T(1,128)S(1)} %bitcast.9), custom_call_target="tpu_custom_call" | custom-call | flops 1100000000 | tf_op jit(solution)/shard_map/norm/pallas_call | solution.py:66
  14.9 4.9 %collective-permute-done.1.refs_2_ = bf16[16,128,128]{2,1,0:T(8,128)(2,1)S(1)} collective-permute-done((bf16[16,128,128]{2,1,0:T(8,128)(2,1)}, bf16[16,128,128]{2,1,0:T(8,128)(2,1)S(1)}, u32[]{:S(2)}, u32[]{:S(2)}) %collective-permute-start.1) | collective-permute-done | bytes 524320 | tf_op jit(solution)/shard_map/ppermute | solution.py:302
  19.8 1.5 joined.1.refs_8_
  21.3 1.6 collective-permute-start.4
  22.9 1.7 collective-permute-start.5
  24.5 0.7 pad_add_fusion.refs_2_.pos_ref
  25.2 14.2 %grads.2 = (bf16[64,128,128]{2,1,0:T(8,128)(2,1)}, bf16[64,128,128]{2,1,0:T(8,128)(2,1)}, bf16[64,128,128]{2,1,0:T(8,128)(2,1)}) custom-call(s32[512]{0:T(512)} %refs_0_.7, s32[512]{0:T(512)} %refs_1_.5, s32[4]{0:T(128)} %pad_add_fusion.refs_2_.pos_ref, bf16[32,128,128]{2,1,0:T(8,128)(2,1)} %copy-done.1, bf16[32,128,128]{2,1,0:T(8,128)(2,1)} %copy-done.2, ...), custom_call_target="tpu_custom_call" | custom-call | flops 2200000000 | tf_op jit(solution)/shard_map/grads/pallas_call | solution.py:126
  39.4 9.4 %collective-permute-done.4.left_ref.refs_0_ = bf16[64,128,128]{2,1,0:T(8,128)(2,1)} collective-permute-done((bf16[64,128,128]{2,1,0:T(8,128)(2,1)}, bf16[64,128,128]{2,1,0:T(8,128)(2,1)}, u32[]{:S(2)}, u32[]{:S(2)}) %collective-permute-start.4) | collective-permute-done | bytes 2097184 | tf_op jit(solution)/shard_map/ppermute | solution.py:302
  49.1 1.3 copy-done.11
  50.4 2.6 %relayed.1 = (bf16[32,128,128]{2,1,0:T(8,128)(2,1)}, bf16[32,128,128]{2,1,0:T(8,128)(2,1)}) custom-call(bf16[64,128,128]{2,1,0:T(8,128)(2,1)} %collective-permute-done.4.left_ref.refs_0_, bf16[64,128,128]{2,1,0:T(8,128)(2,1)} %copy-done.11, bf16[64,128,128]{2,1,0:T(8,128)(2,1)} %get-tuple-element.38.tie_ref.refs_7_), custom_call_target="tpu_custom_call" | custom-call | flops 1100000000 | tf_op jit(solution)/shard_map/relayed/pallas_call | solution.py:277
  53.5 1.6 collective-permute-start.7
  55.1 1.7 collective-permute-start.8
  56.8 8.1 %grads.3 = (bf16[64,128,128]{2,1,0:T(8,128)(2,1)}, bf16[64,128,128]{2,1,0:T(8,128)(2,1)}, bf16[64,128,128]{2,1,0:T(8,128)(2,1)}, bf16[64,128,128]{2,1,0:T(8,128)(2,1)}) custom-call(s32[512]{0:T(512)} %refs_0_.7, s32[512]{0:T(512)} %refs_1_.5, s32[4]{0:T(128)} %pad_add_fusion.refs_2_.pos_ref, ...), custom_call_target="tpu_custom_call", output_to_operand_aliasing={{0}: (7, {}), {1}: (8, {}), {2}: (9, {})} | custom-call | flops 2200000000 | tf_op jit(solution)/shard_map/grads/pallas_call | solution.py:126
  64.9 3.0 %collective-permute-start.14 = (bf16[64,128,128]{2,1,0:T(8,128)(2,1)}, bf16[64,128,128]{2,1,0:T(8,128)(2,1)}, u32[]{:S(2)}, u32[]{:S(2)}) collective-permute-start(bf16[64,128,128]{2,1,0:T(8,128)(2,1)} %get-tuple-element.51), channel_id=1, source_target_pairs={{0,2},{1,3},{2,0},{3,1},{4,68},{5,69},{6,70},{7,71},{8,10},{9,11},... | collective-permute-start | bytes 6291464 | tf_op jit(solution)/shard_map/ppermute | solution.py:302
  67.9 2.8 %collective-permute-done.7.refs_0_ = bf16[32,128,128]{2,1,0:T(8,128)(2,1)S(1)} collective-permute-done((bf16[32,128,128]{2,1,0:T(8,128)(2,1)}, bf16[32,128,128]{2,1,0:T(8,128)(2,1)S(1)}, u32[]{:S(2)}, u32[]{:S(2)}) %collective-permute-start.7) | collective-permute-done | bytes 1048608 | tf_op jit(solution)/shard_map/ppermute | solution.py:302
  70.7 1.5 collective-permute-start.15
  72.2 1.9 %collective-permute-start.16 = (bf16[64,128,128]{2,1,0:T(8,128)(2,1)}, bf16[64,128,128]{2,1,0:T(8,128)(2,1)}, u32[]{:S(2)}, u32[]{:S(2)}) collective-permute-start(bf16[64,128,128]{2,1,0:T(8,128)(2,1)} %get-tuple-element.45.refs_2_), channel_id=1, source_target_pairs={{0,3},{1,0},{2,1},{3,2},{4,100},{5,101},{6,102},{7,103},{8,11},{9,... | collective-permute-start | bytes 6291464 | tf_op jit(solution)/shard_map/ppermute | solution.py:302
  74.2 1.4 copy-done.12
  76.0 2.4 %collective-permute-done.12.refs_16_ = bf16[32,128,128]{2,1,0:T(8,128)(2,1)S(1)} collective-permute-done((bf16[32,128,128]{2,1,0:T(8,128)(2,1)}, bf16[32,128,128]{2,1,0:T(8,128)(2,1)S(1)}, u32[]{:S(2)}, u32[]{:S(2)}) %collective-permute-start.12) | collective-permute-done | bytes 1048608 | tf_op jit(solution)/shard_map/ppermute | solution.py:403
  78.4 1.5 collective-permute-done.13.refs_17_
  79.9 1.0 copy-done.15
  80.9 32.0 %project.1 = (bf16[128,14336]{1,0:T(8,128)(2,1)}, bf16[128,4096]{1,0:T(8,128)(2,1)}, f32[32,128]{1,0:T(8,128)}) custom-call(s32[512]{0:T(512)} %refs_0_.7, s32[512]{0:T(512)} %refs_1_.5, s32[4]{0:T(128)} %pad_add_fusion.refs_2_.pos_ref, bf16[128,4096]{1,0:T(8,128)(2,1)} %refs_3_.1, bf16[128,4096]{1,0:T(8,128)(2,1)} %copy-done.4, f32[128,128]{1,0:T(8,128)} %copy-done.6, ...), custom_call_target="tpu_custom_call" | custom-call | flops 2200000000 | tf_op jit(solution)/shard_map/project/pallas_call | solution.py:216
  113.3 1.9 %collective-permute-done.15.refs_2_ = bf16[64,128,128]{2,1,0:T(8,128)(2,1)} collective-permute-done((bf16[64,128,128]{2,1,0:T(8,128)(2,1)}, bf16[64,128,128]{2,1,0:T(8,128)(2,1)}, u32[]{:S(2)}, u32[]{:S(2)}) %collective-permute-start.15) | collective-permute-done | bytes 2097184 | tf_op jit(solution)/shard_map/ppermute | solution.py:302
  115.4 0.7 copy-done.9
  116.1 4.7 %cut_sum.1 = (bf16[17,128,128]{2,1,0:T(8,128)(2,1)S(1)}, bf16[17,128,128]{2,1,0:T(8,128)(2,1)S(1)}, bf16[17,128,128]{2,1,0:T(8,128)(2,1)S(1)}, bf16[17,128,128]{2,1,0:T(8,128)(2,1)S(1)}) custom-call(bf16[64,128,128]{2,1,0:T(8,128)(2,1)S(1)} %copy-done, bf16[64,128,128]{2,1,0:T(8,128)(2,1)} %collective-permute-done.14.refs_1_, ...), custom_call_target="tpu_custom_call" | custom-call | flops 1100000000 | tf_op jit(solution)/shard_map/cut_sum/pallas_call | solution.py:345
  120.8 2.8 %collective-permute-start.18 = (bf16[17,128,128]{2,1,0:T(8,128)(2,1)S(1)}, bf16[17,128,128]{2,1,0:T(8,128)(2,1)S(1)}, u32[]{:S(2)}, u32[]{:S(2)}) collective-permute-start(bf16[17,128,128]{2,1,0:T(8,128)(2,1)S(1)} %get-tuple-element.55), channel_id=1, source_target_pairs={{0,64},{1,65},{2,66},{3,67},{4,20},{5,21},{6,22},{7,23},{8,72},{9,... | collective-permute-start | bytes 1671176 | tf_op jit(solution)/shard_map/ppermute | solution.py:302
  123.6 21.6 %collective-permute-start.19 = (bf16[17,128,128]{2,1,0:T(8,128)(2,1)S(1)}, bf16[17,128,128]{2,1,0:T(8,128)(2,1)S(1)}, u32[]{:S(2)}, u32[]{:S(2)}) collective-permute-start(bf16[17,128,128]{2,1,0:T(8,128)(2,1)S(1)} %get-tuple-element.56), channel_id=1, source_target_pairs={{0,32},{1,33},{2,34},{3,35},{4,12},{5,13},{6,14},{7,15},{8,40},{9,... | collective-permute-start | bytes 1671176 | tf_op jit(solution)/shard_map/ppermute | solution.py:302
  145.2 7.0 %collective-permute-done.19.refs_2_ = bf16[17,128,128]{2,1,0:T(8,128)(2,1)S(1)} collective-permute-done((bf16[17,128,128]{2,1,0:T(8,128)(2,1)S(1)}, bf16[17,128,128]{2,1,0:T(8,128)(2,1)S(1)}, u32[]{:S(2)}, u32[]{:S(2)}) %collective-permute-start.19) | collective-permute-done | bytes 557088 | tf_op jit(solution)/shard_map/ppermute | solution.py:302
  152.2 6.5 %collective-permute-done.20.refs_3_ = bf16[17,128,128]{2,1,0:T(8,128)(2,1)S(1)} collective-permute-done((bf16[17,128,128]{2,1,0:T(8,128)(2,1)S(1)}, bf16[17,128,128]{2,1,0:T(8,128)(2,1)S(1)}, u32[]{:S(2)}, u32[]{:S(2)}) %collective-permute-start.20) | collective-permute-done | bytes 557088 | tf_op jit(solution)/shard_map/ppermute | solution.py:302
  159.0 2.6 %collective-permute-start.21 = (bf16[5,128,128]{2,1,0:T(8,128)(2,1)S(1)}, bf16[5,128,128]{2,1,0:T(8,128)(2,1)S(1)}, u32[]{:S(2)}, u32[]{:S(2)}) collective-permute-start(bf16[5,128,128]{2,1,0:T(8,128)(2,1)S(1)} %get-tuple-element.59), channel_id=1, source_target_pairs={{0,16},{1,17},{2,18},{3,19},{4,6},{5,7},{6,4},{7,5},{8,24},{9,25},... | collective-permute-start | bytes 491528 | tf_op jit(solution)/shard_map/ppermute | solution.py:302
  162.0 2.8 %collective-permute-start.23 = (bf16[5,128,128]{2,1,0:T(8,128)(2,1)S(1)}, bf16[5,128,128]{2,1,0:T(8,128)(2,1)S(1)}, u32[]{:S(2)}, u32[]{:S(2)}) collective-permute-start(bf16[5,128,128]{2,1,0:T(8,128)(2,1)S(1)} %get-tuple-element.61), channel_id=1, source_target_pairs={{0,24},{1,25},{2,26},{3,27},{4,7},{5,4},{6,5},{7,6},{8,0},{9,1},{1... | collective-permute-start | bytes 491528 | tf_op jit(solution)/shard_map/ppermute | solution.py:302
  164.8 1.1 collective-permute-done.21.refs_1_
  165.9 2.2 %collective-permute-done.22.refs_2_ = bf16[5,128,128]{2,1,0:T(8,128)(2,1)S(1)} collective-permute-done((bf16[5,128,128]{2,1,0:T(8,128)(2,1)S(1)}, bf16[5,128,128]{2,1,0:T(8,128)(2,1)S(1)}, u32[]{:S(2)}, u32[]{:S(2)}) %collective-permute-start.22) | collective-permute-done | bytes 163872 | tf_op jit(solution)/shard_map/ppermute | solution.py:302
  168.2 0.9 collective-permute-start.24
  169.1 0.9 collective-permute-start.25
  170.0 2.3 %collective-permute-start.26 = (bf16[5,128,128]{2,1,0:T(8,128)(2,1)S(1)}, bf16[5,128,128]{2,1,0:T(8,128)(2,1)S(1)}, u32[]{:S(2)}, u32[]{:S(2)}) collective-permute-start(bf16[5,128,128]{2,1,0:T(8,128)(2,1)S(1)} %next_sum.3.refs_0_), channel_id=1, source_target_pairs={{0,3},{1,0},{2,1},{3,2},{4,7},{5,4},{6,5},{7,6},{8,11},{9,8},{10,9... | collective-permute-start | bytes 491528 | tf_op jit(solution)/shard_map/ppermute | solution.py:302
  172.3 2.9 %collective-permute-done.24.refs_1_ = bf16[5,128,128]{2,1,0:T(8,128)(2,1)S(1)} collective-permute-done((bf16[5,128,128]{2,1,0:T(8,128)(2,1)S(1)}, bf16[5,128,128]{2,1,0:T(8,128)(2,1)S(1)}, u32[]{:S(2)}, u32[]{:S(2)}) %collective-permute-start.24) | collective-permute-done | bytes 163872 | tf_op jit(solution)/shard_map/ppermute | solution.py:302
  175.2 1.7 collective-permute-done.25.refs_2_
  176.9 1.6 place.1
  178.4 1.2 collective-permute-done.27
  (55 shorter events, 3.9 us)
Async XLA Ops:
  0.6 24.6 %collective-permute-start.6 = (bf16[128,14336]{1,0:T(8,128)(2,1)}, bf16[128,14336]{1,0:T(8,128)(2,1)}, u32[]{:S(2)}, u32[]{:S(2)}) collective-permute-start(bf16[128,14336]{1,0:T(8,128)(2,1)} %refs_7_.1), channel_id=1, source_target_pairs={{0,4},{4,0},{1,5},{5,1},{2,6},{6,2},{3,7},{7,3},{8,12},{12,8},{9,1... | collective-permute-start | bytes 11010056 | tf_op jit(solution)/shard_map/ppermute | solution.py:403
  0.7 12.0 %collective-permute-start.3 = (bf16[128,4096]{1,0:T(8,128)(2,1)}, bf16[128,4096]{1,0:T(8,128)(2,1)S(1)}, u32[]{:S(2)}, u32[]{:S(2)}) collective-permute-start(bf16[128,4096]{1,0:T(8,128)(2,1)} %refs_3_.1), channel_id=1, source_target_pairs={{0,4},{4,0},{1,5},{5,1},{2,6},{6,2},{3,7},{7,3},{8,12},{12,8},{9,1... | collective-permute-start | bytes 3145736 | tf_op jit(solution)/shard_map/ppermute | solution.py:403
  1.2 13.7 %collective-permute-start = (bf16[16,128,128]{2,1,0:T(8,128)(2,1)}, bf16[16,128,128]{2,1,0:T(8,128)(2,1)S(1)}, u32[]{:S(2)}, u32[]{:S(2)}) collective-permute-start(bf16[16,128,128]{2,1,0:T(8,128)(2,1)} %refs_0_.4), channel_id=1, source_target_pairs={{0,8},{1,9},{2,10},{3,11},{4,36},{5,37},{6,38},{7,39},{8,16},{9,17... | collective-permute-start | bytes 1572872 | tf_op jit(solution)/shard_map/ppermute | solution.py:302
  3.2 16.6 %collective-permute-start.1 = (bf16[16,128,128]{2,1,0:T(8,128)(2,1)}, bf16[16,128,128]{2,1,0:T(8,128)(2,1)S(1)}, u32[]{:S(2)}, u32[]{:S(2)}) collective-permute-start(bf16[16,128,128]{2,1,0:T(8,128)(2,1)} %refs_0_.4), channel_id=1, source_target_pairs={{0,16},{1,17},{2,18},{3,19},{4,68},{5,69},{6,70},{7,71},{8,24},{9,... | collective-permute-start | bytes 1572872 | tf_op jit(solution)/shard_map/ppermute | solution.py:302
  6.8 13.0 %collective-permute-start.2 = (bf16[16,128,128]{2,1,0:T(8,128)(2,1)}, bf16[16,128,128]{2,1,0:T(8,128)(2,1)S(1)}, u32[]{:S(2)}, u32[]{:S(2)}) collective-permute-start(bf16[16,128,128]{2,1,0:T(8,128)(2,1)} %refs_0_.4), channel_id=1, source_target_pairs={{0,24},{1,25},{2,26},{3,27},{4,100},{5,101},{6,102},{7,103},{8,0},... | collective-permute-start | bytes 1572872 | tf_op jit(solution)/shard_map/ppermute | solution.py:302
  7.8 1.2 copy-start.3
  9.0 0.7 copy-start.7
  9.8 2.9 %copy-start.8 = (f32[4096]{0:T(1024)S(1)}, f32[4096]{0:T(1024)}, u32[]{:S(2)}) copy-start(f32[4096]{0:T(1024)} %param.7) | copy-start | bytes 49156
  11.1 1.0 copy-start.4
  12.0 0.6 copy-start.6
  12.7 8.6 %copy-start.1 = (bf16[32,128,128]{2,1,0:T(8,128)(2,1)}, bf16[32,128,128]{2,1,0:T(8,128)(2,1)S(1)}, u32[]{:S(2)}) copy-start(bf16[32,128,128]{2,1,0:T(8,128)(2,1)S(1)} %get-tuple-element.36.refs_4_.refs_3_) | copy-start | bytes 3145732
  12.7 7.1 %copy-start.5 = (bf16[16,128,128]{2,1,0:T(8,128)(2,1)S(1)}, bf16[16,128,128]{2,1,0:T(8,128)(2,1)}, u32[]{:S(2)}) copy-start(bf16[16,128,128]{2,1,0:T(8,128)(2,1)} %refs_0_.4) | copy-start | bytes 1572868
  14.9 6.4 %copy-start.2 = (bf16[32,128,128]{2,1,0:T(8,128)(2,1)}, bf16[32,128,128]{2,1,0:T(8,128)(2,1)S(1)}, u32[]{:S(2)}) copy-start(bf16[32,128,128]{2,1,0:T(8,128)(2,1)S(1)} %get-tuple-element.37.refs_5_.refs_4_) | copy-start | bytes 3145732
  21.3 27.6 %collective-permute-start.4 = (bf16[64,128,128]{2,1,0:T(8,128)(2,1)}, bf16[64,128,128]{2,1,0:T(8,128)(2,1)}, u32[]{:S(2)}, u32[]{:S(2)}) collective-permute-start(bf16[64,128,128]{2,1,0:T(8,128)(2,1)} %joined.1.refs_8_), channel_id=1, source_target_pairs={{0,32},{1,33},{2,34},{3,35},{4,12},{5,13},{6,14},{7,15},{8,40},{9,... | collective-permute-start | bytes 6291464 | tf_op jit(solution)/shard_map/ppermute | solution.py:302
  22.9 26.2 %collective-permute-start.5 = (bf16[64,128,128]{2,1,0:T(8,128)(2,1)}, bf16[64,128,128]{2,1,0:T(8,128)(2,1)S(1)}, u32[]{:S(2)}, u32[]{:S(2)}) collective-permute-start(bf16[64,128,128]{2,1,0:T(8,128)(2,1)} %joined.1.refs_8_), channel_id=1, source_target_pairs={{0,96},{1,97},{2,98},{3,99},{4,28},{5,29},{6,30},{7,31},{8,104},{9... | collective-permute-start | bytes 6291464 | tf_op jit(solution)/shard_map/ppermute | solution.py:302
  24.5 40.4 %collective-permute-start.9 = (bf16[64,128,128]{2,1,0:T(8,128)(2,1)}, bf16[64,128,128]{2,1,0:T(8,128)(2,1)}, u32[]{:S(2)}, u32[]{:S(2)}) collective-permute-start(bf16[64,128,128]{2,1,0:T(8,128)(2,1)} %joined.1.refs_8_), channel_id=1, source_target_pairs={{0,4},{4,0},{1,5},{5,1},{2,6},{6,2},{3,7},{7,3},{8,12},{12,8},{9,1... | collective-permute-start | bytes 6291464 | tf_op jit(solution)/shard_map/ppermute | solution.py:403
  49.1 1.3 copy-start.11
  53.0 21.1 %collective-permute-start.10 = (bf16[64,128,128]{2,1,0:T(8,128)(2,1)}, bf16[64,128,128]{2,1,0:T(8,128)(2,1)S(1)}, u32[]{:S(2)}, u32[]{:S(2)}) collective-permute-start(bf16[64,128,128]{2,1,0:T(8,128)(2,1)} %get-tuple-element.40.refs_9_), channel_id=1, source_target_pairs={{0,4},{4,0},{1,5},{5,1},{2,6},{6,2},{3,7},{7,3},{8,12},{12,8},{9,1... | collective-permute-start | bytes 6291464 | tf_op jit(solution)/shard_map/ppermute | solution.py:403
  53.0 21.1 %collective-permute-start.11 = (bf16[64,128,128]{2,1,0:T(8,128)(2,1)}, bf16[64,128,128]{2,1,0:T(8,128)(2,1)}, u32[]{:S(2)}, u32[]{:S(2)}) collective-permute-start(bf16[64,128,128]{2,1,0:T(8,128)(2,1)} %get-tuple-element.41.refs_10_), channel_id=1, source_target_pairs={{0,4},{4,0},{1,5},{5,1},{2,6},{6,2},{3,7},{7,3},{8,12},{12,8},{9,1... | collective-permute-start | bytes 6291464 | tf_op jit(solution)/shard_map/ppermute | solution.py:403
  53.5 17.2 %collective-permute-start.7 = (bf16[32,128,128]{2,1,0:T(8,128)(2,1)}, bf16[32,128,128]{2,1,0:T(8,128)(2,1)S(1)}, u32[]{:S(2)}, u32[]{:S(2)}) collective-permute-start(bf16[32,128,128]{2,1,0:T(8,128)(2,1)} %get-tuple-element.39.refs_2_.refs_10_), channel_id=1, source_target_pairs={{0,32},{1,33},{2,34},{3,35},{4,12},{5,13},{6,14},{7,15},{8,40},{9,... | collective-permute-start | bytes 3145736 | tf_op jit(solution)/shard_map/ppermute | solution.py:302
  55.1 17.1 %collective-permute-start.8 = (bf16[32,128,128]{2,1,0:T(8,128)(2,1)}, bf16[32,128,128]{2,1,0:T(8,128)(2,1)}, u32[]{:S(2)}, u32[]{:S(2)}) collective-permute-start(bf16[32,128,128]{2,1,0:T(8,128)(2,1)} %get-tuple-element.42), channel_id=1, source_target_pairs={{0,96},{1,97},{2,98},{3,99},{4,28},{5,29},{6,30},{7,31},{8,104},{9... | collective-permute-start | bytes 3145736 | tf_op jit(solution)/shard_map/ppermute | solution.py:302
  64.9 48.4 %collective-permute-start.14 = (bf16[64,128,128]{2,1,0:T(8,128)(2,1)}, bf16[64,128,128]{2,1,0:T(8,128)(2,1)}, u32[]{:S(2)}, u32[]{:S(2)}) collective-permute-start(bf16[64,128,128]{2,1,0:T(8,128)(2,1)} %get-tuple-element.51), channel_id=1, source_target_pairs={{0,2},{1,3},{2,0},{3,1},{4,68},{5,69},{6,70},{7,71},{8,10},{9,11},... | collective-permute-start | bytes 6291464 | tf_op jit(solution)/shard_map/ppermute | solution.py:302
  70.7 3.4 %copy-start.13 = (bf16[32,128,128]{2,1,0:T(8,128)(2,1)}, bf16[32,128,128]{2,1,0:T(8,128)(2,1)S(1)}, u32[]{:S(2)}) copy-start(bf16[32,128,128]{2,1,0:T(8,128)(2,1)S(1)} %collective-permute-done.7.refs_0_) | copy-start | bytes 3145732
  70.7 44.5 %collective-permute-start.15 = (bf16[64,128,128]{2,1,0:T(8,128)(2,1)}, bf16[64,128,128]{2,1,0:T(8,128)(2,1)}, u32[]{:S(2)}, u32[]{:S(2)}) collective-permute-start(bf16[64,128,128]{2,1,0:T(8,128)(2,1)} %get-tuple-element.52), channel_id=1, source_target_pairs={{0,1},{1,2},{2,3},{3,0},{4,36},{5,37},{6,38},{7,39},{8,9},{9,10},{... | collective-permute-start | bytes 6291464 | tf_op jit(solution)/shard_map/ppermute | solution.py:302
  72.2 43.1 %collective-permute-start.16 = (bf16[64,128,128]{2,1,0:T(8,128)(2,1)}, bf16[64,128,128]{2,1,0:T(8,128)(2,1)}, u32[]{:S(2)}, u32[]{:S(2)}) collective-permute-start(bf16[64,128,128]{2,1,0:T(8,128)(2,1)} %get-tuple-element.45.refs_2_), channel_id=1, source_target_pairs={{0,3},{1,0},{2,1},{3,2},{4,100},{5,101},{6,102},{7,103},{8,11},{9,... | collective-permute-start | bytes 6291464 | tf_op jit(solution)/shard_map/ppermute | solution.py:302
  74.1 1.4 copy-start.12
  75.5 2.9 %collective-permute-start.12 = (bf16[32,128,128]{2,1,0:T(8,128)(2,1)}, bf16[32,128,128]{2,1,0:T(8,128)(2,1)S(1)}, u32[]{:S(2)}, u32[]{:S(2)}) collective-permute-start(bf16[32,128,128]{2,1,0:T(8,128)(2,1)} %get-tuple-element.46.refs_11_), channel_id=1, source_target_pairs={{0,4},{4,0},{1,5},{5,1},{2,6},{6,2},{3,7},{7,3},{8,12},{12,8},{9,1... | collective-permute-start | bytes 3145736 | tf_op jit(solution)/shard_map/ppermute | solution.py:403
  75.5 4.4 %collective-permute-start.13 = (bf16[32,128,128]{2,1,0:T(8,128)(2,1)}, bf16[32,128,128]{2,1,0:T(8,128)(2,1)S(1)}, u32[]{:S(2)}, u32[]{:S(2)}) collective-permute-start(bf16[32,128,128]{2,1,0:T(8,128)(2,1)} %get-tuple-element.47.refs_12_), channel_id=1, source_target_pairs={{0,4},{4,0},{1,5},{5,1},{2,6},{6,2},{3,7},{7,3},{8,12},{12,8},{9,1... | collective-permute-start | bytes 3145736 | tf_op jit(solution)/shard_map/ppermute | solution.py:403
  78.4 2.5 %copy-start.14 = (bf16[32,128,128]{2,1,0:T(8,128)(2,1)}, bf16[32,128,128]{2,1,0:T(8,128)(2,1)S(1)}, u32[]{:S(2)}) copy-start(bf16[32,128,128]{2,1,0:T(8,128)(2,1)S(1)} %collective-permute-done.12.refs_16_) | copy-start | bytes 3145732
  79.9 1.0 copy-start.15
  80.9 34.5 %copy-start = (bf16[64,128,128]{2,1,0:T(8,128)(2,1)S(1)}, bf16[64,128,128]{2,1,0:T(8,128)(2,1)}, u32[]{:S(2)}) copy-start(bf16[64,128,128]{2,1,0:T(8,128)(2,1)} %get-tuple-element.50.refs_0_) | copy-start | bytes 6291460
  112.9 2.5 %collective-permute-start.17 = (f32[32,128]{1,0:T(8,128)}, f32[32,128]{1,0:T(8,128)S(1)}, u32[]{:S(2)}, u32[]{:S(2)}) collective-permute-start(f32[32,128]{1,0:T(8,128)} %get-tuple-element.53.refs_4_), channel_id=1, source_target_pairs={{0,4},{4,0},{1,5},{5,1},{2,6},{6,2},{3,7},{7,3},{8,12},{12,8},{9,1... | collective-permute-start | bytes 49160 | tf_op jit(solution)/shard_map/ppermute | solution.py:403
  115.4 0.7 copy-start.9
  120.8 24.4 %collective-permute-start.18 = (bf16[17,128,128]{2,1,0:T(8,128)(2,1)S(1)}, bf16[17,128,128]{2,1,0:T(8,128)(2,1)S(1)}, u32[]{:S(2)}, u32[]{:S(2)}) collective-permute-start(bf16[17,128,128]{2,1,0:T(8,128)(2,1)S(1)} %get-tuple-element.55), channel_id=1, source_target_pairs={{0,64},{1,65},{2,66},{3,67},{4,20},{5,21},{6,22},{7,23},{8,72},{9,... | collective-permute-start | bytes 1671176 | tf_op jit(solution)/shard_map/ppermute | solution.py:302
  123.6 28.6 %collective-permute-start.19 = (bf16[17,128,128]{2,1,0:T(8,128)(2,1)S(1)}, bf16[17,128,128]{2,1,0:T(8,128)(2,1)S(1)}, u32[]{:S(2)}, u32[]{:S(2)}) collective-permute-start(bf16[17,128,128]{2,1,0:T(8,128)(2,1)S(1)} %get-tuple-element.56), channel_id=1, source_target_pairs={{0,32},{1,33},{2,34},{3,35},{4,12},{5,13},{6,14},{7,15},{8,40},{9,... | collective-permute-start | bytes 1671176 | tf_op jit(solution)/shard_map/ppermute | solution.py:302
  145.2 13.5 %collective-permute-start.20 = (bf16[17,128,128]{2,1,0:T(8,128)(2,1)S(1)}, bf16[17,128,128]{2,1,0:T(8,128)(2,1)S(1)}, u32[]{:S(2)}, u32[]{:S(2)}) collective-permute-start(bf16[17,128,128]{2,1,0:T(8,128)(2,1)S(1)} %get-tuple-element.57), channel_id=1, source_target_pairs={{0,96},{1,97},{2,98},{3,99},{4,28},{5,29},{6,30},{7,31},{8,104},{9... | collective-permute-start | bytes 1671176 | tf_op jit(solution)/shard_map/ppermute | solution.py:302
  159.0 17.9 %copy-start.10 = (s32[4]{0:T(128)S(1)}, s32[4]{0:T(128)}, u32[]{:S(2)}) copy-start(s32[4]{0:T(128)} %pad_add_fusion.refs_2_.pos_ref) | copy-start | bytes 52
  159.0 6.9 %collective-permute-start.21 = (bf16[5,128,128]{2,1,0:T(8,128)(2,1)S(1)}, bf16[5,128,128]{2,1,0:T(8,128)(2,1)S(1)}, u32[]{:S(2)}, u32[]{:S(2)}) collective-permute-start(bf16[5,128,128]{2,1,0:T(8,128)(2,1)S(1)} %get-tuple-element.59), channel_id=1, source_target_pairs={{0,16},{1,17},{2,18},{3,19},{4,6},{5,7},{6,4},{7,5},{8,24},{9,25},... | collective-permute-start | bytes 491528 | tf_op jit(solution)/shard_map/ppermute | solution.py:302
  161.6 6.5 %collective-permute-start.22 = (bf16[5,128,128]{2,1,0:T(8,128)(2,1)S(1)}, bf16[5,128,128]{2,1,0:T(8,128)(2,1)S(1)}, u32[]{:S(2)}, u32[]{:S(2)}) collective-permute-start(bf16[5,128,128]{2,1,0:T(8,128)(2,1)S(1)} %get-tuple-element.60), channel_id=1, source_target_pairs={{0,8},{1,9},{2,10},{3,11},{4,5},{5,6},{6,7},{7,4},{8,16},{9,17},{1... | collective-permute-start | bytes 491528 | tf_op jit(solution)/shard_map/ppermute | solution.py:302
  162.0 6.1 %collective-permute-start.23 = (bf16[5,128,128]{2,1,0:T(8,128)(2,1)S(1)}, bf16[5,128,128]{2,1,0:T(8,128)(2,1)S(1)}, u32[]{:S(2)}, u32[]{:S(2)}) collective-permute-start(bf16[5,128,128]{2,1,0:T(8,128)(2,1)S(1)} %get-tuple-element.61), channel_id=1, source_target_pairs={{0,24},{1,25},{2,26},{3,27},{4,7},{5,4},{6,5},{7,6},{8,0},{9,1},{1... | collective-permute-start | bytes 491528 | tf_op jit(solution)/shard_map/ppermute | solution.py:302
  168.2 7.0 %collective-permute-start.24 = (bf16[5,128,128]{2,1,0:T(8,128)(2,1)S(1)}, bf16[5,128,128]{2,1,0:T(8,128)(2,1)S(1)}, u32[]{:S(2)}, u32[]{:S(2)}) collective-permute-start(bf16[5,128,128]{2,1,0:T(8,128)(2,1)S(1)} %next_sum.3.refs_0_), channel_id=1, source_target_pairs={{0,2},{1,3},{2,0},{3,1},{4,6},{5,7},{6,4},{7,5},{8,10},{9,11},{10,... | collective-permute-start | bytes 491528 | tf_op jit(solution)/shard_map/ppermute | solution.py:302
  169.1 7.8 %collective-permute-start.25 = (bf16[5,128,128]{2,1,0:T(8,128)(2,1)S(1)}, bf16[5,128,128]{2,1,0:T(8,128)(2,1)S(1)}, u32[]{:S(2)}, u32[]{:S(2)}) collective-permute-start(bf16[5,128,128]{2,1,0:T(8,128)(2,1)S(1)} %next_sum.3.refs_0_), channel_id=1, source_target_pairs={{0,1},{1,2},{2,3},{3,0},{4,5},{5,6},{6,7},{7,4},{8,9},{9,10},{10,1... | collective-permute-start | bytes 491528 | tf_op jit(solution)/shard_map/ppermute | solution.py:302
  170.0 6.9 %collective-permute-start.26 = (bf16[5,128,128]{2,1,0:T(8,128)(2,1)S(1)}, bf16[5,128,128]{2,1,0:T(8,128)(2,1)S(1)}, u32[]{:S(2)}, u32[]{:S(2)}) collective-permute-start(bf16[5,128,128]{2,1,0:T(8,128)(2,1)S(1)} %next_sum.3.refs_0_), channel_id=1, source_target_pairs={{0,3},{1,0},{2,1},{3,2},{4,7},{5,4},{6,5},{7,6},{8,11},{9,8},{10,9... | collective-permute-start | bytes 491528 | tf_op jit(solution)/shard_map/ppermute | solution.py:302
  178.4 1.2 collective-permute-start.27

commit v14 on v8

--- a/solution.py
+++ b/solution.py
@@ -112,7 +112,7 @@
                 out_ref[t] = dot(left, right).astype(BF)
                 return carry
 
-            lax.fori_loop(0, STEP, one, 0, unroll=8)
+            lax.fori_loop(0, STEP, one, 0, unroll=16)
 
 
 def grads(aheads, rows, cols, pos, turned, turned_other, own, other, carried=(), ties=()):
@@ -177,7 +177,7 @@
         back_acc[:, r] += dot_t(g_ref[:, q], weight)
         return carry
 
-    lax.fori_loop(0, 32, one, 0, unroll=8)
+    lax.fori_loop(0, 32, one, 0, unroll=32)
 
     @pl.when(s == pl.num_programs(0) - 1)
     def _():

time: 170 us -> 170 us (level)
  waiting for transfers between devices: 44.6 us -> 53 us
  Pallas kernels: 79.6 us -> 71.5 us
    ppermute x19, waiting for transfers between devices: 38.9 us -> 47.3 us  [ring(): return lax.ppermute(piece, ALL, pairs)]
    pallas_call x1, Pallas kernels: 37.5 us -> 32 us  [project(): pl.pallas_call(lambda *refs: project_kernel(sources, *refs), out_shape=(j...]
    pallas_call x2, Pallas kernels: 24.9 us -> 22.4 us  [grads(): pl.pallas_call(lambda *refs: grad_kernel(aheads, each, *refs), out_shape=...]
  transfers between devices with their start and end apart: 28 -> 28, of which waited for: 17 -> 18; matrix products, arithmetic and copies ran while one was open for 0% -> 0% of each run, Pallas kernels for 43% -> 38%
where the time goes in v14:
time: 170 us; the launch traced here: 169 us
  Pallas kernels  71.5 us (42%)
  waiting for transfers between devices  53 us (31%)
  starting transfers between devices  36.4 us (21%)
  local copies, waits for them, and re-layouts  5.73 us (3%)
    ppermute x19, waiting for transfers between devices, ring(): return lax.ppermute(piece, ALL, pairs)  47.3 us
    ppermute x19, starting transfers between devices, ring(): return lax.ppermute(piece, ALL, pairs)  34.3 us
    pallas_call x1, Pallas kernels, project(): pl.pallas_call(lambda *refs: project_kernel(sources, *refs), out_shape=(j...  32 us
    pallas_call x2, Pallas kernels, grads(): pl.pallas_call(lambda *refs: grad_kernel(aheads, each, *refs), out_shape=...  22.4 us
    pallas_call x2, Pallas kernels, norm(): pl.pallas_call(norm_kernel, out_shape=(jax.ShapeDtypeStruct((count, width...  7.57 us
    unnamed x24, local copies, waits for them, and re-layouts  5.73 us
    ppermute x9, waiting for transfers between devices, other_core(): return lax.ppermute(value, 'c', [(0, 1), (1, 0)])  5.7 us
    pallas_call x1, Pallas kernels, cut_sum(): pl.pallas_call(kernel, out_shape=[jax.ShapeDtypeStruct((each + 1, T, T),...  4.7 us
  transfers between devices with their start and end apart: 28, of which 18 were waited for; matrix products, arithmetic and copies ran while one was open for 0% of the time, Pallas kernels for 38%

profile of v14, /device:TPU:0, one launch (start us, length us, event | category | flops | bytes accessed | tf_op | source)
XLA Modules:
  0.0 168.6 jit_solution(295769084519996832)
XLA Ops:
  1.2 2.0 %collective-permute-start = (bf16[16,128,128]{2,1,0:T(8,128)(2,1)}, bf16[16,128,128]{2,1,0:T(8,128)(2,1)S(1)}, u32[]{:S(2)}, u32[]{:S(2)}) collective-permute-start(bf16[16,128,128]{2,1,0:T(8,128)(2,1)} %refs_0_.4), channel_id=1, source_target_pairs={{0,8},{1,9},{2,10},{3,11},{4,36},{5,37},{6,38},{7,39},{8,16},{9,17... | collective-permute-start | bytes 1572872 | tf_op jit(solution)/shard_map/ppermute | solution.py:304
  3.2 3.6 %collective-permute-start.1 = (bf16[16,128,128]{2,1,0:T(8,128)(2,1)}, bf16[16,128,128]{2,1,0:T(8,128)(2,1)S(1)}, u32[]{:S(2)}, u32[]{:S(2)}) collective-permute-start(bf16[16,128,128]{2,1,0:T(8,128)(2,1)} %refs_0_.4), channel_id=1, source_target_pairs={{0,16},{1,17},{2,18},{3,19},{4,68},{5,69},{6,70},{7,71},{8,24},{9,... | collective-permute-start | bytes 1572872 | tf_op jit(solution)/shard_map/ppermute | solution.py:304
  6.8 1.0 collective-permute-start.2
  7.8 0.7 collective-permute-done.3.x_ref
  8.5 1.0 copy-done.11
  9.4 3.8 %norm.3 = (bf16[128,4096]{1,0:T(8,128)(2,1)}, bf16[32,128,128]{2,1,0:T(8,128)(2,1)}, f32[128,128]{1,0:T(8,128)}) custom-call(bf16[128,4096]{1,0:T(8,128)(2,1)} %copy-done.11, f32[1,4096]{1,0:T(1,128)} %bitcast.12), custom_call_target="tpu_custom_call" | custom-call | flops 1100000000 | tf_op jit(solution)/shard_map/norm/pallas_call | solution.py:66
  13.2 6.6 %collective-permute-done.1.refs_2_ = bf16[16,128,128]{2,1,0:T(8,128)(2,1)S(1)} collective-permute-done((bf16[16,128,128]{2,1,0:T(8,128)(2,1)}, bf16[16,128,128]{2,1,0:T(8,128)(2,1)S(1)}, u32[]{:S(2)}, u32[]{:S(2)}) %collective-permute-start.1) | collective-permute-done | bytes 524320 | tf_op jit(solution)/shard_map/ppermute | solution.py:304
  19.8 0.8 copy-done.4
  20.6 1.2 copy-done.1
  21.8 1.0 copy-done.5
  23.2 1.6 collective-permute-start.4
  24.9 1.7 collective-permute-start.5
  26.5 3.8 %norm.2 = (bf16[128,4096]{1,0:T(8,128)(2,1)}, bf16[32,128,128]{2,1,0:T(8,128)(2,1)}, f32[128,128]{1,0:T(8,128)}) custom-call(bf16[128,4096]{1,0:T(8,128)(2,1)} %refs_3_.1, f32[1,4096]{1,0:T(1,128)} %bitcast.13), custom_call_target="tpu_custom_call" | custom-call | flops 1100000000 | tf_op jit(solution)/shard_map/norm/pallas_call | solution.py:66
  30.3 0.6 pad_add_fusion.refs_2_.pos_ref
  30.9 14.3 %grads.2 = (bf16[64,128,128]{2,1,0:T(8,128)(2,1)}, bf16[64,128,128]{2,1,0:T(8,128)(2,1)}, bf16[64,128,128]{2,1,0:T(8,128)(2,1)}) custom-call(s32[512]{0:T(512)} %refs_0_.7, s32[512]{0:T(512)} %refs_1_.5, s32[4]{0:T(128)} %pad_add_fusion.refs_2_.pos_ref, bf16[32,128,128]{2,1,0:T(8,128)(2,1)} %get-tuple-element.37.refs_3_, ...), custom_call_target="tpu_custom_call" | custom-call | flops 2200000000 | tf_op jit(solution)/shard_map/grads/pallas_call | solution.py:126
  45.2 5.5 %collective-permute-done.4.left_ref.refs_0_ = bf16[64,128,128]{2,1,0:T(8,128)(2,1)} collective-permute-done((bf16[64,128,128]{2,1,0:T(8,128)(2,1)S(1)}, bf16[64,128,128]{2,1,0:T(8,128)(2,1)}, u32[]{:S(2)}, u32[]{:S(2)}) %collective-permute-start.4) | collective-permute-done | bytes 2097184 | tf_op jit(solution)/shard_map/ppermute | solution.py:304
  51.0 2.6 %relayed.1 = (bf16[32,128,128]{2,1,0:T(8,128)(2,1)}, bf16[32,128,128]{2,1,0:T(8,128)(2,1)}) custom-call(bf16[64,128,128]{2,1,0:T(8,128)(2,1)} %collective-permute-done.4.left_ref.refs_0_, bf16[64,128,128]{2,1,0:T(8,128)(2,1)} %collective-permute-done.5.right_ref.refs_1_, bf16[64,128,128]{2,1,0:T(8,128)(2,1)} %get-tuple-element.38.tie_ref.refs_7_), custom_call_target="tpu_custom_call" | custom-call | flops 1100000000 | tf_op jit(solution)/shard_map/relayed/pallas_call | solution.py:279
  54.1 1.6 collective-permute-start.7
  55.7 1.7 collective-permute-start.8
  57.3 8.1 %grads.3 = (bf16[64,128,128]{2,1,0:T(8,128)(2,1)}, bf16[64,128,128]{2,1,0:T(8,128)(2,1)}, bf16[64,128,128]{2,1,0:T(8,128)(2,1)}, bf16[64,128,128]{2,1,0:T(8,128)(2,1)}) custom-call(s32[512]{0:T(512)} %refs_0_.7, s32[512]{0:T(512)} %refs_1_.5, s32[4]{0:T(128)} %pad_add_fusion.refs_2_.pos_ref, ...), custom_call_target="tpu_custom_call", output_to_operand_aliasing={{0}: (7, {}), {1}: (8, {}), {2}: (9, {})} | custom-call | flops 2200000000 | tf_op jit(solution)/shard_map/grads/pallas_call | solution.py:126
  65.4 1.5 collective-permute-start.14
  66.9 4.7 %collective-permute-done.7.refs_0_ = bf16[32,128,128]{2,1,0:T(8,128)(2,1)S(1)} collective-permute-done((bf16[32,128,128]{2,1,0:T(8,128)(2,1)}, bf16[32,128,128]{2,1,0:T(8,128)(2,1)S(1)}, u32[]{:S(2)}, u32[]{:S(2)}) %collective-permute-start.7) | collective-permute-done | bytes 1048608 | tf_op jit(solution)/shard_map/ppermute | solution.py:304
  71.6 3.0 %collective-permute-start.15 = (bf16[64,128,128]{2,1,0:T(8,128)(2,1)}, bf16[64,128,128]{2,1,0:T(8,128)(2,1)}, u32[]{:S(2)}, u32[]{:S(2)}) collective-permute-start(bf16[64,128,128]{2,1,0:T(8,128)(2,1)} %get-tuple-element.52), channel_id=1, source_target_pairs={{0,2},{1,3},{2,0},{3,1},{4,68},{5,69},{6,70},{7,71},{8,10},{9,11},... | collective-permute-start | bytes 6291464 | tf_op jit(solution)/shard_map/ppermute | solution.py:304
  74.6 1.1 collective-permute-start.16
  76.4 2.4 %collective-permute-done.12.refs_16_ = bf16[32,128,128]{2,1,0:T(8,128)(2,1)S(1)} collective-permute-done((bf16[32,128,128]{2,1,0:T(8,128)(2,1)}, bf16[32,128,128]{2,1,0:T(8,128)(2,1)S(1)}, u32[]{:S(2)}, u32[]{:S(2)}) %collective-permute-start.12) | collective-permute-done | bytes 1048608 | tf_op jit(solution)/shard_map/ppermute | solution.py:405
  78.8 1.5 collective-permute-done.13.refs_17_
  80.3 1.0 copy-done.10
  81.2 32.0 %project.1 = (bf16[128,14336]{1,0:T(8,128)(2,1)}, bf16[128,4096]{1,0:T(8,128)(2,1)}, f32[32,128]{1,0:T(8,128)}) custom-call(s32[512]{0:T(512)} %refs_0_.7, s32[512]{0:T(512)} %refs_1_.5, s32[4]{0:T(128)} %pad_add_fusion.refs_2_.pos_ref, bf16[128,4096]{1,0:T(8,128)(2,1)} %refs_3_.1, bf16[128,4096]{1,0:T(8,128)(2,1)} %get-tuple-element.34.refs_4_, ...), custom_call_target="tpu_custom_call" | custom-call | flops 2200000000 | tf_op jit(solution)/shard_map/project/pallas_call | solution.py:216
  113.6 2.8 %collective-permute-done.15.refs_2_ = bf16[64,128,128]{2,1,0:T(8,128)(2,1)} collective-permute-done((bf16[64,128,128]{2,1,0:T(8,128)(2,1)}, bf16[64,128,128]{2,1,0:T(8,128)(2,1)}, u32[]{:S(2)}, u32[]{:S(2)}) %collective-permute-start.15) | collective-permute-done | bytes 2097184 | tf_op jit(solution)/shard_map/ppermute | solution.py:304
  116.4 5.6 %collective-permute-done.16.refs_3_ = bf16[64,128,128]{2,1,0:T(8,128)(2,1)} collective-permute-done((bf16[64,128,128]{2,1,0:T(8,128)(2,1)}, bf16[64,128,128]{2,1,0:T(8,128)(2,1)}, u32[]{:S(2)}, u32[]{:S(2)}) %collective-permute-start.16) | collective-permute-done | bytes 2097184 | tf_op jit(solution)/shard_map/ppermute | solution.py:304
  122.1 0.7 copy-done.6
  122.8 4.7 %cut_sum.1 = (bf16[17,128,128]{2,1,0:T(8,128)(2,1)S(1)}, bf16[17,128,128]{2,1,0:T(8,128)(2,1)S(1)}, bf16[17,128,128]{2,1,0:T(8,128)(2,1)S(1)}, bf16[17,128,128]{2,1,0:T(8,128)(2,1)S(1)}) custom-call(bf16[64,128,128]{2,1,0:T(8,128)(2,1)S(1)} %copy-done, bf16[64,128,128]{2,1,0:T(8,128)(2,1)} %collective-permute-done.14.refs_1_, ...), custom_call_target="tpu_custom_call" | custom-call | flops 1100000000 | tf_op jit(solution)/shard_map/cut_sum/pallas_call | solution.py:347
  127.9 2.8 %collective-permute-start.19 = (bf16[17,128,128]{2,1,0:T(8,128)(2,1)S(1)}, bf16[17,128,128]{2,1,0:T(8,128)(2,1)S(1)}, u32[]{:S(2)}, u32[]{:S(2)}) collective-permute-start(bf16[17,128,128]{2,1,0:T(8,128)(2,1)S(1)} %get-tuple-element.56), channel_id=1, source_target_pairs={{0,64},{1,65},{2,66},{3,67},{4,20},{5,21},{6,22},{7,23},{8,72},{9,... | collective-permute-start | bytes 1671176 | tf_op jit(solution)/shard_map/ppermute | solution.py:304
  130.7 1.2 collective-permute-start.20
  131.9 12.4 %collective-permute-done.18.refs_1_ = bf16[17,128,128]{2,1,0:T(8,128)(2,1)S(1)} collective-permute-done((bf16[17,128,128]{2,1,0:T(8,128)(2,1)S(1)}, bf16[17,128,128]{2,1,0:T(8,128)(2,1)S(1)}, u32[]{:S(2)}, u32[]{:S(2)}) %collective-permute-start.18) | collective-permute-done | bytes 557088 | tf_op jit(solution)/shard_map/ppermute | solution.py:304
  144.3 0.9 collective-permute-done.20.refs_3_
  145.5 2.7 %collective-permute-start.21 = (bf16[5,128,128]{2,1,0:T(8,128)(2,1)S(1)}, bf16[5,128,128]{2,1,0:T(8,128)(2,1)S(1)}, u32[]{:S(2)}, u32[]{:S(2)}) collective-permute-start(bf16[5,128,128]{2,1,0:T(8,128)(2,1)S(1)} %get-tuple-element.59), channel_id=1, source_target_pairs={{0,8},{1,9},{2,10},{3,11},{4,5},{5,6},{6,7},{7,4},{8,16},{9,17},{1... | collective-permute-start | bytes 491528 | tf_op jit(solution)/shard_map/ppermute | solution.py:304
  148.2 2.1 %collective-permute-start.22 = (bf16[5,128,128]{2,1,0:T(8,128)(2,1)S(1)}, bf16[5,128,128]{2,1,0:T(8,128)(2,1)S(1)}, u32[]{:S(2)}, u32[]{:S(2)}) collective-permute-start(bf16[5,128,128]{2,1,0:T(8,128)(2,1)S(1)} %get-tuple-element.60), channel_id=1, source_target_pairs={{0,16},{1,17},{2,18},{3,19},{4,6},{5,7},{6,4},{7,5},{8,24},{9,25},... | collective-permute-start | bytes 491528 | tf_op jit(solution)/shard_map/ppermute | solution.py:304
  150.3 1.6 collective-permute-start.23
  152.1 3.2 %collective-permute-done.22.refs_2_ = bf16[5,128,128]{2,1,0:T(8,128)(2,1)S(1)} collective-permute-done((bf16[5,128,128]{2,1,0:T(8,128)(2,1)S(1)}, bf16[5,128,128]{2,1,0:T(8,128)(2,1)S(1)}, u32[]{:S(2)}, u32[]{:S(2)}) %collective-permute-start.22) | collective-permute-done | bytes 163872 | tf_op jit(solution)/shard_map/ppermute | solution.py:304
  155.7 1.4 collective-permute-start.24
  157.1 2.7 %collective-permute-start.25 = (bf16[5,128,128]{2,1,0:T(8,128)(2,1)S(1)}, bf16[5,128,128]{2,1,0:T(8,128)(2,1)S(1)}, u32[]{:S(2)}, u32[]{:S(2)}) collective-permute-start(bf16[5,128,128]{2,1,0:T(8,128)(2,1)S(1)} %next_sum.3.refs_0_), channel_id=1, source_target_pairs={{0,2},{1,3},{2,0},{3,1},{4,6},{5,7},{6,4},{7,5},{8,10},{9,11},{10,... | collective-permute-start | bytes 491528 | tf_op jit(solution)/shard_map/ppermute | solution.py:304
  159.9 0.5 collective-permute-start.26
  160.4 1.9 %collective-permute-done.24.refs_1_ = bf16[5,128,128]{2,1,0:T(8,128)(2,1)S(1)} collective-permute-done((bf16[5,128,128]{2,1,0:T(8,128)(2,1)S(1)}, bf16[5,128,128]{2,1,0:T(8,128)(2,1)S(1)}, u32[]{:S(2)}, u32[]{:S(2)}) %collective-permute-start.24) | collective-permute-done | bytes 163872 | tf_op jit(solution)/shard_map/ppermute | solution.py:304
  162.3 2.6 %collective-permute-done.25.refs_2_ = bf16[5,128,128]{2,1,0:T(8,128)(2,1)S(1)} collective-permute-done((bf16[5,128,128]{2,1,0:T(8,128)(2,1)S(1)}, bf16[5,128,128]{2,1,0:T(8,128)(2,1)S(1)}, u32[]{:S(2)}, u32[]{:S(2)}) %collective-permute-start.25) | collective-permute-done | bytes 163872 | tf_op jit(solution)/shard_map/ppermute | solution.py:304
  165.2 1.6 place.1
  166.8 1.2 collective-permute-done.27
  168.0 0.6 select_bitcast_fusion
  (47 shorter events, 4.4 us)
Async XLA Ops:
  0.6 20.0 %copy-start.3 = (bf16[16,128,128]{2,1,0:T(8,128)(2,1)S(1)}, bf16[16,128,128]{2,1,0:T(8,128)(2,1)}, u32[]{:S(2)}) copy-start(bf16[16,128,128]{2,1,0:T(8,128)(2,1)} %refs_0_.4) | copy-start | bytes 1572868
  0.6 30.2 %collective-permute-start.6 = (bf16[128,14336]{1,0:T(8,128)(2,1)}, bf16[128,14336]{1,0:T(8,128)(2,1)}, u32[]{:S(2)}, u32[]{:S(2)}) collective-permute-start(bf16[128,14336]{1,0:T(8,128)(2,1)} %refs_7_.1), channel_id=1, source_target_pairs={{0,4},{4,0},{1,5},{5,1},{2,6},{6,2},{3,7},{7,3},{8,12},{12,8},{9,1... | collective-permute-start | bytes 11010056 | tf_op jit(solution)/shard_map/ppermute | solution.py:405
  0.7 7.7 %collective-permute-start.3 = (bf16[128,4096]{1,0:T(8,128)(2,1)}, bf16[128,4096]{1,0:T(8,128)(2,1)S(1)}, u32[]{:S(2)}, u32[]{:S(2)}) collective-permute-start(bf16[128,4096]{1,0:T(8,128)(2,1)} %refs_3_.1), channel_id=1, source_target_pairs={{0,4},{4,0},{1,5},{5,1},{2,6},{6,2},{3,7},{7,3},{8,12},{12,8},{9,1... | collective-permute-start | bytes 3145736 | tf_op jit(solution)/shard_map/ppermute | solution.py:405
  1.2 12.0 %collective-permute-start = (bf16[16,128,128]{2,1,0:T(8,128)(2,1)}, bf16[16,128,128]{2,1,0:T(8,128)(2,1)S(1)}, u32[]{:S(2)}, u32[]{:S(2)}) collective-permute-start(bf16[16,128,128]{2,1,0:T(8,128)(2,1)} %refs_0_.4), channel_id=1, source_target_pairs={{0,8},{1,9},{2,10},{3,11},{4,36},{5,37},{6,38},{7,39},{8,16},{9,17... | collective-permute-start | bytes 1572872 | tf_op jit(solution)/shard_map/ppermute | solution.py:304
  3.2 16.6 %collective-permute-start.1 = (bf16[16,128,128]{2,1,0:T(8,128)(2,1)}, bf16[16,128,128]{2,1,0:T(8,128)(2,1)S(1)}, u32[]{:S(2)}, u32[]{:S(2)}) collective-permute-start(bf16[16,128,128]{2,1,0:T(8,128)(2,1)} %refs_0_.4), channel_id=1, source_target_pairs={{0,16},{1,17},{2,18},{3,19},{4,68},{5,69},{6,70},{7,71},{8,24},{9,... | collective-permute-start | bytes 1572872 | tf_op jit(solution)/shard_map/ppermute | solution.py:304
  6.8 13.0 %collective-permute-start.2 = (bf16[16,128,128]{2,1,0:T(8,128)(2,1)}, bf16[16,128,128]{2,1,0:T(8,128)(2,1)S(1)}, u32[]{:S(2)}, u32[]{:S(2)}) collective-permute-start(bf16[16,128,128]{2,1,0:T(8,128)(2,1)} %refs_0_.4), channel_id=1, source_target_pairs={{0,24},{1,25},{2,26},{3,27},{4,100},{5,101},{6,102},{7,103},{8,0},... | collective-permute-start | bytes 1572872 | tf_op jit(solution)/shard_map/ppermute | solution.py:304
  8.5 1.0 copy-start.11
  19.8 0.8 copy-start.4
  20.6 1.2 copy-start.1
  21.8 1.0 copy-start.5
  23.2 22.0 %copy-start.2 = (bf16[4,16,128,128]{3,2,1,0:T(8,128)(2,1)}, bf16[4,16,128,128]{3,2,1,0:T(8,128)(2,1)S(1)}, u32[]{:S(2)}) copy-start(bf16[4,16,128,128]{3,2,1,0:T(8,128)(2,1)S(1)} %joined.1) | copy-start | bytes 6291460
  23.2 27.4 %collective-permute-start.4 = (bf16[64,128,128]{2,1,0:T(8,128)(2,1)S(1)}, bf16[64,128,128]{2,1,0:T(8,128)(2,1)}, u32[]{:S(2)}, u32[]{:S(2)}) collective-permute-start(bf16[64,128,128]{2,1,0:T(8,128)(2,1)S(1)} %bitcast.8), channel_id=1, source_target_pairs={{0,32},{1,33},{2,34},{3,35},{4,12},{5,13},{6,14},{7,15},{8,40},{9,... | collective-permute-start | bytes 6291464 | tf_op jit(solution)/shard_map/ppermute | solution.py:304
  24.9 26.1 %collective-permute-start.5 = (bf16[64,128,128]{2,1,0:T(8,128)(2,1)S(1)}, bf16[64,128,128]{2,1,0:T(8,128)(2,1)}, u32[]{:S(2)}, u32[]{:S(2)}) collective-permute-start(bf16[64,128,128]{2,1,0:T(8,128)(2,1)S(1)} %bitcast.9), channel_id=1, source_target_pairs={{0,96},{1,97},{2,98},{3,99},{4,28},{5,29},{6,30},{7,31},{8,104},{9... | collective-permute-start | bytes 6291464 | tf_op jit(solution)/shard_map/ppermute | solution.py:304
  26.5 38.9 %collective-permute-start.9 = (bf16[64,128,128]{2,1,0:T(8,128)(2,1)S(1)}, bf16[64,128,128]{2,1,0:T(8,128)(2,1)}, u32[]{:S(2)}, u32[]{:S(2)}) collective-permute-start(bf16[64,128,128]{2,1,0:T(8,128)(2,1)S(1)} %bitcast.10), channel_id=1, source_target_pairs={{0,4},{4,0},{1,5},{5,1},{2,6},{6,2},{3,7},{7,3},{8,12},{12,8},{9,1... | collective-permute-start | bytes 6291464 | tf_op jit(solution)/shard_map/ppermute | solution.py:405
  53.6 22.2 %collective-permute-start.10 = (bf16[64,128,128]{2,1,0:T(8,128)(2,1)}, bf16[64,128,128]{2,1,0:T(8,128)(2,1)}, u32[]{:S(2)}, u32[]{:S(2)}) collective-permute-start(bf16[64,128,128]{2,1,0:T(8,128)(2,1)} %get-tuple-element.40.refs_9_), channel_id=1, source_target_pairs={{0,4},{4,0},{1,5},{5,1},{2,6},{6,2},{3,7},{7,3},{8,12},{12,8},{9,1... | collective-permute-start | bytes 6291464 | tf_op jit(solution)/shard_map/ppermute | solution.py:405
  53.6 22.2 %collective-permute-start.11 = (bf16[64,128,128]{2,1,0:T(8,128)(2,1)}, bf16[64,128,128]{2,1,0:T(8,128)(2,1)}, u32[]{:S(2)}, u32[]{:S(2)}) collective-permute-start(bf16[64,128,128]{2,1,0:T(8,128)(2,1)} %get-tuple-element.41.refs_10_), channel_id=1, source_target_pairs={{0,4},{4,0},{1,5},{5,1},{2,6},{6,2},{3,7},{7,3},{8,12},{12,8},{9,1... | collective-permute-start | bytes 6291464 | tf_op jit(solution)/shard_map/ppermute | solution.py:405
  54.1 17.5 %collective-permute-start.7 = (bf16[32,128,128]{2,1,0:T(8,128)(2,1)}, bf16[32,128,128]{2,1,0:T(8,128)(2,1)S(1)}, u32[]{:S(2)}, u32[]{:S(2)}) collective-permute-start(bf16[32,128,128]{2,1,0:T(8,128)(2,1)} %get-tuple-element.39.refs_2_.refs_10_), channel_id=1, source_target_pairs={{0,32},{1,33},{2,34},{3,35},{4,12},{5,13},{6,14},{7,15},{8,40},{9,... | collective-permute-start | bytes 3145736 | tf_op jit(solution)/shard_map/ppermute | solution.py:304
  55.7 19.0 %collective-permute-start.8 = (bf16[32,128,128]{2,1,0:T(8,128)(2,1)}, bf16[32,128,128]{2,1,0:T(8,128)(2,1)}, u32[]{:S(2)}, u32[]{:S(2)}) collective-permute-start(bf16[32,128,128]{2,1,0:T(8,128)(2,1)} %get-tuple-element.42), channel_id=1, source_target_pairs={{0,96},{1,97},{2,98},{3,99},{4,28},{5,29},{6,30},{7,31},{8,104},{9... | collective-permute-start | bytes 3145736 | tf_op jit(solution)/shard_map/ppermute | solution.py:304
  65.4 48.2 %collective-permute-start.14 = (bf16[64,128,128]{2,1,0:T(8,128)(2,1)}, bf16[64,128,128]{2,1,0:T(8,128)(2,1)}, u32[]{:S(2)}, u32[]{:S(2)}) collective-permute-start(bf16[64,128,128]{2,1,0:T(8,128)(2,1)} %get-tuple-element.51), channel_id=1, source_target_pairs={{0,1},{1,2},{2,3},{3,0},{4,36},{5,37},{6,38},{7,39},{8,9},{9,10},{... | collective-permute-start | bytes 6291464 | tf_op jit(solution)/shard_map/ppermute | solution.py:304
  71.6 4.2 %copy-start.8 = (bf16[32,128,128]{2,1,0:T(8,128)(2,1)}, bf16[32,128,128]{2,1,0:T(8,128)(2,1)S(1)}, u32[]{:S(2)}) copy-start(bf16[32,128,128]{2,1,0:T(8,128)(2,1)S(1)} %collective-permute-done.7.refs_0_) | copy-start | bytes 3145732
  71.6 44.8 %collective-permute-start.15 = (bf16[64,128,128]{2,1,0:T(8,128)(2,1)}, bf16[64,128,128]{2,1,0:T(8,128)(2,1)}, u32[]{:S(2)}, u32[]{:S(2)}) collective-permute-start(bf16[64,128,128]{2,1,0:T(8,128)(2,1)} %get-tuple-element.52), channel_id=1, source_target_pairs={{0,2},{1,3},{2,0},{3,1},{4,68},{5,69},{6,70},{7,71},{8,10},{9,11},... | collective-permute-start | bytes 6291464 | tf_op jit(solution)/shard_map/ppermute | solution.py:304
  74.6 47.4 %collective-permute-start.16 = (bf16[64,128,128]{2,1,0:T(8,128)(2,1)}, bf16[64,128,128]{2,1,0:T(8,128)(2,1)}, u32[]{:S(2)}, u32[]{:S(2)}) collective-permute-start(bf16[64,128,128]{2,1,0:T(8,128)(2,1)} %get-tuple-element.45.refs_2_), channel_id=1, source_target_pairs={{0,3},{1,0},{2,1},{3,2},{4,100},{5,101},{6,102},{7,103},{8,11},{9,... | collective-permute-start | bytes 6291464 | tf_op jit(solution)/shard_map/ppermute | solution.py:304
  75.8 3.0 %collective-permute-start.12 = (bf16[32,128,128]{2,1,0:T(8,128)(2,1)}, bf16[32,128,128]{2,1,0:T(8,128)(2,1)S(1)}, u32[]{:S(2)}, u32[]{:S(2)}) collective-permute-start(bf16[32,128,128]{2,1,0:T(8,128)(2,1)} %get-tuple-element.46.refs_11_), channel_id=1, source_target_pairs={{0,4},{4,0},{1,5},{5,1},{2,6},{6,2},{3,7},{7,3},{8,12},{12,8},{9,1... | collective-permute-start | bytes 3145736 | tf_op jit(solution)/shard_map/ppermute | solution.py:405
  75.9 4.4 %collective-permute-start.13 = (bf16[32,128,128]{2,1,0:T(8,128)(2,1)}, bf16[32,128,128]{2,1,0:T(8,128)(2,1)S(1)}, u32[]{:S(2)}, u32[]{:S(2)}) collective-permute-start(bf16[32,128,128]{2,1,0:T(8,128)(2,1)} %get-tuple-element.47.refs_12_), channel_id=1, source_target_pairs={{0,4},{4,0},{1,5},{5,1},{2,6},{6,2},{3,7},{7,3},{8,12},{12,8},{9,1... | collective-permute-start | bytes 3145736 | tf_op jit(solution)/shard_map/ppermute | solution.py:405
  78.8 2.5 %copy-start.9 = (bf16[32,128,128]{2,1,0:T(8,128)(2,1)}, bf16[32,128,128]{2,1,0:T(8,128)(2,1)S(1)}, u32[]{:S(2)}) copy-start(bf16[32,128,128]{2,1,0:T(8,128)(2,1)S(1)} %collective-permute-done.12.refs_16_) | copy-start | bytes 3145732
  80.3 1.0 copy-start.10
  81.2 40.9 %copy-start = (bf16[64,128,128]{2,1,0:T(8,128)(2,1)S(1)}, bf16[64,128,128]{2,1,0:T(8,128)(2,1)}, u32[]{:S(2)}) copy-start(bf16[64,128,128]{2,1,0:T(8,128)(2,1)} %get-tuple-element.50.refs_0_) | copy-start | bytes 6291460
  113.2 8.8 %collective-permute-start.17 = (f32[32,128]{1,0:T(8,128)}, f32[32,128]{1,0:T(8,128)S(1)}, u32[]{:S(2)}, u32[]{:S(2)}) collective-permute-start(f32[32,128]{1,0:T(8,128)} %get-tuple-element.53.refs_4_), channel_id=1, source_target_pairs={{0,4},{4,0},{1,5},{5,1},{2,6},{6,2},{3,7},{7,3},{8,12},{12,8},{9,1... | collective-permute-start | bytes 49160 | tf_op jit(solution)/shard_map/ppermute | solution.py:405
  122.1 0.7 copy-start.6
  127.5 16.8 %collective-permute-start.18 = (bf16[17,128,128]{2,1,0:T(8,128)(2,1)S(1)}, bf16[17,128,128]{2,1,0:T(8,128)(2,1)S(1)}, u32[]{:S(2)}, u32[]{:S(2)}) collective-permute-start(bf16[17,128,128]{2,1,0:T(8,128)(2,1)S(1)} %get-tuple-element.55), channel_id=1, source_target_pairs={{0,32},{1,33},{2,34},{3,35},{4,12},{5,13},{6,14},{7,15},{8,40},{9,... | collective-permute-start | bytes 1671176 | tf_op jit(solution)/shard_map/ppermute | solution.py:304
  127.9 16.3 %collective-permute-start.19 = (bf16[17,128,128]{2,1,0:T(8,128)(2,1)S(1)}, bf16[17,128,128]{2,1,0:T(8,128)(2,1)S(1)}, u32[]{:S(2)}, u32[]{:S(2)}) collective-permute-start(bf16[17,128,128]{2,1,0:T(8,128)(2,1)S(1)} %get-tuple-element.56), channel_id=1, source_target_pairs={{0,64},{1,65},{2,66},{3,67},{4,20},{5,21},{6,22},{7,23},{8,72},{9,... | collective-permute-start | bytes 1671176 | tf_op jit(solution)/shard_map/ppermute | solution.py:304
  130.7 14.5 %collective-permute-start.20 = (bf16[17,128,128]{2,1,0:T(8,128)(2,1)S(1)}, bf16[17,128,128]{2,1,0:T(8,128)(2,1)S(1)}, u32[]{:S(2)}, u32[]{:S(2)}) collective-permute-start(bf16[17,128,128]{2,1,0:T(8,128)(2,1)S(1)} %get-tuple-element.57), channel_id=1, source_target_pairs={{0,96},{1,97},{2,98},{3,99},{4,28},{5,29},{6,30},{7,31},{8,104},{9... | collective-permute-start | bytes 1671176 | tf_op jit(solution)/shard_map/ppermute | solution.py:304
  145.5 19.7 %copy-start.7 = (s32[4]{0:T(128)S(1)}, s32[4]{0:T(128)}, u32[]{:S(2)}) copy-start(s32[4]{0:T(128)} %pad_add_fusion.refs_2_.pos_ref) | copy-start | bytes 52
  145.5 6.6 %collective-permute-start.21 = (bf16[5,128,128]{2,1,0:T(8,128)(2,1)S(1)}, bf16[5,128,128]{2,1,0:T(8,128)(2,1)S(1)}, u32[]{:S(2)}, u32[]{:S(2)}) collective-permute-start(bf16[5,128,128]{2,1,0:T(8,128)(2,1)S(1)} %get-tuple-element.59), channel_id=1, source_target_pairs={{0,8},{1,9},{2,10},{3,11},{4,5},{5,6},{6,7},{7,4},{8,16},{9,17},{1... | collective-permute-start | bytes 491528 | tf_op jit(solution)/shard_map/ppermute | solution.py:304
  148.2 7.2 %collective-permute-start.22 = (bf16[5,128,128]{2,1,0:T(8,128)(2,1)S(1)}, bf16[5,128,128]{2,1,0:T(8,128)(2,1)S(1)}, u32[]{:S(2)}, u32[]{:S(2)}) collective-permute-start(bf16[5,128,128]{2,1,0:T(8,128)(2,1)S(1)} %get-tuple-element.60), channel_id=1, source_target_pairs={{0,16},{1,17},{2,18},{3,19},{4,6},{5,7},{6,4},{7,5},{8,24},{9,25},... | collective-permute-start | bytes 491528 | tf_op jit(solution)/shard_map/ppermute | solution.py:304
  150.3 5.3 %collective-permute-start.23 = (bf16[5,128,128]{2,1,0:T(8,128)(2,1)S(1)}, bf16[5,128,128]{2,1,0:T(8,128)(2,1)S(1)}, u32[]{:S(2)}, u32[]{:S(2)}) collective-permute-start(bf16[5,128,128]{2,1,0:T(8,128)(2,1)S(1)} %get-tuple-element.61), channel_id=1, source_target_pairs={{0,24},{1,25},{2,26},{3,27},{4,7},{5,4},{6,5},{7,6},{8,0},{9,1},{1... | collective-permute-start | bytes 491528 | tf_op jit(solution)/shard_map/ppermute | solution.py:304
  155.7 6.6 %collective-permute-start.24 = (bf16[5,128,128]{2,1,0:T(8,128)(2,1)S(1)}, bf16[5,128,128]{2,1,0:T(8,128)(2,1)S(1)}, u32[]{:S(2)}, u32[]{:S(2)}) collective-permute-start(bf16[5,128,128]{2,1,0:T(8,128)(2,1)S(1)} %next_sum.3.refs_0_), channel_id=1, source_target_pairs={{0,1},{1,2},{2,3},{3,0},{4,5},{5,6},{6,7},{7,4},{8,9},{9,10},{10,1... | collective-permute-start | bytes 491528 | tf_op jit(solution)/shard_map/ppermute | solution.py:304
  157.1 7.8 %collective-permute-start.25 = (bf16[5,128,128]{2,1,0:T(8,128)(2,1)S(1)}, bf16[5,128,128]{2,1,0:T(8,128)(2,1)S(1)}, u32[]{:S(2)}, u32[]{:S(2)}) collective-permute-start(bf16[5,128,128]{2,1,0:T(8,128)(2,1)S(1)} %next_sum.3.refs_0_), channel_id=1, source_target_pairs={{0,2},{1,3},{2,0},{3,1},{4,6},{5,7},{6,4},{7,5},{8,10},{9,11},{10,... | collective-permute-start | bytes 491528 | tf_op jit(solution)/shard_map/ppermute | solution.py:304
  159.9 5.3 %collective-permute-start.26 = (bf16[5,128,128]{2,1,0:T(8,128)(2,1)S(1)}, bf16[5,128,128]{2,1,0:T(8,128)(2,1)S(1)}, u32[]{:S(2)}, u32[]{:S(2)}) collective-permute-start(bf16[5,128,128]{2,1,0:T(8,128)(2,1)S(1)} %next_sum.3.refs_0_), channel_id=1, source_target_pairs={{0,3},{1,0},{2,1},{3,2},{4,7},{5,4},{6,5},{7,6},{8,11},{9,8},{10,9... | collective-permute-start | bytes 491528 | tf_op jit(solution)/shard_map/ppermute | solution.py:304
  166.8 1.2 collective-permute-start.27
